TPU v7x, 32 devices: a whole 2x2x4 slice. The times are simulated.
32 devices in a mesh: ctx: 8 (over y, x, core), fsdp: 4 (over z).
Axes of the slice: x: 2, y: 2, z: 4, core: 2. Of those that a mesh axis runs over, the one named last changes fastest.
Arguments:
- hidden: bfloat16 [4, 2, 2048, 768], P('fsdp', None, 'ctx'), may hold values from -6 to 6
- noise_mask: int32 [4, 2048], P('fsdp', 'ctx'), may hold values 0 or 1
- doc_lengths: int32 [4, 16], P('fsdp'), may hold values from 1 to 1024, 2048 in all within a row
- w_qkv: bfloat16 [768, 2304], P('fsdp'), may hold values from -0.21875 to 0.21875
- w_out: bfloat16 [768, 768], P('fsdp'), may hold values from -1.25 to 1.25
- w_up: bfloat16 [768, 3072], P('fsdp'), may hold values from -0.21875 to 0.21875
- b_up: bfloat16 [3072], P('fsdp'), may hold values from -3 to 3
- w_down: bfloat16 [3072, 768], P('fsdp'), may hold values from -0.109375 to 0.109375
- b_down: bfloat16 [768], P('fsdp'), may hold values from -2 to 2
- gain_one: bfloat16 [768], P('fsdp'), may hold values from 0.25 to 1.75
- gain_two: bfloat16 [768], P('fsdp'), may hold values from 0.25 to 1.75
- mask_embed: bfloat16 [768], P('fsdp'), may hold values from -5 to 5
- out_grad: bfloat16 [4, 2, 2048, 768], P('fsdp', None, 'ctx'), may hold values from -6 to 6
Outputs:
- layer_out: bfloat16 [4, 2, 2048, 768], P('fsdp', None, 'ctx')
- input_grad: bfloat16 [4, 2, 2048, 768], P('fsdp', None, 'ctx')
- grad_qkv: float32 [768, 2304], P(('ctx', 'fsdp'))
- grad_out: float32 [768, 768], P(('ctx', 'fsdp'))
- grad_up: float32 [768, 3072], P(('ctx', 'fsdp'))
- grad_up_bias: float32 [3072], P(('ctx', 'fsdp'))
- grad_down: float32 [3072, 768], P(('ctx', 'fsdp'))
- grad_down_bias: float32 [768], P(('ctx', 'fsdp'))
- grad_gain_one: float32 [768], P(('ctx', 'fsdp'))
- grad_gain_two: float32 [768], P(('ctx', 'fsdp'))
- grad_mask_embed: float32 [768], P(('ctx', 'fsdp'))
Inputs may be any that keep to these rules, and one draw needn't show every extreme that they name: Each row of doc_lengths sums to 2048, and its longest document has exactly 1024 positions.
All inputs are finite; a program needn't handle non-finite values. No bound on the sum of `noise_mask` on one device may be relied on, other than what follows from the above.
Results may differ from a plain program's by a relative error of at most 0.015.
Values may be sent and summed in bfloat16 or wider, within the bound.
No kernel may reach another device: no remote copies, remote signals or barrier semaphores. Data moves between devices by JAX's collectives and lax.ppermute only.
A program may use at most 256 MiB of HBM per device.

v0:
```python
import math

import jax
import jax.numpy as jnp
from jax import lax
from jax.sharding import PartitionSpec as P

HEADS = 12
HEAD_DIM = 64
BLOCK = 16


LOWEST = -1e30
EPSILON = 1e-05


def layer_norm(inputs, gain):
    average = jnp.mean(inputs, axis=-1, keepdims=True)
    centered = inputs - average
    variance = jnp.mean(centered * centered, axis=-1, keepdims=True)
    return centered * lax.rsqrt(variance + EPSILON) * gain


def rotary_angles(positions):
    half_dim = HEAD_DIM // 2
    frequency = jnp.exp(
        jnp.arange(half_dim).astype(jnp.float32) * (-2.0 * math.log(10000.0) / HEAD_DIM)
    )
    return positions.astype(jnp.float32)[:, None] * frequency[None, :]


def rotate(heads_in, angles):
    half_dim = heads_in.shape[-1] // 2
    cosine = jnp.cos(angles)[:, None, :]
    sine_part = jnp.sin(angles)[:, None, :]
    first_half = heads_in[..., :half_dim]
    second_half = heads_in[..., half_dim:]
    return jnp.concatenate(
        [
            first_half * cosine - second_half * sine_part,
            second_half * cosine + first_half * sine_part,
        ],
        axis=-1,
    )


def segment_of(positions, doc_ends):
    return jnp.sum((positions[:, None] >= doc_ends[None, :]).astype(jnp.int32), axis=1)


def visible(query_stream, query_position, query_segment, key_stream, key_position, key_segment):
    query_block = query_position // BLOCK
    key_block = key_position // BLOCK
    same_doc = query_segment[:, None] == key_segment[None, :]
    clean_key = key_stream[None, :] == 0
    noisy_query = query_stream[:, None] == 1
    before = key_block[None, :] < query_block[:, None]
    same_block = key_block[None, :] == query_block[:, None]
    from_clean = clean_key & (before | same_block & jnp.logical_not(noisy_query))
    from_noisy = jnp.logical_not(clean_key) & noisy_query & same_block
    return same_doc & (from_clean | from_noisy)


def mix_tile(running, query_rows, key_tile, value_tile, allowed):
    run_max, run_sum, accum = running
    scores = (
        jnp.einsum("qhd,khd->hqk", query_rows, key_tile, preferred_element_type=jnp.float32) * 0.125
    )
    masked = jnp.where(allowed[None], scores, LOWEST)
    new_max = jnp.maximum(run_max, jnp.max(masked, axis=-1))
    exp_terms = jnp.where(allowed[None], jnp.exp(masked - new_max[..., None]), 0.0)
    factor = jnp.exp(run_max - new_max)
    new_sum = run_sum * factor + jnp.sum(exp_terms, axis=-1)
    accum = accum * factor[..., None] + jnp.einsum(
        "hqk,khd->hqd",
        exp_terms.astype(jnp.bfloat16),
        value_tile,
        preferred_element_type=jnp.float32,
    )
    return (new_max, new_sum, accum)


def tile_grads(query_rows, key_tile, value_tile, allowed, row_max, scaled_grad, correction):
    scores = (
        jnp.einsum("qhd,khd->hqk", query_rows, key_tile, preferred_element_type=jnp.float32) * 0.125
    )
    masked = jnp.where(allowed[None], scores, LOWEST)
    exp_terms = jnp.where(allowed[None], jnp.exp(masked - row_max[..., None]), 0.0)
    prob_grad = jnp.einsum(
        "hqd,khd->hqk", scaled_grad, value_tile, preferred_element_type=jnp.float32
    )
    score_grad = (exp_terms * (prob_grad - correction[..., None])).astype(jnp.bfloat16)
    query_part = jnp.einsum(
        "hqk,khd->qhd", score_grad, key_tile, preferred_element_type=jnp.float32
    )
    key_part = jnp.einsum(
        "hqk,qhd->khd", score_grad, query_rows, preferred_element_type=jnp.float32
    )
    value_part = jnp.einsum(
        "hqk,hqd->khd",
        exp_terms.astype(jnp.bfloat16),
        scaled_grad,
        preferred_element_type=jnp.float32,
    )
    return (query_part, key_part, value_part)


def build_inputs(hidden, noise_row, mask_row):
    clean_rows = hidden[0, 0].astype(jnp.float32)
    noisy_rows = jnp.where(
        noise_row[:, None] == 1,
        mask_row.astype(jnp.float32)[None, :],
        hidden[0, 1].astype(jnp.float32),
    )
    return jnp.concatenate([clean_rows, noisy_rows], axis=0)


def project(inputs, gathered, angles):
    row_count = inputs.shape[0]
    model_dim = inputs.shape[1]
    normed = layer_norm(inputs, gathered[6].astype(jnp.float32)).astype(jnp.bfloat16)
    projected = jnp.dot(normed, gathered[0], preferred_element_type=jnp.float32)
    query_rows = rotate(
        projected[:, :model_dim].reshape(row_count, HEADS, HEAD_DIM), angles
    ).astype(jnp.bfloat16)
    key_rows = rotate(
        projected[:, model_dim : 2 * model_dim].reshape(row_count, HEADS, HEAD_DIM), angles
    ).astype(jnp.bfloat16)
    value_rows = (
        projected[:, 2 * model_dim :].reshape(row_count, HEADS, HEAD_DIM).astype(jnp.bfloat16)
    )
    return (normed, query_rows, key_rows, value_rows)


def upper_half(inputs, attended_low, gathered):
    middle = inputs + jnp.dot(attended_low, gathered[1], preferred_element_type=jnp.float32)
    normed_two = layer_norm(middle, gathered[7].astype(jnp.float32)).astype(jnp.bfloat16)
    upper = jnp.dot(normed_two, gathered[2], preferred_element_type=jnp.float32) + gathered[
        3
    ].astype(jnp.float32)
    activated = jax.nn.gelu(upper, approximate=True).astype(jnp.bfloat16)
    return (middle, normed_two, upper, activated)


def shards(
    hidden,
    noise_mask,
    doc_lengths,
    w_qkv,
    w_out,
    w_up,
    b_up,
    w_down,
    b_down,
    gain_one,
    gain_two,
    mask_embed,
    out_grad,
):
    own_params = (w_qkv, w_out, w_up, b_up, w_down, b_down, gain_one, gain_two, mask_embed)
    local_count = hidden.shape[2]
    model_dim = hidden.shape[3]
    row_count = 2 * local_count
    ctx_index = lax.axis_index("ctx")
    offset = ctx_index * local_count
    local_place = offset + jnp.arange(local_count, dtype=jnp.int32)
    positions = jnp.concatenate([local_place, local_place])
    stream = jnp.concatenate(
        [jnp.zeros((local_count,), jnp.int32), jnp.ones((local_count,), jnp.int32)]
    )
    doc_ends = jnp.cumsum(doc_lengths[0])
    segments = segment_of(positions, doc_ends)
    angles = rotary_angles(positions)
    noise_row = noise_mask[0]
    noisy_stream = stream[local_count:]
    noisy_allowed = visible(
        stream, positions, segments, noisy_stream, positions[local_count:], segments[local_count:]
    )
    gathered = (
        lax.all_gather(own_params[0], "fsdp", axis=0, tiled=True),
        lax.all_gather(own_params[1], "fsdp", axis=0, tiled=True),
        lax.all_gather(own_params[2], "fsdp", axis=0, tiled=True),
        lax.all_gather(own_params[3], "fsdp", axis=0, tiled=True),
        lax.all_gather(own_params[4], "fsdp", axis=0, tiled=True),
        lax.all_gather(own_params[5], "fsdp", axis=0, tiled=True),
        lax.all_gather(own_params[6], "fsdp", axis=0, tiled=True),
        lax.all_gather(own_params[7], "fsdp", axis=0, tiled=True),
        lax.all_gather(own_params[8], "fsdp", axis=0, tiled=True),
    )
    inputs = build_inputs(hidden, noise_row, gathered[8])
    normed, query_rows, key_rows, value_rows = project(inputs, gathered, angles)
    clean_keys = key_rows[:local_count].reshape(local_count, model_dim)
    clean_values = value_rows[:local_count].reshape(local_count, model_dim)
    start_state = (
        jnp.full((HEADS, row_count), LOWEST, jnp.float32),
        jnp.zeros((HEADS, row_count), jnp.float32),
        jnp.zeros((HEADS, row_count, HEAD_DIM), jnp.float32),
    )
    running = start_state
    piece_keys = lax.all_gather(clean_keys, "ctx", axis=0, tiled=True)
    piece_values = lax.all_gather(clean_values, "ctx", axis=0, tiled=True)
    piece_rows = piece_keys.shape[0]
    fold_tile_size = math.gcd(piece_rows, 512)

    def step(carried, tile_index):
        tile_start = tile_index * fold_tile_size
        key_tile = lax.dynamic_slice_in_dim(piece_keys, tile_start, fold_tile_size, 0).reshape(
            fold_tile_size, HEADS, HEAD_DIM
        )
        value_tile = lax.dynamic_slice_in_dim(piece_values, tile_start, fold_tile_size, 0).reshape(
            fold_tile_size, HEADS, HEAD_DIM
        )
        key_position = tile_start + jnp.arange(fold_tile_size, dtype=jnp.int32)
        allowed = visible(
            stream,
            positions,
            segments,
            jnp.zeros((fold_tile_size,), jnp.int32),
            key_position,
            segment_of(key_position, doc_ends),
        )
        carried = lax.cond(
            jnp.any(allowed),
            lambda held: mix_tile(held, query_rows, key_tile, value_tile, allowed),
            lambda held: held,
            carried,
        )
        return (carried, None)

    running, _ = lax.scan(step, running, jnp.arange(piece_rows // fold_tile_size))
    run_max, run_sum, accum = mix_tile(
        running, query_rows, key_rows[local_count:], value_rows[local_count:], noisy_allowed
    )
    attended = accum / run_sum[..., None]
    attended_low = (
        jnp.transpose(attended, (1, 0, 2)).reshape(row_count, model_dim).astype(jnp.bfloat16)
    )
    middle, normed_two, upper, activated = upper_half(inputs, attended_low, gathered)
    result = (
        middle
        + jnp.dot(activated, gathered[4], preferred_element_type=jnp.float32)
        + gathered[5].astype(jnp.float32)
    )
    layer_out = result.astype(jnp.bfloat16).reshape(1, 2, local_count, model_dim)
    again = (
        lax.all_gather(own_params[0], "fsdp", axis=0, tiled=True),
        lax.all_gather(own_params[1], "fsdp", axis=0, tiled=True),
        lax.all_gather(own_params[2], "fsdp", axis=0, tiled=True),
        lax.all_gather(own_params[3], "fsdp", axis=0, tiled=True),
        lax.all_gather(own_params[4], "fsdp", axis=0, tiled=True),
        lax.all_gather(own_params[5], "fsdp", axis=0, tiled=True),
        lax.all_gather(own_params[6], "fsdp", axis=0, tiled=True),
        lax.all_gather(own_params[7], "fsdp", axis=0, tiled=True),
        lax.all_gather(own_params[8], "fsdp", axis=0, tiled=True),
    )
    normed, query_rows, key_rows, value_rows = project(inputs, again, angles)
    noisy_keys = key_rows[local_count:]
    noisy_values = value_rows[local_count:]
    middle, normed_two, upper, activated = upper_half(inputs, attended_low, again)
    grad_rows = out_grad[0].reshape(row_count, model_dim)
    grad_float = grad_rows.astype(jnp.float32)
    grad_down = jnp.einsum("qi,qj->ij", activated, grad_rows, preferred_element_type=jnp.float32)
    grad_down_bias = jnp.sum(grad_float, axis=0)
    activated_grad = jnp.einsum(
        "qj,ij->qi", grad_rows, again[4], preferred_element_type=jnp.float32
    )
    _, gelu_pull = jax.vjp(lambda upper_in: jax.nn.gelu(upper_in, approximate=True), upper)
    upper_grad = gelu_pull(activated_grad)[0].astype(jnp.bfloat16)
    grad_up = jnp.einsum("qi,qj->ij", normed_two, upper_grad, preferred_element_type=jnp.float32)
    grad_up_bias = jnp.sum(upper_grad.astype(jnp.float32), axis=0)
    normed_two_grad = jnp.einsum(
        "qj,ij->qi", upper_grad, again[2], preferred_element_type=jnp.float32
    )
    _, second_pull = jax.vjp(layer_norm, middle, again[7].astype(jnp.float32))
    middle_norm_grad, grad_gain_two = second_pull(normed_two_grad)
    middle_grad = (grad_float + middle_norm_grad).astype(jnp.bfloat16)
    grad_out_proj = jnp.einsum(
        "qi,qj->ij", attended_low, middle_grad, preferred_element_type=jnp.float32
    )
    attended_grad = jnp.einsum(
        "qj,ij->qi", middle_grad, again[1], preferred_element_type=jnp.float32
    )
    attended_grad = jnp.transpose(attended_grad.reshape(row_count, HEADS, HEAD_DIM), (1, 0, 2))
    scaled_grad = (attended_grad / run_sum[..., None]).astype(jnp.bfloat16)
    correction = jnp.sum(attended_grad * attended, axis=-1) / run_sum
    pair_rows = (
        lax.all_gather(
            key_rows[:local_count].reshape(local_count, model_dim), "ctx", axis=0, tiled=True
        ),
        lax.all_gather(
            value_rows[:local_count].reshape(local_count, model_dim), "ctx", axis=0, tiled=True
        ),
    )
    pair_keys, pair_values = pair_rows
    total_rows = pair_keys.shape[0]
    tile_size = math.gcd(total_rows, 512)
    zero_tile = jnp.zeros((tile_size, HEADS, HEAD_DIM), jnp.float32)

    def back_step(query_acc, tile_index):
        tile_start = tile_index * tile_size
        key_tile = lax.dynamic_slice_in_dim(pair_keys, tile_start, tile_size, 0).reshape(
            tile_size, HEADS, HEAD_DIM
        )
        value_tile = lax.dynamic_slice_in_dim(pair_values, tile_start, tile_size, 0).reshape(
            tile_size, HEADS, HEAD_DIM
        )
        key_position = tile_start + jnp.arange(tile_size, dtype=jnp.int32)
        allowed = visible(
            stream,
            positions,
            segments,
            jnp.zeros((tile_size,), jnp.int32),
            key_position,
            segment_of(key_position, doc_ends),
        )

        def live_tile(held):
            query_part, key_part, value_part = tile_grads(
                query_rows, key_tile, value_tile, allowed, run_max, scaled_grad, correction
            )
            return (held + query_part, key_part, value_part)

        query_acc, key_part, value_part = lax.cond(
            jnp.any(allowed), live_tile, lambda held: (held, zero_tile, zero_tile), query_acc
        )
        return (
            query_acc,
            (key_part.reshape(tile_size, model_dim), value_part.reshape(tile_size, model_dim)),
        )

    query_acc, (key_terms, value_terms) = lax.scan(
        back_step,
        jnp.zeros((row_count, HEADS, HEAD_DIM), jnp.float32),
        jnp.arange(total_rows // tile_size),
    )
    key_terms = key_terms.reshape(total_rows, model_dim)
    value_terms = value_terms.reshape(total_rows, model_dim)
    clean_key_grad, clean_value_grad = (
        lax.psum_scatter(
            key_terms.astype(jnp.bfloat16), "ctx", scatter_dimension=0, tiled=True
        ).astype(jnp.float32),
        lax.psum_scatter(
            value_terms.astype(jnp.bfloat16), "ctx", scatter_dimension=0, tiled=True
        ).astype(jnp.float32),
    )
    query_part, noisy_key_part, noisy_value_part = tile_grads(
        query_rows, noisy_keys, noisy_values, noisy_allowed, run_max, scaled_grad, correction
    )
    query_grad = (query_acc + query_part) * 0.125
    key_grad = (
        jnp.concatenate(
            [clean_key_grad.reshape(local_count, HEADS, HEAD_DIM), noisy_key_part], axis=0
        )
        * 0.125
    )
    value_grad = jnp.concatenate(
        [clean_value_grad.reshape(local_count, HEADS, HEAD_DIM), noisy_value_part], axis=0
    )
    _, rotate_pull = jax.vjp(lambda heads_in: rotate(heads_in, angles), query_grad)
    query_raw_grad = rotate_pull(query_grad)[0]
    key_raw_grad = rotate_pull(key_grad)[0]
    projected_grad = jnp.concatenate(
        [
            query_raw_grad.reshape(row_count, model_dim),
            key_raw_grad.reshape(row_count, model_dim),
            value_grad.reshape(row_count, model_dim),
        ],
        axis=1,
    ).astype(jnp.bfloat16)
    grad_qkv = jnp.einsum("qi,qj->ij", normed, projected_grad, preferred_element_type=jnp.float32)
    normed_grad = jnp.einsum(
        "qj,ij->qi", projected_grad, again[0], preferred_element_type=jnp.float32
    )
    _, first_pull = jax.vjp(layer_norm, inputs, again[6].astype(jnp.float32))
    inputs_norm_grad, grad_gain_one = first_pull(normed_grad)
    inputs_grad = middle_grad.astype(jnp.float32) + inputs_norm_grad
    noisy_flag = (noise_row == 1)[:, None]
    noisy_grad = inputs_grad[local_count:]
    grad_mask = jnp.sum(jnp.where(noisy_flag, noisy_grad, 0.0), axis=0)
    input_grad = jnp.concatenate(
        [inputs_grad[:local_count], jnp.where(noisy_flag, 0.0, noisy_grad)], axis=0
    )
    input_grad = input_grad.astype(jnp.bfloat16).reshape(1, 2, local_count, model_dim)
    shares = (
        lax.psum_scatter(grad_qkv, ("ctx", "fsdp"), scatter_dimension=0, tiled=True),
        lax.psum_scatter(grad_out_proj, ("ctx", "fsdp"), scatter_dimension=0, tiled=True),
        lax.psum_scatter(grad_up, ("ctx", "fsdp"), scatter_dimension=0, tiled=True),
        lax.psum_scatter(grad_up_bias, ("ctx", "fsdp"), scatter_dimension=0, tiled=True),
        lax.psum_scatter(grad_down, ("ctx", "fsdp"), scatter_dimension=0, tiled=True),
        lax.psum_scatter(grad_down_bias, ("ctx", "fsdp"), scatter_dimension=0, tiled=True),
        lax.psum_scatter(grad_gain_one, ("ctx", "fsdp"), scatter_dimension=0, tiled=True),
        lax.psum_scatter(grad_gain_two, ("ctx", "fsdp"), scatter_dimension=0, tiled=True),
        lax.psum_scatter(grad_mask, ("ctx", "fsdp"), scatter_dimension=0, tiled=True),
    )
    (
        qkv_share,
        out_share,
        up_share,
        up_bias_share,
        down_share,
        down_bias_share,
        gain_one_share,
        gain_two_share,
        mask_share,
    ) = shares
    return (
        layer_out,
        input_grad,
        qkv_share,
        out_share,
        up_share,
        up_bias_share,
        down_share,
        down_bias_share,
        gain_one_share,
        gain_two_share,
        mask_share,
    )


def solution(mesh):
    placed = (
        P("fsdp", None, "ctx", None),
        P("fsdp", "ctx"),
        P("fsdp", None),
        P("fsdp", None),
        P("fsdp", None),
        P("fsdp", None),
        P("fsdp"),
        P("fsdp", None),
        P("fsdp"),
        P("fsdp"),
        P("fsdp"),
        P("fsdp"),
        P("fsdp", None, "ctx", None),
    )
    return jax.shard_map(
        shards,
        mesh=mesh,
        in_specs=placed,
        out_specs=(
            P("fsdp", None, "ctx", None),
            P("fsdp", None, "ctx", None),
            P(("ctx", "fsdp"), None),
            P(("ctx", "fsdp"), None),
            P(("ctx", "fsdp"), None),
            P(("ctx", "fsdp")),
            P(("ctx", "fsdp"), None),
            P(("ctx", "fsdp")),
            P(("ctx", "fsdp")),
            P(("ctx", "fsdp")),
            P(("ctx", "fsdp")),
        ),
        check_vma=False,
    )
```

profile of v0, /device:TPU:0, one launch (start us, length us, event | category | flops | bytes accessed | tf_op | source)
XLA Modules:
  0.0 1109.6 jit_solution(16105895583128936063)
XLA Ops:
  13.2 14.4 %all-reduce.14 = (bf16[768]{0:T(1024)(128)(2,1)S(1)}, bf16[768]{0:T(1024)(128)(2,1)S(1)}, bf16[768]{0:T(1024)(128)(2,1)}, bf16[768]{0:T(1024)(128)(2,1)S(1)}) all-reduce(bf16[768]{0:T(1024)(128)(2,1)S(1)} %dynamic-update-slice.1, bf16[768]{0:T(1024)(128)(2,1)S(1)} %dynamic-update-slice, ...), channel_id=1, replica_groups=mesh['ctx'=8,'fsdp'=4] {'fsdp'}, use_global_device_ids=true, to_apply=%add.5 | all-reduce | flops 3072 | bytes 12288
  29.4 1.4 convert_select_fusion
  31.9 50.5 %all-gather.8.cloned.1.call-done = bf16[768,2304]{1,0:T(8,128)(2,1)} async-done(((bf16[192,2304]{1,0:T(8,128)(2,1)}), bf16[768,2304]{1,0:T(8,128)(2,1)}) %all-gather.8.cloned.1.call-update) | async-done | bytes 3538960 | tf_op jit(solution)/shard_map/all_gather | solution.py:180
  82.4 6.2 fusion.71
  91.3 3.8 fusion.68
  95.1 1.9 copy.93
  97.1 3.0 copy.92
  100.1 2.9 subtract_convert_fusion
  112.8 13.2 %all-gather = bf16[4,1,768]{2,1,0:T(2,128)(2,1)S(1)} all-gather(bf16[1,1,768]{2,1,0:T(2,128)(2,1)} %reshape.610), channel_id=1, replica_groups=mesh['ctx'=8,'fsdp'=4] {'fsdp'}, dimensions={0}, use_global_device_ids=true | all-gather | bytes 7680 | tf_op jit(solution)/shard_map/all_gather | solution.py:183
  126.6 1.6 and_and_fusion
  130.1 5.3 fusion.37
  135.4 4.9 copy.94
  140.3 15.6 %all-gather.10.cloned.1.call-done = bf16[2048,768]{0,1:T(8,128)(2,1)} async-done(((bf16[256,768]{0,1:T(8,128)(2,1)}), bf16[2048,768]{0,1:T(8,128)(2,1)}) %all-gather.10.cloned.1.call-update) | async-done | bytes 3145744 | tf_op jit(solution)/shard_map/all_gather | solution.py:200
  156.2 25.1 %while.37 = (s32[]{:T(128)}, f32[12,512]{1,0:T(8,128)S(1)}, f32[12,512]{1,0:T(8,128)S(1)}, f32[12,512,64]{1,2,0:T(8,128)S(1)}, s32[512]{0:T(512)S(1)}, /*index=5...) while((s32[]{:T(128)}, f32[12,512]{1,0:T(8,128)S(1)}, ...), condition=%wide.region_11.12_spmd, body=%wide.region_4.11_spmd.sunk | while | flops 848873472 | bytes 47867808 | solution.py:230
  159.3 12.3 %conditional.4 = ((f32[12,512]{1,0:T(8,128)S(1)}, f32[12,512]{1,0:T(8,128)S(1)}, f32[12,512,64]{1,2,0:T(8,128)S(1)})) conditional(s32[]{:T(128)} %convert_element_type.260, (f32[12,512]{1,0:T(8,128)S(1)}, f32[12,512]{1,0:T(8,128)S(1)}, f32[12,512,64]{1,2,0:T(8,128)S(1)}) %tuple.153, (pred[512,512]{0,1:T(8,128)(4,1)S(1)}, s32[]{:T(128)}, ...), branch_computations={%region_7.7_spmd, %region_8.10_spmd} | conditional | flops 846999552 | bytes 47579208 | solution.py:222
  159.4 2.2 constant_dynamic-slice_fusion
  161.6 3.2 fusion
  164.8 3.2 fusion.2
  168.0 3.6 multiply_add_fusion
  181.3 4.5 fusion.38
  185.9 4.4 fusion.72
  190.3 2.4 fusion.73
  193.1 84.8 %all-gather.16.cloned.1.call-done = bf16[768,3072]{1,0:T(8,128)(2,1)} async-done(((bf16[192,3072]{1,0:T(8,128)(2,1)}), bf16[768,3072]{1,0:T(8,128)(2,1)}) %all-gather.16.cloned.1.call-update) | async-done | bytes 4718608 | tf_op jit(solution)/shard_map/all_gather | solution.py:182
  277.9 7.4 fusion.60
  285.3 81.9 %all-gather.18.cloned.1.call-done = bf16[3072,768]{1,0:T(8,128)(2,1)} async-done(((bf16[768,768]{1,0:T(8,128)(2,1)}), bf16[3072,768]{1,0:T(8,128)(2,1)}) %all-gather.18.cloned.1.call-update) | async-done | bytes 4718608 | tf_op jit(solution)/shard_map/all_gather | solution.py:184
  367.2 9.7 convert_reduce_fusion.2
  376.9 3.4 multiply_reduce_fusion
  386.4 60.3 %while.38 = (s32[]{:T(128)}, f32[512,12,64]{0,2,1:T(8,128)}, bf16[4,512,768]{2,1,0:T(8,128)(2,1)}, bf16[4,512,768]{2,1,0:T(8,128)(2,1)}, s32[512]{0:T(512)S(1)},...) while((s32[]{:T(128)}, f32[512,12,64]{0,2,1:T(8,128)}, ...), condition=%wide.region_24.25_spmd, body=%wide.region_19.24_spmd.sunk | while | flops 2053282304 | bytes 83462112 | solution.py:331
  389.7 25.5 %conditional.5 = (f32[512,12,64]{0,2,1:T(8,128)}, bf16[1,512,768]{1,2,0:T(8,128)(2,1)}, bf16[1,512,768]{1,2,0:T(8,128)(2,1)}) conditional(s32[]{:T(128)} %convert_element_type.262, f32[512,12,64]{0,2,1:T(8,128)} %get-tuple-element.1203, (pred[512,512]{0,1:T(8,128)(4,1)S(1)}, s32[]{:T(128)}, bf16[2048,768]{0,1:T(8,128)(2,1)}, ...), branch_computations={%region_22.22_spmd, %region_23.23_spmd} | conditional | flops 2051407872 | bytes 76882040 | solution.py:323
  389.8 3.1 constant_dynamic-slice_fusion.2
  393.8 3.0 fusion.74
  396.7 5.1 fusion.16
  401.8 5.6 fusion.11
  407.4 4.1 fusion.75
  411.5 3.7 bitcast_add_fusion
  415.2 1.4 copy.144
  416.6 1.4 copy.145
  422.5 1.9 conditional.5
  425.8 1.4 copy.145
  431.6 1.9 conditional.5
  435.0 1.4 copy.145
  440.7 1.9 conditional.5
  444.1 1.4 copy.145
  448.1 2.1 fusion.77
  450.6 10.1 fusion.62
  462.1 7.1 fusion.59
  470.4 4.3 convolution_convert_fusion
  475.7 4.3 multiply_convert_fusion
  480.0 1.9 convolution_bitcast_fusion
  482.0 2.1 fusion.40
  484.1 54.5 %reduce-scatter.7.cloned.1.call-done = bf16[256,768]{1,0:T(8,128)(2,1)} async-done(((bf16[2048,768]{1,0:T(8,128)(2,1)}), bf16[256,768]{1,0:T(8,128)(2,1)}) %reduce-scatter.7.cloned.1.call-update) | async-done | bytes 393232 | tf_op jit(solution)/shard_map/reduce_scatter | solution.py:339
  538.6 2.0 copy.102
  540.7 1.6 maximum_multiply_fusion
  544.2 2.3 copy.108
  546.5 2.3 copy.107
  548.8 39.8 %reduce-scatter.9.cloned.1.call-done = bf16[256,768]{1,0:T(8,128)(2,1)} async-done(((bf16[2048,768]{1,0:T(8,128)(2,1)}), bf16[256,768]{1,0:T(8,128)(2,1)}) %reduce-scatter.9.cloned.1.call-update) | async-done | bytes 393232 | tf_op jit(solution)/shard_map/reduce_scatter | solution.py:342
  588.7 6.6 fusion.41
  597.3 9.2 add_convert_fusion.3
  606.5 2.8 multiply_reduce_fusion.1
  610.8 39.8 %all-reduce.13 = (f32[3072]{0:T(1024)S(1)}, f32[768]{0:T(1024)S(1)}, f32[768]{0:T(1024)S(1)}, f32[768]{0:T(1024)S(1)}, f32[768]{0:T(1024)S(1)}) all-reduce(f32[3072]{0:T(1024)S(1)} %copy-done.58, f32[768]{0:T(1024)S(1)} %convert_reduce_fusion.3, f32[768]{0:T(1024)S(1)} %copy-done.64, ...), channel_id=7, replica_groups=mesh['ctx'=8,'fsdp'=4] {'ctx','fsdp'}, use_global_device_ids=true, to_apply=%region_33.34.clone | all-reduce | flops 6144 | bytes 49152
  654.6 39.3 %reduce-scatter.13.cloned.1.call-done = f32[24,768]{1,0:T(8,128)} async-done(((f32[768,768]{1,0:T(8,128)}), f32[24,768]{1,0:T(8,128)}) %reduce-scatter.13.cloned.1.call-update) | async-done | bytes 73744 | tf_op jit(solution)/shard_map/reduce_scatter | solution.py:386
  694.0 142.0 %reduce-scatter.17.cloned.1.call-done = f32[96,768]{1,0:T(8,128)} async-done(((f32[3072,768]{1,0:T(8,128)}), f32[96,768]{1,0:T(8,128)}) %reduce-scatter.17.cloned.1.call-update) | async-done | bytes 294928 | tf_op jit(solution)/shard_map/reduce_scatter | solution.py:389
  836.0 141.1 %reduce-scatter.15.cloned.1.call-done = f32[24,3072]{1,0:T(8,128)} async-done(((f32[768,3072]{1,0:T(8,128)}), f32[24,3072]{1,0:T(8,128)}) %reduce-scatter.15.cloned.1.call-update) | async-done | bytes 294928 | tf_op jit(solution)/shard_map/reduce_scatter | solution.py:387
  977.1 125.3 %reduce-scatter.11.cloned.1.call-done = f32[24,2304]{1,0:T(8,128)} async-done(((f32[768,2304]{1,0:T(8,128)}), f32[24,2304]{1,0:T(8,128)}) %reduce-scatter.11.cloned.1.call-update) | async-done | bytes 221200 | tf_op jit(solution)/shard_map/reduce_scatter | solution.py:385
  (309 shorter events, 74.7 us)
Async XLA Ops:
  7.2 75.3 %all-gather.8.cloned.1.call-start = ((), (), s32[]{:S(2)}) async-start(), calls=%async_computation.6 | async-start | bytes 4423680 | tf_op jit(solution)/shard_map/all_gather | solution.py:180
  7.9 127.5 %all-gather.12.cloned.1.call-start = ((), (), s32[]{:S(2)}) async-start(), calls=%async_computation.8 | async-start | bytes 3538944 | tf_op jit(solution)/shard_map/all_gather | solution.py:201
  27.6 61.1 %copy-start.45 = (f32[768]{0:T(1024)}, f32[768]{0:T(1024)S(1)}, u32[]{:S(2)}) copy-start(f32[768]{0:T(1024)S(1)} %convert_element_type.186) | copy-start | bytes 9220
  29.4 160.9 %copy-start.2 = (f32[256,768]{1,0:T(8,128)}, f32[256,768]{1,0:T(8,128)S(1)}, u32[]{:S(2)}) copy-start(f32[256,768]{1,0:T(8,128)S(1)} %bitcast_convert_fusion) | copy-start | bytes 2359300
  30.8 159.5 %copy-start.4 = (f32[256,768]{1,0:T(8,128)}, f32[256,768]{1,0:T(8,128)S(1)}, u32[]{:S(2)}) copy-start(f32[256,768]{1,0:T(8,128)S(1)} %convert_select_fusion) | copy-start | bytes 2359300
  31.0 57.7 %copy-start.39 = (f32[512]{0:T(512)}, f32[512]{0:T(512)S(1)}, u32[]{:S(2)}) copy-start(f32[512]{0:T(512)S(1)} %broadcast_multiply_fusion.1) | copy-start | bytes 6148
  31.9 56.8 %copy-start.43 = (f32[512]{0:T(512)}, f32[512]{0:T(512)S(1)}, u32[]{:S(2)}) copy-start(f32[512]{0:T(512)S(1)} %fusion.47) | copy-start | bytes 6148
  89.7 66.3 %all-gather.10.cloned.1.call-start = ((), (), s32[]{:S(2)}) async-start(), calls=%async_computation.7 | async-start | bytes 3538944 | tf_op jit(solution)/shard_map/all_gather | solution.py:200
  103.0 27.1 %copy-start.13 = (bf16[512,12,32]{0,2,1:T(8,128)(2,1)}, bf16[512,12,32]{0,2,1:T(8,128)(2,1)S(1)}, u32[]{:S(2)}) copy-start(bf16[512,12,32]{0,2,1:T(8,128)(2,1)S(1)} %get-tuple-element.898) | copy-start | bytes 1179652
  103.0 3.9 copy-start.66
  103.0 25.2 %copy-start.25 = (bf16[256,768]{1,0:T(8,128)(2,1)S(1)}, bf16[256,768]{1,0:T(8,128)(2,1)}, u32[]{:S(2)}) copy-start(bf16[256,768]{1,0:T(8,128)(2,1)} %get-tuple-element.882) | copy-start | bytes 1179652
  103.0 26.1 %copy-start.18 = (bf16[512,12,32]{0,2,1:T(8,128)(2,1)S(1)}, bf16[512,12,32]{0,2,1:T(8,128)(2,1)}, u32[]{:S(2)}) copy-start(bf16[512,12,32]{0,2,1:T(8,128)(2,1)} %get-tuple-element.888) | copy-start | bytes 1179652
  103.0 26.1 %copy-start.20 = (bf16[512,12,32]{0,2,1:T(8,128)(2,1)S(1)}, bf16[512,12,32]{0,2,1:T(8,128)(2,1)}, u32[]{:S(2)}) copy-start(bf16[512,12,32]{0,2,1:T(8,128)(2,1)} %get-tuple-element.889) | copy-start | bytes 1179652
  104.5 25.6 %copy-start.16 = (bf16[512,12,32]{0,2,1:T(8,128)(2,1)S(1)}, bf16[512,12,32]{0,2,1:T(8,128)(2,1)}, u32[]{:S(2)}) copy-start(bf16[512,12,32]{0,2,1:T(8,128)(2,1)} %copy-done.15) | copy-start | bytes 1179652
  104.5 85.8 %all-gather.14.cloned.1.call-start = ((), (), s32[]{:S(2)}) async-start(), calls=%async_computation.9 | async-start | bytes 1474560 | tf_op jit(solution)/shard_map/all_gather | solution.py:181
  105.1 172.8 %all-gather.16.cloned.1.call-start = ((), (), s32[]{:S(2)}) async-start(), calls=%async_computation.10 | async-start | bytes 5898240 | tf_op jit(solution)/shard_map/all_gather | solution.py:182
  105.7 261.5 %all-gather.18.cloned.1.call-start = ((), (), s32[]{:S(2)}) async-start(), calls=%async_computation.11 | async-start | bytes 5898240 | tf_op jit(solution)/shard_map/all_gather | solution.py:184
  106.3 432.4 %reduce-scatter.7.cloned.1.call-start = ((), (), s32[]{:S(2)}) async-start(), calls=%async_computation.12 | async-start | bytes 3538944 | tf_op jit(solution)/shard_map/reduce_scatter | solution.py:339
  107.5 272.9 %copy-start.37 = (f32[768]{0:T(1024)}, f32[768]{0:T(1024)S(1)}, u32[]{:S(2)}) copy-start(f32[768]{0:T(1024)S(1)} %convert_element_type.194) | copy-start | bytes 9220
  135.4 20.8 %copy-start.41 = (s32[512,1]{0,1:T(1,128)S(1)}, s32[512,1]{0,1:T(1,128)}, u32[]{:S(2)}) copy-start(s32[512,1]{0,1:T(1,128)} %get-tuple-element.1190) | copy-start | bytes 6148
  135.4 20.8 %copy-start.49 = (s32[16]{0:T(128)S(1)}, s32[16]{0:T(128)}, u32[]{:S(2)}) copy-start(s32[16]{0:T(128)} %reduce.4) | copy-start | bytes 196
  135.4 20.8 %copy-start.51 = (pred[512]{0:T(512)(128)(4,1)S(1)}, pred[512]{0:T(512)(128)(4,1)}, u32[]{:S(2)}) copy-start(pred[512]{0:T(512)(128)(4,1)} %constant.262.clone.1) | copy-start | bytes 1540
  156.2 25.1 %copy-start.55 = (f32[12,512]{1,0:T(8,128)S(1)}, f32[12,512]{1,0:T(8,128)}, u32[]{:S(2)}) copy-start(f32[12,512]{1,0:T(8,128)} %get-tuple-element.909) | copy-start | bytes 73732
  181.3 4.7 copy-start.11
  181.3 4.6 copy-start.33
  192.7 187.7 %copy-start.6 = (f32[512,768]{1,0:T(8,128)}, f32[512,768]{1,0:T(8,128)S(1)}, u32[]{:S(2)}) copy-start(f32[512,768]{1,0:T(8,128)S(1)} %get-tuple-element.914) | copy-start | bytes 4718596
  192.7 187.6 %copy-start.47 = (f32[512]{0:T(512)}, f32[512]{0:T(512)S(1)}, u32[]{:S(2)}) copy-start(f32[512]{0:T(512)S(1)} %broadcast_multiply_fusion) | copy-start | bytes 6148
  193.1 187.3 %copy-start.53 = (f32[512]{0:T(512)}, f32[512]{0:T(512)S(1)}, u32[]{:S(2)}) copy-start(f32[512]{0:T(512)S(1)} %fusion.48) | copy-start | bytes 6148
  193.1 174.1 %copy-start.22 = (bf16[1,2,256,768]{3,2,1,0:T(8,128)(2,1)S(1)}, bf16[1,2,256,768]{3,2,1,0:T(8,128)(2,1)}, u32[]{:S(2)}) copy-start(bf16[1,2,256,768]{3,2,1,0:T(8,128)(2,1)} %param.33) | copy-start | bytes 2359300
  193.1 174.1 %copy-start.59 = (f32[4,1,768]{2,1,0:T(1,128)S(1)}, f32[4,1,768]{2,1,0:T(1,128)}, u32[]{:S(2)}) copy-start(f32[4,1,768]{2,1,0:T(1,128)} %convert_element_type.215) | copy-start | bytes 36868
  367.2 9.7 copy-start.67
  376.9 3.4 copy-start.24
  380.4 1.8 copy-start.68
  383.0 3.4 copy-start.42
  383.0 3.4 copy-start.50
  383.0 3.4 copy-start.52
  407.4 4.1 copy-start.1
  446.8 141.9 %reduce-scatter.9.cloned.1.call-start = ((), (), s32[]{:S(2)}) async-start(), calls=%async_computation.13 | async-start | bytes 3538944 | tf_op jit(solution)/shard_map/reduce_scatter | solution.py:342
  447.5 3.0 copy-start.23
  447.6 3.0 copy-start.60
  447.6 246.4 %reduce-scatter.13.cloned.1.call-start = ((), (), s32[]{:S(2)}) async-start(), calls=%async_computation.15 | async-start | bytes 2433024 | tf_op jit(solution)/shard_map/reduce_scatter | solution.py:386
  450.3 385.7 %reduce-scatter.17.cloned.1.call-start = ((), (), s32[]{:S(2)}) async-start(), calls=%async_computation.17 | async-start | bytes 9732096 | tf_op jit(solution)/shard_map/reduce_scatter | solution.py:389
  460.7 1.4 copy-start.48
  460.7 1.4 copy-start.54
  460.7 516.4 %reduce-scatter.15.cloned.1.call-start = ((), (), s32[]{:S(2)}) async-start(), calls=%async_computation.16 | async-start | bytes 9732096 | tf_op jit(solution)/shard_map/reduce_scatter | solution.py:387
  469.3 6.4 copy-start.35
  469.3 633.1 %reduce-scatter.11.cloned.1.call-start = ((), (), s32[]{:S(2)}) async-start(), calls=%async_computation.14 | async-start | bytes 7299072 | tf_op jit(solution)/shard_map/reduce_scatter | solution.py:385
  475.7 4.3 copy-start.19
  475.7 4.3 copy-start.21
  480.0 2.0 copy-start.14
  480.0 2.0 copy-start.17
  484.1 58.2 %copy-start.31 = (f32[512,32]{0,1:T(8,128)S(1)}, f32[512,32]{0,1:T(8,128)}, u32[]{:S(2)}) copy-start(f32[512,32]{0,1:T(8,128)} %get-tuple-element.900) | copy-start | bytes 196612
  484.1 58.2 %copy-start.32 = (f32[512,32]{0,1:T(8,128)S(1)}, f32[512,32]{0,1:T(8,128)}, u32[]{:S(2)}) copy-start(f32[512,32]{0,1:T(8,128)} %get-tuple-element.901) | copy-start | bytes 196612
  542.8 45.8 %copy-start.3 = (f32[256,768]{1,0:T(8,128)S(1)}, f32[256,768]{1,0:T(8,128)}, u32[]{:S(2)}) copy-start(f32[256,768]{1,0:T(8,128)} %copy-done.2) | copy-start | bytes 2359300
  542.8 45.8 %copy-start.5 = (f32[256,768]{1,0:T(8,128)S(1)}, f32[256,768]{1,0:T(8,128)}, u32[]{:S(2)}) copy-start(f32[256,768]{1,0:T(8,128)} %copy-done.4) | copy-start | bytes 2359300
  542.8 45.8 %copy-start.36 = (bf16[256,768]{1,0:T(8,128)(2,1)S(1)}, bf16[256,768]{1,0:T(8,128)(2,1)}, u32[]{:S(2)}) copy-start(bf16[256,768]{1,0:T(8,128)(2,1)} %copy.106) | copy-start | bytes 1179652
  542.8 45.8 %copy-start.40 = (f32[512]{0:T(512)S(1)}, f32[512]{0:T(512)}, u32[]{:S(2)}) copy-start(f32[512]{0:T(512)} %copy-done.39) | copy-start | bytes 6148
  542.9 45.8 %copy-start.44 = (f32[512]{0:T(512)S(1)}, f32[512]{0:T(512)}, u32[]{:S(2)}) copy-start(f32[512]{0:T(512)} %copy-done.43) | copy-start | bytes 6148
  542.9 45.8 %copy-start.46 = (f32[768]{0:T(1024)S(1)}, f32[768]{0:T(1024)}, u32[]{:S(2)}) copy-start(f32[768]{0:T(1024)} %copy-done.45) | copy-start | bytes 9220
  597.2 9.2 copy-start.12
  597.2 9.2 copy-start.27
  597.3 9.2 copy-start.28
  597.3 9.2 copy-start.69
  606.5 2.8 copy-start.57
  (18 other events, 18.3 us)
Sparse Core Ops, SparseCore 0:
  9.6 72.8 all-gather.7
  89.8 30.8 all-gather.11
  123.1 32.8 all-gather.9
  157.4 30.4 all-gather.13
  189.2 88.5 all-gather.15
  279.3 87.8 all-gather.17
  446.9 91.6 reduce-scatter.6
  542.4 46.2 reduce-scatter.8
  594.5 99.4 reduce-scatter.12
  701.3 134.6 reduce-scatter.16
  842.5 134.6 reduce-scatter.14
  984.2 118.1 reduce-scatter.10
where the time goes:
time: 1120 us; the launch traced here: 1110 us
  waiting for transfers between devices  778 us (69%)
  matrix products  119 us (11%)
  local copies, waits for them, and re-layouts  74.2 us (7%)
  blocking collectives  67.4 us (6%)
  other arithmetic  43.6 us (4%)
  between operations  16 us (1%)
    reduce_scatter x1, waiting for transfers between devices, shards(): lax.psum_scatter(grad_down, ('ctx', 'fsdp'), scatter_dimension=0, tiled=T...  142 us
    reduce_scatter x1, waiting for transfers between devices, shards(): lax.psum_scatter(grad_up, ('ctx', 'fsdp'), scatter_dimension=0, tiled=True)  141 us
    reduce_scatter x1, waiting for transfers between devices, shards(): lax.psum_scatter(grad_qkv, ('ctx', 'fsdp'), scatter_dimension=0, tiled=True)  125 us
    all_gather x1, waiting for transfers between devices, shards(): lax.all_gather(own_params[2], 'fsdp', axis=0, tiled=True)  84.8 us
    all_gather x1, waiting for transfers between devices, shards(): lax.all_gather(own_params[4], 'fsdp', axis=0, tiled=True)  81.9 us
    reduce_scatter x1, waiting for transfers between devices, shards(): lax.psum_scatter(key_terms.astype(jnp.bfloat16), 'ctx', scatter_dimension...  54.5 us
    unnamed x2, blocking collectives  54.2 us
    all_gather x1, waiting for transfers between devices, shards(): lax.all_gather(own_params[0], 'fsdp', axis=0, tiled=True)  50.5 us
  transfers between devices with their start and end apart: 12, of which 10 were waited for; matrix products, arithmetic and copies ran while one was open for 13% of the time, Pallas kernels for 0%

commit v1 on v0

--- a/solution.py
+++ b/solution.py
@@ -1,8 +1,11 @@
+import functools
 import math
 
 import jax
 import jax.numpy as jnp
 from jax import lax
+from jax.experimental import pallas as pl
+from jax.experimental.pallas import tpu as pltpu
 from jax.sharding import PartitionSpec as P
 
 HEADS = 12
@@ -418,7 +421,903 @@
     )
 
 
+CHUNK = 256
+GROUP = 3
+WIDE = GROUP * HEAD_DIM
+HALF = HEAD_DIM // 2
+LANES = GROUP * CHUNK
+BF = jnp.bfloat16
+F32 = jnp.float32
+ANY = pl.BlockSpec(memory_space=pl.ANY)
+VM = pl.BlockSpec(memory_space=pltpu.VMEM)
+SM = pl.BlockSpec(memory_space=pltpu.SMEM)
+GELU_SCALE = math.sqrt(2.0 / math.pi)
+
+
+def swap(v, bit):
+    return lax.ppermute(v, "ctx", [(i, i ^ bit) for i in range(8)])
+
+
+def turn(v, step):
+    return lax.ppermute(v, "fsdp", [(i, (i + step) % 4) for i in range(4)])
+
+
+def mm(a, b, ca=1, cb=0):
+    return lax.dot_general(a, b, (((ca,), (cb,)), ((), ())), preferred_element_type=F32)
+
+
+def flip(v):
+    return jnp.transpose(v.astype(F32)).astype(v.dtype)
+
+
+def call(body, outs, ins, args, scratch=(), limit=40, flops=0, moved=0, grid=None, out_specs=None):
+    shapes = tuple(jax.ShapeDtypeStruct(s, d) for s, d in outs)
+    kwargs = {} if grid is None else {"grid": grid}
+    return pl.pallas_call(
+        body,
+        out_shape=shapes,
+        in_specs=list(ins),
+        out_specs=tuple(out_specs) if out_specs is not None else tuple(VM for _ in outs),
+        scratch_shapes=list(scratch),
+        compiler_params=pltpu.CompilerParams(vmem_limit_bytes=limit * 2**20),
+        cost_estimate=pl.CostEstimate(flops=flops, bytes_accessed=moved, transcendentals=0),
+        **kwargs,
+    )(*args)
+
+
+def run_copies(pairs, sems):
+    copies = [pltpu.make_async_copy(a, b, sems.at[i]) for i, (a, b) in enumerate(pairs)]
+    for copy in copies:
+        copy.start()
+    for copy in copies:
+        copy.wait()
+
+
+def at16(v):
+    return pl.multiple_of(v, 16)
+
+
+def split_rows(meta, own, near, far, dst, unit):
+    c, z = meta[1], meta[3]
+    half = unit // 2
+    pairs = [(own, dst.at[pl.ds(at16(z * unit), unit)])]
+    for t in range(1, 4):
+        zz = lax.rem(z + 4 - t, 4)
+        pairs.append((near[t - 1], dst.at[pl.ds(at16(zz * unit + c * half), half)]))
+        pairs.append((far[t - 1], dst.at[pl.ds(at16(zz * unit + (1 - c) * half), half)]))
+    return pairs
+
+
+def norm_parts(x):
+    mean = jnp.mean(x, axis=-1, keepdims=True)
+    centered = x - mean
+    var = jnp.mean(centered * centered, axis=-1, keepdims=True)
+    scale = lax.rsqrt(var + EPSILON)
+    return centered * scale, scale
+
+
+def unmark(x, embed):
+    x = x.astype(F32)
+    flag = x[:, :1] > 1e38
+    return jnp.where(flag, embed, x), flag
+
+
+def turn_heads(v, cos, sin):
+    parts = []
+    for g in range(GROUP):
+        a = v[g * HEAD_DIM : g * HEAD_DIM + HALF]
+        b = v[g * HEAD_DIM + HALF : (g + 1) * HEAD_DIM]
+        parts += [a * cos - b * sin, b * cos + a * sin]
+    return jnp.concatenate(parts, axis=0)
+
+
+def project_body(count, first, whole, meta, gain, embed, cos, sin, *refs):
+    rows = refs[:count]
+    refs = refs[count:]
+    if whole:
+        (w_ref,) = refs[:1]
+        refs = refs[1:]
+        q_ref, kv_ref, n_ref, mk_ref, xs, w, wp, sems = refs
+        pairs = [(w_ref, w)]
+    else:
+        own, near, far = refs[0], refs[1:4], refs[4:7]
+        q_ref, kv_ref, n_ref, mk_ref, w_out_ref, xs, w, wp, sems = refs[7:]
+        pairs = split_rows(meta, own, near, far, w, 192)
+    pairs += [(rows[i], xs.at[i]) for i in range(count)]
+    run_copies(pairs, sems)
+    for part in range(3):
+        wp[part] = w[:, part * WIDE : (part + 1) * WIDE]
+    if not whole:
+        w_out_ref[...] = w[...]
+
+    @pl.loop(0, count)
+    def _(i):
+        x, flag = unmark(xs[i], embed[...])
+        hat, _ = norm_parts(x)
+        n = (hat * gain[...]).astype(BF)
+        n_ref[i] = n
+        mk_ref[i] = jnp.broadcast_to(jnp.where(flag, 1.0, 0.0), (CHUNK, 128)).astype(BF)
+        co, si = cos[first + i], sin[first + i]
+        q_ref[i] = turn_heads(jnp.transpose(mm(n, wp[0])), co, si).astype(BF)
+        kv_ref[i, :WIDE] = turn_heads(jnp.transpose(mm(n, wp[1])), co, si).astype(BF)
+        kv_ref[i, WIDE:] = jnp.transpose(mm(n, wp[2])).astype(BF)
+
+
+def project_rows(meta, gain, embed, cos, sin, rows, first, weights):
+    count = len(rows)
+    whole = len(weights) == 1
+    dim = rows[0].shape[1]
+    outs = [
+        ((count, WIDE, CHUNK), BF),
+        ((count, 2 * WIDE, CHUNK), BF),
+        ((count, CHUNK, dim), BF),
+        ((count, CHUNK, 128), BF),
+    ]
+    if not whole:
+        outs.append(((dim, 3 * WIDE), BF))
+    return call(
+        functools.partial(project_body, count, first, whole),
+        outs,
+        [SM, VM, VM, VM, VM] + [ANY] * (count + len(weights)),
+        (meta, gain, embed, cos, sin, *rows, *weights),
+        scratch=[
+            pltpu.VMEM((count, CHUNK, dim), BF),
+            pltpu.VMEM((dim, 3 * WIDE), BF),
+            pltpu.VMEM((3, dim, WIDE), BF),
+            pltpu.SemaphoreType.DMA((count + len(weights),)),
+        ],
+        flops=2 * count * CHUNK * dim * 3 * WIDE,
+        moved=count * CHUNK * dim * 6,
+    )
+
+
+def load_heads(meta, na, refs, qs, okv, ckv, sems):
+    q_a, q_b, kv_a, kv_b, r_a, r_b = refs
+    run_copies(
+        [
+            (q_a, qs.at[pl.ds(0, na)]),
+            (q_b, qs.at[pl.ds(na, 8 - na)]),
+            (kv_a, okv.at[pl.ds(0, na)]),
+            (kv_b, okv.at[pl.ds(na, 8 - na)]),
+        ],
+        sems,
+    )
+
+    @pl.when(meta[1] == 0)
+    def _():
+        run_copies([(kv_a, ckv.at[pl.ds(0, na)]), (kv_b, ckv.at[pl.ds(na, 8 - na)])], sems)
+
+    @pl.when(meta[1] != 0)
+    def _():
+        run_copies([(r_a, ckv.at[pl.ds(0, na)]), (r_b, ckv.at[pl.ds(na, 8 - na)])], sems)
+
+
+def thrice(v):
+    return jnp.concatenate([v, v, v], axis=1)
+
+
+def scores_of(keys, stacked, base, low, high):
+    s = mm(keys, stacked) * 0.125
+    place = base + lax.broadcasted_iota(jnp.int32, (CHUNK, LANES), 0)
+    return jnp.where((place >= low) & (place < high), s, LOWEST)
+
+
+def stack_heads(q, stacked):
+    for g in range(GROUP):
+        stacked[g * HEAD_DIM : (g + 1) * HEAD_DIM, g * CHUNK : (g + 1) * CHUNK] = q[
+            g * HEAD_DIM : (g + 1) * HEAD_DIM
+        ]
+
+
+def attend_body(na, meta, bounds, *refs):
+    heads = refs[:6]
+    sends = refs[6:14]
+    o_ref, ml_ref, qs, okv, ckv, okr, ckr, stacked, m_s, l_s, acc, sems = refs[14:]
+    load_heads(meta, na, heads, qs, okv, ckv, sems)
+    stacked[...] = jnp.zeros_like(stacked)
+
+    @pl.loop(0, 8)
+    def _(s):
+        okr[s] = flip(okv[s, :WIDE])
+        ckr[s] = flip(ckv[s, :WIDE])
+
+    r, c = meta[0], meta[1]
+
+    @pl.loop(0, 8)
+    def _(p):
+        s = p ^ r
+        stack_heads(qs[s], stacked)
+        lim = bounds[p]
+        low, high, nlow, nhigh = [thrice(lim[i : i + 1]) for i in range(4)]
+
+        def tile(keys, values, base, lo, hi):
+            masked = scores_of(keys, stacked[...], base, lo, hi)
+            m_old = m_s[...]
+            m_new = jnp.maximum(m_old, jnp.max(masked, axis=0, keepdims=True))
+            e = jnp.exp(masked - m_new)
+            f = jnp.exp(m_old - m_new)
+            m_s[...] = m_new
+            l_s[...] = l_s[...] * f + jnp.sum(e, axis=0, keepdims=True)
+            e = e.astype(BF)
+            for g in range(GROUP):
+                cut = slice(g * CHUNK, (g + 1) * CHUNK)
+                acc[g] = acc[g] * f[:, cut] + mm(
+                    values[g * HEAD_DIM : (g + 1) * HEAD_DIM], e[:, cut]
+                )
+
+        m_s[...] = jnp.full_like(m_s, LOWEST)
+        l_s[...] = jnp.zeros_like(l_s)
+        acc[...] = jnp.zeros_like(acc)
+        tile(okr[s], okv[s, WIDE:], p * CHUNK, nlow, nhigh)
+
+        @pl.loop(meta[4 + p], p + c)
+        def _(k):
+            t = k ^ r ^ c
+            tile(ckr[t], ckv[t, WIDE:], k * CHUNK, low, high)
+
+        total = l_s[...]
+        inv = 1.0 / total
+        out = jnp.concatenate(
+            [acc[g] * inv[:, g * CHUNK : (g + 1) * CHUNK] for g in range(GROUP)], axis=0
+        )
+        o_ref[s] = out
+        ml_ref[s, 0:1] = m_s[...]
+        ml_ref[s, 1:2] = total
+        low_out = out.astype(BF)
+        for i in range(8):
+
+            @pl.when(s == i)
+            def _():
+                sends[i][...] = low_out
+
+
+HEAD_SCRATCH = [
+    pltpu.VMEM((8, WIDE, CHUNK), BF),
+    pltpu.VMEM((8, 2 * WIDE, CHUNK), BF),
+    pltpu.VMEM((8, 2 * WIDE, CHUNK), BF),
+]
+
+
+def attend_rows(meta, bounds, heads):
+    na = heads[0].shape[0]
+    outs = [((WIDE, CHUNK), BF)] * 8 + [((8, WIDE, CHUNK), F32), ((8, 8, LANES), F32)]
+    return call(
+        functools.partial(attend_body, na),
+        outs,
+        [SM, VM] + [ANY] * 6,
+        (meta, bounds, *heads),
+        scratch=HEAD_SCRATCH
+        + [
+            pltpu.VMEM((8, CHUNK, WIDE), BF),
+            pltpu.VMEM((8, CHUNK, WIDE), BF),
+            pltpu.VMEM((WIDE, LANES), BF),
+            pltpu.VMEM((1, LANES), F32),
+            pltpu.VMEM((1, LANES), F32),
+            pltpu.VMEM((GROUP, HEAD_DIM, CHUNK), F32),
+            pltpu.SemaphoreType.DMA((4,)),
+        ],
+        flops=20 * 2 * 2 * CHUNK * LANES * 256,
+        moved=8 * CHUNK * WIDE * 16,
+    )
+
+
+def attend_back_body(na, meta, bounds, cos, sin, o_ref, ml_ref, *refs):
+    heads = refs[:6]
+    grads = refs[6:14]
+    (
+        pq_ref, own_ref, far_ref,
+        qs, okv, ckv, okr, ckr, ovr, cvr, gs,
+        st_q, st_g, row_q, row_g, dk_o, dv_o, dk_c, dv_c, dq, sems,
+    ) = refs[14:]
+    load_heads(meta, na, heads, qs, okv, ckv, sems)
+    run_copies([(grads[i], gs.at[i]) for i in range(8)], sems)
+    for ref in (st_q, st_g, dk_o, dv_o, dk_c, dv_c):
+        ref[...] = jnp.zeros_like(ref)
+
+    @pl.loop(0, 8)
+    def _(s):
+        okr[s] = flip(okv[s, :WIDE])
+        ckr[s] = flip(ckv[s, :WIDE])
+        ovr[s] = flip(okv[s, WIDE:])
+        cvr[s] = flip(ckv[s, WIDE:])
+
+    r, c = meta[0], meta[1]
+    lane = lax.broadcasted_iota(jnp.int32, (CHUNK, WIDE), 1) // HEAD_DIM
+
+    @pl.loop(0, 8)
+    def _(p):
+        s = p ^ r
+        q = qs[s]
+        stack_heads(q, st_q)
+        total = ml_ref[s, 1:2]
+        top = ml_ref[s, 0:1]
+        g_in = gs[s].astype(F32)
+        attended = o_ref[s]
+        scaled, fix = [], []
+        for g in range(GROUP):
+            part = slice(g * HEAD_DIM, (g + 1) * HEAD_DIM)
+            inv = 1.0 / total[:, g * CHUNK : (g + 1) * CHUNK]
+            scaled.append(g_in[part] * inv)
+            fix.append(jnp.sum(g_in[part] * attended[part], axis=0, keepdims=True) * inv)
+        scaled = jnp.concatenate(scaled, axis=0)
+        fix = jnp.concatenate(fix, axis=1)
+        stack_heads(scaled.astype(BF), st_g)
+        q_rows = jnp.transpose(q.astype(F32))
+        g_rows = jnp.transpose(scaled)
+        for g in range(GROUP):
+            row_q[g * CHUNK : (g + 1) * CHUNK] = jnp.where(lane == g, q_rows, 0.0).astype(BF)
+            row_g[g * CHUNK : (g + 1) * CHUNK] = jnp.where(lane == g, g_rows, 0.0).astype(BF)
+        lim = bounds[p]
+        low, high, nlow, nhigh = [thrice(lim[i : i + 1]) for i in range(4)]
+        dq[...] = jnp.zeros_like(dq)
+
+        def tile(k_rows, v_rows, k_cols, base, lo, hi, dk, dv):
+            e = jnp.exp(scores_of(k_rows, st_q[...], base, lo, hi) - top)
+            d = (e * (mm(v_rows, st_g[...]) - fix)).astype(BF)
+            e = e.astype(BF)
+            dv[...] += mm(e, row_g[...])
+            dk[...] += mm(d, row_q[...])
+            for g in range(GROUP):
+                dq[g * HEAD_DIM : (g + 1) * HEAD_DIM] += mm(
+                    k_cols[g * HEAD_DIM : (g + 1) * HEAD_DIM], d[:, g * CHUNK : (g + 1) * CHUNK]
+                )
+
+        tile(okr[s], ovr[s], okv[s, :WIDE], p * CHUNK, nlow, nhigh, dk_o.at[s], dv_o.at[s])
+
+        @pl.loop(meta[4 + p], p + c)
+        def _(k):
+            t = k ^ r ^ c
+            tile(ckr[t], cvr[t], ckv[t, :WIDE], k * CHUNK, low, high, dk_c.at[t], dv_c.at[t])
+
+        pq_ref[s] = turn_heads(dq[...] * 0.125, cos[s], -sin[s]).astype(BF)
+
+    both = 1.0 - c.astype(F32)
+
+    @pl.loop(0, 8)
+    def _(s):
+        dk = jnp.transpose(dk_c[s])
+        dv = jnp.transpose(dv_c[s])
+        far_ref[s, :WIDE] = dk.astype(BF)
+        far_ref[s, WIDE:] = dv.astype(BF)
+        own_ref[s, :WIDE] = jnp.transpose(dk_o[s]) + both * dk
+        own_ref[s, WIDE:] = jnp.transpose(dv_o[s]) + both * dv
+
+
+def attend_back(meta, bounds, cos, sin, attended, stats, heads, grads):
+    na = heads[0].shape[0]
+    rows = pltpu.VMEM((8, CHUNK, WIDE), BF)
+    sums = pltpu.VMEM((8, CHUNK, WIDE), F32)
+    return call(
+        functools.partial(attend_back_body, na),
+        [((8, WIDE, CHUNK), BF), ((8, 2 * WIDE, CHUNK), F32), ((8, 2 * WIDE, CHUNK), BF)],
+        [SM, VM, VM, VM, VM, VM] + [ANY] * 14,
+        (meta, bounds, cos, sin, attended, stats, *heads, *grads),
+        scratch=HEAD_SCRATCH
+        + [rows] * 4
+        + [
+            pltpu.VMEM((8, WIDE, CHUNK), BF),
+            pltpu.VMEM((WIDE, LANES), BF),
+            pltpu.VMEM((WIDE, LANES), BF),
+            pltpu.VMEM((LANES, WIDE), BF),
+            pltpu.VMEM((LANES, WIDE), BF),
+        ]
+        + [sums] * 4
+        + [pltpu.VMEM((WIDE, CHUNK), F32), pltpu.SemaphoreType.DMA((8,))],
+        limit=48,
+        flops=20 * 2 * 5 * CHUNK * LANES * 256,
+        moved=8 * CHUNK * WIDE * 30,
+    )
+
+
+def middle_body(meta, gain, embed, x_ref, *refs):
+    heads = refs[:8]
+    own, near, far = refs[8], refs[9:12], refs[12:15]
+    mid_ref, n_ref, att_ref, w_ref, sems = refs[15:]
+    r = meta[0]
+    pairs = split_rows(meta, own, near, far, w_ref, 192)
+    for s in range(8):
+        d = r ^ s
+        pairs.append((heads[s], att_ref.at[d & 1, pl.ds(at16((d >> 1) * WIDE), WIDE)]))
+    run_copies(pairs, sems)
+    for stream in range(2):
+        x, _ = unmark(x_ref[stream], embed[...])
+        mid = x + mm(att_ref[stream], w_ref[...], 0, 0)
+        hat, _ = norm_parts(mid)
+        mid_ref[stream] = mid
+        n_ref[stream * CHUNK : (stream + 1) * CHUNK] = (hat * gain[...]).astype(BF)
+
+
+def middle_rows(meta, gain, embed, marked, heads, weights):
+    dim = marked.shape[2]
+    return call(
+        middle_body,
+        [((2, CHUNK, dim), F32), ((2 * CHUNK, dim), BF), ((2, dim, CHUNK), BF), ((dim, dim), BF)],
+        [SM, VM, VM, VM] + [ANY] * 15,
+        (meta, gain, embed, marked, *heads, *weights),
+        scratch=[pltpu.SemaphoreType.DMA((15,))],
+        flops=2 * 2 * CHUNK * dim * dim,
+        moved=8 * CHUNK * dim * 2,
+    )
+
+
+def feed_body(meta, bias, *refs):
+    n_own, n_far, g_own, g_far, up_own, down_own, ff_r, ff_x, ff_y, ff_dd, ff_du = refs[:11]
+    downs, ups = (ff_r, ff_x, ff_y, ff_dd), (ff_r, ff_x, ff_y, ff_du)
+    (
+        out_ref, outf_ref, ng_ref, ngf_ref, gu_ref, gd_ref, gb_ref,
+        ns, gs, wu, wd, acts, slopes, acc_o, acc_n, sems,
+    ) = refs[11:]
+    c, h, z = meta[1], meta[2], meta[3]
+    rows = 2 * CHUNK
+    part = bias.shape[1] // 4
+    pairs = [
+        (n_own, ns.at[pl.ds(0, rows)]),
+        (n_far, ns.at[pl.ds(rows, rows)]),
+        (g_own, gs.at[pl.ds(0, rows)]),
+        (g_far, gs.at[pl.ds(rows, rows)]),
+        (down_own.at[pl.ds(at16(c * part), part)], wd.at[pl.ds(at16(z * part), part)]),
+    ]
+    for k in range(4):
+        cols = pl.ds(pl.multiple_of(k * 2 * part + c * part, 128), part)
+        pairs.append((up_own.at[:, cols], wu.at[pl.ds(at16(z * 192), 192), pl.ds(k * part, part)]))
+    for t in range(1, 4):
+        zz = lax.rem(z + 4 - t, 4)
+        for k in range(4):
+            hh = h ^ k
+            pairs.append((downs[k].at[t - 1, pl.ds(0, 96)], wd.at[pl.ds(at16(zz * part + hh * 96), 96)]))
+            dst = pl.ds(at16(zz * 192 + hh * 48), 48)
+            for b in range(2):
+                pairs.append(
+                    (
+                        ups[k].at[t - 1, pl.ds(48 * b + (96 if k < 3 else 0), 48)],
+                        wu.at[dst, pl.ds(2 * part * b, 2 * part)],
+                    )
+                )
+    run_copies(pairs, sems)
+    acc_o[...] = jnp.zeros_like(acc_o)
+    acc_n[...] = jnp.zeros_like(acc_n)
+
+    @pl.loop(0, 4)
+    def _(j):
+        cols = pl.ds(pl.multiple_of(j * part, 128), part)
+        w_up = wu[:, cols]
+        w_down = wd[pl.ds(at16(j * part), part)]
+        b_up = bias[:, cols]
+
+        def rows_of(i, total):
+            span = pl.ds(pl.multiple_of(i * CHUNK, CHUNK), CHUNK)
+            v = mm(ns[span], w_up) + b_up
+            square = v * v
+            th = jnp.tanh(GELU_SCALE * (v + 0.044715 * (v * square)))
+            half = 0.5 * (1.0 + th)
+            act = (v * half).astype(BF)
+            slope = half + (0.5 * v) * (1.0 - th * th) * (
+                GELU_SCALE * (1.0 + (3.0 * 0.044715) * square)
+            )
+            ug = (slope * mm(gs[span], w_down, 1, 1)).astype(BF)
+            acts[span] = act
+            slopes[span] = ug
+            acc_o[span] += mm(act, w_down)
+            acc_n[span] += mm(ug, w_up, 1, 1)
+            return total + jnp.sum(ug.astype(F32), axis=0, keepdims=True)
+
+        gb_ref[:, cols] = lax.fori_loop(0, 4, rows_of, jnp.zeros((1, part), F32))
+        gd_ref[j ^ h] = mm(acts[...], gs[...], 0, 0).astype(BF)
+        gu = mm(ns[...], slopes[...], 0, 0).astype(BF)
+        for k in range(4):
+            gu_ref[h ^ k, :, cols] = gu[192 * k : 192 * (k + 1)]
+
+    out_ref[...] = acc_o[:rows]
+    outf_ref[...] = acc_o[rows:].astype(BF)
+    ng_ref[...] = acc_n[:rows]
+    ngf_ref[...] = acc_n[rows:].astype(BF)
+
+
+def feed_rows(meta, bias, args):
+    rows = 2 * CHUNK
+    dim = args[0].shape[1]
+    hid = bias.shape[1]
+    return call(
+        feed_body,
+        [
+            ((rows, dim), F32),
+            ((rows, dim), BF),
+            ((rows, dim), F32),
+            ((rows, dim), BF),
+            ((4, dim // 4, hid), BF),
+            ((4, hid // 4, dim), BF),
+            ((1, hid), F32),
+        ],
+        [SM, VM] + [ANY] * 11,
+        (meta, bias, *args),
+        scratch=[
+            pltpu.VMEM((2 * rows, dim), BF),
+            pltpu.VMEM((2 * rows, dim), BF),
+            pltpu.VMEM((dim, hid), BF),
+            pltpu.VMEM((hid, dim), BF),
+            pltpu.VMEM((2 * rows, hid // 4), BF),
+            pltpu.VMEM((2 * rows, hid // 4), BF),
+            pltpu.VMEM((2 * rows, dim), F32),
+            pltpu.VMEM((2 * rows, dim), F32),
+            pltpu.SemaphoreType.DMA((45,)),
+        ],
+        limit=48,
+        flops=6 * 2 * 2 * rows * dim * hid,
+        moved=12 * dim * hid,
+    )
+
+
+def middle_back_body(
+    meta, gain, b_down, mid_ref, ng_ref, ngf_ref, out_ref, outf_ref, g_ref, x_ref, w_ref, *refs
+):
+    lay_ref, mg_ref, sum_ref = refs[:3]
+    sends = refs[3:11]
+    gain_sum = jnp.zeros((1, gain.shape[1]), F32)
+    g_sum = gain_sum
+    for stream in range(2):
+        span = slice(stream * CHUNK, (stream + 1) * CHUNK)
+        mid = mid_ref[stream]
+        lay = mid + out_ref[span] + outf_ref[span].astype(F32) + b_down[...]
+        lay_ref[stream] = lay.astype(BF)
+        hat, scale = norm_parts(mid)
+        ng = ng_ref[span] + ngf_ref[span].astype(F32)
+        gain_sum += jnp.sum(ng * hat, axis=0, keepdims=True)
+        t = ng * gain[...]
+        g = g_ref[stream].astype(F32)
+        g_sum += jnp.sum(g, axis=0, keepdims=True)
+        t_mean = jnp.mean(t, axis=-1, keepdims=True)
+        t_hat = jnp.mean(t * hat, axis=-1, keepdims=True)
+        mg = (g + scale * (t - t_mean - hat * t_hat)).astype(BF)
+        mg_ref[stream] = mg
+        if stream == 1:
+            flag = x_ref[1][:, :1].astype(F32) > 1e38
+            sum_ref[2:3] = jnp.sum(jnp.where(flag, mg.astype(F32), 0.0), axis=0, keepdims=True)
+    sum_ref[0:1] = gain_sum
+    sum_ref[1:2] = g_sum
+    for s in range(8):
+        d = meta[0] ^ s
+        rows = w_ref[pl.ds(at16((d >> 1) * WIDE), WIDE)]
+        sends[s][...] = mm(rows, mg_ref[d & 1], 1, 1).astype(BF)
+
+
+def middle_back(meta, gain, b_down, args):
+    dim = gain.shape[1]
+    return call(
+        middle_back_body,
+        [((2, CHUNK, dim), BF), ((2, CHUNK, dim), BF), ((8, dim), F32)]
+        + [((WIDE, CHUNK), BF)] * 8,
+        [SM] + [VM] * 10,
+        (meta, gain, b_down, *args),
+        flops=4 * CHUNK * dim * dim,
+        moved=20 * CHUNK * dim,
+    )
+
+
+def out_grad_body(att_ref, mg_ref, o_ref):
+    o_ref[...] = (mm(att_ref[0], mg_ref[0]) + mm(att_ref[1], mg_ref[1])).astype(BF)
+
+
+def project_back_body(steps, last, meta_free, *refs):
+    own, far, pq, n_ref, mk_ref, cos, sin, w_ref = (meta_free, *refs[:7])
+    refs = refs[7:]
+    if last:
+        carry, vec = refs[:2]
+        refs = refs[2:]
+    ng_ref, gq_ref, gs_ref, wp, acc = refs
+    i = pl.program_id(0)
+
+    @pl.when(i == 0)
+    def _():
+        for part in range(3):
+            wp[part] = w_ref[:, part * WIDE : (part + 1) * WIDE]
+        if last:
+            acc[...] = carry[...]
+            gs_ref[...] = vec[...]
+        else:
+            acc[...] = jnp.zeros_like(acc)
+            gs_ref[...] = jnp.zeros_like(gs_ref)
+
+    kv = own[0] + far[0].astype(F32)
+    parts = [
+        pq[0],
+        turn_heads(kv[:WIDE] * 0.125, cos[0], -sin[0]).astype(BF),
+        kv[WIDE:].astype(BF),
+    ]
+    n = n_ref[0]
+    ng = jnp.zeros((CHUNK, n.shape[1]), F32)
+    for k in range(3):
+        ng += mm(flip(parts[k]), wp[k], 1, 1)
+        acc[k * WIDE : (k + 1) * WIDE] += mm(parts[k], n)
+    ng_ref[0] = ng.astype(BF)
+    gs_ref[0:1] += jnp.sum(ng * n.astype(F32), axis=0, keepdims=True)
+    gs_ref[1:2] += jnp.sum(ng * mk_ref[0][:, :1].astype(F32), axis=0, keepdims=True)
+
+    @pl.when(i == steps - 1)
+    def _():
+        gq_ref[...] = jnp.transpose(acc[...]).astype(BF) if last else acc[...]
+
+
+def pick(order):
+    def at(i):
+        slot = jnp.int32(order[-1])
+        for k in range(len(order) - 2, -1, -1):
+            slot = jnp.where(i == k, order[k], slot)
+        return slot
+
+    return at
+
+
+def project_back(order, own, far, pq, n, mk, cos, sin, w, carry=None):
+    last = carry is not None
+    steps = len(order)
+    dim = n.shape[2]
+    slot = pick(order)
+
+    def chunk(rows, cols):
+        return pl.BlockSpec((1, rows, cols), lambda i: (slot(i), 0, 0))
+
+    def whole(*shape):
+        return pl.BlockSpec(shape, lambda i: tuple(0 for _ in shape))
+
+    wide = 3 * WIDE + HEAD_DIM
+    args = [own, far, pq, n, mk, cos, sin, w]
+    specs = [
+        chunk(2 * WIDE, CHUNK), chunk(2 * WIDE, CHUNK), chunk(WIDE, CHUNK), chunk(CHUNK, dim),
+        chunk(CHUNK, 128), chunk(HALF, CHUNK), chunk(HALF, CHUNK), whole(dim, 3 * WIDE),
+    ]
+    if last:
+        args += list(carry)
+        specs += [whole(wide, dim), whole(8, dim)]
+    gq_shape = (dim, wide) if last else (wide, dim)
+    return call(
+        functools.partial(project_back_body, steps, last),
+        [((steps, CHUNK, dim), BF), (gq_shape, BF if last else F32), ((8, dim), F32)],
+        specs,
+        args,
+        scratch=[pltpu.VMEM((3, dim, WIDE), BF), pltpu.VMEM((wide, dim), F32)],
+        grid=(steps,),
+        out_specs=[
+            pl.BlockSpec((1, CHUNK, dim), lambda i: (i, 0, 0)), whole(*gq_shape), whole(8, dim)
+        ],
+        flops=2 * 2 * steps * CHUNK * dim * 3 * WIDE,
+        moved=steps * CHUNK * dim * 8,
+    )
+
+
+def last_body(meta, gain, embed, x_ref, mg_ref, keep_ref, far_ref, o_ref):
+    c = meta[1]
+    for stream, ng in ((c, keep_ref[...]), (1 - c, far_ref[...].astype(F32))):
+        x, flag = unmark(x_ref[stream], embed[...])
+        hat, scale = norm_parts(x)
+        t = ng * gain[...]
+        t_mean = jnp.mean(t, axis=-1, keepdims=True)
+        t_hat = jnp.mean(t * hat, axis=-1, keepdims=True)
+        grad = mg_ref[stream].astype(F32) + scale * (t - t_mean - hat * t_hat)
+        o_ref[stream] = jnp.where(flag, 0.0, grad).astype(BF)
+
+
+def cut(v, index, size, axis=0):
+    return lax.dynamic_slice_in_dim(v, index * size, size, axis)
+
+
+def at(v, index, axis=0):
+    return lax.dynamic_index_in_dim(v, index, axis, keepdims=False)
+
+
+def shards_by_heads(
+    hidden,
+    noise_mask,
+    doc_lengths,
+    w_qkv,
+    w_out,
+    w_up,
+    b_up,
+    w_down,
+    b_down,
+    gain_one,
+    gain_two,
+    mask_embed,
+    out_grad,
+):
+    r = lax.axis_index("ctx")
+    z = lax.axis_index("fsdp")
+    c, h = r & 1, r >> 1
+    dim = hidden.shape[3]
+    hid = w_up.shape[1]
+    part = hid // 8
+    total = CHUNK * 8
+
+    noisy = jnp.where(noise_mask[0][:, None] == 1, jnp.asarray(jnp.inf, BF), hidden[0, 1])
+    marked = jnp.stack([hidden[0, 0], noisy])
+    mine = at(marked, c)
+    other = swap(at(marked, 1 - c), 1)
+    mine_x, mine_y = swap(mine, 2), swap(mine, 4)
+    other_x, other_y = swap(other, 2), swap(other, 4)
+    mine_d, other_d = swap(mine_x, 4), swap(other_y, 2)
+
+    small = jnp.concatenate([b_up, b_down, gain_one, gain_two, mask_embed])
+    size = small.shape[0]
+    small = jnp.pad(small, (0, 2048 - size)).reshape(16, 128)
+    small = jnp.stack([small] + [turn(small, t) for t in range(1, 4)])
+    small = jnp.take(small, (z - jnp.arange(4)) % 4, axis=0).reshape(4, 2048).astype(F32)
+    quarter = dim // 4
+    bias = at(small[:, : hid // 4].reshape(4, 2, part), c, 1).reshape(1, 4 * part)
+    b_down_all, gain_a, gain_b, embed = [
+        small[:, hid // 4 + k * quarter : hid // 4 + (k + 1) * quarter].reshape(1, dim)
+        for k in range(4)
+    ]
+
+    own_qkv = jnp.concatenate([cut(w_qkv[:, k * dim : (k + 1) * dim], h, WIDE, 1) for k in range(3)], 1)
+    half = cut(own_qkv, c, quarter // 2)
+    near_qkv = [turn(half, t) for t in range(1, 4)]
+    far_qkv = [swap(v, 1) for v in near_qkv]
+    up_rows = cut(w_up, h, quarter // 4).reshape(quarter // 4, 4, 2, part)
+    up_rows = at(up_rows, c, 2)
+    share = jnp.concatenate(
+        [
+            cut(w_down, 4 * c + h, part // 4),
+            up_rows[:, :2].reshape(quarter // 4, 2 * part),
+            up_rows[:, 2:].reshape(quarter // 4, 2 * part),
+        ]
+    )
+    ff_r = jnp.stack([turn(share, t) for t in range(1, 4)])
+    ff_x, ff_y = swap(ff_r, 2), swap(ff_r, 4)
+    ff_dd = swap(ff_x[:, : part // 4], 4)
+    ff_du = swap(ff_y[:, part // 4 :], 2)
+    half = cut(w_out, c, quarter // 2)
+    near_out = [turn(half, t) for t in range(1, 4)]
+    far_out = [swap(v, 1) for v in near_out]
+
+    lengths = doc_lengths[0]
+    index = jnp.arange(lengths.shape[0])
+    ends = jnp.sum(jnp.where(index[None, :] <= index[:, None], lengths[None, :], 0), axis=1)
+    place = jnp.arange(total, dtype=jnp.int32)
+    after = ends[None, :] > place[:, None]
+    start = jnp.max(jnp.where(after, 0, ends[None, :]), axis=1)
+    stop = jnp.min(jnp.where(after, ends[None, :], total), axis=1)
+    block = place // BLOCK * BLOCK
+    limit = jnp.minimum(block + BLOCK, stop)
+    clean = c == 0
+    bounds = jnp.stack(
+        [start, jnp.where(clean, limit, block), jnp.where(clean, start, jnp.maximum(start, block)), limit]
+    )
+    bounds = jnp.pad(bounds.reshape(4, 8, CHUNK).transpose(1, 0, 2), ((0, 0), (0, 4), (0, 0)))
+    meta = jnp.concatenate(
+        [jnp.stack([r, c, h, z]), start[::CHUNK] // CHUNK, jnp.zeros((4,), jnp.int32)]
+    ).astype(jnp.int32)
+    slots = (jnp.arange(8) ^ r)[:, None] * CHUNK + jnp.arange(CHUNK)[None, :]
+    frequency = jnp.exp(jnp.arange(HALF).astype(F32) * (-2.0 * math.log(10000.0) / HEAD_DIM))
+    angles = slots.astype(F32)[:, None, :] * frequency[None, :, None]
+    cos, sin = jnp.cos(angles), jnp.sin(angles)
+
+    rows_a = (mine, other, mine_x, other_x, mine_y, other_y)
+    q_a, kv_a, n_a, mk_a, w_all = project_rows(
+        meta, gain_a, embed, cos, sin, rows_a, 0, (own_qkv, *near_qkv, *far_qkv)
+    )
+    q_b, kv_b, n_b, mk_b = project_rows(meta, gain_a, embed, cos, sin, (mine_d, other_d), 6, (w_all,))
+    give = [(i, i + 1) for i in range(0, 8, 2)]
+    r_a, r_b = lax.ppermute(kv_a, "ctx", give), lax.ppermute(kv_b, "ctx", give)
+    heads = (q_a, q_b, kv_a, kv_b, r_a, r_b)
+    *sends, attended, stats = attend_rows(meta, bounds, heads)
+    got = [sends[0]] + [swap(sends[s], s) for s in range(1, 8)]
+    middle, normed, att, w_out_all = middle_rows(
+        meta, gain_b, embed, marked, got, (w_out, *near_out, *far_out)
+    )
+    grads = out_grad[0]
+    grad_rows = grads.reshape(2 * CHUNK, dim)
+    out_own, out_far, ng_own, ng_far, gu, gd, gbu = feed_rows(
+        meta,
+        bias,
+        (normed, swap(normed, 1), grad_rows, swap(grad_rows, 1), w_up, w_down, ff_r, ff_x, ff_y, ff_dd, ff_du),
+    )
+    ng_far, out_far = swap(ng_far, 1), swap(out_far, 1)
+
+    layer, mid_grad, sums, *sends = middle_back(
+        meta,
+        gain_b,
+        b_down_all,
+        (middle, ng_own, ng_far, out_own, out_far, grads, marked, w_out_all),
+    )
+    got = [sends[0]] + [swap(sends[s], s) for s in range(1, 8)]
+    (go,) = call(
+        out_grad_body, [((dim, dim), BF)], [VM, VM], (att, mid_grad), flops=4 * CHUNK * dim * dim
+    )
+    pq, own_kv, far_kv = attend_back(meta, bounds, cos, sin, attended, stats, heads, got)
+    far_kv = lax.ppermute(far_kv, "ctx", [(b, a) for a, b in give])
+    n_all = jnp.concatenate([n_a, n_b])
+    mk_all = jnp.concatenate([mk_a, mk_b])
+    back = (own_kv, far_kv, pq, n_all, mk_all, cos, sin, w_all)
+    away, *carry = project_back((2, 6, 5, 7), *back)
+    in_x, in_y = swap(away[:2], 2), swap(away[2:], 4)
+    stay, gq, vec = project_back((0, 4, 1, 3), *back, carry=carry)
+    stay = stay.astype(F32)
+    keep = stay[0] + in_x[0].astype(F32)
+    keep += swap((stay[1] + in_x[1].astype(F32)).astype(BF), 4).astype(F32)
+    pair = stay[2] + in_y[0].astype(F32)
+    pair += swap((stay[3] + in_y[1].astype(F32)).astype(BF), 2).astype(F32)
+    pair = swap(pair.astype(BF), 1)
+    (input_grad,) = call(
+        last_body,
+        [((2, CHUNK, dim), BF)],
+        [SM] + [VM] * 6,
+        (meta, gain_a, embed, marked, mid_grad, keep, pair),
+        moved=10 * CHUNK * dim,
+    )
+
+    def line(v):
+        out = at(v, z).astype(F32)
+        for t in range(1, 4):
+            out += turn(at(v, (z + t) % 4).astype(BF), t).astype(F32)
+        return out
+
+    def plane_chip(v, first):
+        one, two = (1, 2) if first == 0 else (2, 1)
+        got = swap(jnp.stack([v[one], v[3]]), 2 * one)
+        low = v[0].astype(F32) + got[0].astype(F32)
+        high = (v[two].astype(F32) + got[1].astype(F32)).astype(BF)
+        return low + swap(high, 2 * two).astype(F32)
+
+    gd = line(plane_chip(gd, 0).reshape(4, part // 4, dim))
+    gu = plane_chip(gu, 1).reshape(2, 4, dim // 32, 4 * part)
+    gu = line(jnp.swapaxes(gu, 0, 1))
+    gu_far = swap(at(gu, 1 - c).astype(BF), 1).astype(F32)
+    gu = at(gu, c)
+    gu = jnp.where(clean, jnp.stack([gu, gu_far]), jnp.stack([gu_far, gu]))
+    gu = gu.reshape(2, dim // 32, 4, part).transpose(1, 2, 0, 3).reshape(dim // 32, hid)
+
+    def over_core(v):
+        v = v.reshape(4, 2, dim // 8, v.shape[-1])
+        return at(v, c, 1).astype(F32) + swap(at(v, 1 - c, 1), 1).astype(F32)
+
+    go = over_core(go).astype(BF)
+    go_sum = at(go, h).astype(F32)
+    for k in range(1, 4):
+        go_sum += swap(at(go, h ^ k), 2 * k).astype(F32)
+    go = line(go_sum.reshape(4, dim // 32, dim))
+
+    gq = over_core(gq)
+    gq = line(jnp.swapaxes(gq.reshape(4, 4, dim // 32, gq.shape[-1]), 0, 1))
+    gq_low = gq.astype(BF)
+    pieces = [at(gq, h)] + [swap(at(gq_low, h ^ k), 2 * k).astype(F32) for k in range(1, 4)]
+    gq = jnp.take(jnp.stack(pieces), jnp.arange(4) ^ h, axis=0)[..., : 3 * WIDE]
+    gq = gq.reshape(4, dim // 32, 3, WIDE).transpose(1, 2, 0, 3).reshape(dim // 32, 3 * dim)
+
+    gbu = gbu.reshape(4, 1, part)
+    gbu = jnp.where(clean, jnp.concatenate([gbu, 0 * gbu], 1), jnp.concatenate([0 * gbu, gbu], 1))
+    flat = jnp.concatenate([gbu.reshape(-1), sums[:3].reshape(-1), vec[:2].reshape(-1)])
+    flat = flat.reshape(-1, 128)
+    for bit in (1, 2, 4):
+        flat = flat + swap(flat, bit)
+    flat = flat + turn(flat, 1) + turn(flat, 2) + turn(flat, 3)
+    flat = flat.reshape(-1)
+    gbu = flat[:hid]
+    g_gain_b, g_b_down, m_direct, g_gain_a, m_norm = [
+        flat[hid + k * dim : hid + (k + 1) * dim] for k in range(5)
+    ]
+    g_gain_a = g_gain_a / gain_a[0]
+    hat, scale = norm_parts(embed)
+    t = m_norm[None] * gain_a
+    t_mean = jnp.mean(t, axis=-1, keepdims=True)
+    t_hat = jnp.mean(t * hat, axis=-1, keepdims=True)
+    g_embed = m_direct + (scale * (t - t_mean - hat * t_hat))[0]
+    own = 4 * r + z
+    return (
+        layer[None],
+        input_grad[None],
+        gq,
+        go,
+        gu,
+        cut(gbu, own, hid // 32),
+        gd,
+        cut(g_b_down, own, dim // 32),
+        cut(g_gain_a, own, dim // 32),
+        cut(g_gain_b, own, dim // 32),
+        cut(g_embed, own, dim // 32),
+    )
+
+
 def solution(mesh):
+    plain = (mesh.shape["ctx"], mesh.shape["fsdp"]) != (8, 4)
     placed = (
         P("fsdp", None, "ctx", None),
         P("fsdp", "ctx"),
@@ -435,7 +1334,7 @@
         P("fsdp", None, "ctx", None),
     )
     return jax.shard_map(
-        shards,
+        shards if plain else shards_by_heads,
         mesh=mesh,
         in_specs=placed,
         out_specs=(

time: 1120 us -> 395 us (0.35)
  waiting for transfers between devices: 778 us -> 87.9 us
  matrix products: 119 us -> 0 us
  Pallas kernels: 0 us -> 114 us
  starting transfers between devices: 0.69 us -> 96.7 us
  blocking collectives: 67.4 us -> 0 us
  other arithmetic: 43.6 us -> 21.5 us
  between operations: 16 us -> 4.57 us
    reduce_scatter x6 -> x0, waiting for transfers between devices: 542 us -> none  [the longest x1 142 us: shards(): lax.psum_scatter(grad_down, ('ctx', 'fsdp'), scatter_dimension=0, tiled=T...]
    all_gather x6 -> x0, waiting for transfers between devices: 233 us -> none  [the longest x1 84.8 us: shards(): lax.all_gather(own_params[2], 'fsdp', axis=0, tiled=True)]
    dot_general x25 -> x0, matrix products: 119 us -> none  [the longest x1 10.1 us: shards(): jnp.einsum('qi,qj->ij', activated, grad_rows, preferred_element_type=jnp....]
    pallas_call x0 -> x11, Pallas kernels: none -> 114 us  [call(): pl.pallas_call(body, out_shape=shapes, in_specs=list(ins), out_specs=tupl...]
    ppermute x0 -> x86, starting transfers between devices: none -> 96.7 us  [the longest x56 59.5 us: swap(): return lax.ppermute(v, 'ctx', [(i, i ^ bit) for i in range(8)])]
    ppermute x0 -> x86, waiting for transfers between devices: none -> 87.9 us  [the longest x27 46 us: turn(): return lax.ppermute(v, 'fsdp', [(i, (i + step) % 4) for i in range(4)])]
    unnamed x2 -> x0, blocking collectives: 54.2 us -> none
    dynamic_update_slice x12 -> x0, local copies, waits for them, and re-layouts: 16.3 us -> none  [shards(): lax.scan(back_step, jnp.zeros((row_count, HEADS, HEAD_DIM), jnp.float32),...]
  transfers between devices with their start and end apart: 12 -> 86, of which waited for: 10 -> 32; matrix products, arithmetic and copies ran while one was open for 13% -> 15% of each run, Pallas kernels for 0% -> 19%
where the time goes in v1:
time: 395 us; the launch traced here: 393 us
  Pallas kernels  114 us (29%)
  starting transfers between devices  96.7 us (24%)
  waiting for transfers between devices  87.9 us (22%)
  local copies, waits for them, and re-layouts  68.4 us (17%)
  other arithmetic  21.5 us (5%)
  between operations  4.57 us (1%)
    pallas_call x11, Pallas kernels, call(): pl.pallas_call(body, out_shape=shapes, in_specs=list(ins), out_specs=tupl...  114 us
    ppermute x56, starting transfers between devices, swap(): return lax.ppermute(v, 'ctx', [(i, i ^ bit) for i in range(8)])  59.5 us
    ppermute x27, waiting for transfers between devices, turn(): return lax.ppermute(v, 'fsdp', [(i, (i + step) % 4) for i in range(4)])  46 us
    ppermute x56, waiting for transfers between devices, swap(): return lax.ppermute(v, 'ctx', [(i, i ^ bit) for i in range(8)])  41.8 us
    ppermute x27, starting transfers between devices, turn(): return lax.ppermute(v, 'fsdp', [(i, (i + step) % 4) for i in range(4)])  32.1 us
    unnamed x189, local copies, waits for them, and re-layouts  31 us
  transfers between devices with their start and end apart: 86, of which 32 were waited for; matrix products, arithmetic and copies ran while one was open for 15% of the time, Pallas kernels for 19%

profile of v1, /device:TPU:0, one launch (start us, length us, event | category | flops | bytes accessed | tf_op | source)
XLA Modules:
  0.0 393.1 jit_solution(14550238784896935727)
XLA Ops:
  0.6 3.4 concatenate.31
  4.1 5.1 %collective-permute-start.2 = (bf16[16,128]{1,0:T(8,128)(2,1)S(1)}, bf16[16,128]{1,0:T(8,128)(2,1)S(1)}, u32[]{:S(2)}, u32[]{:S(2)}) collective-permute-start(bf16[16,128]{1,0:T(8,128)(2,1)S(1)} %get-tuple-element.164), channel_id=1, source_target_pairs={{0,3},{1,0},{2,1},{3,2},{4,7},{5,4},{6,5},{7,6},{8,11},{9,8},{10,9... | collective-permute-start | bytes 12296 | tf_op jit(solution)/shard_map/ppermute | solution.py:442
  12.5 2.5 collective-permute-start.8
  21.4 1.6 collective-permute-start.4
  23.6 1.6 collective-permute-start.6
  26.6 1.5 collective-permute-start.7
  36.2 2.1 collective-permute-start.26
  39.0 2.3 collective-permute-done.5.refs_3_
  50.9 9.7 %shard_map.212 = (bf16[6,192,256]{2,1,0:T(8,128)(2,1)S(1)}, bf16[6,384,256]{2,1,0:T(8,128)(2,1)}, bf16[6,256,768]{2,1,0:T(8,128)(2,1)S(1)}, bf16[6,256,128]{2,1,0:T(8,128)(2,1)S(1)}, bf16[768,576]{1,0:T(8,128)(2,1)S(1)}) custom-call(s32[16]{0:T(128)S(1)} %concatenate.30.meta, f32[1,768]{1,0:T(1,128)S(1)} %reshape.518.gain, f32[1,768]{1,0:T(1,128)S(1)} %reshape.517.embed, ...), custom_call_target="tpu_custom_call" | custom-call | flops 1358954496 | bytes 7077888 | tf_op jit(solution)/shard_map/pallas_call | solution.py:456
  62.9 2.3 collective-permute-start.16
  67.1 1.5 collective-permute-start.14
  68.6 2.0 constant_dynamic-slice_fusion.2
  73.8 2.8 collective-permute-done.14.refs_0_
  76.7 2.0 collective-permute-start.27
  80.9 2.0 collective-permute-start.35
  83.0 3.2 shard_map.213
  90.5 16.8 %collective-permute-done.34 = bf16[192,768]{1,0:T(8,128)(2,1)S(1)} collective-permute-done((bf16[192,768]{1,0:T(8,128)(2,1)S(1)}, bf16[192,768]{1,0:T(8,128)(2,1)S(1)}, u32[]{:S(2)}, u32[]{:S(2)}) %collective-permute-start.34) | collective-permute-done | bytes 294944 | tf_op jit(solution)/shard_map/ppermute | solution.py:442
  110.3 19.4 %shard_map.214 = (bf16[192,256]{1,0:T(8,128)(2,1)S(1)}, bf16[192,256]{1,0:T(8,128)(2,1)S(1)}, bf16[192,256]{1,0:T(8,128)(2,1)S(1)}, bf16[192,256]{1,0:T(8,128)(2...) custom-call(s32[16]{0:T(128)S(1)} %concatenate.30.meta, ...), custom_call_target="tpu_custom_call" | custom-call | flops 4026531840 | bytes 6291456 | tf_op jit(solution)/shard_map/pallas_call | solution.py:456
  130.4 4.6 %collective-permute-start.18 = (bf16[192,256]{1,0:T(8,128)(2,1)S(1)}, bf16[192,256]{1,0:T(8,128)(2,1)S(1)}, u32[]{:S(2)}, u32[]{:S(2)}) collective-permute-start(bf16[192,256]{1,0:T(8,128)(2,1)S(1)} %get-tuple-element.67), channel_id=1, source_target_pairs={{0,4},{4,0},{8,12},{12,8},{16,20},{20,16},{24,28},{28,24},{1,5},{5... | collective-permute-start | bytes 294920 | tf_op jit(solution)/shard_map/ppermute | solution.py:438
  137.8 2.6 collective-permute-done.19.refs_2_
  141.5 1.7 collective-permute-start.23
  145.4 2.8 collective-permute-done.23.refs_6_
  149.6 5.2 %shard_map.215 = (f32[2,256,768]{2,1,0:T(8,128)S(1)}, bf16[512,768]{1,0:T(8,128)(2,1)}, bf16[2,768,256]{2,1,0:T(8,128)(2,1)S(1)}, bf16[768,768]{1,0:T(8,128)(2,1)S(1)}) custom-call(s32[16]{0:T(128)S(1)} %concatenate.30.meta, f32[1,768]{1,0:T(1,128)S(1)} %reshape.515.gain, f32[1,768]{1,0:T(1,128)S(1)} %reshape.517.embed, ...), custom_call_target="tpu_custom_call" | custom-call | flops 603979776 | bytes 3145728 | tf_op jit(solution)/shard_map/pallas_call | solution.py:456
  158.1 1.8 slice.211
  161.2 1.8 slice.212
  163.1 1.7 collective-permute-start.39
  166.9 1.8 constant_dynamic-update-slice_fusion.1
  168.7 4.0 %collective-permute-done.38.refs_9_ = bf16[3,96,768]{2,1,0:T(8,128)(2,1)} collective-permute-done((bf16[3,96,768]{2,1,0:T(8,128)(2,1)}, bf16[3,96,768]{2,1,0:T(8,128)(2,1)}, u32[]{:S(2)}, u32[]{:S(2)}) %collective-permute-start.38) | collective-permute-done | bytes 442400 | tf_op jit(solution)/shard_map/ppermute | solution.py:438
  172.8 2.7 collective-permute-done.39.refs_10_
  175.5 31.2 %shard_map.216 = (f32[512,768]{1,0:T(8,128)}, bf16[512,768]{1,0:T(8,128)(2,1)S(1)}, f32[512,768]{1,0:T(8,128)}, bf16[512,768]{1,0:T(8,128)(2,1)S(1)}, bf16[4,192...) custom-call(s32[16]{0:T(128)S(1)} %concatenate.30.meta, f32[1,1536]{1,0:T(1,128)S(1)} %bitcast.223, ...), custom_call_target="tpu_custom_call" | custom-call | flops 14495514624 | bytes 14155776 | tf_op jit(solution)/shard_map/pallas_call | solution.py:456
  207.5 2.6 fusion.55
  212.4 4.4 %shard_map.217 = (bf16[2,256,768]{2,1,0:T(8,128)(2,1)}, bf16[2,256,768]{2,1,0:T(8,128)(2,1)S(1)}, f32[8,768]{1,0:T(8,128)S(1)}, bf16[192,256]{1,0:T(8,128)(2,1)S...) custom-call(s32[16]{0:T(128)S(1)} %concatenate.30.meta, ...), custom_call_target="tpu_custom_call" | custom-call | flops 603979776 | bytes 3932160 | tf_op jit(solution)/shard_map/pallas_call | solution.py:456
  220.3 1.8 collective-permute-start.43
  228.5 1.9 collective-permute-start.47
  232.3 1.6 collective-permute-start.81
  234.8 1.8 collective-permute-done.48.refs_13_
  236.6 28.8 %shard_map.218 = (bf16[8,192,256]{2,1,0:T(8,128)(2,1)S(1)}, f32[8,384,256]{2,1,0:T(8,128)}, bf16[8,384,256]{2,1,0:T(8,128)(2,1)}) custom-call(s32[16]{0:T(128)S(1)} %concatenate.30.meta, s32[8,8,256]{2,1,0:T(8,128)S(1)} %copy-done.33, f32[8,32,256]{2,1,0:T(8,128)S(1)} %copy-done.8, f32[8,32,256]{2,1,0:T(8,128)S(1)} %get-tuple-element.161.sin.refs_5_, ...), custom_call_target="tpu_custom_call" | custom-call | flops 10066329600 | bytes 11796480 | tf_op jit(solution)/shard_map/pallas_call | solution.py:456
  267.0 1.7 collective-permute-start.65
  270.7 2.5 collective-permute-done.65
  277.4 1.8 collective-permute-done.68
  280.1 2.3 collective-permute-done.66
  283.0 6.0 %collective-permute-done.70 = bf16[192,1536]{1,0:T(8,128)(2,1)S(1)} collective-permute-done((bf16[192,1536]{1,0:T(8,128)(2,1)S(1)}, bf16[192,1536]{1,0:T(8,128)(2,1)S(1)}, u32[]{:S(2)}, u32[]{:S(2)}) %collective-permute-start.70) | collective-permute-done | bytes 589856 | tf_op jit(solution)/shard_map/ppermute | solution.py:438
  291.7 2.9 collective-permute-start.85
  295.4 8.1 %collective-permute-done.72 = bf16[2,24,1536]{2,1,0:T(8,128)(2,1)S(1)} collective-permute-done((bf16[2,24,1536]{2,1,0:T(8,128)(2,1)S(1)}, bf16[2,24,1536]{2,1,0:T(8,128)(2,1)S(1)}, u32[]{:S(2)}, u32[]{:S(2)}) %collective-permute-start.72) | collective-permute-done | bytes 147488 | tf_op jit(solution)/shard_map/ppermute | solution.py:442
  304.2 7.3 %collective-permute-start.74 = (bf16[24,1536]{1,0:T(8,128)(2,1)}, bf16[24,1536]{1,0:T(8,128)(2,1)}, u32[]{:S(2)}, u32[]{:S(2)}) collective-permute-start(bf16[24,1536]{1,0:T(8,128)(2,1)} %fusion.34), channel_id=1, source_target_pairs={{0,4},{4,0},{8,12},{12,8},{16,20},{20,16},{24,28},{28,24},{1,5},{5... | collective-permute-start | bytes 221192 | tf_op jit(solution)/shard_map/ppermute | solution.py:438
  311.5 2.9 collective-permute-done.84
  315.3 3.6 shard_map.219
  320.0 5.0 %shard_map.220 = (bf16[4,256,768]{2,1,0:T(8,128)(2,1)S(1)}, bf16[768,640]{1,0:T(8,128)(2,1)S(1)}, f32[8,768]{1,0:T(8,128)S(1)}) custom-call(f32[8,384,256]{2,1,0:T(8,128)S(1)} %copy-done.4, bf16[8,384,256]{2,1,0:T(8,128)(2,1)S(1)} %collective-permute-done.49.refs_0_, bf16[8,192,256]{2,1,0:T(8,128)(2,1)S(1)} %get-tuple-element.95.refs_1_, ...), custom_call_target="tpu_custom_call" | custom-call | flops 1811939328 | bytes 6291456 | tf_op jit(solution)/shard_map/pallas_call | solution.py:456
  326.0 2.9 collective-permute-start.75
  331.7 1.8 collective-permute-start.76
  333.5 2.2 fusion.16
  335.6 1.9 reshape.531
  340.0 2.0 convert_element_type.269
  343.4 2.1 collective-permute-start.79
  345.5 1.9 collective-permute-start.78
  348.1 3.0 collective-permute-done.78
  359.5 4.0 %collective-permute-done.58 = bf16[4,24,640]{2,1,0:T(8,128)(2,1)S(1)} collective-permute-done((bf16[4,24,640]{2,1,0:T(8,128)(2,1)S(1)}, bf16[4,24,640]{2,1,0:T(8,128)(2,1)S(1)}, u32[]{:S(2)}, u32[]{:S(2)}) %collective-permute-start.58) | collective-permute-done | bytes 122912 | tf_op jit(solution)/shard_map/ppermute | solution.py:442
  363.5 4.6 %collective-permute-done.57 = bf16[4,24,640]{2,1,0:T(8,128)(2,1)S(1)} collective-permute-done((bf16[4,24,640]{2,1,0:T(8,128)(2,1)S(1)}, bf16[4,24,640]{2,1,0:T(8,128)(2,1)S(1)}, u32[]{:S(2)}, u32[]{:S(2)}) %collective-permute-start.57) | collective-permute-done | bytes 122912 | tf_op jit(solution)/shard_map/ppermute | solution.py:442
  368.3 2.4 collective-permute-start.61
  373.1 1.8 collective-permute-start.53
  376.1 5.5 %collective-permute-done.53 = bf16[256,768]{1,0:T(8,128)(2,1)S(1)} collective-permute-done((bf16[256,768]{1,0:T(8,128)(2,1)S(1)}, bf16[256,768]{1,0:T(8,128)(2,1)S(1)}, u32[]{:S(2)}, u32[]{:S(2)}) %collective-permute-start.53) | collective-permute-done | bytes 393248 | tf_op jit(solution)/shard_map/ppermute | solution.py:438
  383.0 2.0 fusion.4
  388.6 1.8 reshape.527
  390.5 2.6 shard_map.221
  (431 shorter events, 115.3 us)
Async XLA Ops:
  4.1 15.8 %collective-permute-start.2 = (bf16[16,128]{1,0:T(8,128)(2,1)S(1)}, bf16[16,128]{1,0:T(8,128)(2,1)S(1)}, u32[]{:S(2)}, u32[]{:S(2)}) collective-permute-start(bf16[16,128]{1,0:T(8,128)(2,1)S(1)} %get-tuple-element.164), channel_id=1, source_target_pairs={{0,3},{1,0},{2,1},{3,2},{4,7},{5,4},{6,5},{7,6},{8,11},{9,8},{10,9... | collective-permute-start | bytes 12296 | tf_op jit(solution)/shard_map/ppermute | solution.py:442
  9.2 12.2 %collective-permute-start.1 = (bf16[16,128]{1,0:T(8,128)(2,1)S(1)}, bf16[16,128]{1,0:T(8,128)(2,1)S(1)}, u32[]{:S(2)}, u32[]{:S(2)}) collective-permute-start(bf16[16,128]{1,0:T(8,128)(2,1)S(1)} %get-tuple-element.164), channel_id=1, source_target_pairs={{0,2},{1,3},{2,0},{3,1},{4,6},{5,7},{6,4},{7,5},{8,10},{9,11},{10,... | collective-permute-start | bytes 12296 | tf_op jit(solution)/shard_map/ppermute | solution.py:442
  9.2 12.2 %collective-permute-start = (bf16[16,128]{1,0:T(8,128)(2,1)S(1)}, bf16[16,128]{1,0:T(8,128)(2,1)S(1)}, u32[]{:S(2)}, u32[]{:S(2)}) collective-permute-start(bf16[16,128]{1,0:T(8,128)(2,1)S(1)} %get-tuple-element.164), channel_id=1, source_target_pairs={{0,1},{1,2},{2,3},{3,0},{4,5},{5,6},{6,7},{7,4},{8,9},{9,10},{10,1... | collective-permute-start | bytes 12296 | tf_op jit(solution)/shard_map/ppermute | solution.py:442
  12.5 11.1 %collective-permute-start.8 = (bf16[96,576]{1,0:T(8,128)(2,1)}, bf16[96,576]{1,0:T(8,128)(2,1)S(1)}, u32[]{:S(2)}, u32[]{:S(2)}) collective-permute-start(bf16[96,576]{1,0:T(8,128)(2,1)} %constant_dynamic-slice_fusion.7), channel_id=1, source_target_pairs={{0,1},{1,2},{2,3},{3,0},{4,5},{5,6},{6,7},{7,4},{8,9},{9,10},{10,1... | collective-permute-start | bytes 331784 | tf_op jit(solution)/shard_map/ppermute | solution.py:442
  15.0 10.2 %collective-permute-start.9 = (bf16[96,576]{1,0:T(8,128)(2,1)}, bf16[96,576]{1,0:T(8,128)(2,1)S(1)}, u32[]{:S(2)}, u32[]{:S(2)}) collective-permute-start(bf16[96,576]{1,0:T(8,128)(2,1)} %constant_dynamic-slice_fusion.7), channel_id=1, source_target_pairs={{0,2},{1,3},{2,0},{3,1},{4,6},{5,7},{6,4},{7,5},{8,10},{9,11},{10,... | collective-permute-start | bytes 331784 | tf_op jit(solution)/shard_map/ppermute | solution.py:442
  19.9 6.7 %collective-permute-start.10 = (bf16[96,576]{1,0:T(8,128)(2,1)}, bf16[96,576]{1,0:T(8,128)(2,1)S(1)}, u32[]{:S(2)}, u32[]{:S(2)}) collective-permute-start(bf16[96,576]{1,0:T(8,128)(2,1)} %constant_dynamic-slice_fusion.7), channel_id=1, source_target_pairs={{0,3},{1,0},{2,1},{3,2},{4,7},{5,4},{6,5},{7,6},{8,11},{9,8},{10,9... | collective-permute-start | bytes 331784 | tf_op jit(solution)/shard_map/ppermute | solution.py:442
  21.4 14.8 %collective-permute-start.4 = (bf16[256,768]{1,0:T(8,128)(2,1)S(1)}, bf16[256,768]{1,0:T(8,128)(2,1)}, u32[]{:S(2)}, u32[]{:S(2)}) collective-permute-start(bf16[256,768]{1,0:T(8,128)(2,1)S(1)} %get-tuple-element.140.refs_0_), channel_id=1, source_target_pairs={{0,8},{4,12},{8,0},{12,4},{16,24},{20,28},{24,16},{28,20},{1,9},{5... | collective-permute-start | bytes 1179656 | tf_op jit(solution)/shard_map/ppermute | solution.py:438
  23.6 14.7 %collective-permute-start.6 = (bf16[256,768]{1,0:T(8,128)(2,1)S(1)}, bf16[256,768]{1,0:T(8,128)(2,1)S(1)}, u32[]{:S(2)}, u32[]{:S(2)}) collective-permute-start(bf16[256,768]{1,0:T(8,128)(2,1)S(1)} %get-tuple-element.140.refs_0_), channel_id=1, source_target_pairs={{0,16},{4,20},{8,24},{12,28},{16,0},{20,4},{24,8},{28,12},{1,17},{... | collective-permute-start | bytes 1179656 | tf_op jit(solution)/shard_map/ppermute | solution.py:438
  25.9 15.5 %collective-permute-start.5 = (bf16[256,768]{1,0:T(8,128)(2,1)S(1)}, bf16[256,768]{1,0:T(8,128)(2,1)S(1)}, u32[]{:S(2)}, u32[]{:S(2)}) collective-permute-start(bf16[256,768]{1,0:T(8,128)(2,1)S(1)} %collective-permute-done.3.refs_1_), channel_id=1, source_target_pairs={{0,8},{4,12},{8,0},{12,4},{16,24},{20,28},{24,16},{28,20},{1,9},{5... | collective-permute-start | bytes 1179656 | tf_op jit(solution)/shard_map/ppermute | solution.py:438
  26.6 16.7 %collective-permute-start.7 = (bf16[256,768]{1,0:T(8,128)(2,1)S(1)}, bf16[256,768]{1,0:T(8,128)(2,1)S(1)}, u32[]{:S(2)}, u32[]{:S(2)}) collective-permute-start(bf16[256,768]{1,0:T(8,128)(2,1)S(1)} %collective-permute-done.3.refs_1_), channel_id=1, source_target_pairs={{0,16},{4,20},{8,24},{12,28},{16,0},{20,4},{24,8},{28,12},{1,17},{... | collective-permute-start | bytes 1179656 | tf_op jit(solution)/shard_map/ppermute | solution.py:438
  35.5 51.6 %collective-permute-start.25 = (bf16[96,768]{1,0:T(8,128)(2,1)}, bf16[96,768]{1,0:T(8,128)(2,1)S(1)}, u32[]{:S(2)}, u32[]{:S(2)}) collective-permute-start(bf16[96,768]{1,0:T(8,128)(2,1)} %constant_dynamic-slice_fusion.6), channel_id=1, source_target_pairs={{0,1},{1,2},{2,3},{3,0},{4,5},{5,6},{6,7},{7,4},{8,9},{9,10},{10,1... | collective-permute-start | bytes 442376 | tf_op jit(solution)/shard_map/ppermute | solution.py:442
  36.2 51.0 %collective-permute-start.26 = (bf16[96,768]{1,0:T(8,128)(2,1)}, bf16[96,768]{1,0:T(8,128)(2,1)S(1)}, u32[]{:S(2)}, u32[]{:S(2)}) collective-permute-start(bf16[96,768]{1,0:T(8,128)(2,1)} %constant_dynamic-slice_fusion.6), channel_id=1, source_target_pairs={{0,2},{1,3},{2,0},{3,1},{4,6},{5,7},{6,4},{7,5},{8,10},{9,11},{10,... | collective-permute-start | bytes 442376 | tf_op jit(solution)/shard_map/ppermute | solution.py:442
  62.9 46.6 %collective-permute-start.16 = (bf16[6,384,256]{2,1,0:T(8,128)(2,1)}, bf16[6,384,256]{2,1,0:T(8,128)(2,1)}, u32[]{:S(2)}, u32[]{:S(2)}) collective-permute-start(bf16[6,384,256]{2,1,0:T(8,128)(2,1)} %get-tuple-element.64.refs_2_), channel_id=1, source_target_pairs={{0,4},{8,12},{16,20},{24,28},{1,5},{9,13},{17,21},{25,29},{2,6},{1... | collective-permute-start | bytes 3538952 | tf_op jit(solution)/shard_map/ppermute | solution.py:1199
  67.1 9.5 %collective-permute-start.14 = (bf16[256,768]{1,0:T(8,128)(2,1)}, bf16[256,768]{1,0:T(8,128)(2,1)S(1)}, u32[]{:S(2)}, u32[]{:S(2)}) collective-permute-start(bf16[256,768]{1,0:T(8,128)(2,1)} %collective-permute-done.4.refs_2_), channel_id=1, source_target_pairs={{0,16},{4,20},{8,24},{12,28},{16,0},{20,4},{24,8},{28,12},{1,17},{... | collective-permute-start | bytes 1179656 | tf_op jit(solution)/shard_map/ppermute | solution.py:438
  71.6 9.3 %collective-permute-start.15 = (bf16[256,768]{1,0:T(8,128)(2,1)}, bf16[256,768]{1,0:T(8,128)(2,1)S(1)}, u32[]{:S(2)}, u32[]{:S(2)}) collective-permute-start(bf16[256,768]{1,0:T(8,128)(2,1)} %copy-done.38), channel_id=1, source_target_pairs={{0,8},{4,12},{8,0},{12,4},{16,24},{20,28},{24,16},{28,20},{1,9},{5... | collective-permute-start | bytes 1179656 | tf_op jit(solution)/shard_map/ppermute | solution.py:438
  76.7 11.5 %collective-permute-start.27 = (bf16[96,768]{1,0:T(8,128)(2,1)}, bf16[96,768]{1,0:T(8,128)(2,1)S(1)}, u32[]{:S(2)}, u32[]{:S(2)}) collective-permute-start(bf16[96,768]{1,0:T(8,128)(2,1)} %constant_dynamic-slice_fusion.6), channel_id=1, source_target_pairs={{0,3},{1,0},{2,1},{3,2},{4,7},{5,4},{6,5},{7,6},{8,11},{9,8},{10,9... | collective-permute-start | bytes 442376 | tf_op jit(solution)/shard_map/ppermute | solution.py:442
  80.9 9.5 %collective-permute-start.35 = (bf16[192,768]{1,0:T(8,128)(2,1)S(1)}, bf16[192,768]{1,0:T(8,128)(2,1)S(1)}, u32[]{:S(2)}, u32[]{:S(2)}) collective-permute-start(bf16[192,768]{1,0:T(8,128)(2,1)S(1)} %pad_maximum_fusion.3), channel_id=1, source_target_pairs={{0,3},{1,0},{2,1},{3,2},{4,7},{5,4},{6,5},{7,6},{8,11},{9,8},{10,9... | collective-permute-start | bytes 884744 | tf_op jit(solution)/shard_map/ppermute | solution.py:442
  87.1 20.2 %collective-permute-start.34 = (bf16[192,768]{1,0:T(8,128)(2,1)S(1)}, bf16[192,768]{1,0:T(8,128)(2,1)S(1)}, u32[]{:S(2)}, u32[]{:S(2)}) collective-permute-start(bf16[192,768]{1,0:T(8,128)(2,1)S(1)} %pad_maximum_fusion.3), channel_id=1, source_target_pairs={{0,2},{1,3},{2,0},{3,1},{4,6},{5,7},{6,4},{7,5},{8,10},{9,11},{10,... | collective-permute-start | bytes 884744 | tf_op jit(solution)/shard_map/ppermute | solution.py:442
  87.2 20.1 %collective-permute-start.33 = (bf16[192,768]{1,0:T(8,128)(2,1)S(1)}, bf16[192,768]{1,0:T(8,128)(2,1)S(1)}, u32[]{:S(2)}, u32[]{:S(2)}) collective-permute-start(bf16[192,768]{1,0:T(8,128)(2,1)S(1)} %pad_maximum_fusion.3), channel_id=1, source_target_pairs={{0,1},{1,2},{2,3},{3,0},{4,5},{5,6},{6,7},{7,4},{8,9},{9,10},{10,1... | collective-permute-start | bytes 884744 | tf_op jit(solution)/shard_map/ppermute | solution.py:442
  88.2 20.7 %collective-permute-start.17 = (bf16[2,384,256]{2,1,0:T(8,128)(2,1)S(1)}, bf16[2,384,256]{2,1,0:T(8,128)(2,1)S(1)}, u32[]{:S(2)}, u32[]{:S(2)}) collective-permute-start(bf16[2,384,256]{2,1,0:T(8,128)(2,1)S(1)} %get-tuple-element.65.refs_3_), channel_id=1, source_target_pairs={{0,4},{8,12},{16,20},{24,28},{1,5},{9,13},{17,21},{25,29},{2,6},{1... | collective-permute-start | bytes 1179656 | tf_op jit(solution)/shard_map/ppermute | solution.py:1199
  90.5 40.0 %collective-permute-start.28 = (bf16[96,768]{1,0:T(8,128)(2,1)S(1)}, bf16[96,768]{1,0:T(8,128)(2,1)S(1)}, u32[]{:S(2)}, u32[]{:S(2)}) collective-permute-start(bf16[96,768]{1,0:T(8,128)(2,1)S(1)} %collective-permute-done.25.refs_9_), channel_id=1, source_target_pairs={{0,4},{4,0},{8,12},{12,8},{16,20},{20,16},{24,28},{28,24},{1,5},{5... | collective-permute-start | bytes 442376 | tf_op jit(solution)/shard_map/ppermute | solution.py:438
  107.3 27.8 %collective-permute-start.29 = (bf16[96,768]{1,0:T(8,128)(2,1)S(1)}, bf16[96,768]{1,0:T(8,128)(2,1)S(1)}, u32[]{:S(2)}, u32[]{:S(2)}) collective-permute-start(bf16[96,768]{1,0:T(8,128)(2,1)S(1)} %collective-permute-done.26.refs_10_), channel_id=1, source_target_pairs={{0,4},{4,0},{8,12},{12,8},{16,20},{20,16},{24,28},{28,24},{1,5},{5... | collective-permute-start | bytes 442376 | tf_op jit(solution)/shard_map/ppermute | solution.py:438
  107.3 29.1 %collective-permute-start.30 = (bf16[96,768]{1,0:T(8,128)(2,1)S(1)}, bf16[96,768]{1,0:T(8,128)(2,1)S(1)}, u32[]{:S(2)}, u32[]{:S(2)}) collective-permute-start(bf16[96,768]{1,0:T(8,128)(2,1)S(1)} %collective-permute-done.27.refs_11_), channel_id=1, source_target_pairs={{0,4},{4,0},{8,12},{12,8},{16,20},{20,16},{24,28},{28,24},{1,5},{5... | collective-permute-start | bytes 442376 | tf_op jit(solution)/shard_map/ppermute | solution.py:438
  108.8 49.3 %collective-permute-start.36 = (bf16[3,192,768]{2,1,0:T(8,128)(2,1)}, bf16[3,192,768]{2,1,0:T(8,128)(2,1)}, u32[]{:S(2)}, u32[]{:S(2)}) collective-permute-start(bf16[3,192,768]{2,1,0:T(8,128)(2,1)} %pad_maximum_fusion.2.refs_6_), channel_id=1, source_target_pairs={{0,8},{4,12},{8,0},{12,4},{16,24},{20,28},{24,16},{28,20},{1,9},{5... | collective-permute-start | bytes 2654216 | tf_op jit(solution)/shard_map/ppermute | solution.py:438
  109.5 51.8 %collective-permute-start.37 = (bf16[3,192,768]{2,1,0:T(8,128)(2,1)}, bf16[3,192,768]{2,1,0:T(8,128)(2,1)}, u32[]{:S(2)}, u32[]{:S(2)}) collective-permute-start(bf16[3,192,768]{2,1,0:T(8,128)(2,1)} %pad_maximum_fusion.2.refs_6_), channel_id=1, source_target_pairs={{0,16},{4,20},{8,24},{12,28},{16,0},{20,4},{24,8},{28,12},{1,17},{... | collective-permute-start | bytes 2654216 | tf_op jit(solution)/shard_map/ppermute | solution.py:438
  130.4 6.1 %collective-permute-start.18 = (bf16[192,256]{1,0:T(8,128)(2,1)S(1)}, bf16[192,256]{1,0:T(8,128)(2,1)S(1)}, u32[]{:S(2)}, u32[]{:S(2)}) collective-permute-start(bf16[192,256]{1,0:T(8,128)(2,1)S(1)} %get-tuple-element.67), channel_id=1, source_target_pairs={{0,4},{4,0},{8,12},{12,8},{16,20},{20,16},{24,28},{28,24},{1,5},{5... | collective-permute-start | bytes 294920 | tf_op jit(solution)/shard_map/ppermute | solution.py:438
  136.5 6.7 %collective-permute-start.21 = (bf16[192,256]{1,0:T(8,128)(2,1)S(1)}, bf16[192,256]{1,0:T(8,128)(2,1)S(1)}, u32[]{:S(2)}, u32[]{:S(2)}) collective-permute-start(bf16[192,256]{1,0:T(8,128)(2,1)S(1)} %get-tuple-element.70), channel_id=1, source_target_pairs={{0,16},{4,20},{8,24},{12,28},{16,0},{20,4},{24,8},{28,12},{1,17},{... | collective-permute-start | bytes 294920 | tf_op jit(solution)/shard_map/ppermute | solution.py:438
  141.5 6.7 %collective-permute-start.23 = (bf16[192,256]{1,0:T(8,128)(2,1)}, bf16[192,256]{1,0:T(8,128)(2,1)S(1)}, u32[]{:S(2)}, u32[]{:S(2)}) collective-permute-start(bf16[192,256]{1,0:T(8,128)(2,1)} %get-tuple-element.72), channel_id=1, source_target_pairs={{0,24},{4,28},{8,16},{12,20},{16,8},{20,12},{24,0},{28,4},{1,25},{... | collective-permute-start | bytes 294920 | tf_op jit(solution)/shard_map/ppermute | solution.py:438
  143.2 6.5 %collective-permute-start.24 = (bf16[192,256]{1,0:T(8,128)(2,1)S(1)}, bf16[192,256]{1,0:T(8,128)(2,1)S(1)}, u32[]{:S(2)}, u32[]{:S(2)}) collective-permute-start(bf16[192,256]{1,0:T(8,128)(2,1)S(1)} %get-tuple-element.73), channel_id=1, source_target_pairs={{0,28},{4,24},{8,20},{12,16},{16,12},{20,8},{24,4},{28,0},{1,29},{... | collective-permute-start | bytes 294920 | tf_op jit(solution)/shard_map/ppermute | solution.py:438
  145.4 23.4 %collective-permute-start.32 = (bf16[512,768]{1,0:T(8,128)(2,1)}, bf16[512,768]{1,0:T(8,128)(2,1)}, u32[]{:S(2)}, u32[]{:S(2)}) collective-permute-start(bf16[512,768]{1,0:T(8,128)(2,1)} %bitcast.19.refs_2_), channel_id=1, source_target_pairs={{0,4},{4,0},{8,12},{12,8},{16,20},{20,16},{24,28},{28,24},{1,5},{5... | collective-permute-start | bytes 2359304 | tf_op jit(solution)/shard_map/ppermute | solution.py:438
  158.0 17.5 %collective-permute-start.31 = (bf16[512,768]{1,0:T(8,128)(2,1)}, bf16[512,768]{1,0:T(8,128)(2,1)}, u32[]{:S(2)}, u32[]{:S(2)}) collective-permute-start(bf16[512,768]{1,0:T(8,128)(2,1)} %get-tuple-element.75.refs_0_), channel_id=1, source_target_pairs={{0,4},{4,0},{8,12},{12,8},{16,20},{20,16},{24,28},{28,24},{1,5},{5... | collective-permute-start | bytes 2359304 | tf_op jit(solution)/shard_map/ppermute | solution.py:438
  160.0 12.8 %collective-permute-start.38 = (bf16[3,96,768]{2,1,0:T(8,128)(2,1)}, bf16[3,96,768]{2,1,0:T(8,128)(2,1)}, u32[]{:S(2)}, u32[]{:S(2)}) collective-permute-start(bf16[3,96,768]{2,1,0:T(8,128)(2,1)} %slice.211), channel_id=1, source_target_pairs={{0,16},{4,20},{8,24},{12,28},{16,0},{20,4},{24,8},{28,12},{1,17},{... | collective-permute-start | bytes 1327112 | tf_op jit(solution)/shard_map/ppermute | solution.py:438
  163.1 12.4 %collective-permute-start.39 = (bf16[3,96,768]{2,1,0:T(8,128)(2,1)}, bf16[3,96,768]{2,1,0:T(8,128)(2,1)}, u32[]{:S(2)}, u32[]{:S(2)}) collective-permute-start(bf16[3,96,768]{2,1,0:T(8,128)(2,1)} %slice.212), channel_id=1, source_target_pairs={{0,8},{4,12},{8,0},{12,4},{16,24},{20,28},{24,16},{28,20},{1,9},{5... | collective-permute-start | bytes 1327112 | tf_op jit(solution)/shard_map/ppermute | solution.py:438
  220.3 8.3 %collective-permute-start.42 = (bf16[192,256]{1,0:T(8,128)(2,1)}, bf16[192,256]{1,0:T(8,128)(2,1)}, u32[]{:S(2)}, u32[]{:S(2)}) collective-permute-start(bf16[192,256]{1,0:T(8,128)(2,1)} %get-tuple-element.86), channel_id=1, source_target_pairs={{0,4},{4,0},{8,12},{12,8},{16,20},{20,16},{24,28},{28,24},{1,5},{5... | collective-permute-start | bytes 294920 | tf_op jit(solution)/shard_map/ppermute | solution.py:438
  220.3 10.1 %collective-permute-start.43 = (bf16[192,256]{1,0:T(8,128)(2,1)}, bf16[192,256]{1,0:T(8,128)(2,1)}, u32[]{:S(2)}, u32[]{:S(2)}) collective-permute-start(bf16[192,256]{1,0:T(8,128)(2,1)} %get-tuple-element.87), channel_id=1, source_target_pairs={{0,8},{4,12},{8,0},{12,4},{16,24},{20,28},{24,16},{28,20},{1,9},{5... | collective-permute-start | bytes 294920 | tf_op jit(solution)/shard_map/ppermute | solution.py:438
  223.3 8.0 %collective-permute-start.44 = (bf16[192,256]{1,0:T(8,128)(2,1)}, bf16[192,256]{1,0:T(8,128)(2,1)}, u32[]{:S(2)}, u32[]{:S(2)}) collective-permute-start(bf16[192,256]{1,0:T(8,128)(2,1)} %copy-done.65), channel_id=1, source_target_pairs={{0,12},{4,8},{8,4},{12,0},{16,28},{20,24},{24,20},{28,16},{1,13},{... | collective-permute-start | bytes 294920 | tf_op jit(solution)/shard_map/ppermute | solution.py:438
  223.6 8.7 %collective-permute-start.45 = (bf16[192,256]{1,0:T(8,128)(2,1)}, bf16[192,256]{1,0:T(8,128)(2,1)}, u32[]{:S(2)}, u32[]{:S(2)}) collective-permute-start(bf16[192,256]{1,0:T(8,128)(2,1)} %copy-done.64), channel_id=1, source_target_pairs={{0,16},{4,20},{8,24},{12,28},{16,0},{20,4},{24,8},{28,12},{1,17},{... | collective-permute-start | bytes 294920 | tf_op jit(solution)/shard_map/ppermute | solution.py:438
  224.5 9.3 %collective-permute-start.46 = (bf16[192,256]{1,0:T(8,128)(2,1)}, bf16[192,256]{1,0:T(8,128)(2,1)}, u32[]{:S(2)}, u32[]{:S(2)}) collective-permute-start(bf16[192,256]{1,0:T(8,128)(2,1)} %copy-done.63), channel_id=1, source_target_pairs={{0,20},{4,16},{8,28},{12,24},{16,4},{20,0},{24,12},{28,8},{1,21},{... | collective-permute-start | bytes 294920 | tf_op jit(solution)/shard_map/ppermute | solution.py:438
  228.5 6.2 %collective-permute-start.47 = (bf16[192,256]{1,0:T(8,128)(2,1)S(1)}, bf16[192,256]{1,0:T(8,128)(2,1)S(1)}, u32[]{:S(2)}, u32[]{:S(2)}) collective-permute-start(bf16[192,256]{1,0:T(8,128)(2,1)S(1)} %copy-done.62), channel_id=1, source_target_pairs={{0,24},{4,28},{8,16},{12,20},{16,8},{20,12},{24,0},{28,4},{1,25},{... | collective-permute-start | bytes 294920 | tf_op jit(solution)/shard_map/ppermute | solution.py:438
  230.4 6.1 %collective-permute-start.48 = (bf16[192,256]{1,0:T(8,128)(2,1)S(1)}, bf16[192,256]{1,0:T(8,128)(2,1)S(1)}, u32[]{:S(2)}, u32[]{:S(2)}) collective-permute-start(bf16[192,256]{1,0:T(8,128)(2,1)S(1)} %copy-done.60), channel_id=1, source_target_pairs={{0,28},{4,24},{8,20},{12,16},{16,12},{20,8},{24,4},{28,0},{1,29},{... | collective-permute-start | bytes 294920 | tf_op jit(solution)/shard_map/ppermute | solution.py:438
  231.3 38.6 %collective-permute-start.69 = (bf16[2,192,1536]{2,1,0:T(8,128)(2,1)}, bf16[2,192,1536]{2,1,0:T(8,128)(2,1)S(1)}, u32[]{:S(2)}, u32[]{:S(2)}) collective-permute-start(bf16[2,192,1536]{2,1,0:T(8,128)(2,1)} %stack.115), channel_id=1, source_target_pairs={{0,16},{4,20},{8,24},{12,28},{16,0},{20,4},{24,8},{28,12},{1,17},{... | collective-permute-start | bytes 3538952 | tf_op jit(solution)/shard_map/ppermute | solution.py:438
  232.3 44.0 %collective-permute-start.81 = (bf16[2,384,768]{2,1,0:T(8,128)(2,1)S(1)}, bf16[2,384,768]{2,1,0:T(8,128)(2,1)S(1)}, u32[]{:S(2)}, u32[]{:S(2)}) collective-permute-start(bf16[2,384,768]{2,1,0:T(8,128)(2,1)S(1)} %copy-done.80), channel_id=1, source_target_pairs={{0,8},{4,12},{8,0},{12,4},{16,24},{20,28},{24,16},{28,20},{1,9},{5... | collective-permute-start | bytes 3538952 | tf_op jit(solution)/shard_map/ppermute | solution.py:438
  233.8 33.0 %collective-permute-start.62 = (bf16[4,96,768]{2,1,0:T(8,128)(2,1)S(1)}, bf16[4,96,768]{2,1,0:T(8,128)(2,1)S(1)}, u32[]{:S(2)}, u32[]{:S(2)}) collective-permute-start(bf16[4,96,768]{2,1,0:T(8,128)(2,1)S(1)} %dynamic-slice_bitcast_fusion), channel_id=1, source_target_pairs={{0,4},{4,0},{8,12},{12,8},{16,20},{20,16},{24,28},{28,24},{1,5},{5... | collective-permute-start | bytes 1769480 | tf_op jit(solution)/shard_map/ppermute | solution.py:438
  265.4 49.8 %collective-permute-start.49 = (bf16[8,384,256]{2,1,0:T(8,128)(2,1)}, bf16[8,384,256]{2,1,0:T(8,128)(2,1)S(1)}, u32[]{:S(2)}, u32[]{:S(2)}) collective-permute-start(bf16[8,384,256]{2,1,0:T(8,128)(2,1)} %get-tuple-element.94), channel_id=1, source_target_pairs={{4,0},{12,8},{20,16},{28,24},{5,1},{13,9},{21,17},{29,25},{6,2},{1... | collective-permute-start | bytes 4718600 | tf_op jit(solution)/shard_map/ppermute | solution.py:1226
  267.0 6.2 %collective-permute-start.65 = (bf16[96,768]{1,0:T(8,128)(2,1)S(1)}, bf16[96,768]{1,0:T(8,128)(2,1)S(1)}, u32[]{:S(2)}, u32[]{:S(2)}) collective-permute-start(bf16[96,768]{1,0:T(8,128)(2,1)S(1)} %get-tuple-element.142), channel_id=1, source_target_pairs={{0,24},{4,28},{8,16},{12,20},{16,8},{20,12},{24,0},{28,4},{1,25},{... | collective-permute-start | bytes 442376 | tf_op jit(solution)/shard_map/ppermute | solution.py:438
  273.2 15.8 %collective-permute-start.70 = (bf16[192,1536]{1,0:T(8,128)(2,1)S(1)}, bf16[192,1536]{1,0:T(8,128)(2,1)S(1)}, u32[]{:S(2)}, u32[]{:S(2)}) collective-permute-start(bf16[192,1536]{1,0:T(8,128)(2,1)S(1)} %fusion.8), channel_id=1, source_target_pairs={{0,8},{4,12},{8,0},{12,4},{16,24},{20,28},{24,16},{28,20},{1,9},{5... | collective-permute-start | bytes 1769480 | tf_op jit(solution)/shard_map/ppermute | solution.py:438
  276.2 6.1 %collective-permute-start.66 = (bf16[24,768]{1,0:T(8,128)(2,1)S(1)}, bf16[24,768]{1,0:T(8,128)(2,1)S(1)}, u32[]{:S(2)}, u32[]{:S(2)}) collective-permute-start(bf16[24,768]{1,0:T(8,128)(2,1)S(1)} %get-tuple-element.144), channel_id=1, source_target_pairs={{0,1},{1,2},{2,3},{3,0},{4,5},{5,6},{6,7},{7,4},{8,9},{9,10},{10,1... | collective-permute-start | bytes 110600 | tf_op jit(solution)/shard_map/ppermute | solution.py:442
  279.1 12.2 %collective-permute-start.82 = (bf16[384,768]{1,0:T(8,128)(2,1)S(1)}, bf16[384,768]{1,0:T(8,128)(2,1)S(1)}, u32[]{:S(2)}, u32[]{:S(2)}) collective-permute-start(bf16[384,768]{1,0:T(8,128)(2,1)S(1)} %fusion.9), channel_id=1, source_target_pairs={{0,16},{4,20},{8,24},{12,28},{16,0},{20,4},{24,8},{28,12},{1,17},{... | collective-permute-start | bytes 1769480 | tf_op jit(solution)/shard_map/ppermute | solution.py:438
  289.4 14.1 %collective-permute-start.72 = (bf16[2,24,1536]{2,1,0:T(8,128)(2,1)S(1)}, bf16[2,24,1536]{2,1,0:T(8,128)(2,1)S(1)}, u32[]{:S(2)}, u32[]{:S(2)}) collective-permute-start(bf16[2,24,1536]{2,1,0:T(8,128)(2,1)S(1)} %get-tuple-element.132), channel_id=1, source_target_pairs={{0,2},{1,3},{2,0},{3,1},{4,6},{5,7},{6,4},{7,5},{8,10},{9,11},{10,... | collective-permute-start | bytes 442376 | tf_op jit(solution)/shard_map/ppermute | solution.py:442
  290.4 13.1 %collective-permute-start.71 = (bf16[2,24,1536]{2,1,0:T(8,128)(2,1)S(1)}, bf16[2,24,1536]{2,1,0:T(8,128)(2,1)S(1)}, u32[]{:S(2)}, u32[]{:S(2)}) collective-permute-start(bf16[2,24,1536]{2,1,0:T(8,128)(2,1)S(1)} %get-tuple-element.130), channel_id=1, source_target_pairs={{0,1},{1,2},{2,3},{3,0},{4,5},{5,6},{6,7},{7,4},{8,9},{9,10},{10,1... | collective-permute-start | bytes 442376 | tf_op jit(solution)/shard_map/ppermute | solution.py:442
  291.7 19.9 %collective-permute-start.85 = (bf16[96,768]{1,0:T(8,128)(2,1)S(1)}, bf16[96,768]{1,0:T(8,128)(2,1)S(1)}, u32[]{:S(2)}, u32[]{:S(2)}) collective-permute-start(bf16[96,768]{1,0:T(8,128)(2,1)S(1)} %get-tuple-element.128), channel_id=1, source_target_pairs={{0,3},{1,0},{2,1},{3,2},{4,7},{5,4},{6,5},{7,6},{8,11},{9,8},{10,9... | collective-permute-start | bytes 442376 | tf_op jit(solution)/shard_map/ppermute | solution.py:442
  295.4 19.1 %collective-permute-start.84 = (bf16[96,768]{1,0:T(8,128)(2,1)S(1)}, bf16[96,768]{1,0:T(8,128)(2,1)S(1)}, u32[]{:S(2)}, u32[]{:S(2)}) collective-permute-start(bf16[96,768]{1,0:T(8,128)(2,1)S(1)} %get-tuple-element.129), channel_id=1, source_target_pairs={{0,2},{1,3},{2,0},{3,1},{4,6},{5,7},{6,4},{7,5},{8,10},{9,11},{10,... | collective-permute-start | bytes 442376 | tf_op jit(solution)/shard_map/ppermute | solution.py:442
  303.4 11.0 %collective-permute-start.83 = (bf16[96,768]{1,0:T(8,128)(2,1)S(1)}, bf16[96,768]{1,0:T(8,128)(2,1)S(1)}, u32[]{:S(2)}, u32[]{:S(2)}) collective-permute-start(bf16[96,768]{1,0:T(8,128)(2,1)S(1)} %get-tuple-element.127), channel_id=1, source_target_pairs={{0,1},{1,2},{2,3},{3,0},{4,5},{5,6},{6,7},{7,4},{8,9},{9,10},{10,1... | collective-permute-start | bytes 442376 | tf_op jit(solution)/shard_map/ppermute | solution.py:442
  304.2 26.4 %collective-permute-start.74 = (bf16[24,1536]{1,0:T(8,128)(2,1)}, bf16[24,1536]{1,0:T(8,128)(2,1)}, u32[]{:S(2)}, u32[]{:S(2)}) collective-permute-start(bf16[24,1536]{1,0:T(8,128)(2,1)} %fusion.34), channel_id=1, source_target_pairs={{0,4},{4,0},{8,12},{12,8},{16,20},{20,16},{24,28},{28,24},{1,5},{5... | collective-permute-start | bytes 221192 | tf_op jit(solution)/shard_map/ppermute | solution.py:438
  342.0 29.8 %collective-permute-start.52 = (bf16[2,256,768]{2,1,0:T(8,128)(2,1)}, bf16[2,256,768]{2,1,0:T(8,128)(2,1)S(1)}, u32[]{:S(2)}, u32[]{:S(2)}) collective-permute-start(bf16[2,256,768]{2,1,0:T(8,128)(2,1)} %get-tuple-element.125), channel_id=1, source_target_pairs={{0,16},{4,20},{8,24},{12,28},{16,0},{20,4},{24,8},{28,12},{1,17},{... | collective-permute-start | bytes 2359304 | tf_op jit(solution)/shard_map/ppermute | solution.py:438
  342.9 28.9 %collective-permute-start.50 = (bf16[2,256,768]{2,1,0:T(8,128)(2,1)}, bf16[2,256,768]{2,1,0:T(8,128)(2,1)}, u32[]{:S(2)}, u32[]{:S(2)}) collective-permute-start(bf16[2,256,768]{2,1,0:T(8,128)(2,1)} %get-tuple-element.126), channel_id=1, source_target_pairs={{0,8},{4,12},{8,0},{12,4},{16,24},{20,28},{24,16},{28,20},{1,9},{5... | collective-permute-start | bytes 2359304 | tf_op jit(solution)/shard_map/ppermute | solution.py:438
  347.5 8.0 %collective-permute-start.55 = (bf16[4,96,640]{2,1,0:T(8,128)(2,1)S(1)}, bf16[4,96,640]{2,1,0:T(8,128)(2,1)}, u32[]{:S(2)}, u32[]{:S(2)}) collective-permute-start(bf16[4,96,640]{2,1,0:T(8,128)(2,1)S(1)} %dynamic-slice_bitcast_fusion.1), channel_id=1, source_target_pairs={{0,4},{4,0},{8,12},{12,8},{16,20},{20,16},{24,28},{28,24},{1,5},{5... | collective-permute-start | bytes 1474568 | tf_op jit(solution)/shard_map/ppermute | solution.py:438
  356.9 6.6 %collective-permute-start.58 = (bf16[4,24,640]{2,1,0:T(8,128)(2,1)S(1)}, bf16[4,24,640]{2,1,0:T(8,128)(2,1)S(1)}, u32[]{:S(2)}, u32[]{:S(2)}) collective-permute-start(bf16[4,24,640]{2,1,0:T(8,128)(2,1)S(1)} %get-tuple-element.134), channel_id=1, source_target_pairs={{0,3},{1,0},{2,1},{3,2},{4,7},{5,4},{6,5},{7,6},{8,11},{9,8},{10,9... | collective-permute-start | bytes 368648 | tf_op jit(solution)/shard_map/ppermute | solution.py:442
  357.7 10.5 %collective-permute-start.57 = (bf16[4,24,640]{2,1,0:T(8,128)(2,1)S(1)}, bf16[4,24,640]{2,1,0:T(8,128)(2,1)S(1)}, u32[]{:S(2)}, u32[]{:S(2)}) collective-permute-start(bf16[4,24,640]{2,1,0:T(8,128)(2,1)S(1)} %get-tuple-element.135), channel_id=1, source_target_pairs={{0,2},{1,3},{2,0},{3,1},{4,6},{5,7},{6,4},{7,5},{8,10},{9,11},{10,... | collective-permute-start | bytes 368648 | tf_op jit(solution)/shard_map/ppermute | solution.py:442
  358.5 9.6 %collective-permute-start.56 = (bf16[4,24,640]{2,1,0:T(8,128)(2,1)S(1)}, bf16[4,24,640]{2,1,0:T(8,128)(2,1)S(1)}, u32[]{:S(2)}, u32[]{:S(2)}) collective-permute-start(bf16[4,24,640]{2,1,0:T(8,128)(2,1)S(1)} %get-tuple-element.133), channel_id=1, source_target_pairs={{0,1},{1,2},{2,3},{3,0},{4,5},{5,6},{6,7},{7,4},{8,9},{9,10},{10,1... | collective-permute-start | bytes 368648 | tf_op jit(solution)/shard_map/ppermute | solution.py:442
  368.3 7.8 %collective-permute-start.61 = (bf16[24,640]{1,0:T(8,128)(2,1)S(1)}, bf16[24,640]{1,0:T(8,128)(2,1)S(1)}, u32[]{:S(2)}, u32[]{:S(2)}) collective-permute-start(bf16[24,640]{1,0:T(8,128)(2,1)S(1)} %get-tuple-element.150), channel_id=1, source_target_pairs={{0,24},{4,28},{8,16},{12,20},{16,8},{20,12},{24,0},{28,4},{1,25},{... | collective-permute-start | bytes 92168 | tf_op jit(solution)/shard_map/ppermute | solution.py:438
  371.5 13.5 %collective-permute-start.59 = (bf16[24,640]{1,0:T(8,128)(2,1)S(1)}, bf16[24,640]{1,0:T(8,128)(2,1)S(1)}, u32[]{:S(2)}, u32[]{:S(2)}) collective-permute-start(bf16[24,640]{1,0:T(8,128)(2,1)S(1)} %get-tuple-element.149), channel_id=1, source_target_pairs={{0,8},{4,12},{8,0},{12,4},{16,24},{20,28},{24,16},{28,20},{1,9},{5... | collective-permute-start | bytes 92168 | tf_op jit(solution)/shard_map/ppermute | solution.py:438
  373.1 8.6 %collective-permute-start.53 = (bf16[256,768]{1,0:T(8,128)(2,1)S(1)}, bf16[256,768]{1,0:T(8,128)(2,1)S(1)}, u32[]{:S(2)}, u32[]{:S(2)}) collective-permute-start(bf16[256,768]{1,0:T(8,128)(2,1)S(1)} %get-tuple-element.121), channel_id=1, source_target_pairs={{0,8},{4,12},{8,0},{12,4},{16,24},{20,28},{24,16},{28,20},{1,9},{5... | collective-permute-start | bytes 1179656 | tf_op jit(solution)/shard_map/ppermute | solution.py:438
  374.8 8.1 %collective-permute-start.51 = (bf16[256,768]{1,0:T(8,128)(2,1)S(1)}, bf16[256,768]{1,0:T(8,128)(2,1)S(1)}, u32[]{:S(2)}, u32[]{:S(2)}) collective-permute-start(bf16[256,768]{1,0:T(8,128)(2,1)S(1)} %get-tuple-element.122), channel_id=1, source_target_pairs={{0,16},{4,20},{8,24},{12,28},{16,0},{20,4},{24,8},{28,12},{1,17},{... | collective-permute-start | bytes 1179656 | tf_op jit(solution)/shard_map/ppermute | solution.py:438
  (115 other events, 1090.3 us)

commit v2 on v1

--- a/solution.py
+++ b/solution.py
@@ -422,14 +422,14 @@
 
 
 CHUNK = 256
+COST = 10**9
 GROUP = 3
 WIDE = GROUP * HEAD_DIM
 HALF = HEAD_DIM // 2
 LANES = GROUP * CHUNK
 BF = jnp.bfloat16
 F32 = jnp.float32
-ANY = pl.BlockSpec(memory_space=pl.ANY)
-VM = pl.BlockSpec(memory_space=pltpu.VMEM)
+HB = pl.BlockSpec(memory_space=pltpu.HBM)
 SM = pl.BlockSpec(memory_space=pltpu.SMEM)
 GELU_SCALE = math.sqrt(2.0 / math.pi)
 
@@ -450,41 +450,67 @@
     return jnp.transpose(v.astype(F32)).astype(v.dtype)
 
 
-def call(body, outs, ins, args, scratch=(), limit=40, flops=0, moved=0, grid=None, out_specs=None):
-    shapes = tuple(jax.ShapeDtypeStruct(s, d) for s, d in outs)
-    kwargs = {} if grid is None else {"grid": grid}
+def call(body, outs, kinds, args, scratch=(), flops=0, moved=0):
+    staged = [i for i, kind in enumerate(kinds) if kind == "V"]
+    space = {"S": SM, "V": HB, "A": HB}
+    count, made = len(args), len(outs)
+
+    def run(*refs):
+        ins, sinks, rest = list(refs[:count]), refs[count : count + made], refs[count + made :]
+        held, results = rest[: len(staged)], rest[len(staged) : len(staged) + made]
+        sem_in, sem_out, sems = rest[len(staged) + made : len(staged) + made + 3]
+        rest = rest[len(staged) + made + 3 :]
+        first = [
+            pltpu.make_async_copy(ins[i], held[k], sem_in.at[k]) for k, i in enumerate(staged)
+        ]
+        for copy in first:
+            copy.start()
+        for k, i in enumerate(staged):
+            ins[i] = held[k]
+
+        def load(pairs):
+            more = [pltpu.make_async_copy(a, b, sems.at[i]) for i, (a, b) in enumerate(pairs)]
+            for copy in more:
+                copy.start()
+            for copy in more + first:
+                copy.wait()
+
+        body(load, *ins, *results, *rest)
+        last = [pltpu.make_async_copy(results[k], sinks[k], sem_out.at[k]) for k in range(made)]
+        for copy in last:
+            copy.start()
+        for copy in last:
+            copy.wait()
+
     return pl.pallas_call(
-        body,
-        out_shape=shapes,
-        in_specs=list(ins),
-        out_specs=tuple(out_specs) if out_specs is not None else tuple(VM for _ in outs),
-        scratch_shapes=list(scratch),
-        compiler_params=pltpu.CompilerParams(vmem_limit_bytes=limit * 2**20),
-        cost_estimate=pl.CostEstimate(flops=flops, bytes_accessed=moved, transcendentals=0),
-        **kwargs,
+        run,
+        out_shape=tuple(jax.ShapeDtypeStruct(s, d) for s, d in outs),
+        in_specs=[space[kind] for kind in kinds],
+        out_specs=tuple(HB for _ in outs),
+        scratch_shapes=[pltpu.VMEM(args[i].shape, args[i].dtype) for i in staged]
+        + [pltpu.VMEM(s, d) for s, d in outs]
+        + [
+            pltpu.SemaphoreType.DMA((max(1, len(staged)),)),
+            pltpu.SemaphoreType.DMA((made,)),
+            pltpu.SemaphoreType.DMA((48,)),
+        ]
+        + list(scratch),
+        compiler_params=pltpu.CompilerParams(vmem_limit_bytes=56 * 2**20),
+        cost_estimate=pl.CostEstimate(flops=1 + flops // COST, bytes_accessed=1 + moved // COST, transcendentals=0),
     )(*args)
-
-
-def run_copies(pairs, sems):
-    copies = [pltpu.make_async_copy(a, b, sems.at[i]) for i, (a, b) in enumerate(pairs)]
-    for copy in copies:
-        copy.start()
-    for copy in copies:
-        copy.wait()
 
 
 def at16(v):
     return pl.multiple_of(v, 16)
 
 
-def split_rows(meta, own, near, far, dst, unit):
-    c, z = meta[1], meta[3]
+def shard_rows(meta, near, far, dst, unit):
     half = unit // 2
-    pairs = [(own, dst.at[pl.ds(at16(z * unit), unit)])]
-    for t in range(1, 4):
-        zz = lax.rem(z + 4 - t, 4)
-        pairs.append((near[t - 1], dst.at[pl.ds(at16(zz * unit + c * half), half)]))
-        pairs.append((far[t - 1], dst.at[pl.ds(at16(zz * unit + (1 - c) * half), half)]))
+    pairs = []
+    for zz in range(4):
+        for core, part in ((meta[1], near), (1 - meta[1], far)):
+            to = at16(zz * unit + core * half)
+            pairs.append((part.at[zz, pl.ds(0, half)], dst.at[pl.ds(to, half)]))
     return pairs
 
 
@@ -511,85 +537,57 @@
     return jnp.concatenate(parts, axis=0)
 
 
-def project_body(count, first, whole, meta, gain, embed, cos, sin, *refs):
-    rows = refs[:count]
-    refs = refs[count:]
-    if whole:
-        (w_ref,) = refs[:1]
-        refs = refs[1:]
-        q_ref, kv_ref, n_ref, mk_ref, xs, w, wp, sems = refs
-        pairs = [(w_ref, w)]
-    else:
-        own, near, far = refs[0], refs[1:4], refs[4:7]
-        q_ref, kv_ref, n_ref, mk_ref, w_out_ref, xs, w, wp, sems = refs[7:]
-        pairs = split_rows(meta, own, near, far, w, 192)
-    pairs += [(rows[i], xs.at[i]) for i in range(count)]
-    run_copies(pairs, sems)
+def project_body(load, meta, gain, embed, cos, sin, *refs):
+    rows, refs = refs[:8], refs[8:]
+    near, far, q_ref, kv_a, kv_b, n_ref, mk_ref, w, xs, wp = refs
+    load(shard_rows(meta, near, far, w, 192) + [(rows[i], xs.at[i]) for i in range(8)])
     for part in range(3):
         wp[part] = w[:, part * WIDE : (part + 1) * WIDE]
-    if not whole:
-        w_out_ref[...] = w[...]
-
-    @pl.loop(0, count)
+
+    @pl.loop(0, 8)
     def _(i):
         x, flag = unmark(xs[i], embed[...])
         hat, _ = norm_parts(x)
         n = (hat * gain[...]).astype(BF)
         n_ref[i] = n
         mk_ref[i] = jnp.broadcast_to(jnp.where(flag, 1.0, 0.0), (CHUNK, 128)).astype(BF)
-        co, si = cos[first + i], sin[first + i]
-        q_ref[i] = turn_heads(jnp.transpose(mm(n, wp[0])), co, si).astype(BF)
-        kv_ref[i, :WIDE] = turn_heads(jnp.transpose(mm(n, wp[1])), co, si).astype(BF)
-        kv_ref[i, WIDE:] = jnp.transpose(mm(n, wp[2])).astype(BF)
-
-
-def project_rows(meta, gain, embed, cos, sin, rows, first, weights):
-    count = len(rows)
-    whole = len(weights) == 1
+        q_ref[i] = turn_heads(jnp.transpose(mm(n, wp[0])), cos[i], sin[i]).astype(BF)
+        keys = turn_heads(jnp.transpose(mm(n, wp[1])), cos[i], sin[i]).astype(BF)
+        values = jnp.transpose(mm(n, wp[2])).astype(BF)
+        for half, ref in enumerate((kv_a, kv_b)):
+
+            @pl.when(i // 4 == half)
+            def _():
+                ref[i % 4, :WIDE] = keys
+                ref[i % 4, WIDE:] = values
+
+
+def project_rows(meta, gain, embed, cos, sin, rows, weights):
     dim = rows[0].shape[1]
-    outs = [
-        ((count, WIDE, CHUNK), BF),
-        ((count, 2 * WIDE, CHUNK), BF),
-        ((count, CHUNK, dim), BF),
-        ((count, CHUNK, 128), BF),
-    ]
-    if not whole:
-        outs.append(((dim, 3 * WIDE), BF))
+    wide = weights[0].shape[-1]
     return call(
-        functools.partial(project_body, count, first, whole),
-        outs,
-        [SM, VM, VM, VM, VM] + [ANY] * (count + len(weights)),
+        project_body,
+        [
+            ((8, WIDE, CHUNK), BF),
+            ((4, 2 * WIDE, CHUNK), BF),
+            ((4, 2 * WIDE, CHUNK), BF),
+            ((8, CHUNK, dim), BF),
+            ((8, CHUNK, 128), BF),
+            ((dim, wide), BF),
+        ],
+        "SVVVV" + "A" * 10,
         (meta, gain, embed, cos, sin, *rows, *weights),
-        scratch=[
-            pltpu.VMEM((count, CHUNK, dim), BF),
-            pltpu.VMEM((dim, 3 * WIDE), BF),
-            pltpu.VMEM((3, dim, WIDE), BF),
-            pltpu.SemaphoreType.DMA((count + len(weights),)),
-        ],
-        flops=2 * count * CHUNK * dim * 3 * WIDE,
-        moved=count * CHUNK * dim * 6,
-    )
-
-
-def load_heads(meta, na, refs, qs, okv, ckv, sems):
-    q_a, q_b, kv_a, kv_b, r_a, r_b = refs
-    run_copies(
-        [
-            (q_a, qs.at[pl.ds(0, na)]),
-            (q_b, qs.at[pl.ds(na, 8 - na)]),
-            (kv_a, okv.at[pl.ds(0, na)]),
-            (kv_b, okv.at[pl.ds(na, 8 - na)]),
-        ],
-        sems,
-    )
-
-    @pl.when(meta[1] == 0)
-    def _():
-        run_copies([(kv_a, ckv.at[pl.ds(0, na)]), (kv_b, ckv.at[pl.ds(na, 8 - na)])], sems)
-
-    @pl.when(meta[1] != 0)
-    def _():
-        run_copies([(r_a, ckv.at[pl.ds(0, na)]), (r_b, ckv.at[pl.ds(na, 8 - na)])], sems)
+        scratch=[pltpu.VMEM((8, CHUNK, dim), BF), pltpu.VMEM((3, dim, WIDE), BF)],
+        flops=2 * 8 * CHUNK * dim * 3 * WIDE,
+        moved=8 * CHUNK * dim * 6,
+    )
+
+
+def head_pairs(refs, qs, kv):
+    pairs = [(refs[0], qs)]
+    for i, ref in enumerate(refs[1:]):
+        pairs.append((ref, kv.at[i // 2, pl.ds(i % 2 * 4, 4)]))
+    return pairs
 
 
 def thrice(v):
@@ -609,17 +607,16 @@
         ]
 
 
-def attend_body(na, meta, bounds, *refs):
-    heads = refs[:6]
-    sends = refs[6:14]
-    o_ref, ml_ref, qs, okv, ckv, okr, ckr, stacked, m_s, l_s, acc, sems = refs[14:]
-    load_heads(meta, na, heads, qs, okv, ckv, sems)
+def attend_body(load, meta, bounds, *refs):
+    heads = refs[:5]
+    send, o_ref, ml_ref, qs, kv, kr, stacked, m_s, l_s, acc = refs[5:]
+    load(head_pairs(heads, qs, kv))
     stacked[...] = jnp.zeros_like(stacked)
 
     @pl.loop(0, 8)
     def _(s):
-        okr[s] = flip(okv[s, :WIDE])
-        ckr[s] = flip(ckv[s, :WIDE])
+        for own in range(2):
+            kr[own, s] = flip(kv[own, s, :WIDE])
 
     r, c = meta[0], meta[1]
 
@@ -648,12 +645,12 @@
         m_s[...] = jnp.full_like(m_s, LOWEST)
         l_s[...] = jnp.zeros_like(l_s)
         acc[...] = jnp.zeros_like(acc)
-        tile(okr[s], okv[s, WIDE:], p * CHUNK, nlow, nhigh)
+        tile(kr[0, s], kv[0, s, WIDE:], p * CHUNK, nlow, nhigh)
 
         @pl.loop(meta[4 + p], p + c)
         def _(k):
             t = k ^ r ^ c
-            tile(ckr[t], ckv[t, WIDE:], k * CHUNK, low, high)
+            tile(kr[c, t], kv[c, t, WIDE:], k * CHUNK, low, high)
 
         total = l_s[...]
         inv = 1.0 / total
@@ -663,63 +660,46 @@
         o_ref[s] = out
         ml_ref[s, 0:1] = m_s[...]
         ml_ref[s, 1:2] = total
-        low_out = out.astype(BF)
-        for i in range(8):
-
-            @pl.when(s == i)
-            def _():
-                sends[i][...] = low_out
-
-
-HEAD_SCRATCH = [
-    pltpu.VMEM((8, WIDE, CHUNK), BF),
-    pltpu.VMEM((8, 2 * WIDE, CHUNK), BF),
-    pltpu.VMEM((8, 2 * WIDE, CHUNK), BF),
-]
+        send[p] = out.astype(BF)
+
+
+HEAD_SCRATCH = [pltpu.VMEM((8, WIDE, CHUNK), BF), pltpu.VMEM((2, 8, 2 * WIDE, CHUNK), BF)]
 
 
 def attend_rows(meta, bounds, heads):
-    na = heads[0].shape[0]
-    outs = [((WIDE, CHUNK), BF)] * 8 + [((8, WIDE, CHUNK), F32), ((8, 8, LANES), F32)]
     return call(
-        functools.partial(attend_body, na),
-        outs,
-        [SM, VM] + [ANY] * 6,
+        attend_body,
+        [((8, WIDE, CHUNK), BF), ((8, WIDE, CHUNK), F32), ((8, 8, LANES), F32)],
+        "SV" + "A" * 5,
         (meta, bounds, *heads),
         scratch=HEAD_SCRATCH
         + [
-            pltpu.VMEM((8, CHUNK, WIDE), BF),
-            pltpu.VMEM((8, CHUNK, WIDE), BF),
+            pltpu.VMEM((2, 8, CHUNK, WIDE), BF),
             pltpu.VMEM((WIDE, LANES), BF),
             pltpu.VMEM((1, LANES), F32),
             pltpu.VMEM((1, LANES), F32),
             pltpu.VMEM((GROUP, HEAD_DIM, CHUNK), F32),
-            pltpu.SemaphoreType.DMA((4,)),
         ],
         flops=20 * 2 * 2 * CHUNK * LANES * 256,
         moved=8 * CHUNK * WIDE * 16,
     )
 
 
-def attend_back_body(na, meta, bounds, cos, sin, o_ref, ml_ref, *refs):
-    heads = refs[:6]
-    grads = refs[6:14]
+def attend_back_body(load, meta, bounds, cos, sin, o_ref, ml_ref, *refs):
+    heads, gs = refs[:5], refs[5]
     (
-        pq_ref, own_ref, far_ref,
-        qs, okv, ckv, okr, ckr, ovr, cvr, gs,
-        st_q, st_g, row_q, row_g, dk_o, dv_o, dk_c, dv_c, dq, sems,
-    ) = refs[14:]
-    load_heads(meta, na, heads, qs, okv, ckv, sems)
-    run_copies([(grads[i], gs.at[i]) for i in range(8)], sems)
+        pq_ref, own_ref, far_a, far_b, far_c, far_d,
+        qs, kv, kr, vr, st_q, st_g, row_q, row_g, dk_o, dv_o, dk_c, dv_c, dq,
+    ) = refs[6:]
     for ref in (st_q, st_g, dk_o, dv_o, dk_c, dv_c):
         ref[...] = jnp.zeros_like(ref)
+    load(head_pairs(heads, qs, kv))
 
     @pl.loop(0, 8)
     def _(s):
-        okr[s] = flip(okv[s, :WIDE])
-        ckr[s] = flip(ckv[s, :WIDE])
-        ovr[s] = flip(okv[s, WIDE:])
-        cvr[s] = flip(ckv[s, WIDE:])
+        for own in range(2):
+            kr[own, s] = flip(kv[own, s, :WIDE])
+            vr[own, s] = flip(kv[own, s, WIDE:])
 
     r, c = meta[0], meta[1]
     lane = lax.broadcasted_iota(jnp.int32, (CHUNK, WIDE), 1) // HEAD_DIM
@@ -731,7 +711,7 @@
         stack_heads(q, st_q)
         total = ml_ref[s, 1:2]
         top = ml_ref[s, 0:1]
-        g_in = gs[s].astype(F32)
+        g_in = gs[p].astype(F32)
         attended = o_ref[s]
         scaled, fix = [], []
         for g in range(GROUP):
@@ -762,63 +742,70 @@
                     k_cols[g * HEAD_DIM : (g + 1) * HEAD_DIM], d[:, g * CHUNK : (g + 1) * CHUNK]
                 )
 
-        tile(okr[s], ovr[s], okv[s, :WIDE], p * CHUNK, nlow, nhigh, dk_o.at[s], dv_o.at[s])
+        tile(kr[0, s], vr[0, s], kv[0, s, :WIDE], p * CHUNK, nlow, nhigh, dk_o.at[s], dv_o.at[s])
 
         @pl.loop(meta[4 + p], p + c)
         def _(k):
             t = k ^ r ^ c
-            tile(ckr[t], cvr[t], ckv[t, :WIDE], k * CHUNK, low, high, dk_c.at[t], dv_c.at[t])
+            tile(kr[c, t], vr[c, t], kv[c, t, :WIDE], k * CHUNK, low, high, dk_c.at[t], dv_c.at[t])
 
         pq_ref[s] = turn_heads(dq[...] * 0.125, cos[s], -sin[s]).astype(BF)
 
     both = 1.0 - c.astype(F32)
 
-    @pl.loop(0, 8)
-    def _(s):
+    for s in range(8):
         dk = jnp.transpose(dk_c[s])
         dv = jnp.transpose(dv_c[s])
-        far_ref[s, :WIDE] = dk.astype(BF)
-        far_ref[s, WIDE:] = dv.astype(BF)
+        far_ref = (far_a, far_b, far_c, far_d)[s // 2]
+        far_ref[s % 2, :WIDE] = dk.astype(BF)
+        far_ref[s % 2, WIDE:] = dv.astype(BF)
         own_ref[s, :WIDE] = jnp.transpose(dk_o[s]) + both * dk
         own_ref[s, WIDE:] = jnp.transpose(dv_o[s]) + both * dv
 
 
 def attend_back(meta, bounds, cos, sin, attended, stats, heads, grads):
-    na = heads[0].shape[0]
-    rows = pltpu.VMEM((8, CHUNK, WIDE), BF)
+    rows = pltpu.VMEM((2, 8, CHUNK, WIDE), BF)
     sums = pltpu.VMEM((8, CHUNK, WIDE), F32)
     return call(
-        functools.partial(attend_back_body, na),
-        [((8, WIDE, CHUNK), BF), ((8, 2 * WIDE, CHUNK), F32), ((8, 2 * WIDE, CHUNK), BF)],
-        [SM, VM, VM, VM, VM, VM] + [ANY] * 14,
-        (meta, bounds, cos, sin, attended, stats, *heads, *grads),
+        attend_back_body,
+        [((8, WIDE, CHUNK), BF), ((8, 2 * WIDE, CHUNK), F32)] + [((2, 2 * WIDE, CHUNK), BF)] * 4,
+        "SVVVVV" + "A" * 5 + "V",
+        (meta, bounds, cos, sin, attended, stats, *heads, grads),
         scratch=HEAD_SCRATCH
-        + [rows] * 4
         + [
-            pltpu.VMEM((8, WIDE, CHUNK), BF),
+            rows,
+            rows,
             pltpu.VMEM((WIDE, LANES), BF),
             pltpu.VMEM((WIDE, LANES), BF),
             pltpu.VMEM((LANES, WIDE), BF),
             pltpu.VMEM((LANES, WIDE), BF),
         ]
         + [sums] * 4
-        + [pltpu.VMEM((WIDE, CHUNK), F32), pltpu.SemaphoreType.DMA((8,))],
-        limit=48,
+        + [pltpu.VMEM((WIDE, CHUNK), F32)],
         flops=20 * 2 * 5 * CHUNK * LANES * 256,
         moved=8 * CHUNK * WIDE * 30,
     )
 
 
-def middle_body(meta, gain, embed, x_ref, *refs):
-    heads = refs[:8]
-    own, near, far = refs[8], refs[9:12], refs[12:15]
-    mid_ref, n_ref, att_ref, w_ref, sems = refs[15:]
-    r = meta[0]
-    pairs = split_rows(meta, own, near, far, w_ref, 192)
-    for s in range(8):
-        d = r ^ s
-        pairs.append((heads[s], att_ref.at[d & 1, pl.ds(at16((d >> 1) * WIDE), WIDE)]))
-    run_copies(pairs, sems)
+def share_pairs(meta, own, parts, dst, unit, skip):
+    h, z = meta[2], meta[3]
+    part = unit // 4
+    pairs = [(own, dst.at[pl.ds(at16(z * unit), unit)])]
+    for t in range(1, 4):
+        zz = (z + 4 - t) & 3
+        for k in range(4):
+            to = at16(zz * unit + (h ^ k) * part)
+            pairs.append((parts[k].at[t - 1, pl.ds(skip, part)], dst.at[pl.ds(to, part)]))
+    return pairs
+
+
+def middle_body(load, meta, gain, embed, x_ref, heads, own, *refs):
+    parts = refs[:4]
+    mid_ref, n_ref, att_ref, w_ref = refs[4:]
+    pairs = share_pairs(meta, own, parts, w_ref, 192, 0)
+    for d in range(8):
+        pairs.append((heads.at[d], att_ref.at[d % 2, pl.ds(d // 2 * WIDE, WIDE)]))
+    load(pairs)
     for stream in range(2):
         x, _ = unmark(x_ref[stream], embed[...])
         mid = x + mm(att_ref[stream], w_ref[...], 0, 0)
@@ -827,26 +814,24 @@
         n_ref[stream * CHUNK : (stream + 1) * CHUNK] = (hat * gain[...]).astype(BF)
 
 
-def middle_rows(meta, gain, embed, marked, heads, weights):
+def middle_rows(meta, gain, embed, marked, heads, own, parts):
     dim = marked.shape[2]
     return call(
         middle_body,
         [((2, CHUNK, dim), F32), ((2 * CHUNK, dim), BF), ((2, dim, CHUNK), BF), ((dim, dim), BF)],
-        [SM, VM, VM, VM] + [ANY] * 15,
-        (meta, gain, embed, marked, *heads, *weights),
-        scratch=[pltpu.SemaphoreType.DMA((15,))],
+        "SVVV" + "A" * 6,
+        (meta, gain, embed, marked, heads, own, *parts),
         flops=2 * 2 * CHUNK * dim * dim,
         moved=8 * CHUNK * dim * 2,
     )
 
 
-def feed_body(meta, bias, *refs):
-    n_own, n_far, g_own, g_far, up_own, down_own, ff_r, ff_x, ff_y, ff_dd, ff_du = refs[:11]
-    downs, ups = (ff_r, ff_x, ff_y, ff_dd), (ff_r, ff_x, ff_y, ff_du)
+def feed_body(load, meta, bias, n_own, n_far, g_own, g_far, up_own, down_own, *refs):
+    shares = refs[:4]
     (
-        out_ref, outf_ref, ng_ref, ngf_ref, gu_ref, gd_ref, gb_ref,
-        ns, gs, wu, wd, acts, slopes, acc_o, acc_n, sems,
-    ) = refs[11:]
+        out_ref, outf_ref, ngf_ref, ng_ref, gb_ref, d_ref, u_ref,
+        ns, gs, wu, wd, acts, slopes,
+    ) = refs[4:]
     c, h, z = meta[1], meta[2], meta[3]
     rows = 2 * CHUNK
     part = bias.shape[1] // 4
@@ -855,62 +840,60 @@
         (n_far, ns.at[pl.ds(rows, rows)]),
         (g_own, gs.at[pl.ds(0, rows)]),
         (g_far, gs.at[pl.ds(rows, rows)]),
-        (down_own.at[pl.ds(at16(c * part), part)], wd.at[pl.ds(at16(z * part), part)]),
     ]
+    pairs += share_pairs(meta, down_own.at[pl.ds(at16(c * part), part)], shares, wd, part, 48)
     for k in range(4):
         cols = pl.ds(pl.multiple_of(k * 2 * part + c * part, 128), part)
         pairs.append((up_own.at[:, cols], wu.at[pl.ds(at16(z * 192), 192), pl.ds(k * part, part)]))
     for t in range(1, 4):
-        zz = lax.rem(z + 4 - t, 4)
+        zz = (z + 4 - t) & 3
         for k in range(4):
-            hh = h ^ k
-            pairs.append((downs[k].at[t - 1, pl.ds(0, 96)], wd.at[pl.ds(at16(zz * part + hh * 96), 96)]))
-            dst = pl.ds(at16(zz * 192 + hh * 48), 48)
+            dst = pl.ds(at16(zz * 192 + (h ^ k) * 48), 48)
             for b in range(2):
                 pairs.append(
                     (
-                        ups[k].at[t - 1, pl.ds(48 * b + (96 if k < 3 else 0), 48)],
+                        shares[k].at[t - 1, pl.ds(144 + 48 * b, 48)],
                         wu.at[dst, pl.ds(2 * part * b, 2 * part)],
                     )
                 )
-    run_copies(pairs, sems)
-    acc_o[...] = jnp.zeros_like(acc_o)
-    acc_n[...] = jnp.zeros_like(acc_n)
+    load(pairs)
+    gb_ref[...] = jnp.zeros_like(gb_ref)
+
+    def forward_and_back(span, out, ng):
+        v = mm(ns[span], wu[...]) + bias[...]
+        square = v * v
+        th = jnp.tanh(v * (GELU_SCALE + (GELU_SCALE * 0.044715) * square))
+        half = 0.5 + 0.5 * th
+        act = (v * half).astype(BF)
+        slope = half + (v * half) * (1.0 - th) * (GELU_SCALE + (3.0 * 0.044715 * GELU_SCALE) * square)
+        acts[span] = act
+        ug = (slope * mm(gs[span], wd[...], 1, 1)).astype(BF)
+        slopes[span] = ug
+        gb_ref[...] += jnp.sum(ug.astype(F32), axis=0, keepdims=True)
+        out[...] = mm(act, wd[...]).astype(out.dtype)
+        ng[...] = mm(ug, wu[...], 1, 1).astype(ng.dtype)
+
+    @pl.loop(0, 2)
+    def _(i):
+        low = pl.ds(pl.multiple_of(i * CHUNK, CHUNK), CHUNK)
+        forward_and_back(low, out_ref.at[low], ng_ref.at[low])
+        forward_and_back(
+            pl.ds(pl.multiple_of(rows + i * CHUNK, CHUNK), CHUNK), outf_ref.at[low], ngf_ref.at[low]
+        )
 
     @pl.loop(0, 4)
     def _(j):
         cols = pl.ds(pl.multiple_of(j * part, 128), part)
-        w_up = wu[:, cols]
-        w_down = wd[pl.ds(at16(j * part), part)]
-        b_up = bias[:, cols]
-
-        def rows_of(i, total):
-            span = pl.ds(pl.multiple_of(i * CHUNK, CHUNK), CHUNK)
-            v = mm(ns[span], w_up) + b_up
-            square = v * v
-            th = jnp.tanh(GELU_SCALE * (v + 0.044715 * (v * square)))
-            half = 0.5 * (1.0 + th)
-            act = (v * half).astype(BF)
-            slope = half + (0.5 * v) * (1.0 - th * th) * (
-                GELU_SCALE * (1.0 + (3.0 * 0.044715) * square)
-            )
-            ug = (slope * mm(gs[span], w_down, 1, 1)).astype(BF)
-            acts[span] = act
-            slopes[span] = ug
-            acc_o[span] += mm(act, w_down)
-            acc_n[span] += mm(ug, w_up, 1, 1)
-            return total + jnp.sum(ug.astype(F32), axis=0, keepdims=True)
-
-        gb_ref[:, cols] = lax.fori_loop(0, 4, rows_of, jnp.zeros((1, part), F32))
-        gd_ref[j ^ h] = mm(acts[...], gs[...], 0, 0).astype(BF)
-        gu = mm(ns[...], slopes[...], 0, 0).astype(BF)
-        for k in range(4):
-            gu_ref[h ^ k, :, cols] = gu[192 * k : 192 * (k + 1)]
-
-    out_ref[...] = acc_o[:rows]
-    outf_ref[...] = acc_o[rows:].astype(BF)
-    ng_ref[...] = acc_n[:rows]
-    ngf_ref[...] = acc_n[rows:].astype(BF)
+        gd = mm(acts[:, cols], gs[...], 0, 0).astype(BF)
+        for b in range(4):
+            d_ref[b, j] = gd[96 * b : 96 * (b + 1)]
+        gu = mm(ns[...], slopes[:, cols], 0, 0)
+        side = pl.ds(pl.multiple_of((j & 1) * part, 128), part)
+        line = pl.ds(at16((j >> 1) * 48), 48)
+        for b in range(16):
+            first = 192 * (b // 4) + 24 * (b % 4)
+            block = jnp.concatenate([gu[first : first + 24], gu[first + 96 : first + 120]])
+            u_ref[b // 4, b % 4, line, side] = block.astype(BF)
 
 
 def feed_rows(meta, bias, args):
@@ -919,39 +902,47 @@
     hid = bias.shape[1]
     return call(
         feed_body,
-        [
-            ((rows, dim), F32),
-            ((rows, dim), BF),
-            ((rows, dim), F32),
-            ((rows, dim), BF),
-            ((4, dim // 4, hid), BF),
-            ((4, hid // 4, dim), BF),
-            ((1, hid), F32),
-        ],
-        [SM, VM] + [ANY] * 11,
+        [((rows, dim), F32), ((rows, dim), BF), ((rows, dim), BF), ((rows, dim), F32)]
+        + [((1, hid), F32)]
+        + [((4, 4, hid // 16, dim), BF)] * 2,
+        "SV" + "A" * 10,
         (meta, bias, *args),
         scratch=[
             pltpu.VMEM((2 * rows, dim), BF),
             pltpu.VMEM((2 * rows, dim), BF),
             pltpu.VMEM((dim, hid), BF),
             pltpu.VMEM((hid, dim), BF),
-            pltpu.VMEM((2 * rows, hid // 4), BF),
-            pltpu.VMEM((2 * rows, hid // 4), BF),
-            pltpu.VMEM((2 * rows, dim), F32),
-            pltpu.VMEM((2 * rows, dim), F32),
-            pltpu.SemaphoreType.DMA((45,)),
+            pltpu.VMEM((2 * rows, hid), BF),
+            pltpu.VMEM((2 * rows, hid), BF),
         ],
-        limit=48,
         flops=6 * 2 * 2 * rows * dim * hid,
         moved=12 * dim * hid,
     )
 
 
+def pack_body(load, meta, w_out, w_down, w_up, share):
+    c, h = meta[1], meta[2]
+    part = w_up.shape[1] // 8
+    pairs = [
+        (w_out.at[pl.ds(at16(48 * h), 48)], share.at[pl.ds(0, 48)]),
+        (w_down.at[pl.ds(at16(part * c + 96 * h), 96)], share.at[pl.ds(48, 96)]),
+    ]
+    for k in range(4):
+        cols = pl.ds(pl.multiple_of((2 * k + c) * part, 128), part)
+        to = share.at[pl.ds(144 + 48 * (k // 2), 48), pl.ds(part * (k % 2), part)]
+        pairs.append((w_up.at[pl.ds(at16(48 * h), 48), cols], to))
+    load(pairs)
+
+
+def pack_share(place, w_out, w_down, w_up):
+    return call(pack_body, [((240, w_out.shape[1]), BF)], "SAAA", (place, w_out, w_down, w_up))[0]
+
+
 def middle_back_body(
-    meta, gain, b_down, mid_ref, ng_ref, ngf_ref, out_ref, outf_ref, g_ref, x_ref, w_ref, *refs
+    load, meta, gain, b_down, mid_ref, ng_ref, out_ref, outf_ref, ngf_ref, g_ref, x_ref, w_ref,
+    lay_ref, mg_ref, sum_ref, send,
 ):
-    lay_ref, mg_ref, sum_ref = refs[:3]
-    sends = refs[3:11]
+    load([])
     gain_sum = jnp.zeros((1, gain.shape[1]), F32)
     g_sum = gain_sum
     for stream in range(2):
@@ -974,117 +965,138 @@
             sum_ref[2:3] = jnp.sum(jnp.where(flag, mg.astype(F32), 0.0), axis=0, keepdims=True)
     sum_ref[0:1] = gain_sum
     sum_ref[1:2] = g_sum
-    for s in range(8):
-        d = meta[0] ^ s
-        rows = w_ref[pl.ds(at16((d >> 1) * WIDE), WIDE)]
-        sends[s][...] = mm(rows, mg_ref[d & 1], 1, 1).astype(BF)
+    for d in range(8):
+        send[d] = mm(w_ref[d // 2 * WIDE : (d // 2 + 1) * WIDE], mg_ref[d % 2], 1, 1).astype(BF)
 
 
 def middle_back(meta, gain, b_down, args):
     dim = gain.shape[1]
     return call(
         middle_back_body,
-        [((2, CHUNK, dim), BF), ((2, CHUNK, dim), BF), ((8, dim), F32)]
-        + [((WIDE, CHUNK), BF)] * 8,
-        [SM] + [VM] * 10,
+        [((2, CHUNK, dim), BF), ((2, CHUNK, dim), BF), ((8, dim), F32), ((8, WIDE, CHUNK), BF)],
+        "S" + "V" * 10,
         (meta, gain, b_down, *args),
         flops=4 * CHUNK * dim * dim,
         moved=20 * CHUNK * dim,
     )
 
 
-def out_grad_body(att_ref, mg_ref, o_ref):
-    o_ref[...] = (mm(att_ref[0], mg_ref[0]) + mm(att_ref[1], mg_ref[1])).astype(BF)
-
-
-def project_back_body(steps, last, meta_free, *refs):
-    own, far, pq, n_ref, mk_ref, cos, sin, w_ref = (meta_free, *refs[:7])
-    refs = refs[7:]
-    if last:
-        carry, vec = refs[:2]
-        refs = refs[2:]
-    ng_ref, gq_ref, gs_ref, wp, acc = refs
+def by_z(grad, ref):
+    for zz in range(4):
+        for h in range(4):
+            first = 192 * h + 24 * zz
+            pair = jnp.concatenate([grad[first : first + 24], grad[first + 96 : first + 120]])
+            ref[zz, 48 * h : 48 * (h + 1)] = pair.astype(BF)
+
+
+def out_grad_body(load, att_ref, mg_ref, o_ref):
+    load([])
+    by_z(mm(att_ref[0], mg_ref[0]) + mm(att_ref[1], mg_ref[1]), o_ref)
+
+
+def project_back_body(
+    own, f0, f1, f2, f3, pq, n_ref, mk_ref, cos, sin, w_ref,
+    away_x, away_y, stay, gq_ref, gs_ref, wp, acc,
+):
     i = pl.program_id(0)
 
     @pl.when(i == 0)
     def _():
         for part in range(3):
             wp[part] = w_ref[:, part * WIDE : (part + 1) * WIDE]
-        if last:
-            acc[...] = carry[...]
-            gs_ref[...] = vec[...]
-        else:
-            acc[...] = jnp.zeros_like(acc)
-            gs_ref[...] = jnp.zeros_like(gs_ref)
-
-    kv = own[0] + far[0].astype(F32)
+        acc[...] = jnp.zeros_like(acc)
+        gs_ref[...] = jnp.zeros_like(gs_ref)
+
+    piece = jnp.where(i % 4 == 0, 1 - i // 4, jnp.where(i == 1, 3, jnp.where(i == 3, 3, jnp.where(i == 7, 1, jnp.where(i == 6, 0, 2)))))
+    far = jnp.where(piece < 2, jnp.where(piece == 0, f0[0], f1[0]), jnp.where(piece == 2, f2[0], f3[0]))
+    kv = own[0] + far.astype(F32)
     parts = [
         pq[0],
         turn_heads(kv[:WIDE] * 0.125, cos[0], -sin[0]).astype(BF),
         kv[WIDE:].astype(BF),
     ]
-    n = n_ref[0]
+    n, mk = n_ref[0], mk_ref[0]
     ng = jnp.zeros((CHUNK, n.shape[1]), F32)
     for k in range(3):
         ng += mm(flip(parts[k]), wp[k], 1, 1)
         acc[k * WIDE : (k + 1) * WIDE] += mm(parts[k], n)
-    ng_ref[0] = ng.astype(BF)
+    low = ng.astype(BF)
+
+    @pl.when(i < 2)
+    def _():
+        away_x[0] = low
+
+    @pl.when((i >= 2) & (i < 4))
+    def _():
+        away_y[0] = low
+
+    @pl.when(i >= 4)
+    def _():
+        stay[0] = ng
+
     gs_ref[0:1] += jnp.sum(ng * n.astype(F32), axis=0, keepdims=True)
-    gs_ref[1:2] += jnp.sum(ng * mk_ref[0][:, :1].astype(F32), axis=0, keepdims=True)
-
-    @pl.when(i == steps - 1)
+    gs_ref[1:2] += jnp.sum(ng * mk[:, :1].astype(F32), axis=0, keepdims=True)
+
+    @pl.when(i == 7)
     def _():
-        gq_ref[...] = jnp.transpose(acc[...]).astype(BF) if last else acc[...]
+        by_z(jnp.transpose(acc[...]), gq_ref)
 
 
 def pick(order):
-    def at(i):
+    def slot_of(i):
         slot = jnp.int32(order[-1])
         for k in range(len(order) - 2, -1, -1):
             slot = jnp.where(i == k, order[k], slot)
         return slot
 
-    return at
-
-
-def project_back(order, own, far, pq, n, mk, cos, sin, w, carry=None):
-    last = carry is not None
-    steps = len(order)
+    return slot_of
+
+
+def project_back(own, far, pq, n, mk, cos, sin, w):
     dim = n.shape[2]
-    slot = pick(order)
-
-    def chunk(rows, cols):
-        return pl.BlockSpec((1, rows, cols), lambda i: (slot(i), 0, 0))
+    wide = w.shape[1] + HEAD_DIM
+    slot = pick((2, 6, 5, 7, 0, 4, 1, 3))
+
+    def block(rows, cols, index):
+        return pl.BlockSpec((1, rows, cols), lambda i: (index(i), 0, 0))
 
     def whole(*shape):
         return pl.BlockSpec(shape, lambda i: tuple(0 for _ in shape))
 
-    wide = 3 * WIDE + HEAD_DIM
-    args = [own, far, pq, n, mk, cos, sin, w]
-    specs = [
-        chunk(2 * WIDE, CHUNK), chunk(2 * WIDE, CHUNK), chunk(WIDE, CHUNK), chunk(CHUNK, dim),
-        chunk(CHUNK, 128), chunk(HALF, CHUNK), chunk(HALF, CHUNK), whole(dim, 3 * WIDE),
-    ]
-    if last:
-        args += list(carry)
-        specs += [whole(wide, dim), whole(8, dim)]
-    gq_shape = (dim, wide) if last else (wide, dim)
-    return call(
-        functools.partial(project_back_body, steps, last),
-        [((steps, CHUNK, dim), BF), (gq_shape, BF if last else F32), ((8, dim), F32)],
-        specs,
-        args,
-        scratch=[pltpu.VMEM((3, dim, WIDE), BF), pltpu.VMEM((wide, dim), F32)],
-        grid=(steps,),
-        out_specs=[
-            pl.BlockSpec((1, CHUNK, dim), lambda i: (i, 0, 0)), whole(*gq_shape), whole(8, dim)
+    return pl.pallas_call(
+        project_back_body,
+        grid=(8,),
+        out_shape=(
+            jax.ShapeDtypeStruct((2, CHUNK, dim), BF),
+            jax.ShapeDtypeStruct((2, CHUNK, dim), BF),
+            jax.ShapeDtypeStruct((4, CHUNK, dim), F32),
+            jax.ShapeDtypeStruct((4, dim // 4, wide), BF),
+            jax.ShapeDtypeStruct((8, dim), F32),
+        ),
+        in_specs=[
+            block(2 * WIDE, CHUNK, slot),
+            *[block(2 * WIDE, CHUNK, lambda i: slot(i) % 2)] * 4,
+            block(WIDE, CHUNK, slot),
+            block(CHUNK, dim, slot), block(CHUNK, 128, slot),
+            block(HALF, CHUNK, slot), block(HALF, CHUNK, slot), whole(*w.shape),
         ],
-        flops=2 * 2 * steps * CHUNK * dim * 3 * WIDE,
-        moved=steps * CHUNK * dim * 8,
-    )
-
-
-def last_body(meta, gain, embed, x_ref, mg_ref, keep_ref, far_ref, o_ref):
+        out_specs=(
+            block(CHUNK, dim, lambda i: jnp.minimum(i, 1)),
+            block(CHUNK, dim, lambda i: jnp.clip(i - 2, 0, 1)),
+            block(CHUNK, dim, lambda i: jnp.clip(i - 4, 0, 3)),
+            whole(4, dim // 4, wide),
+            whole(8, dim),
+        ),
+        scratch_shapes=[pltpu.VMEM((3, dim, WIDE), BF), pltpu.VMEM((wide, dim), F32)],
+        compiler_params=pltpu.CompilerParams(vmem_limit_bytes=56 * 2**20),
+        cost_estimate=pl.CostEstimate(
+            flops=1 + 4 * 8 * CHUNK * dim * 3 * WIDE // COST, bytes_accessed=1, transcendentals=0
+        ),
+    )(own, *far, pq, n, mk, cos, sin, w)
+
+
+def last_body(load, meta, gain, embed, x_ref, mg_ref, keep_ref, far_ref, o_ref):
+    load([])
     c = meta[1]
     for stream, ng in ((c, keep_ref[...]), (1 - c, far_ref[...].astype(F32))):
         x, flag = unmark(x_ref[stream], embed[...])
@@ -1102,6 +1114,27 @@
 
 def at(v, index, axis=0):
     return lax.dynamic_index_in_dim(v, index, axis, keepdims=False)
+
+
+def after(value, *needed):
+    return lax.optimization_barrier((value, *needed))[0]
+
+
+def add(a, b):
+    return a.astype(F32) + b.astype(F32)
+
+
+def exchange(v):
+    return lax.all_to_all(v, "ctx", 0, 0, tiled=True)
+
+
+def exchange_chips(v):
+    groups = [[i + core for i in range(0, 8, 2)] for core in range(2)]
+    return lax.all_to_all(v, "ctx", 0, 0, axis_index_groups=groups, tiled=True)
+
+
+def exchange_z(v):
+    return lax.all_to_all(v, "fsdp", 0, 0, tiled=True)
 
 
 def shards_by_heads(
@@ -1126,58 +1159,46 @@
     hid = w_up.shape[1]
     part = hid // 8
     total = CHUNK * 8
+    clean = c == 0
+
+    share = pack_share(jnp.stack([r, c, h, z]).astype(jnp.int32), w_out, w_down, w_up)
+    ff_t = lax.all_gather(share, "fsdp")
+    hidden = after(hidden, share)
 
     noisy = jnp.where(noise_mask[0][:, None] == 1, jnp.asarray(jnp.inf, BF), hidden[0, 1])
-    marked = jnp.stack([hidden[0, 0], noisy])
-    mine = at(marked, c)
-    other = swap(at(marked, 1 - c), 1)
+    mine = jnp.where(clean, hidden[0, 0], noisy)
+    other = swap(jnp.where(clean, noisy, hidden[0, 0]), 1)
     mine_x, mine_y = swap(mine, 2), swap(mine, 4)
     other_x, other_y = swap(other, 2), swap(other, 4)
-    mine_d, other_d = swap(mine_x, 4), swap(other_y, 2)
-
+    marked = jnp.stack([hidden[0, 0], noisy])
+
+    size = hid // 4 + dim
+    w_qkv = after(w_qkv, other)
     small = jnp.concatenate([b_up, b_down, gain_one, gain_two, mask_embed])
-    size = small.shape[0]
-    small = jnp.pad(small, (0, 2048 - size)).reshape(16, 128)
-    small = jnp.stack([small] + [turn(small, t) for t in range(1, 4)])
-    small = jnp.take(small, (z - jnp.arange(4)) % 4, axis=0).reshape(4, 2048).astype(F32)
+    small = jnp.pad(small, (0, 16 * 3 * WIDE - size)).reshape(16, 3 * WIDE)
+    own_qkv = jnp.concatenate([cut(w_qkv[:, k * dim : (k + 1) * dim], h, WIDE, 1) for k in range(3)], 1)
     quarter = dim // 4
+    half = jnp.concatenate([cut(own_qkv, c, quarter // 2), small])
+    half = jnp.broadcast_to(half, (4, *half.shape))
+    near = exchange_z(half)
+    far = swap(near, 1)
+    small = near[:, quarter // 2 :].reshape(4, -1)[:, :size].astype(F32)
     bias = at(small[:, : hid // 4].reshape(4, 2, part), c, 1).reshape(1, 4 * part)
     b_down_all, gain_a, gain_b, embed = [
         small[:, hid // 4 + k * quarter : hid // 4 + (k + 1) * quarter].reshape(1, dim)
         for k in range(4)
     ]
-
-    own_qkv = jnp.concatenate([cut(w_qkv[:, k * dim : (k + 1) * dim], h, WIDE, 1) for k in range(3)], 1)
-    half = cut(own_qkv, c, quarter // 2)
-    near_qkv = [turn(half, t) for t in range(1, 4)]
-    far_qkv = [swap(v, 1) for v in near_qkv]
-    up_rows = cut(w_up, h, quarter // 4).reshape(quarter // 4, 4, 2, part)
-    up_rows = at(up_rows, c, 2)
-    share = jnp.concatenate(
-        [
-            cut(w_down, 4 * c + h, part // 4),
-            up_rows[:, :2].reshape(quarter // 4, 2 * part),
-            up_rows[:, 2:].reshape(quarter // 4, 2 * part),
-        ]
-    )
-    ff_r = jnp.stack([turn(share, t) for t in range(1, 4)])
-    ff_x, ff_y = swap(ff_r, 2), swap(ff_r, 4)
-    ff_dd = swap(ff_x[:, : part // 4], 4)
-    ff_du = swap(ff_y[:, part // 4 :], 2)
-    half = cut(w_out, c, quarter // 2)
-    near_out = [turn(half, t) for t in range(1, 4)]
-    far_out = [swap(v, 1) for v in near_out]
+    mine_d, other_d = swap(mine_x, 4), swap(other_y, 2)
 
     lengths = doc_lengths[0]
     index = jnp.arange(lengths.shape[0])
     ends = jnp.sum(jnp.where(index[None, :] <= index[:, None], lengths[None, :], 0), axis=1)
     place = jnp.arange(total, dtype=jnp.int32)
-    after = ends[None, :] > place[:, None]
-    start = jnp.max(jnp.where(after, 0, ends[None, :]), axis=1)
-    stop = jnp.min(jnp.where(after, ends[None, :], total), axis=1)
+    later = ends[None, :] > place[:, None]
+    start = jnp.max(jnp.where(later, 0, ends[None, :]), axis=1)
+    stop = jnp.min(jnp.where(later, ends[None, :], total), axis=1)
     block = place // BLOCK * BLOCK
     limit = jnp.minimum(block + BLOCK, stop)
-    clean = c == 0
     bounds = jnp.stack(
         [start, jnp.where(clean, limit, block), jnp.where(clean, start, jnp.maximum(start, block)), limit]
     )
@@ -1189,107 +1210,96 @@
     frequency = jnp.exp(jnp.arange(HALF).astype(F32) * (-2.0 * math.log(10000.0) / HEAD_DIM))
     angles = slots.astype(F32)[:, None, :] * frequency[None, :, None]
     cos, sin = jnp.cos(angles), jnp.sin(angles)
-
-    rows_a = (mine, other, mine_x, other_x, mine_y, other_y)
-    q_a, kv_a, n_a, mk_a, w_all = project_rows(
-        meta, gain_a, embed, cos, sin, rows_a, 0, (own_qkv, *near_qkv, *far_qkv)
-    )
-    q_b, kv_b, n_b, mk_b = project_rows(meta, gain_a, embed, cos, sin, (mine_d, other_d), 6, (w_all,))
-    give = [(i, i + 1) for i in range(0, 8, 2)]
-    r_a, r_b = lax.ppermute(kv_a, "ctx", give), lax.ppermute(kv_b, "ctx", give)
-    heads = (q_a, q_b, kv_a, kv_b, r_a, r_b)
-    *sends, attended, stats = attend_rows(meta, bounds, heads)
-    got = [sends[0]] + [swap(sends[s], s) for s in range(1, 8)]
-    middle, normed, att, w_out_all = middle_rows(
-        meta, gain_b, embed, marked, got, (w_out, *near_out, *far_out)
-    )
     grads = out_grad[0]
     grad_rows = grads.reshape(2 * CHUNK, dim)
-    out_own, out_far, ng_own, ng_far, gu, gd, gbu = feed_rows(
-        meta,
-        bias,
-        (normed, swap(normed, 1), grad_rows, swap(grad_rows, 1), w_up, w_down, ff_r, ff_x, ff_y, ff_dd, ff_du),
+
+    ff_r = jnp.take(ff_t, (z - jnp.arange(1, 4)) % 4, axis=0)
+    near, ff_r = lax.optimization_barrier((near, ff_r))
+    shares = (ff_r, swap(ff_r, 2), swap(ff_r, 4), swap(ff_r, 6))
+    rows = (mine, other, mine_x, other_x, mine_y, other_y, mine_d, other_d)
+    q, *kv, normed_one, marks, w_all = project_rows(meta, gain_a, embed, cos, sin, rows, (near, far))
+    give = [(i, i + 1) for i in range(0, 8, 2)]
+    heads = (q, *kv, *[lax.ppermute(v, "ctx", give) for v in kv])
+    send, attended, stats = attend_rows(meta, bounds, heads)
+    grad_far = swap(after(grad_rows, kv[0]), 1)
+    middle, normed, att, w_out_all = middle_rows(
+        meta, gain_b, embed, marked, exchange(send), w_out, shares
+    )
+    out_own, out_far, ng_far, ng_own, gbu, gd, gu = feed_rows(
+        meta, bias, (normed, swap(normed, 1), grad_rows, grad_far, w_up, w_down, *shares)
     )
     ng_far, out_far = swap(ng_far, 1), swap(out_far, 1)
-
-    layer, mid_grad, sums, *sends = middle_back(
-        meta,
-        gain_b,
-        b_down_all,
-        (middle, ng_own, ng_far, out_own, out_far, grads, marked, w_out_all),
-    )
-    got = [sends[0]] + [swap(sends[s], s) for s in range(1, 8)]
+    gd = lax.psum_scatter(gd.reshape(-1, dim), "fsdp", scatter_dimension=0, tiled=True)
+
+    layer, mid_grad, sums, send = middle_back(
+        meta, gain_b, b_down_all, (middle, ng_own, out_own, out_far, ng_far, grads, marked, w_out_all)
+    )
+    got = exchange(send)
     (go,) = call(
-        out_grad_body, [((dim, dim), BF)], [VM, VM], (att, mid_grad), flops=4 * CHUNK * dim * dim
-    )
-    pq, own_kv, far_kv = attend_back(meta, bounds, cos, sin, attended, stats, heads, got)
-    far_kv = lax.ppermute(far_kv, "ctx", [(b, a) for a, b in give])
-    n_all = jnp.concatenate([n_a, n_b])
-    mk_all = jnp.concatenate([mk_a, mk_b])
-    back = (own_kv, far_kv, pq, n_all, mk_all, cos, sin, w_all)
-    away, *carry = project_back((2, 6, 5, 7), *back)
-    in_x, in_y = swap(away[:2], 2), swap(away[2:], 4)
-    stay, gq, vec = project_back((0, 4, 1, 3), *back, carry=carry)
-    stay = stay.astype(F32)
-    keep = stay[0] + in_x[0].astype(F32)
-    keep += swap((stay[1] + in_x[1].astype(F32)).astype(BF), 4).astype(F32)
-    pair = stay[2] + in_y[0].astype(F32)
-    pair += swap((stay[3] + in_y[1].astype(F32)).astype(BF), 2).astype(F32)
-    pair = swap(pair.astype(BF), 1)
+        out_grad_body, [((4, dim // 4, dim), BF)], "VV", (att, mid_grad), flops=4 * CHUNK * dim * dim
+    )
+    got, gu, go = lax.optimization_barrier((got, gu, go))
+    go = lax.psum_scatter(go.reshape(-1, dim), "fsdp", scatter_dimension=0, tiled=True)
+    gu = exchange_chips(gu)
+    pq, own_kv, *far_kv = attend_back(meta, bounds, cos, sin, attended, stats, heads, got)
+    far_kv = [lax.ppermute(v, "ctx", [(b, a) for a, b in give]) for v in far_kv]
+
+    gu = jnp.sum(after(gu, pq).astype(F32), axis=0).astype(BF).reshape(-1, dim)
+    gd = after(gd, pq).reshape(4, part // 4, dim)
+    *far_kv, gu, gd = lax.optimization_barrier((*far_kv, gu, gd))
+    gu = lax.psum_scatter(gu, "fsdp", scatter_dimension=0, tiled=True)
+
+    away_x, away_y, stay, gq, vec = project_back(
+        own_kv, far_kv, pq, normed_one, marks, cos, sin, w_all
+    )
+    in_x, in_y = swap(away_x, 2), swap(away_y, 4)
+    gd = exchange_chips(gd)
+    gbu = gbu.reshape(4, 1, part)
+    gbu = jnp.where(clean, jnp.concatenate([gbu, 0 * gbu], 1), jnp.concatenate([0 * gbu, gbu], 1))
+    flat = jnp.concatenate([gbu.reshape(-1), sums[:3].reshape(-1), vec[:2].reshape(-1)])
+    wide = gq.shape[2]
+    length = flat.shape[0]
+
+    def parts_of(v):
+        return jnp.pad(v, (0, 16 * wide - length)).reshape(16, wide).astype(BF)
+
+    rows = dim // 4
+    flat = jnp.broadcast_to(parts_of(flat), (4, 16, wide))
+    gq = after(jnp.concatenate([gq, flat], 1).reshape(-1, wide), go)
+    gq = lax.psum_scatter(gq, "fsdp", scatter_dimension=0, tiled=True)
+    over_y, over_x = add(stay[1], in_x[1]).astype(BF), add(stay[3], in_y[1]).astype(BF)
+    near_one, near_two = swap(over_y, 4), swap(over_x, 2)
+    gq = after(gq, over_y, over_x, gd)
+    flat = jnp.broadcast_to(gq[rows:], (8, 16, wide))
+    gq = jnp.concatenate([gq[:rows].reshape(8, dim // 32, wide), flat], 1)
+    go = jnp.pad(go.reshape(8, dim // 32, dim), ((0, 0), (0, 16), (0, 0)))
+    gq = exchange(jnp.concatenate([gq, go], 2))
+    keep = add(stay[0], in_x[0]) + near_one.astype(F32)
+    pair = (add(stay[2], in_y[0]) + near_two.astype(F32)).astype(BF)
+    pair = swap(pair, 1)
+    gu = after(gu, over_y, over_x)
+    gq = after(gq, keep, pair)
     (input_grad,) = call(
         last_body,
         [((2, CHUNK, dim), BF)],
-        [SM] + [VM] * 6,
+        "S" + "V" * 6,
         (meta, gain_a, embed, marked, mid_grad, keep, pair),
         moved=10 * CHUNK * dim,
     )
 
-    def line(v):
-        out = at(v, z).astype(F32)
-        for t in range(1, 4):
-            out += turn(at(v, (z + t) % 4).astype(BF), t).astype(F32)
-        return out
-
-    def plane_chip(v, first):
-        one, two = (1, 2) if first == 0 else (2, 1)
-        got = swap(jnp.stack([v[one], v[3]]), 2 * one)
-        low = v[0].astype(F32) + got[0].astype(F32)
-        high = (v[two].astype(F32) + got[1].astype(F32)).astype(BF)
-        return low + swap(high, 2 * two).astype(F32)
-
-    gd = line(plane_chip(gd, 0).reshape(4, part // 4, dim))
-    gu = plane_chip(gu, 1).reshape(2, 4, dim // 32, 4 * part)
-    gu = line(jnp.swapaxes(gu, 0, 1))
+    gd = jnp.sum(gd.astype(F32), axis=0).reshape(part // 4, dim)
+    gu = gu.astype(F32).reshape(2, 2, dim // 32, 2 * part).transpose(1, 2, 0, 3)
+    gu = gu.reshape(2, dim // 32, 4 * part)
     gu_far = swap(at(gu, 1 - c).astype(BF), 1).astype(F32)
     gu = at(gu, c)
     gu = jnp.where(clean, jnp.stack([gu, gu_far]), jnp.stack([gu_far, gu]))
     gu = gu.reshape(2, dim // 32, 4, part).transpose(1, 2, 0, 3).reshape(dim // 32, hid)
-
-    def over_core(v):
-        v = v.reshape(4, 2, dim // 8, v.shape[-1])
-        return at(v, c, 1).astype(F32) + swap(at(v, 1 - c, 1), 1).astype(F32)
-
-    go = over_core(go).astype(BF)
-    go_sum = at(go, h).astype(F32)
-    for k in range(1, 4):
-        go_sum += swap(at(go, h ^ k), 2 * k).astype(F32)
-    go = line(go_sum.reshape(4, dim // 32, dim))
-
-    gq = over_core(gq)
-    gq = line(jnp.swapaxes(gq.reshape(4, 4, dim // 32, gq.shape[-1]), 0, 1))
-    gq_low = gq.astype(BF)
-    pieces = [at(gq, h)] + [swap(at(gq_low, h ^ k), 2 * k).astype(F32) for k in range(1, 4)]
-    gq = jnp.take(jnp.stack(pieces), jnp.arange(4) ^ h, axis=0)[..., : 3 * WIDE]
+    go = jnp.sum(gq[:, : dim // 32, wide:].astype(F32), axis=0)
+    flat = jnp.sum(gq[:, dim // 32 :, :wide].astype(F32), axis=0).reshape(-1)[:length]
+    gq = gq[:, : dim // 32, :wide].reshape(4, 2, dim // 32, wide)
+    gq = add(gq[:, 0], gq[:, 1])[..., : 3 * WIDE]
     gq = gq.reshape(4, dim // 32, 3, WIDE).transpose(1, 2, 0, 3).reshape(dim // 32, 3 * dim)
 
-    gbu = gbu.reshape(4, 1, part)
-    gbu = jnp.where(clean, jnp.concatenate([gbu, 0 * gbu], 1), jnp.concatenate([0 * gbu, gbu], 1))
-    flat = jnp.concatenate([gbu.reshape(-1), sums[:3].reshape(-1), vec[:2].reshape(-1)])
-    flat = flat.reshape(-1, 128)
-    for bit in (1, 2, 4):
-        flat = flat + swap(flat, bit)
-    flat = flat + turn(flat, 1) + turn(flat, 2) + turn(flat, 3)
-    flat = flat.reshape(-1)
     gbu = flat[:hid]
     g_gain_b, g_b_down, m_direct, g_gain_a, m_norm = [
         flat[hid + k * dim : hid + (k + 1) * dim] for k in range(5)

time: 395 us -> 342 us (0.87)
  local copies, waits for them, and re-layouts: 68.4 us -> 24.9 us
  starting transfers between devices: 96.7 us -> 54.5 us
  between operations: 4.57 us -> 17.2 us
  Pallas kernels: 114 us -> 124 us
  waiting for transfers between devices: 87.9 us -> 95.5 us
    all_to_all x0 -> x6, waiting for transfers between devices: none -> 59.1 us  [the longest x2 21.9 us: exchange_chips(): return lax.all_to_all(v, 'ctx', 0, 0, axis_index_groups=groups, tiled=True)]
    ppermute x30 -> x6, waiting for transfers between devices: 46 us -> 3.58 us  [the longest x4 3.58 us: shards_by_heads(): far_kv = [lax.ppermute(v, 'ctx', [(b, a) for a, b in give]) for v in far_kv]]
    ppermute x56 -> x21, starting transfers between devices: 59.5 us -> 18.1 us  [swap(): return lax.ppermute(v, 'ctx', [(i, i ^ bit) for i in range(8)])]
    ppermute x30 -> x6, starting transfers between devices: 37.2 us -> 8.3 us  [the longest x4 5.17 us: shards_by_heads(): far_kv = [lax.ppermute(v, 'ctx', [(b, a) for a, b in give]) for v in far_kv]]
    all_to_all x0 -> x6, starting transfers between devices: none -> 27.5 us  [the longest x3 14.9 us: exchange(): return lax.all_to_all(v, 'ctx', 0, 0, tiled=True)]
    unnamed x189 -> x58, local copies, waits for them, and re-layouts: 31 us -> 6.44 us
    ppermute x56 -> x21, waiting for transfers between devices: 41.8 us -> 29.1 us  [swap(): return lax.ppermute(v, 'ctx', [(i, i ^ bit) for i in range(8)])]
    pallas_call x11 -> x10, Pallas kernels: 114 us -> 124 us  [the longest x9 110 us: call(): pl.pallas_call(run, out_shape=tuple((jax.ShapeDtypeStruct(s, d) for s, d...]
  transfers between devices with their start and end apart: 86 -> 38, of which waited for: 32 -> 18; matrix products, arithmetic and copies ran while one was open for 15% -> 10% of each run, Pallas kernels for 19% -> 25%
where the time goes in v2:
time: 342 us; the launch traced here: 340 us
  Pallas kernels  124 us (36%)
  waiting for transfers between devices  95.5 us (28%)
  starting transfers between devices  54.5 us (16%)
  local copies, waits for them, and re-layouts  24.9 us (7%)
  other arithmetic  23.4 us (7%)
  between operations  17.2 us (5%)
    pallas_call x9, Pallas kernels, call(): pl.pallas_call(run, out_shape=tuple((jax.ShapeDtypeStruct(s, d) for s, d...  110 us
    ppermute x21, waiting for transfers between devices, swap(): return lax.ppermute(v, 'ctx', [(i, i ^ bit) for i in range(8)])  29.1 us
    all_to_all x2, waiting for transfers between devices, exchange_chips(): return lax.all_to_all(v, 'ctx', 0, 0, axis_index_groups=groups, tiled=True)  21.9 us
    all_to_all x1, waiting for transfers between devices, exchange_z(): return lax.all_to_all(v, 'fsdp', 0, 0, tiled=True)  19.4 us
    ppermute x21, starting transfers between devices, swap(): return lax.ppermute(v, 'ctx', [(i, i ^ bit) for i in range(8)])  18.1 us
    all_to_all x3, waiting for transfers between devices, exchange(): return lax.all_to_all(v, 'ctx', 0, 0, tiled=True)  17.9 us
    all_to_all x3, starting transfers between devices, exchange(): return lax.all_to_all(v, 'ctx', 0, 0, tiled=True)  14.9 us
    pallas_call x1, Pallas kernels, project_back(): pl.pallas_call(project_back_body, grid=(8,), out_shape=(jax.ShapeDtypeStr...  14.6 us
  transfers between devices with their start and end apart: 38, of which 18 were waited for; matrix products, arithmetic and copies ran while one was open for 10% of the time, Pallas kernels for 25%

profile of v2, /device:TPU:0, one launch (start us, length us, event | category | flops | bytes accessed | tf_op | source)
XLA Modules:
  0.0 339.9 jit_solution(6053768513186592844)
XLA Ops:
  7.8 2.9 shard_map.212
  11.1 3.0 collective-permute-start.3
  14.1 1.5 collective-permute-start.1
  16.2 1.2 collective-permute-done.refs_6_
  18.8 4.9 %all-to-all-start = ((bf16[4,112,576]{2,1,0:T(8,128)(2,1)}), bf16[4,112,576]{2,1,0:T(8,128)(2,1)S(1)}, u32[]{:S(2)}, u32[]{:S(2)}) async-start(bf16[4,112,576]{2,1,0:T(8,128)(2,1)} %broadcast_in_dim.96), calls=%async_computation | async-start | bytes 1146880 | tf_op jit(solution)/shard_map/all_to_all | solution.py:1137
  24.8 1.8 multiply_sine_fusion
  27.2 1.5 collective-permute-start.5
  28.7 7.3 %collective-permute-done.4.refs_10_ = bf16[256,768]{1,0:T(8,128)(2,1)} collective-permute-done((bf16[256,768]{1,0:T(8,128)(2,1)}, bf16[256,768]{1,0:T(8,128)(2,1)}, u32[]{:S(2)}, u32[]{:S(2)}) %collective-permute-start.4) | collective-permute-done | bytes 393248 | tf_op jit(solution)/shard_map/ppermute | solution.py:438
  36.6 19.4 %all-to-all-done.refs_13_ = bf16[4,112,576]{2,1,0:T(8,128)(2,1)S(1)} async-done(((bf16[4,112,576]{2,1,0:T(8,128)(2,1)}), bf16[4,112,576]{2,1,0:T(8,128)(2,1)S(1)}, u32[]{:S(2)}, u32[]{:S(2)}) %all-to-all-start) | async-done | bytes 516128 | tf_op jit(solution)/shard_map/all_to_all | solution.py:1137
  60.3 1.2 all-gather.3.cloned.1.call-done
  61.5 2.0 gather_fusion
  63.7 13.9 %shard_map.213 = (bf16[8,192,256]{2,1,0:T(8,128)(2,1)}, bf16[4,384,256]{2,1,0:T(8,128)(2,1)}, bf16[4,384,256]{2,1,0:T(8,128)(2,1)}, bf16[8,256,768]{2,1,0:T(8,12...) custom-call(s32[16]{0:T(128)} %concatenate.34.refs_0_, f32[1,768]{1,0:T(1,128)} %reshape.439.refs_1_, ...), custom_call_target="tpu_custom_call" | custom-call | flops 2 | bytes 1 | tf_op jit(solution)/shard_map/pallas_call | solution.py:485
  77.7 1.8 collective-permute-start.9
  79.5 1.3 collective-permute-start.8
  80.8 2.7 collective-permute-start.12
  85.1 1.0 copy-done.5
  86.3 19.6 %shard_map.214 = (bf16[8,192,256]{2,1,0:T(8,128)(2,1)}, f32[8,192,256]{2,1,0:T(8,128)}, f32[8,8,768]{2,1,0:T(8,128)}) custom-call(s32[16]{0:T(128)} %concatenate.34.refs_0_, s32[8,8,256]{2,1,0:T(8,128)} %pad.18.refs_1_, bf16[8,192,256]{2,1,0:T(8,128)(2,1)} %get-tuple-element.69.refs_2_.refs_6_, bf16[4,384,256]{2,1,0:T(8,128)(2,1)} %get-tuple-element.70.refs_3_.refs_7_, ...), custom_call_target="tpu_custom_call" | custom-call | flops 5 | bytes 1 | tf_op jit(solution)/shard_map/pallas_call | solution.py:485
  105.8 7.1 %all-to-all-start.1 = ((bf16[8,192,256]{2,1,0:T(8,128)(2,1)}), bf16[8,192,256]{2,1,0:T(8,128)(2,1)}, u32[]{:S(2)}, u32[]{:S(2)}) async-start(bf16[8,192,256]{2,1,0:T(8,128)(2,1)} %get-tuple-element.72), calls=%async_computation.1 | async-start | bytes 1572864 | tf_op jit(solution)/shard_map/all_to_all | solution.py:1128
  113.2 1.0 slice_bitcast_fusion
  114.2 1.1 bitcast_select_fusion
  115.3 1.0 pad_maximum_fusion.1.refs_3_.refs_9_
  117.7 13.4 %collective-permute-done.11.refs_8_.refs_10_ = bf16[3,240,768]{2,1,0:T(8,128)(2,1)S(1)} collective-permute-done((bf16[3,240,768]{2,1,0:T(8,128)(2,1)S(1)}, bf16[3,240,768]{2,1,0:T(8,128)(2,1)S(1)}, u32[]{:S(2)}, u32[]{:S(2)}) %collective-permute-start.11) | collective-permute-done | bytes 1105952 | tf_op jit(solution)/shard_map/ppermute | solution.py:438
  131.2 1.8 collective-permute-done.10.refs_7_.refs_9_
  133.0 6.7 %all-to-all-done.1.refs_4_ = bf16[8,192,256]{2,1,0:T(8,128)(2,1)} async-done(((bf16[8,192,256]{2,1,0:T(8,128)(2,1)}), bf16[8,192,256]{2,1,0:T(8,128)(2,1)}, u32[]{:S(2)}, u32[]{:S(2)}) %all-to-all-start.1) | async-done | bytes 786464 | tf_op jit(solution)/shard_map/all_to_all | solution.py:1128
  139.7 6.0 %shard_map.215 = (f32[2,256,768]{2,1,0:T(8,128)}, bf16[512,768]{1,0:T(8,128)(2,1)}, bf16[2,768,256]{2,1,0:T(8,128)(2,1)}, bf16[768,768]{1,0:T(8,128)(2,1)}) custom-call(s32[16]{0:T(128)} %concatenate.34.refs_0_, f32[1,768]{1,0:T(1,128)} %reshape.436.refs_1_, f32[1,768]{1,0:T(1,128)} %reshape.438.refs_2_, ...), custom_call_target="tpu_custom_call" | custom-call | flops 1 | bytes 1 | tf_op jit(solution)/shard_map/pallas_call | solution.py:485
  146.4 1.9 collective-permute-done.13.refs_3_
  149.1 24.2 %shard_map.216 = (f32[512,768]{1,0:T(8,128)}, bf16[512,768]{1,0:T(8,128)(2,1)}, bf16[512,768]{1,0:T(8,128)(2,1)}, f32[512,768]{1,0:T(8,128)}, f32[1,1536]{1,0:T(...) custom-call(s32[16]{0:T(128)} %concatenate.34.refs_0_, f32[1,1536]{1,0:T(1,128)} %bitcast.91, ...), custom_call_target="tpu_custom_call" | custom-call | flops 15 | bytes 1 | tf_op jit(solution)/shard_map/pallas_call | solution.py:485
  173.4 1.1 copy-done.25
  175.7 1.1 collective-permute-done.15.refs_6_
  176.8 1.1 collective-permute-done.16.refs_7_
  178.8 8.1 %shard_map.217 = (bf16[2,256,768]{2,1,0:T(8,128)(2,1)}, bf16[2,256,768]{2,1,0:T(8,128)(2,1)}, f32[8,768]{1,0:T(8,128)}, bf16[8,192,256]{2,1,0:T(8,128)(2,1)}) custom-call(s32[16]{0:T(128)} %concatenate.34.refs_0_, f32[1,768]{1,0:T(1,128)} %reshape.436.refs_1_, f32[1,768]{1,0:T(1,128)} %reshape.437.refs_2_, f32[2,256,768]{2,1,0:T(8,128)} %get-tuple-element.74.refs_3_, ...), custom_call_target="tpu_custom_call" | custom-call | flops 1 | bytes 1 | tf_op jit(solution)/shard_map/pallas_call | solution.py:485
  186.9 3.6 %all-to-all-start.2 = ((bf16[8,192,256]{2,1,0:T(8,128)(2,1)}), bf16[8,192,256]{2,1,0:T(8,128)(2,1)S(1)}, u32[]{:S(2)}, u32[]{:S(2)}) async-start(bf16[8,192,256]{2,1,0:T(8,128)(2,1)} %get-tuple-element.86), calls=%async_computation.2 | async-start | bytes 1572864 | tf_op jit(solution)/shard_map/all_to_all | solution.py:1128
  190.5 3.7 %shard_map.218 = bf16[4,192,768]{2,1,0:T(8,128)(2,1)} custom-call(bf16[2,768,256]{2,1,0:T(8,128)(2,1)} %get-tuple-element.88.refs_0_, bf16[2,256,768]{2,1,0:T(8,128)(2,1)} %get-tuple-element.83.refs_1_.refs_4_), custom_call_target="tpu_custom_call" | custom-call | flops 1 | bytes 1 | tf_op jit(solution)/shard_map/pallas_call | solution.py:485
  194.2 8.8 %all-to-all-done.2.refs_11_ = bf16[8,192,256]{2,1,0:T(8,128)(2,1)S(1)} async-done(((bf16[8,192,256]{2,1,0:T(8,128)(2,1)}), bf16[8,192,256]{2,1,0:T(8,128)(2,1)S(1)}, u32[]{:S(2)}, u32[]{:S(2)}) %all-to-all-start.2) | async-done | bytes 786464 | tf_op jit(solution)/shard_map/all_to_all | solution.py:1128
  203.9 3.6 %all-to-all-start.3 = ((bf16[4,4,96,768]{3,2,1,0:T(8,128)(2,1)}), bf16[4,4,96,768]{3,2,1,0:T(8,128)(2,1)S(1)}, u32[]{:S(2)}, u32[]{:S(2)}) async-start(bf16[4,4,96,768]{3,2,1,0:T(8,128)(2,1)} %get-tuple-element.95), calls=%async_computation.3 | async-start | bytes 4718592 | tf_op jit(solution)/shard_map/all_to_all | solution.py:1133
  207.8 26.5 %shard_map.219 = (bf16[8,192,256]{2,1,0:T(8,128)(2,1)}, f32[8,384,256]{2,1,0:T(8,128)}, bf16[2,384,256]{2,1,0:T(8,128)(2,1)}, bf16[2,384,256]{2,1,0:T(8,128)(2,1...) custom-call(s32[16]{0:T(128)} %concatenate.34.refs_0_, s32[8,8,256]{2,1,0:T(8,128)} %pad.18.refs_1_, ...), custom_call_target="tpu_custom_call" | custom-call | flops 11 | bytes 1 | tf_op jit(solution)/shard_map/pallas_call | solution.py:485
  234.3 1.3 collective-permute-start.17
  235.6 1.3 collective-permute-start.18
  236.9 1.3 collective-permute-start.19
  238.2 1.3 collective-permute-start.20
  239.6 1.4 reduce_sum.85
  241.7 1.3 collective-permute-done.19.f2
  243.1 1.5 collective-permute-done.20.f3
  245.4 14.6 %shard_map.220 = (bf16[2,256,768]{2,1,0:T(8,128)(2,1)}, bf16[2,256,768]{2,1,0:T(8,128)(2,1)}, f32[4,256,768]{2,1,0:T(8,128)}, bf16[4,192,640]{2,1,0:T(8,128)(2,1)}, f32[8,768]{1,0:T(8,128)}) custom-call(f32[8,384,256]{2,1,0:T(8,128)} %get-tuple-element.90.own, bf16[2,384,256]{2,1,0:T(8,128)(2,1)} %copy-done.15, bf16[2,384,256]{2,1,0:T(8,128)(2,1)} %copy-done.16, ...), custom_call_target="tpu_custom_call" | custom-call | flops 4 | bytes 1 | tf_op jit(solution)/shard_map/pallas_call | solution.py:1066
  260.8 2.3 pad_maximum_fusion
  263.1 3.0 collective-permute-start.21
  266.5 4.2 %all-to-all-start.4 = ((bf16[4,96,768]{2,1,0:T(8,128)(2,1)}), bf16[4,96,768]{2,1,0:T(8,128)(2,1)}, u32[]{:S(2)}, u32[]{:S(2)}) async-start(bf16[4,96,768]{2,1,0:T(8,128)(2,1)} %bitcast.82), calls=%async_computation.7 | async-start | bytes 1179648 | tf_op jit(solution)/shard_map/all_to_all | solution.py:1133
  270.8 21.9 %all-to-all-done.4 = bf16[4,96,768]{2,1,0:T(8,128)(2,1)} async-done(((bf16[4,96,768]{2,1,0:T(8,128)(2,1)}), bf16[4,96,768]{2,1,0:T(8,128)(2,1)}, u32[]{:S(2)}, u32[]{:S(2)}) %all-to-all-start.4) | async-done | bytes 589856 | tf_op jit(solution)/shard_map/all_to_all | solution.py:1133
  292.7 1.9 convert_reduce_fusion
  294.6 2.2 fusion.4
  297.1 1.4 collective-permute-start.22
  298.5 0.9 convert_bitcast_fusion
  299.4 2.4 reduce-scatter.9.cloned.1.call-done
  302.6 1.0 slice.145
  303.6 2.0 fusion.1
  305.6 4.2 %all-to-all-start.5 = ((bf16[8,40,1408]{2,1,0:T(8,128)(2,1)}), bf16[8,40,1408]{2,1,0:T(8,128)(2,1)}, u32[]{:S(2)}, u32[]{:S(2)}) async-start(bf16[8,40,1408]{2,1,0:T(8,128)(2,1)} %fusion.1), calls=%async_computation.8 | async-start | bytes 1802240 | tf_op jit(solution)/shard_map/all_to_all | solution.py:1128
  309.9 2.6 fusion.2
  313.1 1.2 collective-permute-done.26
  314.6 1.0 reshape.458
  316.3 5.0 %shard_map.221 = bf16[2,256,768]{2,1,0:T(8,128)(2,1)} custom-call(s32[16]{0:T(128)} %concatenate.34.refs_0_, f32[1,768]{1,0:T(1,128)} %reshape.439.refs_1_, f32[1,768]{1,0:T(1,128)} %reshape.438.refs_2_, bf16[2,256,768]{2,1,0:T(8,128)(2,1)} %pad_maximum_fusion.1.refs_3_.refs_9_, bf16[2,256,768]{2,1,0:T(8,128)(2,1)} %get-tuple-element.83.refs_1_.refs_4_, ...), custom_call_target="tpu_custom_call" | custom-call | flops 1 | bytes 1 | tf_op jit(solution)/shard_map/pallas_call | solution.py:485
  321.3 2.3 all-to-all-done.5
  323.7 0.9 convert_reduce_fusion.2
  324.6 1.6 convert_reduce_fusion.1
  326.3 1.0 slice.147
  (175 shorter events, 27.1 us)
Async XLA Ops:
  7.2 54.3 %all-gather.3.cloned.1.call-start = ((), (), s32[]{:S(2)}) async-start(), calls=%async_computation.14 | async-start | bytes 1843200 | tf_op jit(solution)/shard_map/all_gather | solution.py:1165
  7.8 3.1 copy-start.26
  7.8 3.1 copy-start.7
  10.8 4.8 %copy-start.27 = (s32[1,16]{1,0:T(1,128)S(1)}, s32[1,16]{1,0:T(1,128)}, u32[]{:S(2)}) copy-start(s32[1,16]{1,0:T(1,128)} %param.15) | copy-start | bytes 196
  10.8 4.9 %copy-start.19 = (bf16[768]{0:T(1024)(128)(2,1)S(1)}, bf16[768]{0:T(1024)(128)(2,1)}, u32[]{:S(2)}) copy-start(bf16[768]{0:T(1024)(128)(2,1)} %param.19) | copy-start | bytes 4612
  10.8 4.9 %copy-start.20 = (bf16[192]{0:T(256)(128)(2,1)S(1)}, bf16[192]{0:T(256)(128)(2,1)}, u32[]{:S(2)}) copy-start(bf16[192]{0:T(256)(128)(2,1)} %param.21) | copy-start | bytes 1156
  10.8 4.9 %copy-start.21 = (bf16[192]{0:T(256)(128)(2,1)S(1)}, bf16[192]{0:T(256)(128)(2,1)}, u32[]{:S(2)}) copy-start(bf16[192]{0:T(256)(128)(2,1)} %param.22) | copy-start | bytes 1156
  10.8 4.9 %copy-start.22 = (bf16[192]{0:T(256)(128)(2,1)S(1)}, bf16[192]{0:T(256)(128)(2,1)}, u32[]{:S(2)}) copy-start(bf16[192]{0:T(256)(128)(2,1)} %param.23) | copy-start | bytes 1156
  10.8 4.9 %copy-start.23 = (bf16[192]{0:T(256)(128)(2,1)S(1)}, bf16[192]{0:T(256)(128)(2,1)}, u32[]{:S(2)}) copy-start(bf16[192]{0:T(256)(128)(2,1)} %param.24) | copy-start | bytes 1156
  10.8 6.6 %copy-start.10 = (bf16[192,2304]{1,0:T(8,128)(2,1)S(1)}, bf16[192,2304]{1,0:T(8,128)(2,1)}, u32[]{:S(2)}) copy-start(bf16[192,2304]{1,0:T(8,128)(2,1)} %param.16) | copy-start | bytes 2654212
  11.1 6.8 %copy-start.9 = (bf16[256,768]{1,0:T(8,128)(2,1)}, bf16[256,768]{1,0:T(8,128)(2,1)S(1)}, u32[]{:S(2)}) copy-start(bf16[256,768]{1,0:T(8,128)(2,1)S(1)} %get-tuple-element.134.refs_5_) | copy-start | bytes 1179652
  11.1 52.6 %collective-permute-start.3 = (bf16[256,768]{1,0:T(8,128)(2,1)S(1)}, bf16[256,768]{1,0:T(8,128)(2,1)}, u32[]{:S(2)}, u32[]{:S(2)}) collective-permute-start(bf16[256,768]{1,0:T(8,128)(2,1)S(1)} %get-tuple-element.134.refs_5_), channel_id=1, source_target_pairs={{0,16},{4,20},{8,24},{12,28},{16,0},{20,4},{24,8},{28,12},{1,17},{... | collective-permute-start | bytes 1179656 | tf_op jit(solution)/shard_map/ppermute | solution.py:438
  14.1 13.1 %collective-permute-start.1 = (bf16[256,768]{1,0:T(8,128)(2,1)S(1)}, bf16[256,768]{1,0:T(8,128)(2,1)}, u32[]{:S(2)}, u32[]{:S(2)}) collective-permute-start(bf16[256,768]{1,0:T(8,128)(2,1)S(1)} %get-tuple-element.134.refs_5_), channel_id=1, source_target_pairs={{0,8},{4,12},{8,0},{12,4},{16,24},{20,28},{24,16},{28,20},{1,9},{5... | collective-permute-start | bytes 1179656 | tf_op jit(solution)/shard_map/ppermute | solution.py:438
  15.6 1.9 collective-permute-start
  18.8 37.2 %all-to-all-start = ((bf16[4,112,576]{2,1,0:T(8,128)(2,1)}), bf16[4,112,576]{2,1,0:T(8,128)(2,1)S(1)}, u32[]{:S(2)}, u32[]{:S(2)}) async-start(bf16[4,112,576]{2,1,0:T(8,128)(2,1)} %broadcast_in_dim.96), calls=%async_computation | async-start | bytes 1146880 | tf_op jit(solution)/shard_map/all_to_all | solution.py:1137
  23.7 12.3 %collective-permute-start.4 = (bf16[256,768]{1,0:T(8,128)(2,1)}, bf16[256,768]{1,0:T(8,128)(2,1)}, u32[]{:S(2)}, u32[]{:S(2)}) collective-permute-start(bf16[256,768]{1,0:T(8,128)(2,1)} %collective-permute-done.refs_6_), channel_id=1, source_target_pairs={{0,16},{4,20},{8,24},{12,28},{16,0},{20,4},{24,8},{28,12},{1,17},{... | collective-permute-start | bytes 1179656 | tf_op jit(solution)/shard_map/ppermute | solution.py:438
  26.7 37.1 %collective-permute-start.2 = (bf16[256,768]{1,0:T(8,128)(2,1)}, bf16[256,768]{1,0:T(8,128)(2,1)}, u32[]{:S(2)}, u32[]{:S(2)}) collective-permute-start(bf16[256,768]{1,0:T(8,128)(2,1)} %collective-permute-done.refs_6_), channel_id=1, source_target_pairs={{0,8},{4,12},{8,0},{12,4},{16,24},{20,28},{24,16},{28,20},{1,9},{5... | collective-permute-start | bytes 1179656 | tf_op jit(solution)/shard_map/ppermute | solution.py:438
  27.2 36.5 %collective-permute-start.5 = (bf16[256,768]{1,0:T(8,128)(2,1)}, bf16[256,768]{1,0:T(8,128)(2,1)}, u32[]{:S(2)}, u32[]{:S(2)}) collective-permute-start(bf16[256,768]{1,0:T(8,128)(2,1)} %collective-permute-done.1.refs_7_), channel_id=1, source_target_pairs={{0,16},{4,20},{8,24},{12,28},{16,0},{20,4},{24,8},{28,12},{1,17},{... | collective-permute-start | bytes 1179656 | tf_op jit(solution)/shard_map/ppermute | solution.py:438
  36.0 27.7 %collective-permute-start.6 = (bf16[256,768]{1,0:T(8,128)(2,1)}, bf16[256,768]{1,0:T(8,128)(2,1)}, u32[]{:S(2)}, u32[]{:S(2)}) collective-permute-start(bf16[256,768]{1,0:T(8,128)(2,1)} %collective-permute-done.4.refs_10_), channel_id=1, source_target_pairs={{0,8},{4,12},{8,0},{12,4},{16,24},{20,28},{24,16},{28,20},{1,9},{5... | collective-permute-start | bytes 1179656 | tf_op jit(solution)/shard_map/ppermute | solution.py:438
  56.0 7.7 %copy-start.8 = (bf16[4,112,576]{2,1,0:T(8,128)(2,1)}, bf16[4,112,576]{2,1,0:T(8,128)(2,1)S(1)}, u32[]{:S(2)}) copy-start(bf16[4,112,576]{2,1,0:T(8,128)(2,1)S(1)} %all-to-all-done.refs_13_) | copy-start | bytes 1548292
  57.4 6.3 %collective-permute-start.7 = (bf16[4,112,576]{2,1,0:T(8,128)(2,1)S(1)}, bf16[4,112,576]{2,1,0:T(8,128)(2,1)}, u32[]{:S(2)}, u32[]{:S(2)}) collective-permute-start(bf16[4,112,576]{2,1,0:T(8,128)(2,1)S(1)} %all-to-all-done.refs_13_), channel_id=1, source_target_pairs={{0,4},{4,0},{8,12},{12,8},{16,20},{20,16},{24,28},{28,24},{1,5},{5... | collective-permute-start | bytes 1548296 | tf_op jit(solution)/shard_map/ppermute | solution.py:438
  63.7 20.1 %copy-start = (bf16[3,240,768]{2,1,0:T(8,128)(2,1)}, bf16[3,240,768]{2,1,0:T(8,128)(2,1)S(1)}, u32[]{:S(2)}) copy-start(bf16[3,240,768]{2,1,0:T(8,128)(2,1)S(1)} %broadcast_select_fusion.refs_6_.refs_8_) | copy-start | bytes 3317764
  77.7 7.4 %collective-permute-start.9 = (bf16[4,384,256]{2,1,0:T(8,128)(2,1)}, bf16[4,384,256]{2,1,0:T(8,128)(2,1)S(1)}, u32[]{:S(2)}, u32[]{:S(2)}) collective-permute-start(bf16[4,384,256]{2,1,0:T(8,128)(2,1)} %get-tuple-element.71.refs_4_.refs_8_), channel_id=1, source_target_pairs={{0,4},{8,12},{16,20},{24,28},{1,5},{9,13},{17,21},{25,29},{2,6},{1... | collective-permute-start | bytes 2359304 | tf_op jit(solution)/shard_map/ppermute | solution.py:1222
  79.5 5.6 %collective-permute-start.8 = (bf16[4,384,256]{2,1,0:T(8,128)(2,1)}, bf16[4,384,256]{2,1,0:T(8,128)(2,1)S(1)}, u32[]{:S(2)}, u32[]{:S(2)}) collective-permute-start(bf16[4,384,256]{2,1,0:T(8,128)(2,1)} %get-tuple-element.70.refs_3_.refs_7_), channel_id=1, source_target_pairs={{0,4},{8,12},{16,20},{24,28},{1,5},{9,13},{17,21},{25,29},{2,6},{1... | collective-permute-start | bytes 2359304 | tf_op jit(solution)/shard_map/ppermute | solution.py:1222
  80.8 36.9 %collective-permute-start.12 = (bf16[3,240,768]{2,1,0:T(8,128)(2,1)S(1)}, bf16[3,240,768]{2,1,0:T(8,128)(2,1)S(1)}, u32[]{:S(2)}, u32[]{:S(2)}) collective-permute-start(bf16[3,240,768]{2,1,0:T(8,128)(2,1)S(1)} %broadcast_select_fusion.refs_6_.refs_8_), channel_id=1, source_target_pairs={{0,24},{4,28},{8,16},{12,20},{16,8},{20,12},{24,0},{28,4},{1,25},{... | collective-permute-start | bytes 3317768 | tf_op jit(solution)/shard_map/ppermute | solution.py:438
  83.5 47.7 %collective-permute-start.11 = (bf16[3,240,768]{2,1,0:T(8,128)(2,1)S(1)}, bf16[3,240,768]{2,1,0:T(8,128)(2,1)S(1)}, u32[]{:S(2)}, u32[]{:S(2)}) collective-permute-start(bf16[3,240,768]{2,1,0:T(8,128)(2,1)S(1)} %broadcast_select_fusion.refs_6_.refs_8_), channel_id=1, source_target_pairs={{0,16},{4,20},{8,24},{12,28},{16,0},{20,4},{24,8},{28,12},{1,17},{... | collective-permute-start | bytes 3317768 | tf_op jit(solution)/shard_map/ppermute | solution.py:438
  83.8 49.1 %collective-permute-start.10 = (bf16[3,240,768]{2,1,0:T(8,128)(2,1)S(1)}, bf16[3,240,768]{2,1,0:T(8,128)(2,1)}, u32[]{:S(2)}, u32[]{:S(2)}) collective-permute-start(bf16[3,240,768]{2,1,0:T(8,128)(2,1)S(1)} %broadcast_select_fusion.refs_6_.refs_8_), channel_id=1, source_target_pairs={{0,8},{4,12},{8,0},{12,4},{16,24},{20,28},{24,16},{28,20},{1,9},{5... | collective-permute-start | bytes 3317768 | tf_op jit(solution)/shard_map/ppermute | solution.py:438
  85.1 1.0 copy-start.5
  85.1 1.2 copy-start.6
  105.8 33.8 %all-to-all-start.1 = ((bf16[8,192,256]{2,1,0:T(8,128)(2,1)}), bf16[8,192,256]{2,1,0:T(8,128)(2,1)}, u32[]{:S(2)}, u32[]{:S(2)}) async-start(bf16[8,192,256]{2,1,0:T(8,128)(2,1)} %get-tuple-element.72), calls=%async_computation.1 | async-start | bytes 1572864 | tf_op jit(solution)/shard_map/all_to_all | solution.py:1128
  112.9 128.0 %reduce-scatter.5.cloned.1.call-start = ((), (), s32[]{:S(2)}) async-start(), calls=%async_computation.10 | async-start | bytes 2949120 | tf_op jit(solution)/shard_map/reduce_scatter | solution.py:1232
  117.0 29.4 %collective-permute-start.14 = (bf16[512,768]{1,0:T(8,128)(2,1)}, bf16[512,768]{1,0:T(8,128)(2,1)}, u32[]{:S(2)}, u32[]{:S(2)}) collective-permute-start(bf16[512,768]{1,0:T(8,128)(2,1)} %bitcast.69), channel_id=1, source_target_pairs={{0,4},{4,0},{8,12},{12,8},{16,20},{20,16},{24,28},{28,24},{1,5},{5... | collective-permute-start | bytes 2359304 | tf_op jit(solution)/shard_map/ppermute | solution.py:438
  117.7 22.0 %copy-start.1 = (bf16[3,240,768]{2,1,0:T(8,128)(2,1)}, bf16[3,240,768]{2,1,0:T(8,128)(2,1)S(1)}, u32[]{:S(2)}) copy-start(bf16[3,240,768]{2,1,0:T(8,128)(2,1)S(1)} %collective-permute-done.12.refs_9_.refs_11_) | copy-start | bytes 3317764
  131.2 8.5 %copy-start.2 = (bf16[3,240,768]{2,1,0:T(8,128)(2,1)}, bf16[3,240,768]{2,1,0:T(8,128)(2,1)S(1)}, u32[]{:S(2)}) copy-start(bf16[3,240,768]{2,1,0:T(8,128)(2,1)S(1)} %collective-permute-done.11.refs_8_.refs_10_) | copy-start | bytes 3317764
  145.7 2.6 collective-permute-start.13
  148.2 0.9 copy-start.13
  173.3 1.1 copy-start.25
  173.3 1.4 copy-start.24
  174.5 2.3 collective-permute-start.15
  174.7 3.2 collective-permute-start.16
  176.8 1.1 copy-start.11
  186.9 16.1 %all-to-all-start.2 = ((bf16[8,192,256]{2,1,0:T(8,128)(2,1)}), bf16[8,192,256]{2,1,0:T(8,128)(2,1)S(1)}, u32[]{:S(2)}, u32[]{:S(2)}) async-start(bf16[8,192,256]{2,1,0:T(8,128)(2,1)} %get-tuple-element.86), calls=%async_computation.2 | async-start | bytes 1572864 | tf_op jit(solution)/shard_map/all_to_all | solution.py:1128
  190.5 72.6 %reduce-scatter.7.cloned.1.call-start = ((), (), s32[]{:S(2)}) async-start(), calls=%async_computation.11 | async-start | bytes 1474560 | tf_op jit(solution)/shard_map/reduce_scatter | solution.py:1242
  203.0 0.9 copy-start.3
  203.9 35.6 %all-to-all-start.3 = ((bf16[4,4,96,768]{3,2,1,0:T(8,128)(2,1)}), bf16[4,4,96,768]{3,2,1,0:T(8,128)(2,1)S(1)}, u32[]{:S(2)}, u32[]{:S(2)}) async-start(bf16[4,4,96,768]{3,2,1,0:T(8,128)(2,1)} %get-tuple-element.95), calls=%async_computation.3 | async-start | bytes 4718592 | tf_op jit(solution)/shard_map/all_to_all | solution.py:1133
  207.5 90.9 %reduce-scatter.11.cloned.1.call-start = ((), (), s32[]{:S(2)}) async-start(), calls=%async_computation.13 | async-start | bytes 737280 | tf_op jit(solution)/shard_map/reduce_scatter | solution.py:1250
  234.3 6.6 %collective-permute-start.17 = (bf16[2,384,256]{2,1,0:T(8,128)(2,1)}, bf16[2,384,256]{2,1,0:T(8,128)(2,1)S(1)}, u32[]{:S(2)}, u32[]{:S(2)}) collective-permute-start(bf16[2,384,256]{2,1,0:T(8,128)(2,1)} %get-tuple-element.91), channel_id=1, source_target_pairs={{4,0},{12,8},{20,16},{28,24},{5,1},{13,9},{21,17},{29,25},{6,2},{1... | collective-permute-start | bytes 1179656 | tf_op jit(solution)/shard_map/ppermute | solution.py:1245
  235.6 6.1 %collective-permute-start.18 = (bf16[2,384,256]{2,1,0:T(8,128)(2,1)}, bf16[2,384,256]{2,1,0:T(8,128)(2,1)S(1)}, u32[]{:S(2)}, u32[]{:S(2)}) collective-permute-start(bf16[2,384,256]{2,1,0:T(8,128)(2,1)} %get-tuple-element.92), channel_id=1, source_target_pairs={{4,0},{12,8},{20,16},{28,24},{5,1},{13,9},{21,17},{29,25},{6,2},{1... | collective-permute-start | bytes 1179656 | tf_op jit(solution)/shard_map/ppermute | solution.py:1245
  236.9 6.1 %collective-permute-start.19 = (bf16[2,384,256]{2,1,0:T(8,128)(2,1)}, bf16[2,384,256]{2,1,0:T(8,128)(2,1)S(1)}, u32[]{:S(2)}, u32[]{:S(2)}) collective-permute-start(bf16[2,384,256]{2,1,0:T(8,128)(2,1)} %get-tuple-element.93), channel_id=1, source_target_pairs={{4,0},{12,8},{20,16},{28,24},{5,1},{13,9},{21,17},{29,25},{6,2},{1... | collective-permute-start | bytes 1179656 | tf_op jit(solution)/shard_map/ppermute | solution.py:1245
  238.2 6.3 %collective-permute-start.20 = (bf16[2,384,256]{2,1,0:T(8,128)(2,1)}, bf16[2,384,256]{2,1,0:T(8,128)(2,1)}, u32[]{:S(2)}, u32[]{:S(2)}) collective-permute-start(bf16[2,384,256]{2,1,0:T(8,128)(2,1)} %get-tuple-element.94), channel_id=1, source_target_pairs={{4,0},{12,8},{20,16},{28,24},{5,1},{13,9},{21,17},{29,25},{6,2},{1... | collective-permute-start | bytes 1179656 | tf_op jit(solution)/shard_map/ppermute | solution.py:1245
  239.6 5.0 %copy-start.18 = (f32[1,1536]{1,0:T(1,128)S(1)}, f32[1,1536]{1,0:T(1,128)}, u32[]{:S(2)}) copy-start(f32[1,1536]{1,0:T(1,128)} %get-tuple-element.111) | copy-start | bytes 18436
  240.9 4.5 %copy-start.15 = (bf16[2,384,256]{2,1,0:T(8,128)(2,1)}, bf16[2,384,256]{2,1,0:T(8,128)(2,1)S(1)}, u32[]{:S(2)}) copy-start(bf16[2,384,256]{2,1,0:T(8,128)(2,1)S(1)} %collective-permute-done.17.f0) | copy-start | bytes 1179652
  241.7 3.7 %copy-start.16 = (bf16[2,384,256]{2,1,0:T(8,128)(2,1)}, bf16[2,384,256]{2,1,0:T(8,128)(2,1)S(1)}, u32[]{:S(2)}) copy-start(bf16[2,384,256]{2,1,0:T(8,128)(2,1)S(1)} %collective-permute-done.18.f1) | copy-start | bytes 1179652
  243.0 2.4 copy-start.17
  244.5 57.3 %reduce-scatter.9.cloned.1.call-start = ((), (), s32[]{:S(2)}) async-start(), calls=%async_computation.12 | async-start | bytes 1331200 | tf_op jit(solution)/shard_map/reduce_scatter | solution.py:1269
  263.1 31.4 %copy-start.4 = (f32[4,256,768]{2,1,0:T(8,128)S(1)}, f32[4,256,768]{2,1,0:T(8,128)}, u32[]{:S(2)}) copy-start(f32[4,256,768]{2,1,0:T(8,128)} %get-tuple-element.107) | copy-start | bytes 9437188
  263.1 31.4 %collective-permute-start.21 = (bf16[2,256,768]{2,1,0:T(8,128)(2,1)}, bf16[2,256,768]{2,1,0:T(8,128)(2,1)}, u32[]{:S(2)}, u32[]{:S(2)}) collective-permute-start(bf16[2,256,768]{2,1,0:T(8,128)(2,1)} %get-tuple-element.108), channel_id=1, source_target_pairs={{0,8},{4,12},{8,0},{12,4},{16,24},{20,28},{24,16},{28,20},{1,9},{5... | collective-permute-start | bytes 2359304 | tf_op jit(solution)/shard_map/ppermute | solution.py:438
  266.2 28.4 %collective-permute-start.23 = (bf16[2,256,768]{2,1,0:T(8,128)(2,1)}, bf16[2,256,768]{2,1,0:T(8,128)(2,1)}, u32[]{:S(2)}, u32[]{:S(2)}) collective-permute-start(bf16[2,256,768]{2,1,0:T(8,128)(2,1)} %get-tuple-element.109), channel_id=1, source_target_pairs={{0,16},{4,20},{8,24},{12,28},{16,0},{20,4},{24,8},{28,12},{1,17},{... | collective-permute-start | bytes 2359304 | tf_op jit(solution)/shard_map/ppermute | solution.py:438
  266.5 26.2 %all-to-all-start.4 = ((bf16[4,96,768]{2,1,0:T(8,128)(2,1)}), bf16[4,96,768]{2,1,0:T(8,128)(2,1)}, u32[]{:S(2)}, u32[]{:S(2)}) async-start(bf16[4,96,768]{2,1,0:T(8,128)(2,1)} %bitcast.82), calls=%async_computation.7 | async-start | bytes 1179648 | tf_op jit(solution)/shard_map/all_to_all | solution.py:1133
  296.7 13.1 %collective-permute-start.24 = (bf16[256,768]{1,0:T(8,128)(2,1)}, bf16[256,768]{1,0:T(8,128)(2,1)}, u32[]{:S(2)}, u32[]{:S(2)}) collective-permute-start(bf16[256,768]{1,0:T(8,128)(2,1)} %get-tuple-element.129), channel_id=1, source_target_pairs={{0,8},{4,12},{8,0},{12,4},{16,24},{20,28},{24,16},{28,20},{1,9},{5... | collective-permute-start | bytes 1179656 | tf_op jit(solution)/shard_map/ppermute | solution.py:438
  297.1 12.8 %collective-permute-start.22 = (bf16[256,768]{1,0:T(8,128)(2,1)}, bf16[256,768]{1,0:T(8,128)(2,1)}, u32[]{:S(2)}, u32[]{:S(2)}) collective-permute-start(bf16[256,768]{1,0:T(8,128)(2,1)} %get-tuple-element.130), channel_id=1, source_target_pairs={{0,16},{4,20},{8,24},{12,28},{16,0},{20,4},{24,8},{28,12},{1,17},{... | collective-permute-start | bytes 1179656 | tf_op jit(solution)/shard_map/ppermute | solution.py:438
  305.6 18.1 %all-to-all-start.5 = ((bf16[8,40,1408]{2,1,0:T(8,128)(2,1)}), bf16[8,40,1408]{2,1,0:T(8,128)(2,1)}, u32[]{:S(2)}, u32[]{:S(2)}) async-start(bf16[8,40,1408]{2,1,0:T(8,128)(2,1)} %fusion.1), calls=%async_computation.8 | async-start | bytes 1802240 | tf_op jit(solution)/shard_map/all_to_all | solution.py:1128
  312.4 3.1 collective-permute-start.25
  312.8 1.4 collective-permute-start.26
  (2 other events, 1.6 us)
Sparse Core Ops, SparseCore 0:
  11.0 50.4 all-gather.2
  173.5 46.2 reduce-scatter.4
  222.2 28.6 reduce-scatter.6
  253.0 20.6 reduce-scatter.10
  275.8 25.9 reduce-scatter.8

commit v3 on v2

--- a/solution.py
+++ b/solution.py
@@ -594,10 +594,33 @@
     return jnp.concatenate([v, v, v], axis=1)
 
 
-def scores_of(keys, stacked, base, low, high):
-    s = mm(keys, stacked) * 0.125
+def scores_of(keys, stacked, base, low, high, plain):
+    s = mm(keys, stacked)
+    if plain:
+        return s
     place = base + lax.broadcasted_iota(jnp.int32, (CHUNK, LANES), 0)
     return jnp.where((place >= low) & (place < high), s, LOWEST)
+
+
+def each_tile(meta, p, lims, tile):
+    r, c = meta[0], meta[1]
+
+    @pl.loop(meta[4 + p], p + c + 1)
+    def _(k):
+        own = k == p + c
+        source = jnp.where(own, 0, c)
+        slot = jnp.where(own, p ^ r, k ^ r ^ c)
+        base = jnp.where(own, p, k) * CHUNK
+        whole = (k < p) & (meta[12 + p] <= base)
+
+        @pl.when(whole)
+        def _():
+            tile(source, slot, own, base, None, None, True)
+
+        @pl.when(jnp.logical_not(whole))
+        def _():
+            low, high, nlow, nhigh = lims
+            tile(source, slot, own, base, jnp.where(own, nlow, low), jnp.where(own, nhigh, high), False)
 
 
 def stack_heads(q, stacked):
@@ -618,17 +641,16 @@
         for own in range(2):
             kr[own, s] = flip(kv[own, s, :WIDE])
 
-    r, c = meta[0], meta[1]
+    r = meta[0]
 
     @pl.loop(0, 8)
     def _(p):
         s = p ^ r
-        stack_heads(qs[s], stacked)
-        lim = bounds[p]
-        low, high, nlow, nhigh = [thrice(lim[i : i + 1]) for i in range(4)]
-
-        def tile(keys, values, base, lo, hi):
-            masked = scores_of(keys, stacked[...], base, lo, hi)
+        stack_heads(qs[s] * 0.125, stacked)
+        lims = [thrice(bounds[p, i : i + 1]) for i in range(4)]
+
+        def tile(source, slot, own, base, lo, hi, plain):
+            masked = scores_of(kr[source, slot], stacked[...], base, lo, hi, plain)
             m_old = m_s[...]
             m_new = jnp.maximum(m_old, jnp.max(masked, axis=0, keepdims=True))
             e = jnp.exp(masked - m_new)
@@ -638,20 +660,13 @@
             e = e.astype(BF)
             for g in range(GROUP):
                 cut = slice(g * CHUNK, (g + 1) * CHUNK)
-                acc[g] = acc[g] * f[:, cut] + mm(
-                    values[g * HEAD_DIM : (g + 1) * HEAD_DIM], e[:, cut]
-                )
+                first = WIDE + g * HEAD_DIM
+                acc[g] = acc[g] * f[:, cut] + mm(kv[source, slot, first : first + HEAD_DIM], e[:, cut])
 
         m_s[...] = jnp.full_like(m_s, LOWEST)
         l_s[...] = jnp.zeros_like(l_s)
         acc[...] = jnp.zeros_like(acc)
-        tile(kr[0, s], kv[0, s, WIDE:], p * CHUNK, nlow, nhigh)
-
-        @pl.loop(meta[4 + p], p + c)
-        def _(k):
-            t = k ^ r ^ c
-            tile(kr[c, t], kv[c, t, WIDE:], k * CHUNK, low, high)
-
+        each_tile(meta, p, lims, tile)
         total = l_s[...]
         inv = 1.0 / total
         out = jnp.concatenate(
@@ -688,10 +703,10 @@
 def attend_back_body(load, meta, bounds, cos, sin, o_ref, ml_ref, *refs):
     heads, gs = refs[:5], refs[5]
     (
-        pq_ref, own_ref, far_a, far_b, far_c, far_d,
-        qs, kv, kr, vr, st_q, st_g, row_q, row_g, dk_o, dv_o, dk_c, dv_c, dq,
+        pq_ref, own_ref, far_a, far_b,
+        qs, kv, kr, vr, st_q, st_g, row_q, row_g, dk, dv, dq,
     ) = refs[6:]
-    for ref in (st_q, st_g, dk_o, dv_o, dk_c, dv_c):
+    for ref in (st_q, st_g, dk, dv):
         ref[...] = jnp.zeros_like(ref)
     load(head_pairs(heads, qs, kv))
 
@@ -707,7 +722,7 @@
     @pl.loop(0, 8)
     def _(p):
         s = p ^ r
-        q = qs[s]
+        q = qs[s] * 0.125
         stack_heads(q, st_q)
         total = ml_ref[s, 1:2]
         top = ml_ref[s, 0:1]
@@ -727,48 +742,45 @@
         for g in range(GROUP):
             row_q[g * CHUNK : (g + 1) * CHUNK] = jnp.where(lane == g, q_rows, 0.0).astype(BF)
             row_g[g * CHUNK : (g + 1) * CHUNK] = jnp.where(lane == g, g_rows, 0.0).astype(BF)
-        lim = bounds[p]
-        low, high, nlow, nhigh = [thrice(lim[i : i + 1]) for i in range(4)]
+        lims = [thrice(bounds[p, i : i + 1]) for i in range(4)]
         dq[...] = jnp.zeros_like(dq)
 
-        def tile(k_rows, v_rows, k_cols, base, lo, hi, dk, dv):
-            e = jnp.exp(scores_of(k_rows, st_q[...], base, lo, hi) - top)
-            d = (e * (mm(v_rows, st_g[...]) - fix)).astype(BF)
+        def tile(source, slot, own, base, lo, hi, plain):
+            e = jnp.exp(scores_of(kr[source, slot], st_q[...], base, lo, hi, plain) - top)
+            d = (e * (mm(vr[source, slot], st_g[...]) - fix)).astype(BF)
             e = e.astype(BF)
-            dv[...] += mm(e, row_g[...])
-            dk[...] += mm(d, row_q[...])
+            kind = jnp.where(own, 0, 1)
+            dv[kind, slot] += mm(e, row_g[...])
+            dk[kind, slot] += mm(d, row_q[...])
             for g in range(GROUP):
-                dq[g * HEAD_DIM : (g + 1) * HEAD_DIM] += mm(
-                    k_cols[g * HEAD_DIM : (g + 1) * HEAD_DIM], d[:, g * CHUNK : (g + 1) * CHUNK]
-                )
-
-        tile(kr[0, s], vr[0, s], kv[0, s, :WIDE], p * CHUNK, nlow, nhigh, dk_o.at[s], dv_o.at[s])
-
-        @pl.loop(meta[4 + p], p + c)
-        def _(k):
-            t = k ^ r ^ c
-            tile(kr[c, t], vr[c, t], kv[c, t, :WIDE], k * CHUNK, low, high, dk_c.at[t], dv_c.at[t])
-
+                part = slice(g * HEAD_DIM, (g + 1) * HEAD_DIM)
+                dq[part] += mm(kv[source, slot, part], d[:, g * CHUNK : (g + 1) * CHUNK])
+
+        each_tile(meta, p, lims, tile)
         pq_ref[s] = turn_heads(dq[...] * 0.125, cos[s], -sin[s]).astype(BF)
 
     both = 1.0 - c.astype(F32)
 
-    for s in range(8):
-        dk = jnp.transpose(dk_c[s])
-        dv = jnp.transpose(dv_c[s])
-        far_ref = (far_a, far_b, far_c, far_d)[s // 2]
-        far_ref[s % 2, :WIDE] = dk.astype(BF)
-        far_ref[s % 2, WIDE:] = dv.astype(BF)
-        own_ref[s, :WIDE] = jnp.transpose(dk_o[s]) + both * dk
-        own_ref[s, WIDE:] = jnp.transpose(dv_o[s]) + both * dv
+    @pl.loop(0, 8)
+    def _(s):
+        far_k, far_v = jnp.transpose(dk[1, s]), jnp.transpose(dv[1, s])
+        for half, far_ref in enumerate((far_a, far_b)):
+
+            @pl.when(s // 4 == half)
+            def _():
+                far_ref[s % 4, :WIDE] = far_k.astype(BF)
+                far_ref[s % 4, WIDE:] = far_v.astype(BF)
+
+        own_ref[s, :WIDE] = jnp.transpose(dk[0, s]) + both * far_k
+        own_ref[s, WIDE:] = jnp.transpose(dv[0, s]) + both * far_v
 
 
 def attend_back(meta, bounds, cos, sin, attended, stats, heads, grads):
     rows = pltpu.VMEM((2, 8, CHUNK, WIDE), BF)
-    sums = pltpu.VMEM((8, CHUNK, WIDE), F32)
+    sums = pltpu.VMEM((2, 8, CHUNK, WIDE), F32)
     return call(
         attend_back_body,
-        [((8, WIDE, CHUNK), BF), ((8, 2 * WIDE, CHUNK), F32)] + [((2, 2 * WIDE, CHUNK), BF)] * 4,
+        [((8, WIDE, CHUNK), BF), ((8, 2 * WIDE, CHUNK), F32)] + [((4, 2 * WIDE, CHUNK), BF)] * 2,
         "SVVVVV" + "A" * 5 + "V",
         (meta, bounds, cos, sin, attended, stats, *heads, grads),
         scratch=HEAD_SCRATCH
@@ -780,7 +792,7 @@
             pltpu.VMEM((LANES, WIDE), BF),
             pltpu.VMEM((LANES, WIDE), BF),
         ]
-        + [sums] * 4
+        + [sums] * 2
         + [pltpu.VMEM((WIDE, CHUNK), F32)],
         flops=20 * 2 * 5 * CHUNK * LANES * 256,
         moved=8 * CHUNK * WIDE * 30,
@@ -800,18 +812,19 @@
 
 
 def middle_body(load, meta, gain, embed, x_ref, heads, own, *refs):
-    parts = refs[:4]
     mid_ref, n_ref, att_ref, w_ref = refs[4:]
-    pairs = share_pairs(meta, own, parts, w_ref, 192, 0)
+    pairs = share_pairs(meta, own, refs[:4], w_ref, 192, 0)
     for d in range(8):
         pairs.append((heads.at[d], att_ref.at[d % 2, pl.ds(d // 2 * WIDE, WIDE)]))
     load(pairs)
-    for stream in range(2):
+
+    @pl.loop(0, 2)
+    def _(stream):
         x, _ = unmark(x_ref[stream], embed[...])
         mid = x + mm(att_ref[stream], w_ref[...], 0, 0)
         hat, _ = norm_parts(mid)
         mid_ref[stream] = mid
-        n_ref[stream * CHUNK : (stream + 1) * CHUNK] = (hat * gain[...]).astype(BF)
+        n_ref[pl.ds(pl.multiple_of(stream * CHUNK, CHUNK), CHUNK)] = (hat * gain[...]).astype(BF)
 
 
 def middle_rows(meta, gain, embed, marked, heads, own, parts):
@@ -827,11 +840,11 @@
 
 
 def feed_body(load, meta, bias, n_own, n_far, g_own, g_far, up_own, down_own, *refs):
-    shares = refs[:4]
+    shares, refs = refs[:4], refs[4:]
     (
         out_ref, outf_ref, ngf_ref, ng_ref, gb_ref, d_ref, u_ref,
         ns, gs, wu, wd, acts, slopes,
-    ) = refs[4:]
+    ) = refs
     c, h, z = meta[1], meta[2], meta[3]
     rows = 2 * CHUNK
     part = bias.shape[1] // 4
@@ -859,7 +872,9 @@
     load(pairs)
     gb_ref[...] = jnp.zeros_like(gb_ref)
 
-    def forward_and_back(span, out, ng):
+    @pl.loop(0, 4)
+    def _(i):
+        span = pl.ds(pl.multiple_of(i * CHUNK, CHUNK), CHUNK)
         v = mm(ns[span], wu[...]) + bias[...]
         square = v * v
         th = jnp.tanh(v * (GELU_SCALE + (GELU_SCALE * 0.044715) * square))
@@ -870,23 +885,26 @@
         ug = (slope * mm(gs[span], wd[...], 1, 1)).astype(BF)
         slopes[span] = ug
         gb_ref[...] += jnp.sum(ug.astype(F32), axis=0, keepdims=True)
-        out[...] = mm(act, wd[...]).astype(out.dtype)
-        ng[...] = mm(ug, wu[...], 1, 1).astype(ng.dtype)
-
-    @pl.loop(0, 2)
-    def _(i):
-        low = pl.ds(pl.multiple_of(i * CHUNK, CHUNK), CHUNK)
-        forward_and_back(low, out_ref.at[low], ng_ref.at[low])
-        forward_and_back(
-            pl.ds(pl.multiple_of(rows + i * CHUNK, CHUNK), CHUNK), outf_ref.at[low], ngf_ref.at[low]
-        )
+        out = mm(act, wd[...]).astype(BF)
+        ng = mm(ug, wu[...], 1, 1).astype(BF)
+        to = pl.ds(pl.multiple_of((i & 1) * CHUNK, CHUNK), CHUNK)
+
+        @pl.when(i < 2)
+        def _():
+            out_ref[to] = out
+            ng_ref[to] = ng
+
+        @pl.when(i >= 2)
+        def _():
+            outf_ref[to] = out
+            ngf_ref[to] = ng
 
     @pl.loop(0, 4)
     def _(j):
         cols = pl.ds(pl.multiple_of(j * part, 128), part)
         gd = mm(acts[:, cols], gs[...], 0, 0).astype(BF)
         for b in range(4):
-            d_ref[b, j] = gd[96 * b : 96 * (b + 1)]
+            d_ref[b, j ^ h] = gd[96 * b : 96 * (b + 1)]
         gu = mm(ns[...], slopes[:, cols], 0, 0)
         side = pl.ds(pl.multiple_of((j & 1) * part, 128), part)
         line = pl.ds(at16((j >> 1) * 48), 48)
@@ -902,7 +920,7 @@
     hid = bias.shape[1]
     return call(
         feed_body,
-        [((rows, dim), F32), ((rows, dim), BF), ((rows, dim), BF), ((rows, dim), F32)]
+        [((rows, dim), BF)] * 4
         + [((1, hid), F32)]
         + [((4, 4, hid // 16, dim), BF)] * 2,
         "SV" + "A" * 10,
@@ -943,30 +961,28 @@
     lay_ref, mg_ref, sum_ref, send,
 ):
     load([])
-    gain_sum = jnp.zeros((1, gain.shape[1]), F32)
-    g_sum = gain_sum
-    for stream in range(2):
-        span = slice(stream * CHUNK, (stream + 1) * CHUNK)
+    sum_ref[...] = jnp.zeros_like(sum_ref)
+
+    @pl.loop(0, 2)
+    def _(stream):
+        span = pl.ds(pl.multiple_of(stream * CHUNK, CHUNK), CHUNK)
         mid = mid_ref[stream]
-        lay = mid + out_ref[span] + outf_ref[span].astype(F32) + b_down[...]
+        lay = mid + out_ref[span].astype(F32) + outf_ref[span].astype(F32) + b_down[...]
         lay_ref[stream] = lay.astype(BF)
         hat, scale = norm_parts(mid)
-        ng = ng_ref[span] + ngf_ref[span].astype(F32)
-        gain_sum += jnp.sum(ng * hat, axis=0, keepdims=True)
+        ng = ng_ref[span].astype(F32) + ngf_ref[span].astype(F32)
+        sum_ref[0:1] += jnp.sum(ng * hat, axis=0, keepdims=True)
         t = ng * gain[...]
         g = g_ref[stream].astype(F32)
-        g_sum += jnp.sum(g, axis=0, keepdims=True)
+        sum_ref[1:2] += jnp.sum(g, axis=0, keepdims=True)
         t_mean = jnp.mean(t, axis=-1, keepdims=True)
         t_hat = jnp.mean(t * hat, axis=-1, keepdims=True)
         mg = (g + scale * (t - t_mean - hat * t_hat)).astype(BF)
         mg_ref[stream] = mg
-        if stream == 1:
-            flag = x_ref[1][:, :1].astype(F32) > 1e38
-            sum_ref[2:3] = jnp.sum(jnp.where(flag, mg.astype(F32), 0.0), axis=0, keepdims=True)
-    sum_ref[0:1] = gain_sum
-    sum_ref[1:2] = g_sum
-    for d in range(8):
-        send[d] = mm(w_ref[d // 2 * WIDE : (d // 2 + 1) * WIDE], mg_ref[d % 2], 1, 1).astype(BF)
+        flag = (x_ref[stream][:, :1].astype(F32) > 1e38) & (stream == 1)
+        sum_ref[2:3] += jnp.sum(jnp.where(flag, mg.astype(F32), 0.0), axis=0, keepdims=True)
+        for d in range(4):
+            send[2 * d + stream] = mm(w_ref[d * WIDE : (d + 1) * WIDE], mg, 1, 1).astype(BF)
 
 
 def middle_back(meta, gain, b_down, args):
@@ -989,13 +1005,17 @@
             ref[zz, 48 * h : 48 * (h + 1)] = pair.astype(BF)
 
 
-def out_grad_body(load, att_ref, mg_ref, o_ref):
-    load([])
-    by_z(mm(att_ref[0], mg_ref[0]) + mm(att_ref[1], mg_ref[1]), o_ref)
+def out_grad_body(load, att_ref, mg_ref, up, o_ref):
+    load([(up.at[h], o_ref.at[h, :, pl.ds(0, 96)]) for h in range(4)])
+    grad = mm(att_ref[0], mg_ref[0]) + mm(att_ref[1], mg_ref[1])
+    for b in range(16):
+        first = 192 * (b // 4) + 24 * (b % 4)
+        pair = jnp.concatenate([grad[first : first + 24], grad[first + 96 : first + 120]])
+        o_ref[b // 4, b % 4, 96:] = pair.astype(BF)
 
 
 def project_back_body(
-    own, f0, f1, f2, f3, pq, n_ref, mk_ref, cos, sin, w_ref,
+    own, f0, f1, pq, n_ref, mk_ref, cos, sin, w_ref,
     away_x, away_y, stay, gq_ref, gs_ref, wp, acc,
 ):
     i = pl.program_id(0)
@@ -1007,12 +1027,12 @@
         acc[...] = jnp.zeros_like(acc)
         gs_ref[...] = jnp.zeros_like(gs_ref)
 
-    piece = jnp.where(i % 4 == 0, 1 - i // 4, jnp.where(i == 1, 3, jnp.where(i == 3, 3, jnp.where(i == 7, 1, jnp.where(i == 6, 0, 2)))))
-    far = jnp.where(piece < 2, jnp.where(piece == 0, f0[0], f1[0]), jnp.where(piece == 2, f2[0], f3[0]))
+    early = (i == 0) | (i == 4) | (i == 6) | (i == 7)
+    far = jnp.where(early, f0[0], f1[0])
     kv = own[0] + far.astype(F32)
     parts = [
         pq[0],
-        turn_heads(kv[:WIDE] * 0.125, cos[0], -sin[0]).astype(BF),
+        turn_heads(kv[:WIDE], cos[0], -sin[0]).astype(BF),
         kv[WIDE:].astype(BF),
     ]
     n, mk = n_ref[0], mk_ref[0]
@@ -1075,7 +1095,7 @@
         ),
         in_specs=[
             block(2 * WIDE, CHUNK, slot),
-            *[block(2 * WIDE, CHUNK, lambda i: slot(i) % 2)] * 4,
+            *[block(2 * WIDE, CHUNK, lambda i: slot(i) % 4)] * 2,
             block(WIDE, CHUNK, slot),
             block(CHUNK, dim, slot), block(CHUNK, 128, slot),
             block(HALF, CHUNK, slot), block(HALF, CHUNK, slot), whole(*w.shape),
@@ -1097,8 +1117,10 @@
 
 def last_body(load, meta, gain, embed, x_ref, mg_ref, keep_ref, far_ref, o_ref):
     load([])
-    c = meta[1]
-    for stream, ng in ((c, keep_ref[...]), (1 - c, far_ref[...].astype(F32))):
+
+    @pl.loop(0, 2)
+    def _(stream):
+        ng = jnp.where(stream == meta[1], keep_ref[...], far_ref[...].astype(F32))
         x, flag = unmark(x_ref[stream], embed[...])
         hat, scale = norm_parts(x)
         t = ng * gain[...]
@@ -1106,6 +1128,56 @@
         t_hat = jnp.mean(t * hat, axis=-1, keepdims=True)
         grad = mg_ref[stream].astype(F32) + scale * (t - t_mean - hat * t_hat)
         o_ref[stream] = jnp.where(flag, 0.0, grad).astype(BF)
+
+
+def finish_body(load, meta, gain, embed, x_ref, up_own, up_far, *refs):
+    gd_refs, (gq_ref, go_ref, gu_ref, gd_ref, bu_ref, rows_ref, sums) = refs[:4], refs[4:]
+    load([])
+    r, c, z = meta[0], meta[1], meta[3]
+    own = 4 * r + z
+    small = gq_ref.shape[0]
+    for h in range(4):
+        part = x_ref[2 * h, :small].astype(F32) + x_ref[2 * h + 1, :small].astype(F32)
+        for k in range(3):
+            first = k * 4 * WIDE + h * WIDE
+            gq_ref[:, first : first + WIDE] = part[:, k * WIDE : (k + 1) * WIDE]
+    total = add(gd_refs[0][...], gd_refs[1][...])
+    gd_ref[...] = total + add(gd_refs[2][...], gd_refs[3][...])
+
+    rows = up_own[...].astype(F32)
+    mine = [jnp.where(c == 0, rows[48 * q : 48 * q + 24], rows[48 * q + 24 : 48 * q + 48]) for q in range(3)]
+    go_ref[...] = mine[2] + up_far[2].astype(F32)
+    part = gu_ref.shape[1] // 8
+    for q in range(2):
+        for side in range(2):
+            lanes = slice(side * part, (side + 1) * part)
+            for core, block in ((c, mine[q]), (1 - c, up_far[q].astype(F32))):
+                first = pl.multiple_of((2 * (2 * q + side) + core) * part, 128)
+                gu_ref[:, pl.ds(first, part)] = block[:, lanes]
+
+    total = x_ref[0, small:, :part].astype(F32)
+    for d in range(1, 8):
+        total += x_ref[d, small:, :part].astype(F32)
+    sums[...] = total
+
+    def pair(i):
+        return total[8 + 2 * i : 10 + 2 * i]
+
+    def over(v):
+        return jnp.sum(v, keepdims=True) * (1.0 / (2 * part))
+
+    centered = embed[...] - over(embed[...])
+    scale = lax.rsqrt(over(centered * centered) + EPSILON)
+    hat = centered * scale
+    t = pair(4) * gain[...]
+    sums[12:14] = pair(2) + scale * (t - over(t) - hat * over(t * hat))
+    sums[14:16] = pair(3) / gain[...]
+    row = sums[pl.ds(own // 4, 1)]
+    bu_ref[...] = pltpu.roll(row, (4 * 96 - own % 4 * 96) % part, 1)[:, :96]
+    shift = (16 * 24 - own % 16 * 24) % part
+    for i in range(4):
+        row = sums[pl.ds(8 + 2 * i + own // 16, 1)]
+        rows_ref[i : i + 1] = pltpu.roll(row, shift, 1)[:, :24]
 
 
 def cut(v, index, size, axis=0):
@@ -1172,24 +1244,6 @@
     other_x, other_y = swap(other, 2), swap(other, 4)
     marked = jnp.stack([hidden[0, 0], noisy])
 
-    size = hid // 4 + dim
-    w_qkv = after(w_qkv, other)
-    small = jnp.concatenate([b_up, b_down, gain_one, gain_two, mask_embed])
-    small = jnp.pad(small, (0, 16 * 3 * WIDE - size)).reshape(16, 3 * WIDE)
-    own_qkv = jnp.concatenate([cut(w_qkv[:, k * dim : (k + 1) * dim], h, WIDE, 1) for k in range(3)], 1)
-    quarter = dim // 4
-    half = jnp.concatenate([cut(own_qkv, c, quarter // 2), small])
-    half = jnp.broadcast_to(half, (4, *half.shape))
-    near = exchange_z(half)
-    far = swap(near, 1)
-    small = near[:, quarter // 2 :].reshape(4, -1)[:, :size].astype(F32)
-    bias = at(small[:, : hid // 4].reshape(4, 2, part), c, 1).reshape(1, 4 * part)
-    b_down_all, gain_a, gain_b, embed = [
-        small[:, hid // 4 + k * quarter : hid // 4 + (k + 1) * quarter].reshape(1, dim)
-        for k in range(4)
-    ]
-    mine_d, other_d = swap(mine_x, 4), swap(other_y, 2)
-
     lengths = doc_lengths[0]
     index = jnp.arange(lengths.shape[0])
     ends = jnp.sum(jnp.where(index[None, :] <= index[:, None], lengths[None, :], 0), axis=1)
@@ -1204,23 +1258,46 @@
     )
     bounds = jnp.pad(bounds.reshape(4, 8, CHUNK).transpose(1, 0, 2), ((0, 0), (0, 4), (0, 0)))
     meta = jnp.concatenate(
-        [jnp.stack([r, c, h, z]), start[::CHUNK] // CHUNK, jnp.zeros((4,), jnp.int32)]
+        [jnp.stack([r, c, h, z]), start[::CHUNK] // CHUNK, start[CHUNK - 1 :: CHUNK]]
     ).astype(jnp.int32)
     slots = (jnp.arange(8) ^ r)[:, None] * CHUNK + jnp.arange(CHUNK)[None, :]
     frequency = jnp.exp(jnp.arange(HALF).astype(F32) * (-2.0 * math.log(10000.0) / HEAD_DIM))
     angles = slots.astype(F32)[:, None, :] * frequency[None, :, None]
     cos, sin = jnp.cos(angles), jnp.sin(angles)
+    size = hid // 4 + dim
+    w_qkv = after(w_qkv, other)
+    small = jnp.concatenate([b_up, b_down, gain_one, gain_two, mask_embed])
+    small = jnp.pad(small, (0, 16 * 3 * WIDE - size)).reshape(16, 3 * WIDE)
+    own_qkv = jnp.concatenate([cut(w_qkv[:, k * dim : (k + 1) * dim], h, WIDE, 1) for k in range(3)], 1)
+    quarter = dim // 4
+    half = jnp.concatenate([cut(own_qkv, c, quarter // 2), small])
+    half = jnp.broadcast_to(half, (4, *half.shape))
+    near = exchange_z(half)
+    mine_x, mine_y, other_x, other_y, cos, sin, bounds, meta = lax.optimization_barrier(
+        (mine_x, mine_y, other_x, other_y, cos, sin, bounds, meta)
+    )
+    mine_d, other_d = swap(mine_x, 4), swap(other_y, 2)
+    mine_d, other_d, near = lax.optimization_barrier((mine_d, other_d, near))
+    far = swap(near, 1)
+    small = near[:, quarter // 2 :].reshape(4, -1)[:, :size].astype(F32)
+    bias = at(small[:, : hid // 4].reshape(4, 2, part), c, 1).reshape(1, 4 * part)
+    b_down_all, gain_a, gain_b, embed = [
+        small[:, hid // 4 + k * quarter : hid // 4 + (k + 1) * quarter].reshape(1, dim)
+        for k in range(4)
+    ]
+
     grads = out_grad[0]
     grad_rows = grads.reshape(2 * CHUNK, dim)
 
     ff_r = jnp.take(ff_t, (z - jnp.arange(1, 4)) % 4, axis=0)
-    near, ff_r = lax.optimization_barrier((near, ff_r))
+    far, ff_r = lax.optimization_barrier((far, ff_r))
     shares = (ff_r, swap(ff_r, 2), swap(ff_r, 4), swap(ff_r, 6))
     rows = (mine, other, mine_x, other_x, mine_y, other_y, mine_d, other_d)
     q, *kv, normed_one, marks, w_all = project_rows(meta, gain_a, embed, cos, sin, rows, (near, far))
     give = [(i, i + 1) for i in range(0, 8, 2)]
     heads = (q, *kv, *[lax.ppermute(v, "ctx", give) for v in kv])
     send, attended, stats = attend_rows(meta, bounds, heads)
+    send, *shares = lax.optimization_barrier((send, *shares))
     grad_far = swap(after(grad_rows, kv[0]), 1)
     middle, normed, att, w_out_all = middle_rows(
         meta, gain_b, embed, marked, exchange(send), w_out, shares
@@ -1235,25 +1312,23 @@
         meta, gain_b, b_down_all, (middle, ng_own, out_own, out_far, ng_far, grads, marked, w_out_all)
     )
     got = exchange(send)
-    (go,) = call(
-        out_grad_body, [((4, dim // 4, dim), BF)], "VV", (att, mid_grad), flops=4 * CHUNK * dim * dim
-    )
-    got, gu, go = lax.optimization_barrier((got, gu, go))
-    go = lax.psum_scatter(go.reshape(-1, dim), "fsdp", scatter_dimension=0, tiled=True)
-    gu = exchange_chips(gu)
+    (up_out,) = call(
+        out_grad_body, [((4, 4, part // 4 + dim // 16, dim), BF)], "VVA", (att, mid_grad, gu), flops=4 * CHUNK * dim * dim
+    )
+    got, up_out = lax.optimization_barrier((got, up_out))
+    up_out = exchange_chips(up_out)
     pq, own_kv, *far_kv = attend_back(meta, bounds, cos, sin, attended, stats, heads, got)
     far_kv = [lax.ppermute(v, "ctx", [(b, a) for a, b in give]) for v in far_kv]
 
-    gu = jnp.sum(after(gu, pq).astype(F32), axis=0).astype(BF).reshape(-1, dim)
+    up_out = jnp.sum(after(up_out, pq).astype(F32), axis=0).astype(BF).reshape(-1, dim)
     gd = after(gd, pq).reshape(4, part // 4, dim)
-    *far_kv, gu, gd = lax.optimization_barrier((*far_kv, gu, gd))
-    gu = lax.psum_scatter(gu, "fsdp", scatter_dimension=0, tiled=True)
+    *far_kv, up_out, gd = lax.optimization_barrier((*far_kv, up_out, gd))
+    up_out = lax.psum_scatter(up_out, "fsdp", scatter_dimension=0, tiled=True)
 
     away_x, away_y, stay, gq, vec = project_back(
         own_kv, far_kv, pq, normed_one, marks, cos, sin, w_all
     )
     in_x, in_y = swap(away_x, 2), swap(away_y, 4)
-    gd = exchange_chips(gd)
     gbu = gbu.reshape(4, 1, part)
     gbu = jnp.where(clean, jnp.concatenate([gbu, 0 * gbu], 1), jnp.concatenate([0 * gbu, gbu], 1))
     flat = jnp.concatenate([gbu.reshape(-1), sums[:3].reshape(-1), vec[:2].reshape(-1)])
@@ -1261,24 +1336,26 @@
     length = flat.shape[0]
 
     def parts_of(v):
-        return jnp.pad(v, (0, 16 * wide - length)).reshape(16, wide).astype(BF)
+        v = v.reshape(length // part, part)
+        return jnp.pad(v, ((0, 24 - length // part), (0, wide - part))).astype(BF)
 
     rows = dim // 4
-    flat = jnp.broadcast_to(parts_of(flat), (4, 16, wide))
-    gq = after(jnp.concatenate([gq, flat], 1).reshape(-1, wide), go)
+    flat = jnp.broadcast_to(parts_of(flat), (4, 24, wide))
+    gq = jnp.concatenate([gq, flat], 1).reshape(-1, wide)
     gq = lax.psum_scatter(gq, "fsdp", scatter_dimension=0, tiled=True)
     over_y, over_x = add(stay[1], in_x[1]).astype(BF), add(stay[3], in_y[1]).astype(BF)
     near_one, near_two = swap(over_y, 4), swap(over_x, 2)
-    gq = after(gq, over_y, over_x, gd)
-    flat = jnp.broadcast_to(gq[rows:], (8, 16, wide))
+    gd = after(gd, over_y, over_x)
+    gd = [gd[0]] + [swap(gd[k], 2 * k) for k in range(1, 4)]
+    gq = after(gq, over_y, over_x)
+    flat = jnp.broadcast_to(gq[rows:], (8, 24, wide))
     gq = jnp.concatenate([gq[:rows].reshape(8, dim // 32, wide), flat], 1)
-    go = jnp.pad(go.reshape(8, dim // 32, dim), ((0, 0), (0, 16), (0, 0)))
-    gq = exchange(jnp.concatenate([gq, go], 2))
+    near_one, near_two, gq = lax.optimization_barrier((near_one, near_two, gq))
+    gq = exchange(gq)
     keep = add(stay[0], in_x[0]) + near_one.astype(F32)
     pair = (add(stay[2], in_y[0]) + near_two.astype(F32)).astype(BF)
     pair = swap(pair, 1)
-    gu = after(gu, over_y, over_x)
-    gq = after(gq, keep, pair)
+    *gd, gq = lax.optimization_barrier((*gd, gq, keep, pair))[:5]
     (input_grad,) = call(
         last_body,
         [((2, CHUNK, dim), BF)],
@@ -1287,42 +1364,37 @@
         moved=10 * CHUNK * dim,
     )
 
-    gd = jnp.sum(gd.astype(F32), axis=0).reshape(part // 4, dim)
-    gu = gu.astype(F32).reshape(2, 2, dim // 32, 2 * part).transpose(1, 2, 0, 3)
-    gu = gu.reshape(2, dim // 32, 4 * part)
-    gu_far = swap(at(gu, 1 - c).astype(BF), 1).astype(F32)
-    gu = at(gu, c)
-    gu = jnp.where(clean, jnp.stack([gu, gu_far]), jnp.stack([gu_far, gu]))
-    gu = gu.reshape(2, dim // 32, 4, part).transpose(1, 2, 0, 3).reshape(dim // 32, hid)
-    go = jnp.sum(gq[:, : dim // 32, wide:].astype(F32), axis=0)
-    flat = jnp.sum(gq[:, dim // 32 :, :wide].astype(F32), axis=0).reshape(-1)[:length]
-    gq = gq[:, : dim // 32, :wide].reshape(4, 2, dim // 32, wide)
-    gq = add(gq[:, 0], gq[:, 1])[..., : 3 * WIDE]
-    gq = gq.reshape(4, dim // 32, 3, WIDE).transpose(1, 2, 0, 3).reshape(dim // 32, 3 * dim)
-
-    gbu = flat[:hid]
-    g_gain_b, g_b_down, m_direct, g_gain_a, m_norm = [
-        flat[hid + k * dim : hid + (k + 1) * dim] for k in range(5)
-    ]
-    g_gain_a = g_gain_a / gain_a[0]
-    hat, scale = norm_parts(embed)
-    t = m_norm[None] * gain_a
-    t_mean = jnp.mean(t, axis=-1, keepdims=True)
-    t_hat = jnp.mean(t * hat, axis=-1, keepdims=True)
-    g_embed = m_direct + (scale * (t - t_mean - hat * t_hat))[0]
-    own = 4 * r + z
+    up_sum = after(up_out, input_grad)
+    up_out = up_sum.reshape(3, 2, dim // 32, dim)
+    up_far = swap(at(up_out, 1 - c, 1), 1)
+    small = dim // 32
+    gq, go, gu, gd, gbu, rows = call(
+        finish_body,
+        [
+            ((small, 3 * dim), F32),
+            ((small, dim), F32),
+            ((small, hid), F32),
+            ((part // 4, dim), F32),
+            ((1, hid // 32), F32),
+            ((4, small), F32),
+        ],
+        "S" + "V" * 9,
+        (meta, gain_a.reshape(2, part), embed.reshape(2, part), gq, up_sum, up_far, *gd),
+        scratch=[pltpu.VMEM((24, part), F32)],
+        moved=8 * dim * dim,
+    )
     return (
         layer[None],
         input_grad[None],
         gq,
         go,
         gu,
-        cut(gbu, own, hid // 32),
+        gbu[0],
         gd,
-        cut(g_b_down, own, dim // 32),
-        cut(g_gain_a, own, dim // 32),
-        cut(g_gain_b, own, dim // 32),
-        cut(g_embed, own, dim // 32),
+        rows[1],
+        rows[3],
+        rows[0],
+        rows[2],
     )
 
 

time: 342 us -> 328 us (0.959)
  starting transfers between devices: 54.5 us -> 44.3 us
  other arithmetic: 23.4 us -> 14 us
  Pallas kernels: 124 us -> 132 us
    all_to_all x2 -> x1, waiting for transfers between devices: 21.9 us -> 7.83 us  [exchange_chips(): return lax.all_to_all(v, 'ctx', 0, 0, axis_index_groups=groups, tiled=True)]
    ppermute x21 -> x24, waiting for transfers between devices: 29.1 us -> 37.5 us  [swap(): return lax.ppermute(v, 'ctx', [(i, i ^ bit) for i in range(8)])]
    pallas_call x9 -> x10, Pallas kernels: 110 us -> 118 us  [call(): pl.pallas_call(run, out_shape=tuple((jax.ShapeDtypeStruct(s, d) for s, d...]
    reduce_sum x7 -> x1, other arithmetic: 7.79 us -> 1.66 us  [shards_by_heads(): jnp.sum(after(up_out, pq).astype(F32), axis=0).astype(BF).reshape(-1, dim)]
    all_gather x1, waiting for transfers between devices: 1.18 us -> 5.24 us  [shards_by_heads(): ff_t = lax.all_gather(share, 'fsdp')]
    all_to_all x2 -> x1, starting transfers between devices: 7.78 us -> 3.73 us  [exchange_chips(): return lax.all_to_all(v, 'ctx', 0, 0, axis_index_groups=groups, tiled=True)]
    optimization_barrier x0 -> x1, waiting for transfers between devices: none -> 3.73 us  [after(): return lax.optimization_barrier((value, *needed))[0]]
    ppermute x4 -> x2, waiting for transfers between devices: 3.58 us -> 0.01 us  [shards_by_heads(): far_kv = [lax.ppermute(v, 'ctx', [(b, a) for a, b in give]) for v in far_kv]]
  transfers between devices with their start and end apart: 38 -> 37, of which waited for: 18 -> 20; matrix products, arithmetic and copies ran while one was open for 10% -> 8% of each run, Pallas kernels for 25% -> 26%
where the time goes in v3:
time: 328 us; the launch traced here: 327 us
  Pallas kernels  132 us (40%)
  waiting for transfers between devices  96.5 us (29%)
  starting transfers between devices  44.3 us (14%)
  local copies, waits for them, and re-layouts  26.1 us (8%)
  between operations  14.6 us (4%)
  other arithmetic  14 us (4%)
    pallas_call x10, Pallas kernels, call(): pl.pallas_call(run, out_shape=tuple((jax.ShapeDtypeStruct(s, d) for s, d...  118 us
    ppermute x24, waiting for transfers between devices, swap(): return lax.ppermute(v, 'ctx', [(i, i ^ bit) for i in range(8)])  37.5 us
    all_to_all x1, waiting for transfers between devices, exchange_z(): return lax.all_to_all(v, 'fsdp', 0, 0, tiled=True)  19 us
    ppermute x24, starting transfers between devices, swap(): return lax.ppermute(v, 'ctx', [(i, i ^ bit) for i in range(8)])  18.4 us
    all_to_all x3, waiting for transfers between devices, exchange(): return lax.all_to_all(v, 'ctx', 0, 0, tiled=True)  16.9 us
    pallas_call x1, Pallas kernels, project_back(): pl.pallas_call(project_back_body, grid=(8,), out_shape=(jax.ShapeDtypeStr...  13.9 us
    all_to_all x3, starting transfers between devices, exchange(): return lax.all_to_all(v, 'ctx', 0, 0, tiled=True)  11.5 us
    unnamed x88, local copies, waits for them, and re-layouts  8.55 us
  transfers between devices with their start and end apart: 37, of which 20 were waited for; matrix products, arithmetic and copies ran while one was open for 8% of the time, Pallas kernels for 26%

profile of v3, /device:TPU:0, one launch (start us, length us, event | category | flops | bytes accessed | tf_op | source)
XLA Modules:
  0.0 326.9 jit_solution(10476537583970657507)
XLA Ops:
  7.8 2.9 shard_map.212
  11.1 3.0 collective-permute-start.1
  14.1 1.5 collective-permute-start
  16.3 1.1 collective-permute-done.2.refs_6_
  17.9 0.9 broadcast_in_dim.92
  18.8 4.9 %all-to-all-start = ((bf16[4,112,576]{2,1,0:T(8,128)(2,1)}), bf16[4,112,576]{2,1,0:T(8,128)(2,1)S(1)}, u32[]{:S(2)}, u32[]{:S(2)}) async-start(bf16[4,112,576]{2,1,0:T(8,128)(2,1)} %broadcast_in_dim.92), calls=%async_computation | async-start | bytes 1146880 | tf_op jit(solution)/shard_map/all_to_all | solution.py:1209
  26.1 1.8 multiply_sine_fusion
  27.9 6.8 %collective-permute-done.4.refs_10_ = bf16[256,768]{1,0:T(8,128)(2,1)S(1)} collective-permute-done((bf16[256,768]{1,0:T(8,128)(2,1)}, bf16[256,768]{1,0:T(8,128)(2,1)S(1)}, u32[]{:S(2)}, u32[]{:S(2)}) %collective-permute-start.4) | collective-permute-done | bytes 393248 | tf_op jit(solution)/shard_map/ppermute | solution.py:438
  34.9 1.5 collective-permute-start.5
  37.0 19.0 %all-to-all-done.refs_13_ = bf16[4,112,576]{2,1,0:T(8,128)(2,1)S(1)} async-done(((bf16[4,112,576]{2,1,0:T(8,128)(2,1)}), bf16[4,112,576]{2,1,0:T(8,128)(2,1)S(1)}, u32[]{:S(2)}, u32[]{:S(2)}) %all-to-all-start) | async-done | bytes 516128 | tf_op jit(solution)/shard_map/all_to_all | solution.py:1209
  56.3 5.2 %all-gather.3.cloned.1.call-done = bf16[960,768]{1,0:T(8,128)(2,1)} async-done(((bf16[240,768]{1,0:T(8,128)(2,1)}), bf16[960,768]{1,0:T(8,128)(2,1)}) %all-gather.3.cloned.1.call-update) | async-done | bytes 1474576 | tf_op jit(solution)/shard_map/all_gather | solution.py:1237
  61.5 2.0 gather_fusion
  63.7 2.4 collective-permute-start.12
  68.7 13.9 %shard_map.213 = (bf16[8,192,256]{2,1,0:T(8,128)(2,1)}, bf16[4,384,256]{2,1,0:T(8,128)(2,1)}, bf16[4,384,256]{2,1,0:T(8,128)(2,1)}, bf16[8,256,768]{2,1,0:T(8,12...) custom-call(s32[20]{0:T(128)} %concatenate.29.refs_0_, f32[1,768]{1,0:T(1,128)} %reshape.353.refs_1_, ...), custom_call_target="tpu_custom_call" | custom-call | flops 2 | bytes 1 | tf_op jit(solution)/shard_map/pallas_call | solution.py:485
  82.6 1.3 collective-permute-start.9
  83.9 1.3 collective-permute-start.8
  86.0 1.3 collective-permute-done.8.refs_5_.refs_9_
  87.3 0.9 copy-done.6
  88.2 20.3 %shard_map.214 = (bf16[8,192,256]{2,1,0:T(8,128)(2,1)}, f32[8,192,256]{2,1,0:T(8,128)}, f32[8,8,768]{2,1,0:T(8,128)}) custom-call(s32[20]{0:T(128)} %concatenate.29.refs_0_, s32[8,8,256]{2,1,0:T(8,128)} %pad.13.refs_1_, bf16[8,192,256]{2,1,0:T(8,128)(2,1)} %get-tuple-element.104.refs_2_.refs_6_, bf16[4,384,256]{2,1,0:T(8,128)(2,1)} %get-tuple-element.105.refs_3_.refs_7_, ...), custom_call_target="tpu_custom_call" | custom-call | flops 5 | bytes 1 | tf_op jit(solution)/shard_map/pallas_call | solution.py:485
  108.6 6.0 %collective-permute-done.11.refs_8_.refs_10_ = bf16[3,240,768]{2,1,0:T(8,128)(2,1)S(1)} collective-permute-done((bf16[3,240,768]{2,1,0:T(8,128)(2,1)S(1)}, bf16[3,240,768]{2,1,0:T(8,128)(2,1)S(1)}, u32[]{:S(2)}, u32[]{:S(2)}) %collective-permute-start.11) | collective-permute-done | bytes 1105952 | tf_op jit(solution)/shard_map/ppermute | solution.py:438
  114.7 4.4 %all-to-all-start.1 = ((bf16[8,192,256]{2,1,0:T(8,128)(2,1)}), bf16[8,192,256]{2,1,0:T(8,128)(2,1)}, u32[]{:S(2)}, u32[]{:S(2)}) async-start(bf16[8,192,256]{2,1,0:T(8,128)(2,1)} %get-tuple-element.109), calls=%async_computation.1 | async-start | bytes 1572864 | tf_op jit(solution)/shard_map/all_to_all | solution.py:1200
  119.3 1.0 slice_bitcast_fusion
  120.5 0.9 pad_maximum_fusion.1.refs_3_.refs_9_
  122.2 9.4 %all-to-all-done.1.refs_4_ = bf16[8,192,256]{2,1,0:T(8,128)(2,1)} async-done(((bf16[8,192,256]{2,1,0:T(8,128)(2,1)}), bf16[8,192,256]{2,1,0:T(8,128)(2,1)}, u32[]{:S(2)}, u32[]{:S(2)}) %all-to-all-start.1) | async-done | bytes 786464 | tf_op jit(solution)/shard_map/all_to_all | solution.py:1200
  131.7 6.3 %shard_map.215 = (f32[2,256,768]{2,1,0:T(8,128)}, bf16[512,768]{1,0:T(8,128)(2,1)}, bf16[2,768,256]{2,1,0:T(8,128)(2,1)}, bf16[768,768]{1,0:T(8,128)(2,1)}) custom-call(s32[20]{0:T(128)} %concatenate.29.refs_0_, f32[1,768]{1,0:T(1,128)} %reshape.350.refs_1_, f32[1,768]{1,0:T(1,128)} %reshape.352.refs_2_, ...), custom_call_target="tpu_custom_call" | custom-call | flops 1 | bytes 1 | tf_op jit(solution)/shard_map/pallas_call | solution.py:485
  138.7 1.8 collective-permute-done.13.refs_3_
  140.5 0.9 copy-done.17
  141.4 25.2 %shard_map.216 = (bf16[512,768]{1,0:T(8,128)(2,1)}, bf16[512,768]{1,0:T(8,128)(2,1)}, bf16[512,768]{1,0:T(8,128)(2,1)}, bf16[512,768]{1,0:T(8,128)(2,1)}, f32[1,...) custom-call(s32[20]{0:T(128)} %concatenate.29.refs_0_, f32[1,1536]{1,0:T(1,128)} %bitcast.90, ...), custom_call_target="tpu_custom_call" | custom-call | flops 15 | bytes 1 | tf_op jit(solution)/shard_map/pallas_call | solution.py:485
  166.7 1.1 copy-done.40
  168.9 1.1 collective-permute-done.15.refs_6_
  170.0 1.1 collective-permute-done.16.refs_7_
  171.2 0.9 copy-done.15
  172.1 8.1 %shard_map.217 = (bf16[2,256,768]{2,1,0:T(8,128)(2,1)}, bf16[2,256,768]{2,1,0:T(8,128)(2,1)}, f32[8,768]{1,0:T(8,128)}, bf16[8,192,256]{2,1,0:T(8,128)(2,1)}) custom-call(s32[20]{0:T(128)} %concatenate.29.refs_0_, f32[1,768]{1,0:T(1,128)} %reshape.350.refs_1_, f32[1,768]{1,0:T(1,128)} %reshape.351.refs_2_, f32[2,256,768]{2,1,0:T(8,128)} %get-tuple-element.114.refs_3_, ...), custom_call_target="tpu_custom_call" | custom-call | flops 1 | bytes 1 | tf_op jit(solution)/shard_map/pallas_call | solution.py:485
  180.2 3.6 %all-to-all-start.2 = ((bf16[8,192,256]{2,1,0:T(8,128)(2,1)}), bf16[8,192,256]{2,1,0:T(8,128)(2,1)S(1)}, u32[]{:S(2)}, u32[]{:S(2)}) async-start(bf16[8,192,256]{2,1,0:T(8,128)(2,1)} %get-tuple-element.126), calls=%async_computation.2 | async-start | bytes 1572864 | tf_op jit(solution)/shard_map/all_to_all | solution.py:1200
  183.8 5.1 %shard_map.218 = bf16[4,4,144,768]{3,2,1,0:T(8,128)(2,1)} custom-call(bf16[2,768,256]{2,1,0:T(8,128)(2,1)} %get-tuple-element.127.refs_0_, bf16[2,256,768]{2,1,0:T(8,128)(2,1)} %get-tuple-element.123.refs_1_.refs_4_, bf16[4,4,96,768]{3,2,1,0:T(8,128)(2,1)} %get-tuple-element.128.refs_2_), custom_call_target="tpu_custom_call" | custom-call | flops 1 | bytes 1 | tf_op jit(solution)/shard_map/pallas_call | solution.py:485
  188.8 7.4 %all-to-all-done.2.refs_11_ = bf16[8,192,256]{2,1,0:T(8,128)(2,1)S(1)} async-done(((bf16[8,192,256]{2,1,0:T(8,128)(2,1)}), bf16[8,192,256]{2,1,0:T(8,128)(2,1)S(1)}, u32[]{:S(2)}, u32[]{:S(2)}) %all-to-all-start.2) | async-done | bytes 786464 | tf_op jit(solution)/shard_map/all_to_all | solution.py:1200
  196.3 0.9 copy-done.3
  197.2 3.7 %all-to-all-start.3 = ((bf16[4,4,144,768]{3,2,1,0:T(8,128)(2,1)}), bf16[4,4,144,768]{3,2,1,0:T(8,128)(2,1)S(1)}, u32[]{:S(2)}, u32[]{:S(2)}) async-start(bf16[4,4,144,768]{3,2,1,0:T(8,128)(2,1)} %shard_map.218), calls=%async_computation.3 | async-start | bytes 7077888 | tf_op jit(solution)/shard_map/all_to_all | solution.py:1205
  201.0 26.9 %shard_map.219 = (bf16[8,192,256]{2,1,0:T(8,128)(2,1)}, f32[8,384,256]{2,1,0:T(8,128)}, bf16[4,384,256]{2,1,0:T(8,128)(2,1)}, bf16[4,384,256]{2,1,0:T(8,128)(2,1)}) custom-call(s32[20]{0:T(128)} %concatenate.29.refs_0_, s32[8,8,256]{2,1,0:T(8,128)} %pad.13.refs_1_, f32[8,32,256]{2,1,0:T(8,128)} %get-tuple-element.97.refs_3_.refs_2_.cos, ...), custom_call_target="tpu_custom_call" | custom-call | flops 11 | bytes 1 | tf_op jit(solution)/shard_map/pallas_call | solution.py:485
  227.9 1.3 collective-permute-start.17
  229.2 1.5 collective-permute-start.18
  232.8 7.8 %all-to-all-done.3 = bf16[4,4,144,768]{3,2,1,0:T(8,128)(2,1)S(1)} async-done(((bf16[4,4,144,768]{3,2,1,0:T(8,128)(2,1)}), bf16[4,4,144,768]{3,2,1,0:T(8,128)(2,1)S(1)}, u32[]{:S(2)}, u32[]{:S(2)}) %all-to-all-start.3) | async-done | bytes 3538976 | tf_op jit(solution)/shard_map/all_to_all | solution.py:1205
  240.6 1.7 reduce_sum.22
  242.3 13.9 %shard_map.220 = (bf16[2,256,768]{2,1,0:T(8,128)(2,1)}, bf16[2,256,768]{2,1,0:T(8,128)(2,1)}, f32[4,256,768]{2,1,0:T(8,128)}, bf16[4,192,640]{2,1,0:T(8,128)(2,1)}, f32[8,768]{1,0:T(8,128)}) custom-call(f32[8,384,256]{2,1,0:T(8,128)} %get-tuple-element.130.own, bf16[4,384,256]{2,1,0:T(8,128)(2,1)} %collective-permute-done.17.f0, ...), custom_call_target="tpu_custom_call" | custom-call | flops 4 | bytes 1 | tf_op jit(solution)/shard_map/pallas_call | solution.py:1086
  257.0 2.5 pad_maximum_fusion
  260.1 1.6 collective-permute-start.21
  261.7 15.8 %collective-permute-done.19 = bf16[2,256,768]{2,1,0:T(8,128)(2,1)} collective-permute-done((bf16[2,256,768]{2,1,0:T(8,128)(2,1)}, bf16[2,256,768]{2,1,0:T(8,128)(2,1)}, u32[]{:S(2)}, u32[]{:S(2)}) %collective-permute-start.19) | collective-permute-done | bytes 786464 | tf_op jit(solution)/shard_map/ppermute | solution.py:438
  277.5 1.3 collective-permute-done.21
  278.8 2.1 fusion.2
  281.9 3.7 %reduce-scatter.10.cloned.1.call-done = bf16[216,640]{1,0:T(8,128)(2,1)} async-done(((bf16[864,640]{1,0:T(8,128)(2,1)}), bf16[216,640]{1,0:T(8,128)(2,1)}) %reduce-scatter.10.cloned.1.call-update) | async-done | bytes 276496 | tf_op jit(solution)/shard_map/optimization_barrier | solution.py:1192
  285.6 0.8 slice.129
  286.4 1.0 slice.128
  287.4 0.8 pad_maximum_fusion.2
  288.2 1.9 collective-permute-done.22
  290.2 0.7 copy-done.19
  290.9 2.5 fusion
  293.4 3.6 %all-to-all-start.4 = ((bf16[8,48,640]{2,1,0:T(8,128)(2,1)}), bf16[8,48,640]{2,1,0:T(8,128)(2,1)S(1)}, u32[]{:S(2)}, u32[]{:S(2)}) async-start(bf16[8,48,640]{2,1,0:T(8,128)(2,1)} %pad_maximum_fusion.2), calls=%async_computation.5 | async-start | bytes 983040 | tf_op jit(solution)/shard_map/all_to_all | solution.py:1200
  297.7 2.8 collective-permute-start.26
  301.2 0.7 copy-done.20
  302.0 5.1 %shard_map.221 = bf16[2,256,768]{2,1,0:T(8,128)(2,1)} custom-call(s32[20]{0:T(128)} %concatenate.29.refs_0_, f32[1,768]{1,0:T(1,128)} %reshape.353.refs_1_, f32[1,768]{1,0:T(1,128)} %reshape.352.refs_2_, bf16[2,256,768]{2,1,0:T(8,128)(2,1)} %pad_maximum_fusion.1.refs_3_.refs_9_, bf16[2,256,768]{2,1,0:T(8,128)(2,1)} %get-tuple-element.123.refs_1_.refs_4_, ...), custom_call_target="tpu_custom_call" | custom-call | flops 1 | bytes 1 | tf_op jit(solution)/shard_map/pallas_call | solution.py:485
  307.1 4.3 %reduce-scatter.8.cloned.1.call-done.refs_4_ = bf16[144,768]{1,0:T(8,128)(2,1)} async-done(((bf16[576,768]{1,0:T(8,128)(2,1)}), bf16[144,768]{1,0:T(8,128)(2,1)}) %reduce-scatter.8.cloned.1.call-update) | async-done | bytes 221200 | tf_op jit(solution)/shard_map/reduce_scatter | solution.py:1326
  311.3 0.9 dynamic-slice_bitcast_fusion
  315.2 3.9 %shard_map.222 = (f32[24,2304]{1,0:T(8,128)}, f32[24,768]{1,0:T(8,128)}, f32[24,3072]{1,0:T(8,128)}, f32[96,768]{1,0:T(8,128)}, f32[1,96]{1,0:T(1,128)}, /*index=5*/f32[4,24]{1,0:T(4,128)}) custom-call(s32[20]{0:T(128)} %concatenate.29.refs_0_, f32[2,384]{1,0:T(2,128)} %reshape_reshape.6.refs_1_, f32[2,384]{1,0:T(2,128)} %reshape_reshape.7.refs_2_, ...), custom_call_target="tpu_custom_call" | custom-call | flops 1 | bytes 1 | tf_op jit(solution)/shard_map/pallas_call | solution.py:485
  319.1 1.3 slice_bitcast_fusion.5
  (179 shorter events, 20.8 us)
Async XLA Ops:
  7.2 54.3 %all-gather.3.cloned.1.call-start = ((), (), s32[]{:S(2)}) async-start(), calls=%async_computation.10 | async-start | bytes 1843200 | tf_op jit(solution)/shard_map/all_gather | solution.py:1237
  7.8 3.1 copy-start.41
  7.8 3.1 copy-start.7
  10.8 4.8 %copy-start.42 = (s32[1,16]{1,0:T(1,128)S(1)}, s32[1,16]{1,0:T(1,128)}, u32[]{:S(2)}) copy-start(s32[1,16]{1,0:T(1,128)} %param.15) | copy-start | bytes 196
  10.8 5.3 %copy-start.34 = (bf16[768]{0:T(1024)(128)(2,1)S(1)}, bf16[768]{0:T(1024)(128)(2,1)}, u32[]{:S(2)}) copy-start(bf16[768]{0:T(1024)(128)(2,1)} %param.19) | copy-start | bytes 4612
  10.8 5.3 %copy-start.35 = (bf16[192]{0:T(256)(128)(2,1)S(1)}, bf16[192]{0:T(256)(128)(2,1)}, u32[]{:S(2)}) copy-start(bf16[192]{0:T(256)(128)(2,1)} %param.21) | copy-start | bytes 1156
  10.8 5.3 %copy-start.36 = (bf16[192]{0:T(256)(128)(2,1)S(1)}, bf16[192]{0:T(256)(128)(2,1)}, u32[]{:S(2)}) copy-start(bf16[192]{0:T(256)(128)(2,1)} %param.22) | copy-start | bytes 1156
  10.8 5.2 %copy-start.37 = (bf16[192]{0:T(256)(128)(2,1)S(1)}, bf16[192]{0:T(256)(128)(2,1)}, u32[]{:S(2)}) copy-start(bf16[192]{0:T(256)(128)(2,1)} %param.23) | copy-start | bytes 1156
  10.8 5.2 %copy-start.38 = (bf16[192]{0:T(256)(128)(2,1)S(1)}, bf16[192]{0:T(256)(128)(2,1)}, u32[]{:S(2)}) copy-start(bf16[192]{0:T(256)(128)(2,1)} %param.24) | copy-start | bytes 1156
  10.8 6.6 %copy-start.13 = (bf16[192,2304]{1,0:T(8,128)(2,1)S(1)}, bf16[192,2304]{1,0:T(8,128)(2,1)}, u32[]{:S(2)}) copy-start(bf16[192,2304]{1,0:T(8,128)(2,1)} %param.16) | copy-start | bytes 2654212
  11.1 6.7 %copy-start.12 = (bf16[256,768]{1,0:T(8,128)(2,1)}, bf16[256,768]{1,0:T(8,128)(2,1)S(1)}, u32[]{:S(2)}) copy-start(bf16[256,768]{1,0:T(8,128)(2,1)S(1)} %get-tuple-element.181.refs_5_) | copy-start | bytes 1179652
  11.1 16.8 %collective-permute-start.1 = (bf16[256,768]{1,0:T(8,128)(2,1)S(1)}, bf16[256,768]{1,0:T(8,128)(2,1)S(1)}, u32[]{:S(2)}, u32[]{:S(2)}) collective-permute-start(bf16[256,768]{1,0:T(8,128)(2,1)S(1)} %get-tuple-element.181.refs_5_), channel_id=1, source_target_pairs={{0,16},{4,20},{8,24},{12,28},{16,0},{20,4},{24,8},{28,12},{1,17},{... | collective-permute-start | bytes 1179656 | tf_op jit(solution)/shard_map/ppermute | solution.py:438
  14.1 13.8 %collective-permute-start = (bf16[256,768]{1,0:T(8,128)(2,1)S(1)}, bf16[256,768]{1,0:T(8,128)(2,1)S(1)}, u32[]{:S(2)}, u32[]{:S(2)}) collective-permute-start(bf16[256,768]{1,0:T(8,128)(2,1)S(1)} %get-tuple-element.181.refs_5_), channel_id=1, source_target_pairs={{0,8},{4,12},{8,0},{12,4},{16,24},{20,28},{24,16},{28,20},{1,9},{5... | collective-permute-start | bytes 1179656 | tf_op jit(solution)/shard_map/ppermute | solution.py:438
  15.6 1.9 collective-permute-start.2
  18.8 37.2 %all-to-all-start = ((bf16[4,112,576]{2,1,0:T(8,128)(2,1)}), bf16[4,112,576]{2,1,0:T(8,128)(2,1)S(1)}, u32[]{:S(2)}, u32[]{:S(2)}) async-start(bf16[4,112,576]{2,1,0:T(8,128)(2,1)} %broadcast_in_dim.92), calls=%async_computation | async-start | bytes 1146880 | tf_op jit(solution)/shard_map/all_to_all | solution.py:1209
  23.6 11.1 %collective-permute-start.4 = (bf16[256,768]{1,0:T(8,128)(2,1)}, bf16[256,768]{1,0:T(8,128)(2,1)S(1)}, u32[]{:S(2)}, u32[]{:S(2)}) collective-permute-start(bf16[256,768]{1,0:T(8,128)(2,1)} %collective-permute-done.2.refs_6_), channel_id=1, source_target_pairs={{0,16},{4,20},{8,24},{12,28},{16,0},{20,4},{24,8},{28,12},{1,17},{... | collective-permute-start | bytes 1179656 | tf_op jit(solution)/shard_map/ppermute | solution.py:438
  24.1 10.8 %collective-permute-start.3 = (bf16[256,768]{1,0:T(8,128)(2,1)}, bf16[256,768]{1,0:T(8,128)(2,1)S(1)}, u32[]{:S(2)}, u32[]{:S(2)}) collective-permute-start(bf16[256,768]{1,0:T(8,128)(2,1)} %collective-permute-done.2.refs_6_), channel_id=1, source_target_pairs={{0,8},{4,12},{8,0},{12,4},{16,24},{20,28},{24,16},{28,20},{1,9},{5... | collective-permute-start | bytes 1179656 | tf_op jit(solution)/shard_map/ppermute | solution.py:438
  27.9 33.7 %copy-start.21 = (bf16[256,768]{1,0:T(8,128)(2,1)}, bf16[256,768]{1,0:T(8,128)(2,1)S(1)}, u32[]{:S(2)}) copy-start(bf16[256,768]{1,0:T(8,128)(2,1)S(1)} %collective-permute-done.1.refs_9_) | copy-start | bytes 1179652
  27.9 33.7 %copy-start.22 = (bf16[256,768]{1,0:T(8,128)(2,1)}, bf16[256,768]{1,0:T(8,128)(2,1)S(1)}, u32[]{:S(2)}) copy-start(bf16[256,768]{1,0:T(8,128)(2,1)S(1)} %collective-permute-done.refs_7_) | copy-start | bytes 1179652
  34.7 26.8 %copy-start.23 = (bf16[256,768]{1,0:T(8,128)(2,1)}, bf16[256,768]{1,0:T(8,128)(2,1)S(1)}, u32[]{:S(2)}) copy-start(bf16[256,768]{1,0:T(8,128)(2,1)S(1)} %collective-permute-done.4.refs_10_) | copy-start | bytes 1179652
  34.9 26.6 %copy-start.24 = (bf16[256,768]{1,0:T(8,128)(2,1)}, bf16[256,768]{1,0:T(8,128)(2,1)S(1)}, u32[]{:S(2)}) copy-start(bf16[256,768]{1,0:T(8,128)(2,1)S(1)} %collective-permute-done.3.refs_8_) | copy-start | bytes 1179652
  34.9 21.0 %collective-permute-start.5 = (bf16[256,768]{1,0:T(8,128)(2,1)S(1)}, bf16[256,768]{1,0:T(8,128)(2,1)S(1)}, u32[]{:S(2)}, u32[]{:S(2)}) collective-permute-start(bf16[256,768]{1,0:T(8,128)(2,1)S(1)} %collective-permute-done.refs_7_), channel_id=1, source_target_pairs={{0,16},{4,20},{8,24},{12,28},{16,0},{20,4},{24,8},{28,12},{1,17},{... | collective-permute-start | bytes 1179656 | tf_op jit(solution)/shard_map/ppermute | solution.py:438
  36.5 19.5 %collective-permute-start.6 = (bf16[256,768]{1,0:T(8,128)(2,1)S(1)}, bf16[256,768]{1,0:T(8,128)(2,1)S(1)}, u32[]{:S(2)}, u32[]{:S(2)}) collective-permute-start(bf16[256,768]{1,0:T(8,128)(2,1)S(1)} %collective-permute-done.4.refs_10_), channel_id=1, source_target_pairs={{0,8},{4,12},{8,0},{12,4},{16,24},{20,28},{24,16},{28,20},{1,9},{5... | collective-permute-start | bytes 1179656 | tf_op jit(solution)/shard_map/ppermute | solution.py:438
  56.0 7.6 %copy-start.10 = (bf16[4,112,576]{2,1,0:T(8,128)(2,1)}, bf16[4,112,576]{2,1,0:T(8,128)(2,1)S(1)}, u32[]{:S(2)}) copy-start(bf16[4,112,576]{2,1,0:T(8,128)(2,1)S(1)} %all-to-all-done.refs_13_) | copy-start | bytes 1548292
  56.0 7.6 %copy-start.25 = (bf16[256,768]{1,0:T(8,128)(2,1)}, bf16[256,768]{1,0:T(8,128)(2,1)S(1)}, u32[]{:S(2)}) copy-start(bf16[256,768]{1,0:T(8,128)(2,1)S(1)} %collective-permute-done.5.refs_11_) | copy-start | bytes 1179652
  56.0 5.5 %copy-start.26 = (bf16[256,768]{1,0:T(8,128)(2,1)}, bf16[256,768]{1,0:T(8,128)(2,1)S(1)}, u32[]{:S(2)}) copy-start(bf16[256,768]{1,0:T(8,128)(2,1)S(1)} %collective-permute-done.6.refs_12_) | copy-start | bytes 1179652
  56.0 7.8 %collective-permute-start.7 = (bf16[4,112,576]{2,1,0:T(8,128)(2,1)S(1)}, bf16[4,112,576]{2,1,0:T(8,128)(2,1)}, u32[]{:S(2)}, u32[]{:S(2)}) collective-permute-start(bf16[4,112,576]{2,1,0:T(8,128)(2,1)S(1)} %all-to-all-done.refs_13_), channel_id=1, source_target_pairs={{0,4},{4,0},{8,12},{12,8},{16,20},{20,16},{24,28},{28,24},{1,5},{5... | collective-permute-start | bytes 1548296 | tf_op jit(solution)/shard_map/ppermute | solution.py:438
  63.7 18.9 %copy-start = (bf16[3,240,768]{2,1,0:T(8,128)(2,1)}, bf16[3,240,768]{2,1,0:T(8,128)(2,1)S(1)}, u32[]{:S(2)}) copy-start(bf16[3,240,768]{2,1,0:T(8,128)(2,1)S(1)} %broadcast_select_fusion.refs_6_.refs_8_) | copy-start | bytes 3317764
  63.7 44.8 %collective-permute-start.12 = (bf16[3,240,768]{2,1,0:T(8,128)(2,1)S(1)}, bf16[3,240,768]{2,1,0:T(8,128)(2,1)S(1)}, u32[]{:S(2)}, u32[]{:S(2)}) collective-permute-start(bf16[3,240,768]{2,1,0:T(8,128)(2,1)S(1)} %broadcast_select_fusion.refs_6_.refs_8_), channel_id=1, source_target_pairs={{0,24},{4,28},{8,16},{12,20},{16,8},{20,12},{24,0},{28,4},{1,25},{... | collective-permute-start | bytes 3317768 | tf_op jit(solution)/shard_map/ppermute | solution.py:438
  66.2 48.3 %collective-permute-start.11 = (bf16[3,240,768]{2,1,0:T(8,128)(2,1)S(1)}, bf16[3,240,768]{2,1,0:T(8,128)(2,1)S(1)}, u32[]{:S(2)}, u32[]{:S(2)}) collective-permute-start(bf16[3,240,768]{2,1,0:T(8,128)(2,1)S(1)} %broadcast_select_fusion.refs_6_.refs_8_), channel_id=1, source_target_pairs={{0,16},{4,20},{8,24},{12,28},{16,0},{20,4},{24,8},{28,12},{1,17},{... | collective-permute-start | bytes 3317768 | tf_op jit(solution)/shard_map/ppermute | solution.py:438
  66.7 48.0 %collective-permute-start.10 = (bf16[3,240,768]{2,1,0:T(8,128)(2,1)S(1)}, bf16[3,240,768]{2,1,0:T(8,128)(2,1)}, u32[]{:S(2)}, u32[]{:S(2)}) collective-permute-start(bf16[3,240,768]{2,1,0:T(8,128)(2,1)S(1)} %broadcast_select_fusion.refs_6_.refs_8_), channel_id=1, source_target_pairs={{0,8},{4,12},{8,0},{12,4},{16,24},{20,28},{24,16},{28,20},{1,9},{5... | collective-permute-start | bytes 3317768 | tf_op jit(solution)/shard_map/ppermute | solution.py:438
  82.6 3.4 %collective-permute-start.9 = (bf16[4,384,256]{2,1,0:T(8,128)(2,1)}, bf16[4,384,256]{2,1,0:T(8,128)(2,1)S(1)}, u32[]{:S(2)}, u32[]{:S(2)}) collective-permute-start(bf16[4,384,256]{2,1,0:T(8,128)(2,1)} %get-tuple-element.106.refs_4_.refs_8_), channel_id=1, source_target_pairs={{0,4},{8,12},{16,20},{24,28},{1,5},{9,13},{17,21},{25,29},{2,6},{1... | collective-permute-start | bytes 2359304 | tf_op jit(solution)/shard_map/ppermute | solution.py:1298
  83.9 3.4 %collective-permute-start.8 = (bf16[4,384,256]{2,1,0:T(8,128)(2,1)}, bf16[4,384,256]{2,1,0:T(8,128)(2,1)S(1)}, u32[]{:S(2)}, u32[]{:S(2)}) collective-permute-start(bf16[4,384,256]{2,1,0:T(8,128)(2,1)} %get-tuple-element.105.refs_3_.refs_7_), channel_id=1, source_target_pairs={{0,4},{8,12},{16,20},{24,28},{1,5},{9,13},{17,21},{25,29},{2,6},{1... | collective-permute-start | bytes 2359304 | tf_op jit(solution)/shard_map/ppermute | solution.py:1298
  108.5 11.8 %copy-start.1 = (bf16[3,240,768]{2,1,0:T(8,128)(2,1)}, bf16[3,240,768]{2,1,0:T(8,128)(2,1)S(1)}, u32[]{:S(2)}) copy-start(bf16[3,240,768]{2,1,0:T(8,128)(2,1)S(1)} %collective-permute-done.12.refs_9_.refs_11_) | copy-start | bytes 3317764
  114.5 5.8 %copy-start.2 = (bf16[3,240,768]{2,1,0:T(8,128)(2,1)}, bf16[3,240,768]{2,1,0:T(8,128)(2,1)S(1)}, u32[]{:S(2)}) copy-start(bf16[3,240,768]{2,1,0:T(8,128)(2,1)S(1)} %collective-permute-done.11.refs_8_.refs_10_) | copy-start | bytes 3317764
  114.7 5.6 %copy-start.8 = (bf16[1,2,256,768]{3,2,1,0:T(8,128)(2,1)S(1)}, bf16[1,2,256,768]{3,2,1,0:T(8,128)(2,1)}, u32[]{:S(2)}) copy-start(bf16[1,2,256,768]{3,2,1,0:T(8,128)(2,1)} %param.13) | copy-start | bytes 2359300
  114.7 17.0 %all-to-all-start.1 = ((bf16[8,192,256]{2,1,0:T(8,128)(2,1)}), bf16[8,192,256]{2,1,0:T(8,128)(2,1)}, u32[]{:S(2)}, u32[]{:S(2)}) async-start(bf16[8,192,256]{2,1,0:T(8,128)(2,1)} %get-tuple-element.109), calls=%async_computation.1 | async-start | bytes 1572864 | tf_op jit(solution)/shard_map/all_to_all | solution.py:1200
  119.1 123.2 %reduce-scatter.6.cloned.1.call-start = ((), (), s32[]{:S(2)}) async-start(), calls=%async_computation.8 | async-start | bytes 2949120 | tf_op jit(solution)/shard_map/reduce_scatter | solution.py:1309
  122.1 16.6 %collective-permute-start.14 = (bf16[512,768]{1,0:T(8,128)(2,1)S(1)}, bf16[512,768]{1,0:T(8,128)(2,1)S(1)}, u32[]{:S(2)}, u32[]{:S(2)}) collective-permute-start(bf16[512,768]{1,0:T(8,128)(2,1)S(1)} %bitcast.77), channel_id=1, source_target_pairs={{0,4},{4,0},{8,12},{12,8},{16,20},{20,16},{24,28},{28,24},{1,5},{5... | collective-permute-start | bytes 2359304 | tf_op jit(solution)/shard_map/ppermute | solution.py:438
  138.0 2.6 collective-permute-start.13
  138.7 1.9 copy-start.16
  167.7 2.3 collective-permute-start.15
  168.0 3.2 collective-permute-start.16
  180.2 16.1 %all-to-all-start.2 = ((bf16[8,192,256]{2,1,0:T(8,128)(2,1)}), bf16[8,192,256]{2,1,0:T(8,128)(2,1)S(1)}, u32[]{:S(2)}, u32[]{:S(2)}) async-start(bf16[8,192,256]{2,1,0:T(8,128)(2,1)} %get-tuple-element.126), calls=%async_computation.2 | async-start | bytes 1572864 | tf_op jit(solution)/shard_map/all_to_all | solution.py:1200
  197.2 43.4 %all-to-all-start.3 = ((bf16[4,4,144,768]{3,2,1,0:T(8,128)(2,1)}), bf16[4,4,144,768]{3,2,1,0:T(8,128)(2,1)S(1)}, u32[]{:S(2)}, u32[]{:S(2)}) async-start(bf16[4,4,144,768]{3,2,1,0:T(8,128)(2,1)} %shard_map.218), calls=%async_computation.3 | async-start | bytes 7077888 | tf_op jit(solution)/shard_map/all_to_all | solution.py:1205
  200.9 84.7 %reduce-scatter.10.cloned.1.call-start = ((), (), s32[]{:S(2)}) async-start(), calls=%async_computation.11 | async-start | bytes 1382400
  201.0 29.8 %copy-start.31 = (f32[1,1536]{1,0:T(1,128)S(1)}, f32[1,1536]{1,0:T(1,128)}, u32[]{:S(2)}) copy-start(f32[1,1536]{1,0:T(1,128)} %get-tuple-element.147) | copy-start | bytes 18436
  227.9 14.3 %collective-permute-start.17 = (bf16[4,384,256]{2,1,0:T(8,128)(2,1)}, bf16[4,384,256]{2,1,0:T(8,128)(2,1)}, u32[]{:S(2)}, u32[]{:S(2)}) collective-permute-start(bf16[4,384,256]{2,1,0:T(8,128)(2,1)} %get-tuple-element.131), channel_id=1, source_target_pairs={{4,0},{12,8},{20,16},{28,24},{5,1},{13,9},{21,17},{29,25},{6,2},{1... | collective-permute-start | bytes 2359304 | tf_op jit(solution)/shard_map/ppermute | solution.py:1321
  229.2 13.0 %collective-permute-start.18 = (bf16[4,384,256]{2,1,0:T(8,128)(2,1)}, bf16[4,384,256]{2,1,0:T(8,128)(2,1)}, u32[]{:S(2)}, u32[]{:S(2)}) collective-permute-start(bf16[4,384,256]{2,1,0:T(8,128)(2,1)} %get-tuple-element.132), channel_id=1, source_target_pairs={{4,0},{12,8},{20,16},{28,24},{5,1},{13,9},{21,17},{29,25},{6,2},{1... | collective-permute-start | bytes 2359304 | tf_op jit(solution)/shard_map/ppermute | solution.py:1321
  242.2 14.7 %copy-start.32 = (bf16[3072]{0:T(1024)(128)(2,1)S(1)}, bf16[3072]{0:T(1024)(128)(2,1)}, u32[]{:S(2)}) copy-start(bf16[3072]{0:T(1024)(128)(2,1)} %select_n.186) | copy-start | bytes 18436
  242.3 14.7 %copy-start.33 = (bf16[2304]{0:T(1024)(128)(2,1)S(1)}, bf16[2304]{0:T(1024)(128)(2,1)}, u32[]{:S(2)}) copy-start(bf16[2304]{0:T(1024)(128)(2,1)} %reshape.360) | copy-start | bytes 13828
  257.0 21.8 %copy-start.4 = (f32[4,256,768]{2,1,0:T(8,128)S(1)}, f32[4,256,768]{2,1,0:T(8,128)}, u32[]{:S(2)}) copy-start(f32[4,256,768]{2,1,0:T(8,128)} %get-tuple-element.143) | copy-start | bytes 9437188
  259.5 51.8 %reduce-scatter.8.cloned.1.call-start = ((), (), s32[]{:S(2)}) async-start(), calls=%async_computation.9 | async-start | bytes 1105920 | tf_op jit(solution)/shard_map/reduce_scatter | solution.py:1326
  259.6 17.9 %collective-permute-start.19 = (bf16[2,256,768]{2,1,0:T(8,128)(2,1)}, bf16[2,256,768]{2,1,0:T(8,128)(2,1)}, u32[]{:S(2)}, u32[]{:S(2)}) collective-permute-start(bf16[2,256,768]{2,1,0:T(8,128)(2,1)} %get-tuple-element.144), channel_id=1, source_target_pairs={{0,8},{4,12},{8,0},{12,4},{16,24},{20,28},{24,16},{28,20},{1,9},{5... | collective-permute-start | bytes 2359304 | tf_op jit(solution)/shard_map/ppermute | solution.py:438
  260.1 18.7 %collective-permute-start.21 = (bf16[2,256,768]{2,1,0:T(8,128)(2,1)}, bf16[2,256,768]{2,1,0:T(8,128)(2,1)}, u32[]{:S(2)}, u32[]{:S(2)}) collective-permute-start(bf16[2,256,768]{2,1,0:T(8,128)(2,1)} %get-tuple-element.145), channel_id=1, source_target_pairs={{0,16},{4,20},{8,24},{12,28},{16,0},{20,4},{24,8},{28,12},{1,17},{... | collective-permute-start | bytes 2359304 | tf_op jit(solution)/shard_map/ppermute | solution.py:438
  280.9 9.2 %collective-permute-start.22 = (bf16[256,768]{1,0:T(8,128)(2,1)}, bf16[256,768]{1,0:T(8,128)(2,1)S(1)}, u32[]{:S(2)}, u32[]{:S(2)}) collective-permute-start(bf16[256,768]{1,0:T(8,128)(2,1)} %get-tuple-element.175), channel_id=1, source_target_pairs={{0,8},{4,12},{8,0},{12,4},{16,24},{20,28},{24,16},{28,20},{1,9},{5... | collective-permute-start | bytes 1179656 | tf_op jit(solution)/shard_map/ppermute | solution.py:438
  281.4 9.5 %collective-permute-start.20 = (bf16[256,768]{1,0:T(8,128)(2,1)}, bf16[256,768]{1,0:T(8,128)(2,1)}, u32[]{:S(2)}, u32[]{:S(2)}) collective-permute-start(bf16[256,768]{1,0:T(8,128)(2,1)} %get-tuple-element.176), channel_id=1, source_target_pairs={{0,16},{4,20},{8,24},{12,28},{16,0},{20,4},{24,8},{28,12},{1,17},{... | collective-permute-start | bytes 1179656 | tf_op jit(solution)/shard_map/ppermute | solution.py:438
  293.4 3.6 %copy-start.18 = (bf16[384,768]{1,0:T(8,128)(2,1)S(1)}, bf16[384,768]{1,0:T(8,128)(2,1)}, u32[]{:S(2)}) copy-start(bf16[384,768]{1,0:T(8,128)(2,1)} %reduce-scatter.6.cloned.1.call-done) | copy-start | bytes 1769476
  293.4 7.8 %collective-permute-start.23 = (bf16[256,768]{1,0:T(8,128)(2,1)S(1)}, bf16[256,768]{1,0:T(8,128)(2,1)S(1)}, u32[]{:S(2)}, u32[]{:S(2)}) collective-permute-start(bf16[256,768]{1,0:T(8,128)(2,1)S(1)} %get-tuple-element.173), channel_id=1, source_target_pairs={{0,4},{4,0},{8,12},{12,8},{16,20},{20,16},{24,28},{28,24},{1,5},{5... | collective-permute-start | bytes 1179656 | tf_op jit(solution)/shard_map/ppermute | solution.py:438
  293.4 20.2 %all-to-all-start.4 = ((bf16[8,48,640]{2,1,0:T(8,128)(2,1)}), bf16[8,48,640]{2,1,0:T(8,128)(2,1)S(1)}, u32[]{:S(2)}, u32[]{:S(2)}) async-start(bf16[8,48,640]{2,1,0:T(8,128)(2,1)} %pad_maximum_fusion.2), calls=%async_computation.5 | async-start | bytes 983040 | tf_op jit(solution)/shard_map/all_to_all | solution.py:1200
  297.7 15.9 %collective-permute-start.26 = (bf16[96,768]{1,0:T(8,128)(2,1)S(1)}, bf16[96,768]{1,0:T(8,128)(2,1)S(1)}, u32[]{:S(2)}, u32[]{:S(2)}) collective-permute-start(bf16[96,768]{1,0:T(8,128)(2,1)S(1)} %get-tuple-element.182), channel_id=1, source_target_pairs={{0,24},{4,28},{8,16},{12,20},{16,8},{20,12},{24,0},{28,4},{1,25},{... | collective-permute-start | bytes 442376 | tf_op jit(solution)/shard_map/ppermute | solution.py:438
  300.6 13.0 %collective-permute-start.25 = (bf16[96,768]{1,0:T(8,128)(2,1)S(1)}, bf16[96,768]{1,0:T(8,128)(2,1)S(1)}, u32[]{:S(2)}, u32[]{:S(2)}) collective-permute-start(bf16[96,768]{1,0:T(8,128)(2,1)S(1)} %get-tuple-element.183), channel_id=1, source_target_pairs={{0,16},{4,20},{8,24},{12,28},{16,0},{20,4},{24,8},{28,12},{1,17},{... | collective-permute-start | bytes 442376 | tf_op jit(solution)/shard_map/ppermute | solution.py:438
  301.1 12.5 %collective-permute-start.24 = (bf16[96,768]{1,0:T(8,128)(2,1)S(1)}, bf16[96,768]{1,0:T(8,128)(2,1)S(1)}, u32[]{:S(2)}, u32[]{:S(2)}) collective-permute-start(bf16[96,768]{1,0:T(8,128)(2,1)S(1)} %get-tuple-element.184), channel_id=1, source_target_pairs={{0,8},{4,12},{8,0},{12,4},{16,24},{20,28},{24,16},{28,20},{1,9},{5... | collective-permute-start | bytes 442376 | tf_op jit(solution)/shard_map/ppermute | solution.py:438
  312.2 1.4 collective-permute-start.27
  (16 other events, 15.4 us)
Sparse Core Ops, SparseCore 0:
  11.0 50.4 all-gather.2
  166.8 45.2 reduce-scatter.5
  259.7 25.9 reduce-scatter.9
  287.8 23.4 reduce-scatter.7

commit v4 on v3

--- a/solution.py
+++ b/solution.py
@@ -598,29 +598,46 @@
     s = mm(keys, stacked)
     if plain:
         return s
-    place = base + lax.broadcasted_iota(jnp.int32, (CHUNK, LANES), 0)
+    place = base + lax.broadcasted_iota(jnp.int32, s.shape, 0)
     return jnp.where((place >= low) & (place < high), s, LOWEST)
 
 
-def each_tile(meta, p, lims, tile):
+def head_lanes(v, g):
+    return None if v is None else v[:, g * CHUNK : (g + 1) * CHUNK]
+
+
+def each_tile(meta, p, lims, tile, halves):
     r, c = meta[0], meta[1]
 
-    @pl.loop(meta[4 + p], p + c + 1)
+    @pl.loop(meta[4 + p], p + 1)
     def _(k):
-        own = k == p + c
-        source = jnp.where(own, 0, c)
+        own = (k == p) & (c == 0)
         slot = jnp.where(own, p ^ r, k ^ r ^ c)
-        base = jnp.where(own, p, k) * CHUNK
-        whole = (k < p) & (meta[12 + p] <= base)
+        whole = (k < p) & (meta[12 + p] <= k * CHUNK)
 
         @pl.when(whole)
         def _():
-            tile(source, slot, own, base, None, None, True)
+            tile(slot, own, k * CHUNK, None, None, True)
 
         @pl.when(jnp.logical_not(whole))
         def _():
-            low, high, nlow, nhigh = lims
-            tile(source, slot, own, base, jnp.where(own, nlow, low), jnp.where(own, nhigh, high), False)
+            tile(slot, own, k * CHUNK, lims[0], lims[1], False)
+
+    @pl.when(c != 0)
+    def _():
+        halves(p ^ r, p * CHUNK, lims[2], lims[3])
+
+
+HALF_CHUNK = CHUNK // 2
+
+
+def half_lanes(v, half):
+    return jnp.concatenate([v[:, half_span(g, half)] for g in range(GROUP)], axis=1)
+
+
+def half_span(g, half):
+    first = g * CHUNK + half * HALF_CHUNK
+    return slice(first, first + HALF_CHUNK)
 
 
 def stack_heads(q, stacked):
@@ -641,7 +658,7 @@
         for own in range(2):
             kr[own, s] = flip(kv[own, s, :WIDE])
 
-    r = meta[0]
+    r, c = meta[0], meta[1]
 
     @pl.loop(0, 8)
     def _(p):
@@ -649,24 +666,48 @@
         stack_heads(qs[s] * 0.125, stacked)
         lims = [thrice(bounds[p, i : i + 1]) for i in range(4)]
 
-        def tile(source, slot, own, base, lo, hi, plain):
-            masked = scores_of(kr[source, slot], stacked[...], base, lo, hi, plain)
-            m_old = m_s[...]
-            m_new = jnp.maximum(m_old, jnp.max(masked, axis=0, keepdims=True))
-            e = jnp.exp(masked - m_new)
-            f = jnp.exp(m_old - m_new)
-            m_s[...] = m_new
-            l_s[...] = l_s[...] * f + jnp.sum(e, axis=0, keepdims=True)
-            e = e.astype(BF)
+        def tile(slot, own, base, lo, hi, plain):
+            keys = kr[c, slot]
+            scores = [
+                scores_of(keys, head_lanes(stacked, g), base, head_lanes(lo, g), head_lanes(hi, g), plain)
+                for g in range(GROUP)
+            ]
             for g in range(GROUP):
                 cut = slice(g * CHUNK, (g + 1) * CHUNK)
                 first = WIDE + g * HEAD_DIM
-                acc[g] = acc[g] * f[:, cut] + mm(kv[source, slot, first : first + HEAD_DIM], e[:, cut])
+                m_old = m_s[:, cut]
+                m_new = jnp.maximum(m_old, jnp.max(scores[g], axis=0, keepdims=True))
+                e = jnp.exp(scores[g] - m_new)
+                f = jnp.exp(m_old - m_new)
+                m_s[:, cut] = m_new
+                l_s[:, cut] = l_s[:, cut] * f + jnp.sum(e, axis=0, keepdims=True)
+                acc[g] = acc[g] * f + mm(kv[c, slot, first : first + HEAD_DIM], e.astype(BF))
+
+        def halves(slot, base, lo, hi):
+            for half in range(2):
+                keys = slice(half * HALF_CHUNK, (half + 1) * HALF_CHUNK)
+                masked = scores_of(
+                    kr[0, slot, keys], half_lanes(stacked[...], half), base + half * HALF_CHUNK,
+                    half_lanes(lo, half), half_lanes(hi, half), False,
+                )
+                m_old = half_lanes(m_s[...], half)
+                m_new = jnp.maximum(m_old, jnp.max(masked, axis=0, keepdims=True))
+                e = jnp.exp(masked - m_new)
+                f = jnp.exp(m_old - m_new)
+                total = half_lanes(l_s[...], half) * f + jnp.sum(e, axis=0, keepdims=True)
+                e = e.astype(BF)
+                for g in range(GROUP):
+                    cut = slice(g * HALF_CHUNK, (g + 1) * HALF_CHUNK)
+                    first = WIDE + g * HEAD_DIM
+                    m_s[:, half_span(g, half)] = m_new[:, cut]
+                    l_s[:, half_span(g, half)] = total[:, cut]
+                    new = mm(kv[0, slot, first : first + HEAD_DIM, keys], e[:, cut])
+                    acc[g, :, keys] = acc[g, :, keys] * f[:, cut] + new
 
         m_s[...] = jnp.full_like(m_s, LOWEST)
         l_s[...] = jnp.zeros_like(l_s)
         acc[...] = jnp.zeros_like(acc)
-        each_tile(meta, p, lims, tile)
+        each_tile(meta, p, lims, tile, halves)
         total = l_s[...]
         inv = 1.0 / total
         out = jnp.concatenate(
@@ -700,22 +741,30 @@
     )
 
 
+def rows_body(load, *refs):
+    kv, (k_rows, v_rows) = refs[:4], refs[4:]
+    load([])
+    for i in range(4):
+
+        @pl.loop(0, 4)
+        def _(s):
+            k_rows[i // 2, i % 2 * 4 + s] = flip(kv[i][s, :WIDE])
+            v_rows[i // 2, i % 2 * 4 + s] = flip(kv[i][s, WIDE:])
+
+
+def rows_of_heads(heads):
+    return call(rows_body, [((2, 8, CHUNK, WIDE), BF)] * 2, "VVVV", heads[1:], flops=1)
+
+
 def attend_back_body(load, meta, bounds, cos, sin, o_ref, ml_ref, *refs):
-    heads, gs = refs[:5], refs[5]
+    heads, k_rows, v_rows, gs = refs[:5], refs[5], refs[6], refs[7]
     (
         pq_ref, own_ref, far_a, far_b,
         qs, kv, kr, vr, st_q, st_g, row_q, row_g, dk, dv, dq,
-    ) = refs[6:]
+    ) = refs[8:]
     for ref in (st_q, st_g, dk, dv):
         ref[...] = jnp.zeros_like(ref)
-    load(head_pairs(heads, qs, kv))
-
-    @pl.loop(0, 8)
-    def _(s):
-        for own in range(2):
-            kr[own, s] = flip(kv[own, s, :WIDE])
-            vr[own, s] = flip(kv[own, s, WIDE:])
-
+    load(head_pairs(heads, qs, kv) + [(k_rows, kr), (v_rows, vr)])
     r, c = meta[0], meta[1]
     lane = lax.broadcasted_iota(jnp.int32, (CHUNK, WIDE), 1) // HEAD_DIM
 
@@ -745,18 +794,36 @@
         lims = [thrice(bounds[p, i : i + 1]) for i in range(4)]
         dq[...] = jnp.zeros_like(dq)
 
-        def tile(source, slot, own, base, lo, hi, plain):
-            e = jnp.exp(scores_of(kr[source, slot], st_q[...], base, lo, hi, plain) - top)
-            d = (e * (mm(vr[source, slot], st_g[...]) - fix)).astype(BF)
+        def tile(slot, own, base, lo, hi, plain):
+            e = jnp.exp(scores_of(kr[c, slot], st_q[...], base, lo, hi, plain) - top)
+            d = (e * (mm(vr[c, slot], st_g[...]) - fix)).astype(BF)
             e = e.astype(BF)
             kind = jnp.where(own, 0, 1)
             dv[kind, slot] += mm(e, row_g[...])
             dk[kind, slot] += mm(d, row_q[...])
             for g in range(GROUP):
                 part = slice(g * HEAD_DIM, (g + 1) * HEAD_DIM)
-                dq[part] += mm(kv[source, slot, part], d[:, g * CHUNK : (g + 1) * CHUNK])
-
-        each_tile(meta, p, lims, tile)
+                dq[part] += mm(kv[c, slot, part], d[:, g * CHUNK : (g + 1) * CHUNK])
+
+        def halves(slot, base, lo, hi):
+            for half in range(2):
+                keys = slice(half * HALF_CHUNK, (half + 1) * HALF_CHUNK)
+                s_half = scores_of(
+                    kr[0, slot, keys], half_lanes(st_q[...], half), base + half * HALF_CHUNK,
+                    half_lanes(lo, half), half_lanes(hi, half), False,
+                )
+                e = jnp.exp(s_half - half_lanes(top, half))
+                d = e * (mm(vr[0, slot, keys], half_lanes(st_g[...], half)) - half_lanes(fix, half))
+                e, d = e.astype(BF), d.astype(BF)
+                rows_of = [jnp.concatenate([ref[half_span(g, half)] for g in range(GROUP)]) for ref in (row_g, row_q)]
+                dv[0, slot, keys] += mm(e, rows_of[0])
+                dk[0, slot, keys] += mm(d, rows_of[1])
+                for g in range(GROUP):
+                    part = slice(g * HEAD_DIM, (g + 1) * HEAD_DIM)
+                    cut = slice(g * HALF_CHUNK, (g + 1) * HALF_CHUNK)
+                    dq[part, keys] += mm(kv[0, slot, part, keys], d[:, cut])
+
+        each_tile(meta, p, lims, tile, halves)
         pq_ref[s] = turn_heads(dq[...] * 0.125, cos[s], -sin[s]).astype(BF)
 
     both = 1.0 - c.astype(F32)
@@ -771,18 +838,18 @@
                 far_ref[s % 4, :WIDE] = far_k.astype(BF)
                 far_ref[s % 4, WIDE:] = far_v.astype(BF)
 
-        own_ref[s, :WIDE] = jnp.transpose(dk[0, s]) + both * far_k
-        own_ref[s, WIDE:] = jnp.transpose(dv[0, s]) + both * far_v
-
-
-def attend_back(meta, bounds, cos, sin, attended, stats, heads, grads):
+        own_ref[s, :WIDE] = (jnp.transpose(dk[0, s]) + both * far_k).astype(BF)
+        own_ref[s, WIDE:] = (jnp.transpose(dv[0, s]) + both * far_v).astype(BF)
+
+
+def attend_back(meta, bounds, cos, sin, attended, stats, heads, rows_first, grads):
     rows = pltpu.VMEM((2, 8, CHUNK, WIDE), BF)
     sums = pltpu.VMEM((2, 8, CHUNK, WIDE), F32)
     return call(
         attend_back_body,
-        [((8, WIDE, CHUNK), BF), ((8, 2 * WIDE, CHUNK), F32)] + [((4, 2 * WIDE, CHUNK), BF)] * 2,
-        "SVVVVV" + "A" * 5 + "V",
-        (meta, bounds, cos, sin, attended, stats, *heads, grads),
+        [((8, WIDE, CHUNK), BF), ((8, 2 * WIDE, CHUNK), BF)] + [((4, 2 * WIDE, CHUNK), BF)] * 2,
+        "SVVVVV" + "A" * 7 + "V",
+        (meta, bounds, cos, sin, attended, stats, *heads, *rows_first, grads),
         scratch=HEAD_SCRATCH
         + [
             rows,
@@ -911,7 +978,7 @@
         for b in range(16):
             first = 192 * (b // 4) + 24 * (b % 4)
             block = jnp.concatenate([gu[first : first + 24], gu[first + 96 : first + 120]])
-            u_ref[b // 4, b % 4, line, side] = block.astype(BF)
+            u_ref[(b // 4) ^ h, b % 4, line, side] = block.astype(BF)
 
 
 def feed_rows(meta, bias, args):
@@ -1005,18 +1072,25 @@
             ref[zz, 48 * h : 48 * (h + 1)] = pair.astype(BF)
 
 
-def out_grad_body(load, att_ref, mg_ref, up, o_ref):
-    load([(up.at[h], o_ref.at[h, :, pl.ds(0, 96)]) for h in range(4)])
+def out_grad_body(load, meta, att_ref, mg_ref, up, *o_refs):
+    load([(up.at[k], o_refs[k].at[:, pl.ds(0, 96)]) for k in range(4)])
     grad = mm(att_ref[0], mg_ref[0]) + mm(att_ref[1], mg_ref[1])
-    for b in range(16):
-        first = 192 * (b // 4) + 24 * (b % 4)
-        pair = jnp.concatenate([grad[first : first + 24], grad[first + 96 : first + 120]])
-        o_ref[b // 4, b % 4, 96:] = pair.astype(BF)
+    for owner in range(4):
+        blocks = []
+        for b in range(4):
+            first = 192 * owner + 24 * b
+            blocks.append(jnp.concatenate([grad[first : first + 24], grad[first + 96 : first + 120]]).astype(BF))
+        for k in range(4):
+
+            @pl.when((owner ^ meta[2]) == k)
+            def _():
+                for b in range(4):
+                    o_refs[k][b, 96:] = blocks[b]
 
 
 def project_back_body(
-    own, f0, f1, pq, n_ref, mk_ref, cos, sin, w_ref,
-    away_x, away_y, stay, gq_ref, gs_ref, wp, acc,
+    own, f0, f1, pq, n_ref, mk_ref, cos, sin, w_ref, flat,
+    away_x, away_y, stay, gq_ref, wp, acc, gs_ref, sums,
 ):
     i = pl.program_id(0)
 
@@ -1029,7 +1103,7 @@
 
     early = (i == 0) | (i == 4) | (i == 6) | (i == 7)
     far = jnp.where(early, f0[0], f1[0])
-    kv = own[0] + far.astype(F32)
+    kv = own[0].astype(F32) + far.astype(F32)
     parts = [
         pq[0],
         turn_heads(kv[:WIDE], cos[0], -sin[0]).astype(BF),
@@ -1060,6 +1134,17 @@
     @pl.when(i == 7)
     def _():
         by_z(jnp.transpose(acc[...]), gq_ref)
+        part = sums.shape[1]
+        sums[...] = flat[...]
+        for k in range(2):
+            for side in range(2):
+                to = 14 + 2 * k + side
+                sums[to : to + 1] = gs_ref[k : k + 1, side * part : (side + 1) * part]
+        tail = sums[...].astype(BF)
+        rows = gq_ref.shape[1] - 24
+        for zz in range(4):
+            gq_ref[zz, rows:] = jnp.zeros((24, gq_ref.shape[2]), BF)
+            gq_ref[zz, rows:, :part] = tail
 
 
 def pick(order):
@@ -1072,7 +1157,7 @@
     return slot_of
 
 
-def project_back(own, far, pq, n, mk, cos, sin, w):
+def project_back(own, far, pq, n, mk, cos, sin, w, flat):
     dim = n.shape[2]
     wide = w.shape[1] + HEAD_DIM
     slot = pick((2, 6, 5, 7, 0, 4, 1, 3))
@@ -1090,29 +1175,32 @@
             jax.ShapeDtypeStruct((2, CHUNK, dim), BF),
             jax.ShapeDtypeStruct((2, CHUNK, dim), BF),
             jax.ShapeDtypeStruct((4, CHUNK, dim), F32),
-            jax.ShapeDtypeStruct((4, dim // 4, wide), BF),
-            jax.ShapeDtypeStruct((8, dim), F32),
+            jax.ShapeDtypeStruct((4, dim // 4 + 24, wide), BF),
         ),
         in_specs=[
             block(2 * WIDE, CHUNK, slot),
             *[block(2 * WIDE, CHUNK, lambda i: slot(i) % 4)] * 2,
             block(WIDE, CHUNK, slot),
             block(CHUNK, dim, slot), block(CHUNK, 128, slot),
-            block(HALF, CHUNK, slot), block(HALF, CHUNK, slot), whole(*w.shape),
+            block(HALF, CHUNK, slot), block(HALF, CHUNK, slot), whole(*w.shape), whole(*flat.shape),
         ],
         out_specs=(
             block(CHUNK, dim, lambda i: jnp.minimum(i, 1)),
             block(CHUNK, dim, lambda i: jnp.clip(i - 2, 0, 1)),
             block(CHUNK, dim, lambda i: jnp.clip(i - 4, 0, 3)),
-            whole(4, dim // 4, wide),
-            whole(8, dim),
+            whole(4, dim // 4 + 24, wide),
         ),
-        scratch_shapes=[pltpu.VMEM((3, dim, WIDE), BF), pltpu.VMEM((wide, dim), F32)],
+        scratch_shapes=[
+            pltpu.VMEM((3, dim, WIDE), BF),
+            pltpu.VMEM((wide, dim), F32),
+            pltpu.VMEM((8, dim), F32),
+            pltpu.VMEM(flat.shape, F32),
+        ],
         compiler_params=pltpu.CompilerParams(vmem_limit_bytes=56 * 2**20),
         cost_estimate=pl.CostEstimate(
             flops=1 + 4 * 8 * CHUNK * dim * 3 * WIDE // COST, bytes_accessed=1, transcendentals=0
         ),
-    )(own, *far, pq, n, mk, cos, sin, w)
+    )(own, *far, pq, n, mk, cos, sin, w, flat)
 
 
 def last_body(load, meta, gain, embed, x_ref, mg_ref, keep_ref, far_ref, o_ref):
@@ -1299,9 +1387,10 @@
     send, attended, stats = attend_rows(meta, bounds, heads)
     send, *shares = lax.optimization_barrier((send, *shares))
     grad_far = swap(after(grad_rows, kv[0]), 1)
-    middle, normed, att, w_out_all = middle_rows(
-        meta, gain_b, embed, marked, exchange(send), w_out, shares
-    )
+    heads_late = lax.optimization_barrier((*heads, send))[:5]
+    rows_first = rows_of_heads(heads_late)
+    got, *rows_first = lax.optimization_barrier((exchange(send), *rows_first))
+    middle, normed, att, w_out_all = middle_rows(meta, gain_b, embed, marked, got, w_out, shares)
     out_own, out_far, ng_far, ng_own, gbu, gd, gu = feed_rows(
         meta, bias, (normed, swap(normed, 1), grad_rows, grad_far, w_up, w_down, *shares)
     )
@@ -1312,36 +1401,34 @@
         meta, gain_b, b_down_all, (middle, ng_own, out_own, out_far, ng_far, grads, marked, w_out_all)
     )
     got = exchange(send)
-    (up_out,) = call(
-        out_grad_body, [((4, 4, part // 4 + dim // 16, dim), BF)], "VVA", (att, mid_grad, gu), flops=4 * CHUNK * dim * dim
-    )
-    got, up_out = lax.optimization_barrier((got, up_out))
-    up_out = exchange_chips(up_out)
-    pq, own_kv, *far_kv = attend_back(meta, bounds, cos, sin, attended, stats, heads, got)
+    up_out = call(
+        out_grad_body,
+        [((4, part // 4 + dim // 16, dim), BF)] * 4,
+        "SVVA",
+        (meta, att, mid_grad, gu),
+        flops=4 * CHUNK * dim * dim,
+    )
+    gbu = gbu.reshape(4, 1, part)
+    gbu = jnp.where(clean, jnp.concatenate([gbu, 0 * gbu], 1), jnp.concatenate([0 * gbu, gbu], 1))
+    flat = jnp.concatenate([gbu.reshape(8, part), sums[:3].reshape(6, part), jnp.zeros((10, part), F32)])
+    got, flat, *up_out = lax.optimization_barrier((got, flat, *up_out))
+    up_out = [up_out[0]] + [swap(up_out[k], 2 * k) for k in range(1, 4)]
+    pq, own_kv, *far_kv = attend_back(meta, bounds, cos, sin, attended, stats, heads, rows_first, got)
     far_kv = [lax.ppermute(v, "ctx", [(b, a) for a, b in give]) for v in far_kv]
 
-    up_out = jnp.sum(after(up_out, pq).astype(F32), axis=0).astype(BF).reshape(-1, dim)
+    *up_out, _ = lax.optimization_barrier((*up_out, pq))
+    up_out = (add(up_out[0], up_out[1]) + add(up_out[2], up_out[3])).astype(BF).reshape(-1, dim)
     gd = after(gd, pq).reshape(4, part // 4, dim)
     *far_kv, up_out, gd = lax.optimization_barrier((*far_kv, up_out, gd))
     up_out = lax.psum_scatter(up_out, "fsdp", scatter_dimension=0, tiled=True)
 
-    away_x, away_y, stay, gq, vec = project_back(
-        own_kv, far_kv, pq, normed_one, marks, cos, sin, w_all
+    away_x, away_y, stay, gq = project_back(
+        own_kv, far_kv, pq, normed_one, marks, cos, sin, w_all, flat
     )
     in_x, in_y = swap(away_x, 2), swap(away_y, 4)
-    gbu = gbu.reshape(4, 1, part)
-    gbu = jnp.where(clean, jnp.concatenate([gbu, 0 * gbu], 1), jnp.concatenate([0 * gbu, gbu], 1))
-    flat = jnp.concatenate([gbu.reshape(-1), sums[:3].reshape(-1), vec[:2].reshape(-1)])
     wide = gq.shape[2]
-    length = flat.shape[0]
-
-    def parts_of(v):
-        v = v.reshape(length // part, part)
-        return jnp.pad(v, ((0, 24 - length // part), (0, wide - part))).astype(BF)
-
     rows = dim // 4
-    flat = jnp.broadcast_to(parts_of(flat), (4, 24, wide))
-    gq = jnp.concatenate([gq, flat], 1).reshape(-1, wide)
+    gq = gq.reshape(-1, wide)
     gq = lax.psum_scatter(gq, "fsdp", scatter_dimension=0, tiled=True)
     over_y, over_x = add(stay[1], in_x[1]).astype(BF), add(stay[3], in_y[1]).astype(BF)
     near_one, near_two = swap(over_y, 4), swap(over_x, 2)

time: 328 us -> 322 us (0.982)
  waiting for transfers between devices: 96.5 us -> 91.6 us
    ppermute x24 -> x27, waiting for transfers between devices: 37.5 us -> 56 us  [swap(): return lax.ppermute(v, 'ctx', [(i, i ^ bit) for i in range(8)])]
    all_to_all x3, waiting for transfers between devices: 16.9 us -> 8.97 us  [exchange(): return lax.all_to_all(v, 'ctx', 0, 0, tiled=True)]
    all_to_all x1 -> x0, waiting for transfers between devices: 7.83 us -> none  [exchange_chips(): return lax.all_to_all(v, 'ctx', 0, 0, axis_index_groups=groups, tiled=True)]
    ppermute x24 -> x27, starting transfers between devices: 18.4 us -> 22.7 us  [swap(): return lax.ppermute(v, 'ctx', [(i, i ^ bit) for i in range(8)])]
    all_to_all x1 -> x0, starting transfers between devices: 3.73 us -> none  [exchange_chips(): return lax.all_to_all(v, 'ctx', 0, 0, axis_index_groups=groups, tiled=True)]
    optimization_barrier x1, waiting for transfers between devices: 3.73 us -> 0.37 us  [after(): return lax.optimization_barrier((value, *needed))[0]]
    reduce_scatter x1, waiting for transfers between devices: 4.25 us -> 0.91 us  [shards_by_heads(): up_out = lax.psum_scatter(up_out, 'fsdp', scatter_dimension=0, tiled=True)]
    unnamed x88 -> x92, local copies, waits for them, and re-layouts: 8.55 us -> 11.4 us
  transfers between devices with their start and end apart: 37 -> 39, of which waited for: 20 -> 21; matrix products, arithmetic and copies ran while one was open for 8% -> 8% of each run, Pallas kernels for 26% -> 27%
where the time goes in v4:
time: 322 us; the launch traced here: 321 us
  Pallas kernels  131 us (41%)
  waiting for transfers between devices  91.6 us (28%)
  starting transfers between devices  43.8 us (14%)
  local copies, waits for them, and re-layouts  27.5 us (9%)
  between operations  14.5 us (5%)
  other arithmetic  12.4 us (4%)
    pallas_call x11, Pallas kernels, call(): pl.pallas_call(run, out_shape=tuple((jax.ShapeDtypeStruct(s, d) for s, d...  118 us
    ppermute x27, waiting for transfers between devices, swap(): return lax.ppermute(v, 'ctx', [(i, i ^ bit) for i in range(8)])  56 us
    ppermute x27, starting transfers between devices, swap(): return lax.ppermute(v, 'ctx', [(i, i ^ bit) for i in range(8)])  22.7 us
    all_to_all x1, waiting for transfers between devices, exchange_z(): return lax.all_to_all(v, 'fsdp', 0, 0, tiled=True)  19.1 us
    pallas_call x1, Pallas kernels, project_back(): pl.pallas_call(project_back_body, grid=(8,), out_shape=(jax.ShapeDtypeStr...  13.8 us
    unnamed x92, local copies, waits for them, and re-layouts  11.4 us
    all_to_all x3, starting transfers between devices, exchange(): return lax.all_to_all(v, 'ctx', 0, 0, tiled=True)  10.6 us
    all_to_all x3, waiting for transfers between devices, exchange(): return lax.all_to_all(v, 'ctx', 0, 0, tiled=True)  8.97 us
  transfers between devices with their start and end apart: 39, of which 21 were waited for; matrix products, arithmetic and copies ran while one was open for 8% of the time, Pallas kernels for 27%

profile of v4, /device:TPU:0, one launch (start us, length us, event | category | flops | bytes accessed | tf_op | source)
XLA Modules:
  0.0 321.2 jit_solution(17995301419004179689)
XLA Ops:
  7.8 3.0 shard_map.212
  11.1 3.0 collective-permute-start.1
  14.1 1.5 collective-permute-start
  16.3 1.1 collective-permute-done.2.refs_6_
  17.9 0.9 broadcast_in_dim.92
  18.8 4.9 %all-to-all-start = ((bf16[4,112,576]{2,1,0:T(8,128)(2,1)}), bf16[4,112,576]{2,1,0:T(8,128)(2,1)}, u32[]{:S(2)}, u32[]{:S(2)}) async-start(bf16[4,112,576]{2,1,0:T(8,128)(2,1)} %broadcast_in_dim.92), calls=%async_computation | async-start | bytes 1146880 | tf_op jit(solution)/shard_map/all_to_all | solution.py:1297
  26.1 1.8 multiply_sine_fusion
  27.9 6.8 %collective-permute-done.4.refs_10_ = bf16[256,768]{1,0:T(8,128)(2,1)S(1)} collective-permute-done((bf16[256,768]{1,0:T(8,128)(2,1)}, bf16[256,768]{1,0:T(8,128)(2,1)S(1)}, u32[]{:S(2)}, u32[]{:S(2)}) %collective-permute-start.4) | collective-permute-done | bytes 393248 | tf_op jit(solution)/shard_map/ppermute | solution.py:438
  35.0 1.5 collective-permute-start.5
  37.0 19.1 %all-to-all-done.refs_13_ = bf16[4,112,576]{2,1,0:T(8,128)(2,1)} async-done(((bf16[4,112,576]{2,1,0:T(8,128)(2,1)}), bf16[4,112,576]{2,1,0:T(8,128)(2,1)}, u32[]{:S(2)}, u32[]{:S(2)}) %all-to-all-start) | async-done | bytes 516128 | tf_op jit(solution)/shard_map/all_to_all | solution.py:1297
  56.2 1.0 slice.108
  57.4 4.1 %all-gather.3.cloned.1.call-done = bf16[960,768]{1,0:T(8,128)(2,1)} async-done(((bf16[240,768]{1,0:T(8,128)(2,1)}), bf16[960,768]{1,0:T(8,128)(2,1)}) %all-gather.3.cloned.1.call-update) | async-done | bytes 1474576 | tf_op jit(solution)/shard_map/all_gather | solution.py:1325
  61.5 2.0 gather_fusion
  63.7 2.4 collective-permute-start.12
  68.7 13.9 %shard_map.213 = (bf16[8,192,256]{2,1,0:T(8,128)(2,1)}, bf16[4,384,256]{2,1,0:T(8,128)(2,1)}, bf16[4,384,256]{2,1,0:T(8,128)(2,1)}, bf16[8,256,768]{2,1,0:T(8,12...) custom-call(s32[20]{0:T(128)} %concatenate.25.refs_0_, f32[1,768]{1,0:T(1,128)} %reshape.343.refs_1_, ...), custom_call_target="tpu_custom_call" | custom-call | flops 2 | bytes 1 | tf_op jit(solution)/shard_map/pallas_call | solution.py:485
  82.6 1.3 collective-permute-start.9
  84.0 1.3 collective-permute-start.8
  86.0 1.3 collective-permute-done.8.refs_5_.refs_2_.refs_9_
  87.4 0.9 copy-done.2
  88.3 16.0 %shard_map.214 = (bf16[8,192,256]{2,1,0:T(8,128)(2,1)}, f32[8,192,256]{2,1,0:T(8,128)}, f32[8,8,768]{2,1,0:T(8,128)}) custom-call(s32[20]{0:T(128)} %concatenate.25.refs_0_, s32[8,8,256]{2,1,0:T(8,128)} %pad.8.refs_1_, bf16[8,192,256]{2,1,0:T(8,128)(2,1)} %get-tuple-element.123.refs_2_.refs_6_, ...), custom_call_target="tpu_custom_call" | custom-call | flops 5 | bytes 1 | tf_op jit(solution)/shard_map/pallas_call | solution.py:485
  104.3 10.3 %collective-permute-done.11.refs_8_.refs_10_ = bf16[3,240,768]{2,1,0:T(8,128)(2,1)} collective-permute-done((bf16[3,240,768]{2,1,0:T(8,128)(2,1)S(1)}, bf16[3,240,768]{2,1,0:T(8,128)(2,1)}, u32[]{:S(2)}, u32[]{:S(2)}) %collective-permute-start.11) | collective-permute-done | bytes 1105952 | tf_op jit(solution)/shard_map/ppermute | solution.py:438
  114.7 3.5 %all-to-all-start.1 = ((bf16[8,192,256]{2,1,0:T(8,128)(2,1)}), bf16[8,192,256]{2,1,0:T(8,128)(2,1)S(1)}, u32[]{:S(2)}, u32[]{:S(2)}) async-start(bf16[8,192,256]{2,1,0:T(8,128)(2,1)} %get-tuple-element.128), calls=%async_computation.1 | async-start | bytes 1572864 | tf_op jit(solution)/shard_map/all_to_all | solution.py:1288
  118.6 1.0 pad_maximum_fusion.refs_3_.refs_9_
  120.5 6.6 %shard_map.215 = (bf16[2,8,256,192]{3,2,1,0:T(8,128)(2,1)}, bf16[2,8,256,192]{3,2,1,0:T(8,128)(2,1)}) custom-call(bf16[4,384,256]{2,1,0:T(8,128)(2,1)} %get-tuple-element.129.refs_3_.refs_0_.refs_7_, bf16[4,384,256]{2,1,0:T(8,128)(2,1)} %get-tuple-element.130.refs_4_.refs_1_.refs_8_, bf16[4,384,256]{2,1,0:T(8,128)(2,1)} %copy-done.2, ...), custom_call_target="tpu_custom_call" | custom-call | flops 1 | bytes 1 | tf_op jit(solution)/shard_map/pallas_call | solution.py:485
  127.1 3.7 %all-to-all-done.1.refs_4_ = bf16[8,192,256]{2,1,0:T(8,128)(2,1)S(1)} async-done(((bf16[8,192,256]{2,1,0:T(8,128)(2,1)}), bf16[8,192,256]{2,1,0:T(8,128)(2,1)S(1)}, u32[]{:S(2)}, u32[]{:S(2)}) %all-to-all-start.1) | async-done | bytes 786464 | tf_op jit(solution)/shard_map/all_to_all | solution.py:1288
  130.8 0.9 copy-done.6
  131.7 6.3 %shard_map.216 = (f32[2,256,768]{2,1,0:T(8,128)}, bf16[512,768]{1,0:T(8,128)(2,1)}, bf16[2,768,256]{2,1,0:T(8,128)(2,1)}, bf16[768,768]{1,0:T(8,128)(2,1)}) custom-call(s32[20]{0:T(128)} %concatenate.25.refs_0_, f32[1,768]{1,0:T(1,128)} %reshape.340.refs_1_, f32[1,768]{1,0:T(1,128)} %reshape.342.refs_2_, ...), custom_call_target="tpu_custom_call" | custom-call | flops 1 | bytes 1 | tf_op jit(solution)/shard_map/pallas_call | solution.py:485
  138.7 1.8 collective-permute-done.13.refs_3_
  140.5 0.9 copy-done.21
  141.4 25.1 %shard_map.217 = (bf16[512,768]{1,0:T(8,128)(2,1)}, bf16[512,768]{1,0:T(8,128)(2,1)}, bf16[512,768]{1,0:T(8,128)(2,1)}, bf16[512,768]{1,0:T(8,128)(2,1)}, f32[1,...) custom-call(s32[20]{0:T(128)} %concatenate.25.refs_0_, f32[1,1536]{1,0:T(1,128)} %bitcast.90, ...), custom_call_target="tpu_custom_call" | custom-call | flops 15 | bytes 1 | tf_op jit(solution)/shard_map/pallas_call | solution.py:485
  166.6 1.1 copy-done.42
  168.8 1.1 collective-permute-done.15.refs_6_
  169.9 1.1 collective-permute-done.16.refs_7_
  171.1 0.9 copy-done.19
  172.0 8.1 %shard_map.218 = (bf16[2,256,768]{2,1,0:T(8,128)(2,1)}, bf16[2,256,768]{2,1,0:T(8,128)(2,1)}, f32[8,768]{1,0:T(8,128)}, bf16[8,192,256]{2,1,0:T(8,128)(2,1)}) custom-call(s32[20]{0:T(128)} %concatenate.25.refs_0_, f32[1,768]{1,0:T(1,128)} %reshape.340.refs_1_, f32[1,768]{1,0:T(1,128)} %reshape.341.refs_2_, f32[2,256,768]{2,1,0:T(8,128)} %get-tuple-element.140.refs_3_, ...), custom_call_target="tpu_custom_call" | custom-call | flops 1 | bytes 1 | tf_op jit(solution)/shard_map/pallas_call | solution.py:485
  180.1 3.6 %all-to-all-start.2 = ((bf16[8,192,256]{2,1,0:T(8,128)(2,1)}), bf16[8,192,256]{2,1,0:T(8,128)(2,1)S(1)}, u32[]{:S(2)}, u32[]{:S(2)}) async-start(bf16[8,192,256]{2,1,0:T(8,128)(2,1)} %get-tuple-element.154), calls=%async_computation.2 | async-start | bytes 1572864 | tf_op jit(solution)/shard_map/all_to_all | solution.py:1288
  183.9 6.3 %shard_map.219 = (bf16[4,144,768]{2,1,0:T(8,128)(2,1)}, bf16[4,144,768]{2,1,0:T(8,128)(2,1)}, bf16[4,144,768]{2,1,0:T(8,128)(2,1)}, bf16[4,144,768]{2,1,0:T(8,128)(2,1)}) custom-call(s32[20]{0:T(128)} %concatenate.25.refs_0_, bf16[2,768,256]{2,1,0:T(8,128)(2,1)} %get-tuple-element.157.refs_1_, bf16[2,256,768]{2,1,0:T(8,128)(2,1)} %get-tuple-element.149.refs_2_.refs_4_, ...), custom_call_target="tpu_custom_call" | custom-call | flops 1 | bytes 1 | tf_op jit(solution)/shard_map/pallas_call | solution.py:485
  190.9 5.3 %all-to-all-done.2.refs_13_ = bf16[8,192,256]{2,1,0:T(8,128)(2,1)S(1)} async-done(((bf16[8,192,256]{2,1,0:T(8,128)(2,1)}), bf16[8,192,256]{2,1,0:T(8,128)(2,1)S(1)}, u32[]{:S(2)}, u32[]{:S(2)}) %all-to-all-start.2) | async-done | bytes 786464 | tf_op jit(solution)/shard_map/all_to_all | solution.py:1288
  197.3 2.4 collective-permute-start.21
  199.7 23.3 %shard_map.220 = (bf16[8,192,256]{2,1,0:T(8,128)(2,1)}, bf16[8,384,256]{2,1,0:T(8,128)(2,1)}, bf16[4,384,256]{2,1,0:T(8,128)(2,1)}, bf16[4,384,256]{2,1,0:T(8,128)(2,1)}) custom-call(s32[20]{0:T(128)} %concatenate.25.refs_0_, s32[8,8,256]{2,1,0:T(8,128)} %pad.8.refs_1_, f32[8,32,256]{2,1,0:T(8,128)} %get-tuple-element.116.refs_3_.refs_2_.cos, ...), custom_call_target="tpu_custom_call" | custom-call | flops 11 | bytes 1 | tf_op jit(solution)/shard_map/pallas_call | solution.py:485
  223.0 1.3 collective-permute-start.17
  224.3 1.3 collective-permute-start.18
  225.6 11.7 %collective-permute-done.20 = bf16[4,144,768]{2,1,0:T(8,128)(2,1)S(1)} collective-permute-done((bf16[4,144,768]{2,1,0:T(8,128)(2,1)}, bf16[4,144,768]{2,1,0:T(8,128)(2,1)S(1)}, u32[]{:S(2)}, u32[]{:S(2)}) %collective-permute-start.20) | collective-permute-done | bytes 884768 | tf_op jit(solution)/shard_map/ppermute | solution.py:438
  237.3 1.4 add_convert_fusion
  238.7 0.9 copy-done.16
  239.8 13.8 %shard_map.221 = (bf16[2,256,768]{2,1,0:T(8,128)(2,1)}, bf16[2,256,768]{2,1,0:T(8,128)(2,1)}, f32[4,256,768]{2,1,0:T(8,128)}, bf16[4,216,640]{2,1,0:T(8,128)(2,1)}) custom-call(bf16[8,384,256]{2,1,0:T(8,128)(2,1)} %get-tuple-element.164.own, bf16[4,384,256]{2,1,0:T(8,128)(2,1)} %copy-done.16, bf16[4,384,256]{2,1,0:T(8,128)(2,1)} %copy-done.17, ...), custom_call_target="tpu_custom_call" | custom-call | flops 4 | bytes 1 | tf_op jit(solution)/shard_map/pallas_call | solution.py:1171
  254.1 1.5 collective-permute-start.24
  255.6 16.9 %collective-permute-done.22 = bf16[2,256,768]{2,1,0:T(8,128)(2,1)S(1)} collective-permute-done((bf16[2,256,768]{2,1,0:T(8,128)(2,1)}, bf16[2,256,768]{2,1,0:T(8,128)(2,1)S(1)}, u32[]{:S(2)}, u32[]{:S(2)}) %collective-permute-start.22) | collective-permute-done | bytes 786464 | tf_op jit(solution)/shard_map/ppermute | solution.py:438
  273.4 0.9 copy-done.14
  274.3 2.8 fusion.2
  277.9 1.2 collective-permute-start.23
  279.5 0.9 slice.123
  280.4 1.0 slice.122
  281.4 0.8 pad_maximum_fusion.1
  282.3 4.3 %collective-permute-done.25 = bf16[256,768]{1,0:T(8,128)(2,1)S(1)} collective-permute-done((bf16[256,768]{1,0:T(8,128)(2,1)}, bf16[256,768]{1,0:T(8,128)(2,1)S(1)}, u32[]{:S(2)}, u32[]{:S(2)}) %collective-permute-start.25) | collective-permute-done | bytes 393248 | tf_op jit(solution)/shard_map/ppermute | solution.py:438
  287.3 2.3 fusion
  289.6 3.5 %all-to-all-start.3 = ((bf16[8,48,640]{2,1,0:T(8,128)(2,1)}), bf16[8,48,640]{2,1,0:T(8,128)(2,1)S(1)}, u32[]{:S(2)}, u32[]{:S(2)}) async-start(bf16[8,48,640]{2,1,0:T(8,128)(2,1)} %pad_maximum_fusion.1), calls=%async_computation.4 | async-start | bytes 983040 | tf_op jit(solution)/shard_map/all_to_all | solution.py:1288
  293.1 1.8 slice_bitcast_fusion.1
  295.0 2.8 collective-permute-start.29
  299.2 5.1 %shard_map.222 = bf16[2,256,768]{2,1,0:T(8,128)(2,1)} custom-call(s32[20]{0:T(128)} %concatenate.25.refs_0_, f32[1,768]{1,0:T(1,128)} %reshape.343.refs_1_, f32[1,768]{1,0:T(1,128)} %reshape.342.refs_2_, bf16[2,256,768]{2,1,0:T(8,128)(2,1)} %pad_maximum_fusion.refs_3_.refs_9_, bf16[2,256,768]{2,1,0:T(8,128)(2,1)} %get-tuple-element.149.refs_2_.refs_4_, ...), custom_call_target="tpu_custom_call" | custom-call | flops 1 | bytes 1 | tf_op jit(solution)/shard_map/pallas_call | solution.py:485
  304.3 0.9 reduce-scatter.8.cloned.1.call-done.refs_4_
  305.2 0.9 dynamic-slice_bitcast_fusion
  309.5 3.9 %shard_map.223 = (f32[24,2304]{1,0:T(8,128)}, f32[24,768]{1,0:T(8,128)}, f32[24,3072]{1,0:T(8,128)}, f32[96,768]{1,0:T(8,128)}, f32[1,96]{1,0:T(1,128)}, /*index=5*/f32[4,24]{1,0:T(4,128)}) custom-call(s32[20]{0:T(128)} %concatenate.25.refs_0_, f32[2,384]{1,0:T(2,128)} %reshape_reshape.6.refs_1_, f32[2,384]{1,0:T(2,128)} %reshape_reshape.7.refs_2_, ...), custom_call_target="tpu_custom_call" | custom-call | flops 1 | bytes 1 | tf_op jit(solution)/shard_map/pallas_call | solution.py:485
  313.3 1.3 slice_bitcast_fusion.5
  (184 shorter events, 22.4 us)
Async XLA Ops:
  7.2 54.3 %all-gather.3.cloned.1.call-start = ((), (), s32[]{:S(2)}) async-start(), calls=%async_computation.9 | async-start | bytes 1843200 | tf_op jit(solution)/shard_map/all_gather | solution.py:1325
  7.8 3.1 copy-start.43
  7.8 3.1 copy-start.5
  10.8 4.8 %copy-start.44 = (s32[1,16]{1,0:T(1,128)S(1)}, s32[1,16]{1,0:T(1,128)}, u32[]{:S(2)}) copy-start(s32[1,16]{1,0:T(1,128)} %param.15) | copy-start | bytes 196
  10.8 5.3 %copy-start.36 = (bf16[768]{0:T(1024)(128)(2,1)S(1)}, bf16[768]{0:T(1024)(128)(2,1)}, u32[]{:S(2)}) copy-start(bf16[768]{0:T(1024)(128)(2,1)} %param.19) | copy-start | bytes 4612
  10.8 5.3 %copy-start.37 = (bf16[192]{0:T(256)(128)(2,1)S(1)}, bf16[192]{0:T(256)(128)(2,1)}, u32[]{:S(2)}) copy-start(bf16[192]{0:T(256)(128)(2,1)} %param.21) | copy-start | bytes 1156
  10.8 5.3 %copy-start.38 = (bf16[192]{0:T(256)(128)(2,1)S(1)}, bf16[192]{0:T(256)(128)(2,1)}, u32[]{:S(2)}) copy-start(bf16[192]{0:T(256)(128)(2,1)} %param.22) | copy-start | bytes 1156
  10.8 5.3 %copy-start.39 = (bf16[192]{0:T(256)(128)(2,1)S(1)}, bf16[192]{0:T(256)(128)(2,1)}, u32[]{:S(2)}) copy-start(bf16[192]{0:T(256)(128)(2,1)} %param.23) | copy-start | bytes 1156
  10.8 5.2 %copy-start.40 = (bf16[192]{0:T(256)(128)(2,1)S(1)}, bf16[192]{0:T(256)(128)(2,1)}, u32[]{:S(2)}) copy-start(bf16[192]{0:T(256)(128)(2,1)} %param.24) | copy-start | bytes 1156
  10.9 6.6 %copy-start.10 = (bf16[192,2304]{1,0:T(8,128)(2,1)S(1)}, bf16[192,2304]{1,0:T(8,128)(2,1)}, u32[]{:S(2)}) copy-start(bf16[192,2304]{1,0:T(8,128)(2,1)} %param.16) | copy-start | bytes 2654212
  11.1 6.8 %copy-start.9 = (bf16[256,768]{1,0:T(8,128)(2,1)}, bf16[256,768]{1,0:T(8,128)(2,1)S(1)}, u32[]{:S(2)}) copy-start(bf16[256,768]{1,0:T(8,128)(2,1)S(1)} %get-tuple-element.219.refs_5_) | copy-start | bytes 1179652
  11.1 16.8 %collective-permute-start.1 = (bf16[256,768]{1,0:T(8,128)(2,1)S(1)}, bf16[256,768]{1,0:T(8,128)(2,1)S(1)}, u32[]{:S(2)}, u32[]{:S(2)}) collective-permute-start(bf16[256,768]{1,0:T(8,128)(2,1)S(1)} %get-tuple-element.219.refs_5_), channel_id=1, source_target_pairs={{0,16},{4,20},{8,24},{12,28},{16,0},{20,4},{24,8},{28,12},{1,17},{... | collective-permute-start | bytes 1179656 | tf_op jit(solution)/shard_map/ppermute | solution.py:438
  14.1 13.8 %collective-permute-start = (bf16[256,768]{1,0:T(8,128)(2,1)S(1)}, bf16[256,768]{1,0:T(8,128)(2,1)S(1)}, u32[]{:S(2)}, u32[]{:S(2)}) collective-permute-start(bf16[256,768]{1,0:T(8,128)(2,1)S(1)} %get-tuple-element.219.refs_5_), channel_id=1, source_target_pairs={{0,8},{4,12},{8,0},{12,4},{16,24},{20,28},{24,16},{28,20},{1,9},{5... | collective-permute-start | bytes 1179656 | tf_op jit(solution)/shard_map/ppermute | solution.py:438
  15.6 1.9 collective-permute-start.2
  18.8 37.3 %all-to-all-start = ((bf16[4,112,576]{2,1,0:T(8,128)(2,1)}), bf16[4,112,576]{2,1,0:T(8,128)(2,1)}, u32[]{:S(2)}, u32[]{:S(2)}) async-start(bf16[4,112,576]{2,1,0:T(8,128)(2,1)} %broadcast_in_dim.92), calls=%async_computation | async-start | bytes 1146880 | tf_op jit(solution)/shard_map/all_to_all | solution.py:1297
  23.6 11.1 %collective-permute-start.4 = (bf16[256,768]{1,0:T(8,128)(2,1)}, bf16[256,768]{1,0:T(8,128)(2,1)S(1)}, u32[]{:S(2)}, u32[]{:S(2)}) collective-permute-start(bf16[256,768]{1,0:T(8,128)(2,1)} %collective-permute-done.2.refs_6_), channel_id=1, source_target_pairs={{0,16},{4,20},{8,24},{12,28},{16,0},{20,4},{24,8},{28,12},{1,17},{... | collective-permute-start | bytes 1179656 | tf_op jit(solution)/shard_map/ppermute | solution.py:438
  24.2 10.8 %collective-permute-start.3 = (bf16[256,768]{1,0:T(8,128)(2,1)}, bf16[256,768]{1,0:T(8,128)(2,1)S(1)}, u32[]{:S(2)}, u32[]{:S(2)}) collective-permute-start(bf16[256,768]{1,0:T(8,128)(2,1)} %collective-permute-done.2.refs_6_), channel_id=1, source_target_pairs={{0,8},{4,12},{8,0},{12,4},{16,24},{20,28},{24,16},{28,20},{1,9},{5... | collective-permute-start | bytes 1179656 | tf_op jit(solution)/shard_map/ppermute | solution.py:438
  27.9 35.8 %copy-start.24 = (bf16[256,768]{1,0:T(8,128)(2,1)}, bf16[256,768]{1,0:T(8,128)(2,1)S(1)}, u32[]{:S(2)}) copy-start(bf16[256,768]{1,0:T(8,128)(2,1)S(1)} %collective-permute-done.1.refs_9_) | copy-start | bytes 1179652
  27.9 33.6 %copy-start.25 = (bf16[256,768]{1,0:T(8,128)(2,1)}, bf16[256,768]{1,0:T(8,128)(2,1)S(1)}, u32[]{:S(2)}) copy-start(bf16[256,768]{1,0:T(8,128)(2,1)S(1)} %collective-permute-done.refs_7_) | copy-start | bytes 1179652
  34.7 26.8 %copy-start.26 = (bf16[256,768]{1,0:T(8,128)(2,1)}, bf16[256,768]{1,0:T(8,128)(2,1)S(1)}, u32[]{:S(2)}) copy-start(bf16[256,768]{1,0:T(8,128)(2,1)S(1)} %collective-permute-done.4.refs_10_) | copy-start | bytes 1179652
  35.0 26.6 %copy-start.27 = (bf16[256,768]{1,0:T(8,128)(2,1)}, bf16[256,768]{1,0:T(8,128)(2,1)S(1)}, u32[]{:S(2)}) copy-start(bf16[256,768]{1,0:T(8,128)(2,1)S(1)} %collective-permute-done.3.refs_8_) | copy-start | bytes 1179652
  35.0 21.1 %collective-permute-start.5 = (bf16[256,768]{1,0:T(8,128)(2,1)S(1)}, bf16[256,768]{1,0:T(8,128)(2,1)S(1)}, u32[]{:S(2)}, u32[]{:S(2)}) collective-permute-start(bf16[256,768]{1,0:T(8,128)(2,1)S(1)} %collective-permute-done.refs_7_), channel_id=1, source_target_pairs={{0,16},{4,20},{8,24},{12,28},{16,0},{20,4},{24,8},{28,12},{1,17},{... | collective-permute-start | bytes 1179656 | tf_op jit(solution)/shard_map/ppermute | solution.py:438
  36.5 19.6 %collective-permute-start.6 = (bf16[256,768]{1,0:T(8,128)(2,1)S(1)}, bf16[256,768]{1,0:T(8,128)(2,1)S(1)}, u32[]{:S(2)}, u32[]{:S(2)}) collective-permute-start(bf16[256,768]{1,0:T(8,128)(2,1)S(1)} %collective-permute-done.4.refs_10_), channel_id=1, source_target_pairs={{0,8},{4,12},{8,0},{12,4},{16,24},{20,28},{24,16},{28,20},{1,9},{5... | collective-permute-start | bytes 1179656 | tf_op jit(solution)/shard_map/ppermute | solution.py:438
  56.1 5.5 %copy-start.28 = (bf16[256,768]{1,0:T(8,128)(2,1)}, bf16[256,768]{1,0:T(8,128)(2,1)S(1)}, u32[]{:S(2)}) copy-start(bf16[256,768]{1,0:T(8,128)(2,1)S(1)} %collective-permute-done.5.refs_11_) | copy-start | bytes 1179652
  56.1 5.4 %copy-start.29 = (bf16[256,768]{1,0:T(8,128)(2,1)}, bf16[256,768]{1,0:T(8,128)(2,1)S(1)}, u32[]{:S(2)}) copy-start(bf16[256,768]{1,0:T(8,128)(2,1)S(1)} %collective-permute-done.6.refs_12_) | copy-start | bytes 1179652
  56.1 7.6 %collective-permute-start.7 = (bf16[4,112,576]{2,1,0:T(8,128)(2,1)}, bf16[4,112,576]{2,1,0:T(8,128)(2,1)}, u32[]{:S(2)}, u32[]{:S(2)}) collective-permute-start(bf16[4,112,576]{2,1,0:T(8,128)(2,1)} %all-to-all-done.refs_13_), channel_id=1, source_target_pairs={{0,4},{4,0},{8,12},{12,8},{16,20},{20,16},{24,28},{28,24},{1,5},{5... | collective-permute-start | bytes 1548296 | tf_op jit(solution)/shard_map/ppermute | solution.py:438
  63.7 18.9 %copy-start = (bf16[3,240,768]{2,1,0:T(8,128)(2,1)}, bf16[3,240,768]{2,1,0:T(8,128)(2,1)S(1)}, u32[]{:S(2)}) copy-start(bf16[3,240,768]{2,1,0:T(8,128)(2,1)S(1)} %broadcast_select_fusion.refs_6_.refs_8_) | copy-start | bytes 3317764
  63.7 40.6 %collective-permute-start.12 = (bf16[3,240,768]{2,1,0:T(8,128)(2,1)S(1)}, bf16[3,240,768]{2,1,0:T(8,128)(2,1)}, u32[]{:S(2)}, u32[]{:S(2)}) collective-permute-start(bf16[3,240,768]{2,1,0:T(8,128)(2,1)S(1)} %broadcast_select_fusion.refs_6_.refs_8_), channel_id=1, source_target_pairs={{0,24},{4,28},{8,16},{12,20},{16,8},{20,12},{24,0},{28,4},{1,25},{... | collective-permute-start | bytes 3317768 | tf_op jit(solution)/shard_map/ppermute | solution.py:438
  66.2 48.5 %collective-permute-start.11 = (bf16[3,240,768]{2,1,0:T(8,128)(2,1)S(1)}, bf16[3,240,768]{2,1,0:T(8,128)(2,1)}, u32[]{:S(2)}, u32[]{:S(2)}) collective-permute-start(bf16[3,240,768]{2,1,0:T(8,128)(2,1)S(1)} %broadcast_select_fusion.refs_6_.refs_8_), channel_id=1, source_target_pairs={{0,16},{4,20},{8,24},{12,28},{16,0},{20,4},{24,8},{28,12},{1,17},{... | collective-permute-start | bytes 3317768 | tf_op jit(solution)/shard_map/ppermute | solution.py:438
  66.7 48.0 %collective-permute-start.10 = (bf16[3,240,768]{2,1,0:T(8,128)(2,1)S(1)}, bf16[3,240,768]{2,1,0:T(8,128)(2,1)}, u32[]{:S(2)}, u32[]{:S(2)}) collective-permute-start(bf16[3,240,768]{2,1,0:T(8,128)(2,1)S(1)} %broadcast_select_fusion.refs_6_.refs_8_), channel_id=1, source_target_pairs={{0,8},{4,12},{8,0},{12,4},{16,24},{20,28},{24,16},{28,20},{1,9},{5... | collective-permute-start | bytes 3317768 | tf_op jit(solution)/shard_map/ppermute | solution.py:438
  82.6 3.4 %collective-permute-start.9 = (bf16[4,384,256]{2,1,0:T(8,128)(2,1)}, bf16[4,384,256]{2,1,0:T(8,128)(2,1)S(1)}, u32[]{:S(2)}, u32[]{:S(2)}) collective-permute-start(bf16[4,384,256]{2,1,0:T(8,128)(2,1)} %get-tuple-element.130.refs_4_.refs_1_.refs_8_), channel_id=1, source_target_pairs={{0,4},{8,12},{16,20},{24,28},{1,5},{9,13},{17,21},{25,29},{2,6},{1... | collective-permute-start | bytes 2359304 | tf_op jit(solution)/shard_map/ppermute | solution.py:1386
  84.0 3.4 %collective-permute-start.8 = (bf16[4,384,256]{2,1,0:T(8,128)(2,1)}, bf16[4,384,256]{2,1,0:T(8,128)(2,1)S(1)}, u32[]{:S(2)}, u32[]{:S(2)}) collective-permute-start(bf16[4,384,256]{2,1,0:T(8,128)(2,1)} %get-tuple-element.129.refs_3_.refs_0_.refs_7_), channel_id=1, source_target_pairs={{0,4},{8,12},{16,20},{24,28},{1,5},{9,13},{17,21},{25,29},{2,6},{1... | collective-permute-start | bytes 2359304 | tf_op jit(solution)/shard_map/ppermute | solution.py:1386
  114.7 16.1 %all-to-all-start.1 = ((bf16[8,192,256]{2,1,0:T(8,128)(2,1)}), bf16[8,192,256]{2,1,0:T(8,128)(2,1)S(1)}, u32[]{:S(2)}, u32[]{:S(2)}) async-start(bf16[8,192,256]{2,1,0:T(8,128)(2,1)} %get-tuple-element.128), calls=%async_computation.1 | async-start | bytes 1572864 | tf_op jit(solution)/shard_map/all_to_all | solution.py:1288
  118.3 2.0 copy-start.7
  118.3 120.4 %reduce-scatter.6.cloned.1.call-start = ((), (), s32[]{:S(2)}) async-start(), calls=%async_computation.7 | async-start | bytes 2949120 | tf_op jit(solution)/shard_map/reduce_scatter | solution.py:1398
  120.3 18.4 %collective-permute-start.14 = (bf16[512,768]{1,0:T(8,128)(2,1)S(1)}, bf16[512,768]{1,0:T(8,128)(2,1)S(1)}, u32[]{:S(2)}, u32[]{:S(2)}) collective-permute-start(bf16[512,768]{1,0:T(8,128)(2,1)S(1)} %bitcast.76), channel_id=1, source_target_pairs={{0,4},{4,0},{8,12},{12,8},{16,20},{20,16},{24,28},{28,24},{1,5},{5... | collective-permute-start | bytes 2359304 | tf_op jit(solution)/shard_map/ppermute | solution.py:438
  138.0 2.6 collective-permute-start.13
  167.7 2.3 collective-permute-start.15
  167.9 3.2 collective-permute-start.16
  180.1 3.7 %copy-start.34 = (f32[1,1536]{1,0:T(1,128)S(1)}, f32[1,1536]{1,0:T(1,128)}, u32[]{:S(2)}) copy-start(f32[1,1536]{1,0:T(1,128)} %get-tuple-element.155) | copy-start | bytes 18436
  180.1 16.1 %all-to-all-start.2 = ((bf16[8,192,256]{2,1,0:T(8,128)(2,1)}), bf16[8,192,256]{2,1,0:T(8,128)(2,1)S(1)}, u32[]{:S(2)}, u32[]{:S(2)}) async-start(bf16[8,192,256]{2,1,0:T(8,128)(2,1)} %get-tuple-element.154), calls=%async_computation.2 | async-start | bytes 1572864 | tf_op jit(solution)/shard_map/all_to_all | solution.py:1288
  183.7 95.9 %reduce-scatter.10.cloned.1.call-start = ((), (), s32[]{:S(2)}) async-start(), calls=%async_computation.10 | async-start | bytes 1382400
  183.9 6.4 %copy-start.35 = (f32[8,768]{1,0:T(8,128)S(1)}, f32[8,768]{1,0:T(8,128)}, u32[]{:S(2)}) copy-start(f32[8,768]{1,0:T(8,128)} %get-tuple-element.156) | copy-start | bytes 73732
  196.2 3.5 %copy-start.3 = (bf16[8,192,256]{2,1,0:T(8,128)(2,1)}, bf16[8,192,256]{2,1,0:T(8,128)(2,1)S(1)}, u32[]{:S(2)}) copy-start(bf16[8,192,256]{2,1,0:T(8,128)(2,1)S(1)} %all-to-all-done.2.refs_13_) | copy-start | bytes 2359300
  196.2 29.4 %collective-permute-start.19 = (bf16[4,144,768]{2,1,0:T(8,128)(2,1)}, bf16[4,144,768]{2,1,0:T(8,128)(2,1)S(1)}, u32[]{:S(2)}, u32[]{:S(2)}) collective-permute-start(bf16[4,144,768]{2,1,0:T(8,128)(2,1)} %get-tuple-element.168), channel_id=1, source_target_pairs={{0,8},{4,12},{8,0},{12,4},{16,24},{20,28},{24,16},{28,20},{1,9},{5... | collective-permute-start | bytes 2654216 | tf_op jit(solution)/shard_map/ppermute | solution.py:438
  196.7 40.6 %collective-permute-start.20 = (bf16[4,144,768]{2,1,0:T(8,128)(2,1)}, bf16[4,144,768]{2,1,0:T(8,128)(2,1)S(1)}, u32[]{:S(2)}, u32[]{:S(2)}) collective-permute-start(bf16[4,144,768]{2,1,0:T(8,128)(2,1)} %get-tuple-element.169), channel_id=1, source_target_pairs={{0,16},{4,20},{8,24},{12,28},{16,0},{20,4},{24,8},{28,12},{1,17},{... | collective-permute-start | bytes 2654216 | tf_op jit(solution)/shard_map/ppermute | solution.py:438
  197.3 40.0 %collective-permute-start.21 = (bf16[4,144,768]{2,1,0:T(8,128)(2,1)}, bf16[4,144,768]{2,1,0:T(8,128)(2,1)S(1)}, u32[]{:S(2)}, u32[]{:S(2)}) collective-permute-start(bf16[4,144,768]{2,1,0:T(8,128)(2,1)} %get-tuple-element.170), channel_id=1, source_target_pairs={{0,24},{4,28},{8,16},{12,20},{16,8},{20,12},{24,0},{28,4},{1,25},{... | collective-permute-start | bytes 2654216 | tf_op jit(solution)/shard_map/ppermute | solution.py:438
  199.7 37.6 %copy-start.11 = (bf16[4,144,768]{2,1,0:T(8,128)(2,1)S(1)}, bf16[4,144,768]{2,1,0:T(8,128)(2,1)}, u32[]{:S(2)}) copy-start(bf16[4,144,768]{2,1,0:T(8,128)(2,1)} %get-tuple-element.172) | copy-start | bytes 2654212
  223.0 15.6 %collective-permute-start.17 = (bf16[4,384,256]{2,1,0:T(8,128)(2,1)}, bf16[4,384,256]{2,1,0:T(8,128)(2,1)S(1)}, u32[]{:S(2)}, u32[]{:S(2)}) collective-permute-start(bf16[4,384,256]{2,1,0:T(8,128)(2,1)} %get-tuple-element.165), channel_id=1, source_target_pairs={{4,0},{12,8},{20,16},{28,24},{5,1},{13,9},{21,17},{29,25},{6,2},{1... | collective-permute-start | bytes 2359304 | tf_op jit(solution)/shard_map/ppermute | solution.py:1417
  224.3 14.4 %collective-permute-start.18 = (bf16[4,384,256]{2,1,0:T(8,128)(2,1)}, bf16[4,384,256]{2,1,0:T(8,128)(2,1)S(1)}, u32[]{:S(2)}, u32[]{:S(2)}) collective-permute-start(bf16[4,384,256]{2,1,0:T(8,128)(2,1)} %get-tuple-element.166), channel_id=1, source_target_pairs={{4,0},{12,8},{20,16},{28,24},{5,1},{13,9},{21,17},{29,25},{6,2},{1... | collective-permute-start | bytes 2359304 | tf_op jit(solution)/shard_map/ppermute | solution.py:1417
  253.7 51.5 %reduce-scatter.8.cloned.1.call-start = ((), (), s32[]{:S(2)}) async-start(), calls=%async_computation.8 | async-start | bytes 1105920 | tf_op jit(solution)/shard_map/reduce_scatter | solution.py:1423
  253.7 18.7 %collective-permute-start.22 = (bf16[2,256,768]{2,1,0:T(8,128)(2,1)}, bf16[2,256,768]{2,1,0:T(8,128)(2,1)S(1)}, u32[]{:S(2)}, u32[]{:S(2)}) collective-permute-start(bf16[2,256,768]{2,1,0:T(8,128)(2,1)} %get-tuple-element.185), channel_id=1, source_target_pairs={{0,8},{4,12},{8,0},{12,4},{16,24},{20,28},{24,16},{28,20},{1,9},{5... | collective-permute-start | bytes 2359304 | tf_op jit(solution)/shard_map/ppermute | solution.py:438
  254.1 18.5 %collective-permute-start.24 = (bf16[2,256,768]{2,1,0:T(8,128)(2,1)}, bf16[2,256,768]{2,1,0:T(8,128)(2,1)S(1)}, u32[]{:S(2)}, u32[]{:S(2)}) collective-permute-start(bf16[2,256,768]{2,1,0:T(8,128)(2,1)} %get-tuple-element.186), channel_id=1, source_target_pairs={{0,16},{4,20},{8,24},{12,28},{16,0},{20,4},{24,8},{28,12},{1,17},{... | collective-permute-start | bytes 2359304 | tf_op jit(solution)/shard_map/ppermute | solution.py:438
  274.3 13.1 %copy-start.4 = (f32[4,256,768]{2,1,0:T(8,128)S(1)}, f32[4,256,768]{2,1,0:T(8,128)}, u32[]{:S(2)}) copy-start(f32[4,256,768]{2,1,0:T(8,128)} %get-tuple-element.184) | copy-start | bytes 9437188
  277.1 9.4 %collective-permute-start.25 = (bf16[256,768]{1,0:T(8,128)(2,1)}, bf16[256,768]{1,0:T(8,128)(2,1)S(1)}, u32[]{:S(2)}, u32[]{:S(2)}) collective-permute-start(bf16[256,768]{1,0:T(8,128)(2,1)} %get-tuple-element.213), channel_id=1, source_target_pairs={{0,8},{4,12},{8,0},{12,4},{16,24},{20,28},{24,16},{28,20},{1,9},{5... | collective-permute-start | bytes 1179656 | tf_op jit(solution)/shard_map/ppermute | solution.py:438
  277.9 9.4 %collective-permute-start.23 = (bf16[256,768]{1,0:T(8,128)(2,1)}, bf16[256,768]{1,0:T(8,128)(2,1)}, u32[]{:S(2)}, u32[]{:S(2)}) collective-permute-start(bf16[256,768]{1,0:T(8,128)(2,1)} %get-tuple-element.214), channel_id=1, source_target_pairs={{0,16},{4,20},{8,24},{12,28},{16,0},{20,4},{24,8},{28,12},{1,17},{... | collective-permute-start | bytes 1179656 | tf_op jit(solution)/shard_map/ppermute | solution.py:438
  279.5 7.8 %copy-start.13 = (bf16[2,256,768]{2,1,0:T(8,128)(2,1)S(1)}, bf16[2,256,768]{2,1,0:T(8,128)(2,1)}, u32[]{:S(2)}) copy-start(bf16[2,256,768]{2,1,0:T(8,128)(2,1)} %copy-done.12) | copy-start | bytes 2359300
  279.5 7.8 %copy-start.15 = (bf16[2,256,768]{2,1,0:T(8,128)(2,1)S(1)}, bf16[2,256,768]{2,1,0:T(8,128)(2,1)}, u32[]{:S(2)}) copy-start(bf16[2,256,768]{2,1,0:T(8,128)(2,1)} %copy-done.14) | copy-start | bytes 2359300
  289.6 8.8 %collective-permute-start.26 = (bf16[256,768]{1,0:T(8,128)(2,1)S(1)}, bf16[256,768]{1,0:T(8,128)(2,1)S(1)}, u32[]{:S(2)}, u32[]{:S(2)}) collective-permute-start(bf16[256,768]{1,0:T(8,128)(2,1)S(1)} %get-tuple-element.211), channel_id=1, source_target_pairs={{0,4},{4,0},{8,12},{12,8},{16,20},{20,16},{24,28},{28,24},{1,5},{5... | collective-permute-start | bytes 1179656 | tf_op jit(solution)/shard_map/ppermute | solution.py:438
  289.6 18.3 %all-to-all-start.3 = ((bf16[8,48,640]{2,1,0:T(8,128)(2,1)}), bf16[8,48,640]{2,1,0:T(8,128)(2,1)S(1)}, u32[]{:S(2)}, u32[]{:S(2)}) async-start(bf16[8,48,640]{2,1,0:T(8,128)(2,1)} %pad_maximum_fusion.1), calls=%async_computation.4 | async-start | bytes 983040 | tf_op jit(solution)/shard_map/all_to_all | solution.py:1288
  295.0 12.5 %collective-permute-start.29 = (bf16[96,768]{1,0:T(8,128)(2,1)S(1)}, bf16[96,768]{1,0:T(8,128)(2,1)S(1)}, u32[]{:S(2)}, u32[]{:S(2)}) collective-permute-start(bf16[96,768]{1,0:T(8,128)(2,1)S(1)} %get-tuple-element.220), channel_id=1, source_target_pairs={{0,24},{4,28},{8,16},{12,20},{16,8},{20,12},{24,0},{28,4},{1,25},{... | collective-permute-start | bytes 442376 | tf_op jit(solution)/shard_map/ppermute | solution.py:438
  297.8 10.1 %collective-permute-start.28 = (bf16[96,768]{1,0:T(8,128)(2,1)S(1)}, bf16[96,768]{1,0:T(8,128)(2,1)S(1)}, u32[]{:S(2)}, u32[]{:S(2)}) collective-permute-start(bf16[96,768]{1,0:T(8,128)(2,1)S(1)} %get-tuple-element.221), channel_id=1, source_target_pairs={{0,16},{4,20},{8,24},{12,28},{16,0},{20,4},{24,8},{28,12},{1,17},{... | collective-permute-start | bytes 442376 | tf_op jit(solution)/shard_map/ppermute | solution.py:438
  298.3 9.6 %collective-permute-start.27 = (bf16[96,768]{1,0:T(8,128)(2,1)S(1)}, bf16[96,768]{1,0:T(8,128)(2,1)S(1)}, u32[]{:S(2)}, u32[]{:S(2)}) collective-permute-start(bf16[96,768]{1,0:T(8,128)(2,1)S(1)} %get-tuple-element.222), channel_id=1, source_target_pairs={{0,8},{4,12},{8,0},{12,4},{16,24},{20,28},{24,16},{28,20},{1,9},{5... | collective-permute-start | bytes 442376 | tf_op jit(solution)/shard_map/ppermute | solution.py:438
  306.1 1.8 collective-permute-start.30
  (20 other events, 19.4 us)
Sparse Core Ops, SparseCore 0:
  11.0 50.4 all-gather.2
  166.7 45.2 reduce-scatter.5
  253.8 25.6 reduce-scatter.9
  281.7 23.4 reduce-scatter.7

commit v5 on v4

--- a/solution.py
+++ b/solution.py
@@ -450,14 +450,19 @@
     return jnp.transpose(v.astype(F32)).astype(v.dtype)
 
 
-def call(body, outs, kinds, args, scratch=(), flops=0, moved=0):
+def call(body, outs, kinds, args, scratch=(), flops=0, moved=0, raw=()):
     staged = [i for i, kind in enumerate(kinds) if kind == "V"]
     space = {"S": SM, "V": HB, "A": HB}
-    count, made = len(args), len(outs)
+    count = len(args)
+    kept = [k for k in range(len(outs)) if k not in raw]
+    made = len(kept)
 
     def run(*refs):
-        ins, sinks, rest = list(refs[:count]), refs[count : count + made], refs[count + made :]
-        held, results = rest[: len(staged)], rest[len(staged) : len(staged) + made]
+        ins, sinks, rest = list(refs[:count]), list(refs[count : count + len(outs)]), refs[count + len(outs) :]
+        held, buffers = rest[: len(staged)], rest[len(staged) : len(staged) + made]
+        results = list(sinks)
+        for i, k in enumerate(kept):
+            results[k] = buffers[i]
         sem_in, sem_out, sems = rest[len(staged) + made : len(staged) + made + 3]
         rest = rest[len(staged) + made + 3 :]
         first = [
@@ -476,7 +481,7 @@
                 copy.wait()
 
         body(load, *ins, *results, *rest)
-        last = [pltpu.make_async_copy(results[k], sinks[k], sem_out.at[k]) for k in range(made)]
+        last = [pltpu.make_async_copy(results[k], sinks[k], sem_out.at[i]) for i, k in enumerate(kept)]
         for copy in last:
             copy.start()
         for copy in last:
@@ -488,7 +493,7 @@
         in_specs=[space[kind] for kind in kinds],
         out_specs=tuple(HB for _ in outs),
         scratch_shapes=[pltpu.VMEM(args[i].shape, args[i].dtype) for i in staged]
-        + [pltpu.VMEM(s, d) for s, d in outs]
+        + [pltpu.VMEM(*outs[k]) for k in kept]
         + [
             pltpu.SemaphoreType.DMA((max(1, len(staged)),)),
             pltpu.SemaphoreType.DMA((made,)),
@@ -539,7 +544,7 @@
 
 def project_body(load, meta, gain, embed, cos, sin, *refs):
     rows, refs = refs[:8], refs[8:]
-    near, far, q_ref, kv_a, kv_b, n_ref, mk_ref, w, xs, wp = refs
+    near, far, q_ref, kv_a, kv_b, n_out, mk_ref, w, xs, wp, n_ref, out_sems = refs
     load(shard_rows(meta, near, far, w, 192) + [(rows[i], xs.at[i]) for i in range(8)])
     for part in range(3):
         wp[part] = w[:, part * WIDE : (part + 1) * WIDE]
@@ -550,6 +555,7 @@
         hat, _ = norm_parts(x)
         n = (hat * gain[...]).astype(BF)
         n_ref[i] = n
+        pltpu.make_async_copy(n_ref.at[i], n_out.at[i], out_sems.at[i]).start()
         mk_ref[i] = jnp.broadcast_to(jnp.where(flag, 1.0, 0.0), (CHUNK, 128)).astype(BF)
         q_ref[i] = turn_heads(jnp.transpose(mm(n, wp[0])), cos[i], sin[i]).astype(BF)
         keys = turn_heads(jnp.transpose(mm(n, wp[1])), cos[i], sin[i]).astype(BF)
@@ -560,6 +566,9 @@
             def _():
                 ref[i % 4, :WIDE] = keys
                 ref[i % 4, WIDE:] = values
+
+    for i in range(8):
+        pltpu.make_async_copy(n_ref.at[i], n_out.at[i], out_sems.at[i]).wait()
 
 
 def project_rows(meta, gain, embed, cos, sin, rows, weights):
@@ -577,7 +586,13 @@
         ],
         "SVVVV" + "A" * 10,
         (meta, gain, embed, cos, sin, *rows, *weights),
-        scratch=[pltpu.VMEM((8, CHUNK, dim), BF), pltpu.VMEM((3, dim, WIDE), BF)],
+        scratch=[
+            pltpu.VMEM((8, CHUNK, dim), BF),
+            pltpu.VMEM((3, dim, WIDE), BF),
+            pltpu.VMEM((8, CHUNK, dim), BF),
+            pltpu.SemaphoreType.DMA((8,)),
+        ],
+        raw=(3,),
         flops=2 * 8 * CHUNK * dim * 3 * WIDE,
         moved=8 * CHUNK * dim * 6,
     )
@@ -909,8 +924,8 @@
 def feed_body(load, meta, bias, n_own, n_far, g_own, g_far, up_own, down_own, *refs):
     shares, refs = refs[:4], refs[4:]
     (
-        out_ref, outf_ref, ngf_ref, ng_ref, gb_ref, d_ref, u_ref,
-        ns, gs, wu, wd, acts, slopes,
+        *sinks, gb_ref, d_out, u_ref,
+        ns, gs, wu, wd, acts, slopes, out_ref, outf_ref, ngf_ref, ng_ref, d_ref, out_sems,
     ) = refs
     c, h, z = meta[1], meta[2], meta[3]
     rows = 2 * CHUNK
@@ -966,12 +981,20 @@
             outf_ref[to] = out
             ngf_ref[to] = ng
 
+    early = [
+        pltpu.make_async_copy(ref, sinks[k], out_sems.at[k])
+        for k, ref in enumerate((out_ref, outf_ref, ngf_ref, ng_ref))
+    ]
+    for copy in early:
+        copy.start()
+
     @pl.loop(0, 4)
     def _(j):
         cols = pl.ds(pl.multiple_of(j * part, 128), part)
         gd = mm(acts[:, cols], gs[...], 0, 0).astype(BF)
         for b in range(4):
             d_ref[b, j ^ h] = gd[96 * b : 96 * (b + 1)]
+        pltpu.make_async_copy(d_ref.at[:, j ^ h], d_out.at[:, j ^ h], out_sems.at[4 + j]).start()
         gu = mm(ns[...], slopes[:, cols], 0, 0)
         side = pl.ds(pl.multiple_of((j & 1) * part, 128), part)
         line = pl.ds(at16((j >> 1) * 48), 48)
@@ -979,6 +1002,11 @@
             first = 192 * (b // 4) + 24 * (b % 4)
             block = jnp.concatenate([gu[first : first + 24], gu[first + 96 : first + 120]])
             u_ref[(b // 4) ^ h, b % 4, line, side] = block.astype(BF)
+
+    for copy in early:
+        copy.wait()
+    for j in range(4):
+        pltpu.make_async_copy(d_ref.at[:, j ^ h], d_out.at[:, j ^ h], out_sems.at[4 + j]).wait()
 
 
 def feed_rows(meta, bias, args):
@@ -999,7 +1027,10 @@
             pltpu.VMEM((hid, dim), BF),
             pltpu.VMEM((2 * rows, hid), BF),
             pltpu.VMEM((2 * rows, hid), BF),
-        ],
+        ]
+        + [pltpu.VMEM((rows, dim), BF)] * 4
+        + [pltpu.VMEM((4, 4, hid // 16, dim), BF), pltpu.SemaphoreType.DMA((8,))],
+        raw=(0, 1, 2, 3, 5),
         flops=6 * 2 * 2 * rows * dim * hid,
         moved=12 * dim * hid,
     )

time: 322 us -> 322 us (level)
  Pallas kernels: 131 us -> 136 us
  waiting for transfers between devices: 91.6 us -> 87 us
    ppermute x27, waiting for transfers between devices: 56 us -> 51.4 us  [swap(): return lax.ppermute(v, 'ctx', [(i, i ^ bit) for i in range(8)])]
    pallas_call x11, Pallas kernels: 118 us -> 122 us  [call(): pl.pallas_call(run, out_shape=tuple((jax.ShapeDtypeStruct(s, d) for s, d...]
  transfers between devices with their start and end apart: 39 -> 39, of which waited for: 21 -> 21; matrix products, arithmetic and copies ran while one was open for 8% -> 8% of each run, Pallas kernels for 27% -> 28%
where the time goes in v5:
time: 322 us; the launch traced here: 321 us
  Pallas kernels  136 us (42%)
  waiting for transfers between devices  87 us (27%)
  starting transfers between devices  43.8 us (14%)
  local copies, waits for them, and re-layouts  27.5 us (9%)
  between operations  14.5 us (5%)
  other arithmetic  12.4 us (4%)
    pallas_call x11, Pallas kernels, call(): pl.pallas_call(run, out_shape=tuple((jax.ShapeDtypeStruct(s, d) for s, d...  122 us
    ppermute x27, waiting for transfers between devices, swap(): return lax.ppermute(v, 'ctx', [(i, i ^ bit) for i in range(8)])  51.4 us
    ppermute x27, starting transfers between devices, swap(): return lax.ppermute(v, 'ctx', [(i, i ^ bit) for i in range(8)])  22.7 us
    all_to_all x1, waiting for transfers between devices, exchange_z(): return lax.all_to_all(v, 'fsdp', 0, 0, tiled=True)  19.1 us
    pallas_call x1, Pallas kernels, project_back(): pl.pallas_call(project_back_body, grid=(8,), out_shape=(jax.ShapeDtypeStr...  13.8 us
    unnamed x92, local copies, waits for them, and re-layouts  11.4 us
    all_to_all x3, starting transfers between devices, exchange(): return lax.all_to_all(v, 'ctx', 0, 0, tiled=True)  10.6 us
    all_to_all x3, waiting for transfers between devices, exchange(): return lax.all_to_all(v, 'ctx', 0, 0, tiled=True)  8.98 us
  transfers between devices with their start and end apart: 39, of which 21 were waited for; matrix products, arithmetic and copies ran while one was open for 8% of the time, Pallas kernels for 28%

profile of v5, /device:TPU:0, one launch (start us, length us, event | category | flops | bytes accessed | tf_op | source)
XLA Modules:
  0.0 320.8 jit_solution(6215274409681927850)
XLA Ops:
  7.8 3.0 shard_map.212
  11.1 3.0 collective-permute-start.1
  14.1 1.5 collective-permute-start
  16.3 1.1 collective-permute-done.2.refs_6_
  17.9 0.9 broadcast_in_dim.92
  18.8 4.9 %all-to-all-start = ((bf16[4,112,576]{2,1,0:T(8,128)(2,1)}), bf16[4,112,576]{2,1,0:T(8,128)(2,1)}, u32[]{:S(2)}, u32[]{:S(2)}) async-start(bf16[4,112,576]{2,1,0:T(8,128)(2,1)} %broadcast_in_dim.92), calls=%async_computation | async-start | bytes 1146880 | tf_op jit(solution)/shard_map/all_to_all | solution.py:1328
  26.1 1.8 multiply_sine_fusion
  27.9 6.8 %collective-permute-done.4.refs_10_ = bf16[256,768]{1,0:T(8,128)(2,1)S(1)} collective-permute-done((bf16[256,768]{1,0:T(8,128)(2,1)}, bf16[256,768]{1,0:T(8,128)(2,1)S(1)}, u32[]{:S(2)}, u32[]{:S(2)}) %collective-permute-start.4) | collective-permute-done | bytes 393248 | tf_op jit(solution)/shard_map/ppermute | solution.py:438
  35.0 1.5 collective-permute-start.5
  37.0 19.1 %all-to-all-done.refs_13_ = bf16[4,112,576]{2,1,0:T(8,128)(2,1)} async-done(((bf16[4,112,576]{2,1,0:T(8,128)(2,1)}), bf16[4,112,576]{2,1,0:T(8,128)(2,1)}, u32[]{:S(2)}, u32[]{:S(2)}) %all-to-all-start) | async-done | bytes 516128 | tf_op jit(solution)/shard_map/all_to_all | solution.py:1328
  56.2 1.0 slice.108
  57.4 4.1 %all-gather.3.cloned.1.call-done = bf16[960,768]{1,0:T(8,128)(2,1)} async-done(((bf16[240,768]{1,0:T(8,128)(2,1)}), bf16[960,768]{1,0:T(8,128)(2,1)}) %all-gather.3.cloned.1.call-update) | async-done | bytes 1474576 | tf_op jit(solution)/shard_map/all_gather | solution.py:1356
  61.5 2.0 gather_fusion
  63.7 2.4 collective-permute-start.12
  68.7 13.2 %shard_map.213 = (bf16[8,192,256]{2,1,0:T(8,128)(2,1)}, bf16[4,384,256]{2,1,0:T(8,128)(2,1)}, bf16[4,384,256]{2,1,0:T(8,128)(2,1)}, bf16[8,256,768]{2,1,0:T(8,12...) custom-call(s32[20]{0:T(128)} %concatenate.25.refs_0_, f32[1,768]{1,0:T(1,128)} %reshape.343.refs_1_, ...), custom_call_target="tpu_custom_call" | custom-call | flops 2 | bytes 1 | tf_op jit(solution)/shard_map/pallas_call | solution.py:490
  82.0 1.3 collective-permute-start.9
  83.3 1.3 collective-permute-start.8
  85.4 1.3 collective-permute-done.8.refs_5_.refs_2_.refs_9_
  86.7 0.9 copy-done.2
  87.7 18.5 %shard_map.214 = (bf16[8,192,256]{2,1,0:T(8,128)(2,1)}, f32[8,192,256]{2,1,0:T(8,128)}, f32[8,8,768]{2,1,0:T(8,128)}) custom-call(s32[20]{0:T(128)} %concatenate.25.refs_0_, s32[8,8,256]{2,1,0:T(8,128)} %pad.8.refs_1_, bf16[8,192,256]{2,1,0:T(8,128)(2,1)} %get-tuple-element.123.refs_2_.refs_6_, ...), custom_call_target="tpu_custom_call" | custom-call | flops 5 | bytes 1 | tf_op jit(solution)/shard_map/pallas_call | solution.py:490
  106.1 8.5 %collective-permute-done.11.refs_8_.refs_10_ = bf16[3,240,768]{2,1,0:T(8,128)(2,1)} collective-permute-done((bf16[3,240,768]{2,1,0:T(8,128)(2,1)S(1)}, bf16[3,240,768]{2,1,0:T(8,128)(2,1)}, u32[]{:S(2)}, u32[]{:S(2)}) %collective-permute-start.11) | collective-permute-done | bytes 1105952 | tf_op jit(solution)/shard_map/ppermute | solution.py:438
  114.7 3.5 %all-to-all-start.1 = ((bf16[8,192,256]{2,1,0:T(8,128)(2,1)}), bf16[8,192,256]{2,1,0:T(8,128)(2,1)S(1)}, u32[]{:S(2)}, u32[]{:S(2)}) async-start(bf16[8,192,256]{2,1,0:T(8,128)(2,1)} %get-tuple-element.128), calls=%async_computation.1 | async-start | bytes 1572864 | tf_op jit(solution)/shard_map/all_to_all | solution.py:1319
  118.6 1.0 pad_maximum_fusion.refs_3_.refs_9_
  120.5 6.6 %shard_map.215 = (bf16[2,8,256,192]{3,2,1,0:T(8,128)(2,1)}, bf16[2,8,256,192]{3,2,1,0:T(8,128)(2,1)}) custom-call(bf16[4,384,256]{2,1,0:T(8,128)(2,1)} %get-tuple-element.129.refs_3_.refs_0_.refs_7_, bf16[4,384,256]{2,1,0:T(8,128)(2,1)} %get-tuple-element.130.refs_4_.refs_1_.refs_8_, bf16[4,384,256]{2,1,0:T(8,128)(2,1)} %copy-done.2, ...), custom_call_target="tpu_custom_call" | custom-call | flops 1 | bytes 1 | tf_op jit(solution)/shard_map/pallas_call | solution.py:490
  127.1 3.7 %all-to-all-done.1.refs_4_ = bf16[8,192,256]{2,1,0:T(8,128)(2,1)S(1)} async-done(((bf16[8,192,256]{2,1,0:T(8,128)(2,1)}), bf16[8,192,256]{2,1,0:T(8,128)(2,1)S(1)}, u32[]{:S(2)}, u32[]{:S(2)}) %all-to-all-start.1) | async-done | bytes 786464 | tf_op jit(solution)/shard_map/all_to_all | solution.py:1319
  130.8 0.9 copy-done.6
  131.7 6.3 %shard_map.216 = (f32[2,256,768]{2,1,0:T(8,128)}, bf16[512,768]{1,0:T(8,128)(2,1)}, bf16[2,768,256]{2,1,0:T(8,128)(2,1)}, bf16[768,768]{1,0:T(8,128)(2,1)}) custom-call(s32[20]{0:T(128)} %concatenate.25.refs_0_, f32[1,768]{1,0:T(1,128)} %reshape.340.refs_1_, f32[1,768]{1,0:T(1,128)} %reshape.342.refs_2_, ...), custom_call_target="tpu_custom_call" | custom-call | flops 1 | bytes 1 | tf_op jit(solution)/shard_map/pallas_call | solution.py:490
  138.7 1.8 collective-permute-done.13.refs_3_
  140.5 0.9 copy-done.21
  141.4 24.8 %shard_map.217 = (bf16[512,768]{1,0:T(8,128)(2,1)}, bf16[512,768]{1,0:T(8,128)(2,1)}, bf16[512,768]{1,0:T(8,128)(2,1)}, bf16[512,768]{1,0:T(8,128)(2,1)}, f32[1,...) custom-call(s32[20]{0:T(128)} %concatenate.25.refs_0_, f32[1,1536]{1,0:T(1,128)} %bitcast.90, ...), custom_call_target="tpu_custom_call" | custom-call | flops 15 | bytes 1 | tf_op jit(solution)/shard_map/pallas_call | solution.py:490
  166.2 1.1 copy-done.42
  168.5 1.1 collective-permute-done.15.refs_6_
  169.6 1.1 collective-permute-done.16.refs_7_
  170.7 0.9 copy-done.19
  171.6 8.1 %shard_map.218 = (bf16[2,256,768]{2,1,0:T(8,128)(2,1)}, bf16[2,256,768]{2,1,0:T(8,128)(2,1)}, f32[8,768]{1,0:T(8,128)}, bf16[8,192,256]{2,1,0:T(8,128)(2,1)}) custom-call(s32[20]{0:T(128)} %concatenate.25.refs_0_, f32[1,768]{1,0:T(1,128)} %reshape.340.refs_1_, f32[1,768]{1,0:T(1,128)} %reshape.341.refs_2_, f32[2,256,768]{2,1,0:T(8,128)} %get-tuple-element.140.refs_3_, ...), custom_call_target="tpu_custom_call" | custom-call | flops 1 | bytes 1 | tf_op jit(solution)/shard_map/pallas_call | solution.py:490
  179.7 3.6 %all-to-all-start.2 = ((bf16[8,192,256]{2,1,0:T(8,128)(2,1)}), bf16[8,192,256]{2,1,0:T(8,128)(2,1)S(1)}, u32[]{:S(2)}, u32[]{:S(2)}) async-start(bf16[8,192,256]{2,1,0:T(8,128)(2,1)} %get-tuple-element.154), calls=%async_computation.2 | async-start | bytes 1572864 | tf_op jit(solution)/shard_map/all_to_all | solution.py:1319
  183.5 6.3 %shard_map.219 = (bf16[4,144,768]{2,1,0:T(8,128)(2,1)}, bf16[4,144,768]{2,1,0:T(8,128)(2,1)}, bf16[4,144,768]{2,1,0:T(8,128)(2,1)}, bf16[4,144,768]{2,1,0:T(8,128)(2,1)}) custom-call(s32[20]{0:T(128)} %concatenate.25.refs_0_, bf16[2,768,256]{2,1,0:T(8,128)(2,1)} %get-tuple-element.157.refs_1_, bf16[2,256,768]{2,1,0:T(8,128)(2,1)} %get-tuple-element.149.refs_2_.refs_4_, ...), custom_call_target="tpu_custom_call" | custom-call | flops 1 | bytes 1 | tf_op jit(solution)/shard_map/pallas_call | solution.py:490
  190.6 5.3 %all-to-all-done.2.refs_13_ = bf16[8,192,256]{2,1,0:T(8,128)(2,1)S(1)} async-done(((bf16[8,192,256]{2,1,0:T(8,128)(2,1)}), bf16[8,192,256]{2,1,0:T(8,128)(2,1)S(1)}, u32[]{:S(2)}, u32[]{:S(2)}) %all-to-all-start.2) | async-done | bytes 786464 | tf_op jit(solution)/shard_map/all_to_all | solution.py:1319
  197.0 2.4 collective-permute-start.21
  199.3 26.1 %shard_map.220 = (bf16[8,192,256]{2,1,0:T(8,128)(2,1)}, bf16[8,384,256]{2,1,0:T(8,128)(2,1)}, bf16[4,384,256]{2,1,0:T(8,128)(2,1)}, bf16[4,384,256]{2,1,0:T(8,128)(2,1)}) custom-call(s32[20]{0:T(128)} %concatenate.25.refs_0_, s32[8,8,256]{2,1,0:T(8,128)} %pad.8.refs_1_, f32[8,32,256]{2,1,0:T(8,128)} %get-tuple-element.116.refs_3_.refs_2_.cos, ...), custom_call_target="tpu_custom_call" | custom-call | flops 11 | bytes 1 | tf_op jit(solution)/shard_map/pallas_call | solution.py:490
  225.4 1.3 collective-permute-start.17
  226.7 1.3 collective-permute-start.18
  228.0 8.9 %collective-permute-done.20 = bf16[4,144,768]{2,1,0:T(8,128)(2,1)S(1)} collective-permute-done((bf16[4,144,768]{2,1,0:T(8,128)(2,1)}, bf16[4,144,768]{2,1,0:T(8,128)(2,1)S(1)}, u32[]{:S(2)}, u32[]{:S(2)}) %collective-permute-start.20) | collective-permute-done | bytes 884768 | tf_op jit(solution)/shard_map/ppermute | solution.py:438
  237.0 1.4 add_convert_fusion
  238.3 0.9 copy-done.16
  239.5 13.8 %shard_map.221 = (bf16[2,256,768]{2,1,0:T(8,128)(2,1)}, bf16[2,256,768]{2,1,0:T(8,128)(2,1)}, f32[4,256,768]{2,1,0:T(8,128)}, bf16[4,216,640]{2,1,0:T(8,128)(2,1)}) custom-call(bf16[8,384,256]{2,1,0:T(8,128)(2,1)} %get-tuple-element.164.own, bf16[4,384,256]{2,1,0:T(8,128)(2,1)} %copy-done.16, bf16[4,384,256]{2,1,0:T(8,128)(2,1)} %copy-done.17, ...), custom_call_target="tpu_custom_call" | custom-call | flops 4 | bytes 1 | tf_op jit(solution)/shard_map/pallas_call | solution.py:1202
  253.7 1.5 collective-permute-start.24
  255.2 16.9 %collective-permute-done.22 = bf16[2,256,768]{2,1,0:T(8,128)(2,1)S(1)} collective-permute-done((bf16[2,256,768]{2,1,0:T(8,128)(2,1)}, bf16[2,256,768]{2,1,0:T(8,128)(2,1)S(1)}, u32[]{:S(2)}, u32[]{:S(2)}) %collective-permute-start.22) | collective-permute-done | bytes 786464 | tf_op jit(solution)/shard_map/ppermute | solution.py:438
  273.0 0.9 copy-done.14
  273.9 2.8 fusion.2
  277.6 1.2 collective-permute-start.23
  279.2 0.9 slice.123
  280.0 1.0 slice.122
  281.0 0.8 pad_maximum_fusion.1
  281.9 4.3 %collective-permute-done.25 = bf16[256,768]{1,0:T(8,128)(2,1)S(1)} collective-permute-done((bf16[256,768]{1,0:T(8,128)(2,1)}, bf16[256,768]{1,0:T(8,128)(2,1)S(1)}, u32[]{:S(2)}, u32[]{:S(2)}) %collective-permute-start.25) | collective-permute-done | bytes 393248 | tf_op jit(solution)/shard_map/ppermute | solution.py:438
  287.0 2.3 fusion
  289.3 3.5 %all-to-all-start.3 = ((bf16[8,48,640]{2,1,0:T(8,128)(2,1)}), bf16[8,48,640]{2,1,0:T(8,128)(2,1)S(1)}, u32[]{:S(2)}, u32[]{:S(2)}) async-start(bf16[8,48,640]{2,1,0:T(8,128)(2,1)} %pad_maximum_fusion.1), calls=%async_computation.4 | async-start | bytes 983040 | tf_op jit(solution)/shard_map/all_to_all | solution.py:1319
  292.8 1.8 slice_bitcast_fusion.1
  294.6 2.8 collective-permute-start.29
  298.9 5.1 %shard_map.222 = bf16[2,256,768]{2,1,0:T(8,128)(2,1)} custom-call(s32[20]{0:T(128)} %concatenate.25.refs_0_, f32[1,768]{1,0:T(1,128)} %reshape.343.refs_1_, f32[1,768]{1,0:T(1,128)} %reshape.342.refs_2_, bf16[2,256,768]{2,1,0:T(8,128)(2,1)} %pad_maximum_fusion.refs_3_.refs_9_, bf16[2,256,768]{2,1,0:T(8,128)(2,1)} %get-tuple-element.149.refs_2_.refs_4_, ...), custom_call_target="tpu_custom_call" | custom-call | flops 1 | bytes 1 | tf_op jit(solution)/shard_map/pallas_call | solution.py:490
  303.9 0.9 reduce-scatter.8.cloned.1.call-done.refs_4_
  304.9 0.9 dynamic-slice_bitcast_fusion
  309.1 3.9 %shard_map.223 = (f32[24,2304]{1,0:T(8,128)}, f32[24,768]{1,0:T(8,128)}, f32[24,3072]{1,0:T(8,128)}, f32[96,768]{1,0:T(8,128)}, f32[1,96]{1,0:T(1,128)}, /*index=5*/f32[4,24]{1,0:T(4,128)}) custom-call(s32[20]{0:T(128)} %concatenate.25.refs_0_, f32[2,384]{1,0:T(2,128)} %reshape_reshape.6.refs_1_, f32[2,384]{1,0:T(2,128)} %reshape_reshape.7.refs_2_, ...), custom_call_target="tpu_custom_call" | custom-call | flops 1 | bytes 1 | tf_op jit(solution)/shard_map/pallas_call | solution.py:490
  313.0 1.3 slice_bitcast_fusion.5
  (184 shorter events, 22.4 us)
Async XLA Ops:
  7.2 54.3 %all-gather.3.cloned.1.call-start = ((), (), s32[]{:S(2)}) async-start(), calls=%async_computation.9 | async-start | bytes 1843200 | tf_op jit(solution)/shard_map/all_gather | solution.py:1356
  7.8 3.1 copy-start.43
  7.8 3.1 copy-start.5
  10.8 4.8 %copy-start.44 = (s32[1,16]{1,0:T(1,128)S(1)}, s32[1,16]{1,0:T(1,128)}, u32[]{:S(2)}) copy-start(s32[1,16]{1,0:T(1,128)} %param.15) | copy-start | bytes 196
  10.8 5.3 %copy-start.36 = (bf16[768]{0:T(1024)(128)(2,1)S(1)}, bf16[768]{0:T(1024)(128)(2,1)}, u32[]{:S(2)}) copy-start(bf16[768]{0:T(1024)(128)(2,1)} %param.19) | copy-start | bytes 4612
  10.8 5.3 %copy-start.37 = (bf16[192]{0:T(256)(128)(2,1)S(1)}, bf16[192]{0:T(256)(128)(2,1)}, u32[]{:S(2)}) copy-start(bf16[192]{0:T(256)(128)(2,1)} %param.21) | copy-start | bytes 1156
  10.8 5.3 %copy-start.38 = (bf16[192]{0:T(256)(128)(2,1)S(1)}, bf16[192]{0:T(256)(128)(2,1)}, u32[]{:S(2)}) copy-start(bf16[192]{0:T(256)(128)(2,1)} %param.22) | copy-start | bytes 1156
  10.8 5.3 %copy-start.39 = (bf16[192]{0:T(256)(128)(2,1)S(1)}, bf16[192]{0:T(256)(128)(2,1)}, u32[]{:S(2)}) copy-start(bf16[192]{0:T(256)(128)(2,1)} %param.23) | copy-start | bytes 1156
  10.8 5.2 %copy-start.40 = (bf16[192]{0:T(256)(128)(2,1)S(1)}, bf16[192]{0:T(256)(128)(2,1)}, u32[]{:S(2)}) copy-start(bf16[192]{0:T(256)(128)(2,1)} %param.24) | copy-start | bytes 1156
  10.9 6.6 %copy-start.10 = (bf16[192,2304]{1,0:T(8,128)(2,1)S(1)}, bf16[192,2304]{1,0:T(8,128)(2,1)}, u32[]{:S(2)}) copy-start(bf16[192,2304]{1,0:T(8,128)(2,1)} %param.16) | copy-start | bytes 2654212
  11.1 6.8 %copy-start.9 = (bf16[256,768]{1,0:T(8,128)(2,1)}, bf16[256,768]{1,0:T(8,128)(2,1)S(1)}, u32[]{:S(2)}) copy-start(bf16[256,768]{1,0:T(8,128)(2,1)S(1)} %get-tuple-element.219.refs_5_) | copy-start | bytes 1179652
  11.1 16.8 %collective-permute-start.1 = (bf16[256,768]{1,0:T(8,128)(2,1)S(1)}, bf16[256,768]{1,0:T(8,128)(2,1)S(1)}, u32[]{:S(2)}, u32[]{:S(2)}) collective-permute-start(bf16[256,768]{1,0:T(8,128)(2,1)S(1)} %get-tuple-element.219.refs_5_), channel_id=1, source_target_pairs={{0,16},{4,20},{8,24},{12,28},{16,0},{20,4},{24,8},{28,12},{1,17},{... | collective-permute-start | bytes 1179656 | tf_op jit(solution)/shard_map/ppermute | solution.py:438
  14.1 13.8 %collective-permute-start = (bf16[256,768]{1,0:T(8,128)(2,1)S(1)}, bf16[256,768]{1,0:T(8,128)(2,1)S(1)}, u32[]{:S(2)}, u32[]{:S(2)}) collective-permute-start(bf16[256,768]{1,0:T(8,128)(2,1)S(1)} %get-tuple-element.219.refs_5_), channel_id=1, source_target_pairs={{0,8},{4,12},{8,0},{12,4},{16,24},{20,28},{24,16},{28,20},{1,9},{5... | collective-permute-start | bytes 1179656 | tf_op jit(solution)/shard_map/ppermute | solution.py:438
  15.6 1.9 collective-permute-start.2
  18.8 37.3 %all-to-all-start = ((bf16[4,112,576]{2,1,0:T(8,128)(2,1)}), bf16[4,112,576]{2,1,0:T(8,128)(2,1)}, u32[]{:S(2)}, u32[]{:S(2)}) async-start(bf16[4,112,576]{2,1,0:T(8,128)(2,1)} %broadcast_in_dim.92), calls=%async_computation | async-start | bytes 1146880 | tf_op jit(solution)/shard_map/all_to_all | solution.py:1328
  23.6 11.1 %collective-permute-start.4 = (bf16[256,768]{1,0:T(8,128)(2,1)}, bf16[256,768]{1,0:T(8,128)(2,1)S(1)}, u32[]{:S(2)}, u32[]{:S(2)}) collective-permute-start(bf16[256,768]{1,0:T(8,128)(2,1)} %collective-permute-done.2.refs_6_), channel_id=1, source_target_pairs={{0,16},{4,20},{8,24},{12,28},{16,0},{20,4},{24,8},{28,12},{1,17},{... | collective-permute-start | bytes 1179656 | tf_op jit(solution)/shard_map/ppermute | solution.py:438
  24.2 10.8 %collective-permute-start.3 = (bf16[256,768]{1,0:T(8,128)(2,1)}, bf16[256,768]{1,0:T(8,128)(2,1)S(1)}, u32[]{:S(2)}, u32[]{:S(2)}) collective-permute-start(bf16[256,768]{1,0:T(8,128)(2,1)} %collective-permute-done.2.refs_6_), channel_id=1, source_target_pairs={{0,8},{4,12},{8,0},{12,4},{16,24},{20,28},{24,16},{28,20},{1,9},{5... | collective-permute-start | bytes 1179656 | tf_op jit(solution)/shard_map/ppermute | solution.py:438
  27.9 35.8 %copy-start.24 = (bf16[256,768]{1,0:T(8,128)(2,1)}, bf16[256,768]{1,0:T(8,128)(2,1)S(1)}, u32[]{:S(2)}) copy-start(bf16[256,768]{1,0:T(8,128)(2,1)S(1)} %collective-permute-done.1.refs_9_) | copy-start | bytes 1179652
  27.9 33.6 %copy-start.25 = (bf16[256,768]{1,0:T(8,128)(2,1)}, bf16[256,768]{1,0:T(8,128)(2,1)S(1)}, u32[]{:S(2)}) copy-start(bf16[256,768]{1,0:T(8,128)(2,1)S(1)} %collective-permute-done.refs_7_) | copy-start | bytes 1179652
  34.7 26.8 %copy-start.26 = (bf16[256,768]{1,0:T(8,128)(2,1)}, bf16[256,768]{1,0:T(8,128)(2,1)S(1)}, u32[]{:S(2)}) copy-start(bf16[256,768]{1,0:T(8,128)(2,1)S(1)} %collective-permute-done.4.refs_10_) | copy-start | bytes 1179652
  35.0 26.6 %copy-start.27 = (bf16[256,768]{1,0:T(8,128)(2,1)}, bf16[256,768]{1,0:T(8,128)(2,1)S(1)}, u32[]{:S(2)}) copy-start(bf16[256,768]{1,0:T(8,128)(2,1)S(1)} %collective-permute-done.3.refs_8_) | copy-start | bytes 1179652
  35.0 21.1 %collective-permute-start.5 = (bf16[256,768]{1,0:T(8,128)(2,1)S(1)}, bf16[256,768]{1,0:T(8,128)(2,1)S(1)}, u32[]{:S(2)}, u32[]{:S(2)}) collective-permute-start(bf16[256,768]{1,0:T(8,128)(2,1)S(1)} %collective-permute-done.refs_7_), channel_id=1, source_target_pairs={{0,16},{4,20},{8,24},{12,28},{16,0},{20,4},{24,8},{28,12},{1,17},{... | collective-permute-start | bytes 1179656 | tf_op jit(solution)/shard_map/ppermute | solution.py:438
  36.5 19.6 %collective-permute-start.6 = (bf16[256,768]{1,0:T(8,128)(2,1)S(1)}, bf16[256,768]{1,0:T(8,128)(2,1)S(1)}, u32[]{:S(2)}, u32[]{:S(2)}) collective-permute-start(bf16[256,768]{1,0:T(8,128)(2,1)S(1)} %collective-permute-done.4.refs_10_), channel_id=1, source_target_pairs={{0,8},{4,12},{8,0},{12,4},{16,24},{20,28},{24,16},{28,20},{1,9},{5... | collective-permute-start | bytes 1179656 | tf_op jit(solution)/shard_map/ppermute | solution.py:438
  56.1 5.5 %copy-start.28 = (bf16[256,768]{1,0:T(8,128)(2,1)}, bf16[256,768]{1,0:T(8,128)(2,1)S(1)}, u32[]{:S(2)}) copy-start(bf16[256,768]{1,0:T(8,128)(2,1)S(1)} %collective-permute-done.5.refs_11_) | copy-start | bytes 1179652
  56.1 5.4 %copy-start.29 = (bf16[256,768]{1,0:T(8,128)(2,1)}, bf16[256,768]{1,0:T(8,128)(2,1)S(1)}, u32[]{:S(2)}) copy-start(bf16[256,768]{1,0:T(8,128)(2,1)S(1)} %collective-permute-done.6.refs_12_) | copy-start | bytes 1179652
  56.1 7.6 %collective-permute-start.7 = (bf16[4,112,576]{2,1,0:T(8,128)(2,1)}, bf16[4,112,576]{2,1,0:T(8,128)(2,1)}, u32[]{:S(2)}, u32[]{:S(2)}) collective-permute-start(bf16[4,112,576]{2,1,0:T(8,128)(2,1)} %all-to-all-done.refs_13_), channel_id=1, source_target_pairs={{0,4},{4,0},{8,12},{12,8},{16,20},{20,16},{24,28},{28,24},{1,5},{5... | collective-permute-start | bytes 1548296 | tf_op jit(solution)/shard_map/ppermute | solution.py:438
  63.7 18.2 %copy-start = (bf16[3,240,768]{2,1,0:T(8,128)(2,1)}, bf16[3,240,768]{2,1,0:T(8,128)(2,1)S(1)}, u32[]{:S(2)}) copy-start(bf16[3,240,768]{2,1,0:T(8,128)(2,1)S(1)} %broadcast_select_fusion.refs_6_.refs_8_) | copy-start | bytes 3317764
  63.7 42.4 %collective-permute-start.12 = (bf16[3,240,768]{2,1,0:T(8,128)(2,1)S(1)}, bf16[3,240,768]{2,1,0:T(8,128)(2,1)}, u32[]{:S(2)}, u32[]{:S(2)}) collective-permute-start(bf16[3,240,768]{2,1,0:T(8,128)(2,1)S(1)} %broadcast_select_fusion.refs_6_.refs_8_), channel_id=1, source_target_pairs={{0,24},{4,28},{8,16},{12,20},{16,8},{20,12},{24,0},{28,4},{1,25},{... | collective-permute-start | bytes 3317768 | tf_op jit(solution)/shard_map/ppermute | solution.py:438
  66.2 48.5 %collective-permute-start.11 = (bf16[3,240,768]{2,1,0:T(8,128)(2,1)S(1)}, bf16[3,240,768]{2,1,0:T(8,128)(2,1)}, u32[]{:S(2)}, u32[]{:S(2)}) collective-permute-start(bf16[3,240,768]{2,1,0:T(8,128)(2,1)S(1)} %broadcast_select_fusion.refs_6_.refs_8_), channel_id=1, source_target_pairs={{0,16},{4,20},{8,24},{12,28},{16,0},{20,4},{24,8},{28,12},{1,17},{... | collective-permute-start | bytes 3317768 | tf_op jit(solution)/shard_map/ppermute | solution.py:438
  66.7 48.0 %collective-permute-start.10 = (bf16[3,240,768]{2,1,0:T(8,128)(2,1)S(1)}, bf16[3,240,768]{2,1,0:T(8,128)(2,1)}, u32[]{:S(2)}, u32[]{:S(2)}) collective-permute-start(bf16[3,240,768]{2,1,0:T(8,128)(2,1)S(1)} %broadcast_select_fusion.refs_6_.refs_8_), channel_id=1, source_target_pairs={{0,8},{4,12},{8,0},{12,4},{16,24},{20,28},{24,16},{28,20},{1,9},{5... | collective-permute-start | bytes 3317768 | tf_op jit(solution)/shard_map/ppermute | solution.py:438
  82.0 3.4 %collective-permute-start.9 = (bf16[4,384,256]{2,1,0:T(8,128)(2,1)}, bf16[4,384,256]{2,1,0:T(8,128)(2,1)S(1)}, u32[]{:S(2)}, u32[]{:S(2)}) collective-permute-start(bf16[4,384,256]{2,1,0:T(8,128)(2,1)} %get-tuple-element.130.refs_4_.refs_1_.refs_8_), channel_id=1, source_target_pairs={{0,4},{8,12},{16,20},{24,28},{1,5},{9,13},{17,21},{25,29},{2,6},{1... | collective-permute-start | bytes 2359304 | tf_op jit(solution)/shard_map/ppermute | solution.py:1417
  83.3 3.4 %collective-permute-start.8 = (bf16[4,384,256]{2,1,0:T(8,128)(2,1)}, bf16[4,384,256]{2,1,0:T(8,128)(2,1)S(1)}, u32[]{:S(2)}, u32[]{:S(2)}) collective-permute-start(bf16[4,384,256]{2,1,0:T(8,128)(2,1)} %get-tuple-element.129.refs_3_.refs_0_.refs_7_), channel_id=1, source_target_pairs={{0,4},{8,12},{16,20},{24,28},{1,5},{9,13},{17,21},{25,29},{2,6},{1... | collective-permute-start | bytes 2359304 | tf_op jit(solution)/shard_map/ppermute | solution.py:1417
  114.7 16.1 %all-to-all-start.1 = ((bf16[8,192,256]{2,1,0:T(8,128)(2,1)}), bf16[8,192,256]{2,1,0:T(8,128)(2,1)S(1)}, u32[]{:S(2)}, u32[]{:S(2)}) async-start(bf16[8,192,256]{2,1,0:T(8,128)(2,1)} %get-tuple-element.128), calls=%async_computation.1 | async-start | bytes 1572864 | tf_op jit(solution)/shard_map/all_to_all | solution.py:1319
  118.3 2.0 copy-start.7
  118.3 120.0 %reduce-scatter.6.cloned.1.call-start = ((), (), s32[]{:S(2)}) async-start(), calls=%async_computation.7 | async-start | bytes 2949120 | tf_op jit(solution)/shard_map/reduce_scatter | solution.py:1429
  120.3 18.4 %collective-permute-start.14 = (bf16[512,768]{1,0:T(8,128)(2,1)S(1)}, bf16[512,768]{1,0:T(8,128)(2,1)S(1)}, u32[]{:S(2)}, u32[]{:S(2)}) collective-permute-start(bf16[512,768]{1,0:T(8,128)(2,1)S(1)} %bitcast.76), channel_id=1, source_target_pairs={{0,4},{4,0},{8,12},{12,8},{16,20},{20,16},{24,28},{28,24},{1,5},{5... | collective-permute-start | bytes 2359304 | tf_op jit(solution)/shard_map/ppermute | solution.py:438
  138.0 2.6 collective-permute-start.13
  167.3 2.3 collective-permute-start.15
  167.5 3.2 collective-permute-start.16
  179.7 3.7 %copy-start.34 = (f32[1,1536]{1,0:T(1,128)S(1)}, f32[1,1536]{1,0:T(1,128)}, u32[]{:S(2)}) copy-start(f32[1,1536]{1,0:T(1,128)} %get-tuple-element.155) | copy-start | bytes 18436
  179.7 16.1 %all-to-all-start.2 = ((bf16[8,192,256]{2,1,0:T(8,128)(2,1)}), bf16[8,192,256]{2,1,0:T(8,128)(2,1)S(1)}, u32[]{:S(2)}, u32[]{:S(2)}) async-start(bf16[8,192,256]{2,1,0:T(8,128)(2,1)} %get-tuple-element.154), calls=%async_computation.2 | async-start | bytes 1572864 | tf_op jit(solution)/shard_map/all_to_all | solution.py:1319
  183.3 95.9 %reduce-scatter.10.cloned.1.call-start = ((), (), s32[]{:S(2)}) async-start(), calls=%async_computation.10 | async-start | bytes 1382400
  183.5 6.3 %copy-start.35 = (f32[8,768]{1,0:T(8,128)S(1)}, f32[8,768]{1,0:T(8,128)}, u32[]{:S(2)}) copy-start(f32[8,768]{1,0:T(8,128)} %get-tuple-element.156) | copy-start | bytes 73732
  195.8 3.5 %copy-start.3 = (bf16[8,192,256]{2,1,0:T(8,128)(2,1)}, bf16[8,192,256]{2,1,0:T(8,128)(2,1)S(1)}, u32[]{:S(2)}) copy-start(bf16[8,192,256]{2,1,0:T(8,128)(2,1)S(1)} %all-to-all-done.2.refs_13_) | copy-start | bytes 2359300
  195.8 32.2 %collective-permute-start.19 = (bf16[4,144,768]{2,1,0:T(8,128)(2,1)}, bf16[4,144,768]{2,1,0:T(8,128)(2,1)S(1)}, u32[]{:S(2)}, u32[]{:S(2)}) collective-permute-start(bf16[4,144,768]{2,1,0:T(8,128)(2,1)} %get-tuple-element.168), channel_id=1, source_target_pairs={{0,8},{4,12},{8,0},{12,4},{16,24},{20,28},{24,16},{28,20},{1,9},{5... | collective-permute-start | bytes 2654216 | tf_op jit(solution)/shard_map/ppermute | solution.py:438
  196.3 40.6 %collective-permute-start.20 = (bf16[4,144,768]{2,1,0:T(8,128)(2,1)}, bf16[4,144,768]{2,1,0:T(8,128)(2,1)S(1)}, u32[]{:S(2)}, u32[]{:S(2)}) collective-permute-start(bf16[4,144,768]{2,1,0:T(8,128)(2,1)} %get-tuple-element.169), channel_id=1, source_target_pairs={{0,16},{4,20},{8,24},{12,28},{16,0},{20,4},{24,8},{28,12},{1,17},{... | collective-permute-start | bytes 2654216 | tf_op jit(solution)/shard_map/ppermute | solution.py:438
  197.0 40.0 %collective-permute-start.21 = (bf16[4,144,768]{2,1,0:T(8,128)(2,1)}, bf16[4,144,768]{2,1,0:T(8,128)(2,1)S(1)}, u32[]{:S(2)}, u32[]{:S(2)}) collective-permute-start(bf16[4,144,768]{2,1,0:T(8,128)(2,1)} %get-tuple-element.170), channel_id=1, source_target_pairs={{0,24},{4,28},{8,16},{12,20},{16,8},{20,12},{24,0},{28,4},{1,25},{... | collective-permute-start | bytes 2654216 | tf_op jit(solution)/shard_map/ppermute | solution.py:438
  199.3 37.6 %copy-start.11 = (bf16[4,144,768]{2,1,0:T(8,128)(2,1)S(1)}, bf16[4,144,768]{2,1,0:T(8,128)(2,1)}, u32[]{:S(2)}) copy-start(bf16[4,144,768]{2,1,0:T(8,128)(2,1)} %get-tuple-element.172) | copy-start | bytes 2654212
  225.4 12.9 %collective-permute-start.17 = (bf16[4,384,256]{2,1,0:T(8,128)(2,1)}, bf16[4,384,256]{2,1,0:T(8,128)(2,1)S(1)}, u32[]{:S(2)}, u32[]{:S(2)}) collective-permute-start(bf16[4,384,256]{2,1,0:T(8,128)(2,1)} %get-tuple-element.165), channel_id=1, source_target_pairs={{4,0},{12,8},{20,16},{28,24},{5,1},{13,9},{21,17},{29,25},{6,2},{1... | collective-permute-start | bytes 2359304 | tf_op jit(solution)/shard_map/ppermute | solution.py:1448
  226.7 11.6 %collective-permute-start.18 = (bf16[4,384,256]{2,1,0:T(8,128)(2,1)}, bf16[4,384,256]{2,1,0:T(8,128)(2,1)S(1)}, u32[]{:S(2)}, u32[]{:S(2)}) collective-permute-start(bf16[4,384,256]{2,1,0:T(8,128)(2,1)} %get-tuple-element.166), channel_id=1, source_target_pairs={{4,0},{12,8},{20,16},{28,24},{5,1},{13,9},{21,17},{29,25},{6,2},{1... | collective-permute-start | bytes 2359304 | tf_op jit(solution)/shard_map/ppermute | solution.py:1448
  253.3 51.6 %reduce-scatter.8.cloned.1.call-start = ((), (), s32[]{:S(2)}) async-start(), calls=%async_computation.8 | async-start | bytes 1105920 | tf_op jit(solution)/shard_map/reduce_scatter | solution.py:1454
  253.4 18.7 %collective-permute-start.22 = (bf16[2,256,768]{2,1,0:T(8,128)(2,1)}, bf16[2,256,768]{2,1,0:T(8,128)(2,1)S(1)}, u32[]{:S(2)}, u32[]{:S(2)}) collective-permute-start(bf16[2,256,768]{2,1,0:T(8,128)(2,1)} %get-tuple-element.185), channel_id=1, source_target_pairs={{0,8},{4,12},{8,0},{12,4},{16,24},{20,28},{24,16},{28,20},{1,9},{5... | collective-permute-start | bytes 2359304 | tf_op jit(solution)/shard_map/ppermute | solution.py:438
  253.7 18.5 %collective-permute-start.24 = (bf16[2,256,768]{2,1,0:T(8,128)(2,1)}, bf16[2,256,768]{2,1,0:T(8,128)(2,1)S(1)}, u32[]{:S(2)}, u32[]{:S(2)}) collective-permute-start(bf16[2,256,768]{2,1,0:T(8,128)(2,1)} %get-tuple-element.186), channel_id=1, source_target_pairs={{0,16},{4,20},{8,24},{12,28},{16,0},{20,4},{24,8},{28,12},{1,17},{... | collective-permute-start | bytes 2359304 | tf_op jit(solution)/shard_map/ppermute | solution.py:438
  273.9 13.1 %copy-start.4 = (f32[4,256,768]{2,1,0:T(8,128)S(1)}, f32[4,256,768]{2,1,0:T(8,128)}, u32[]{:S(2)}) copy-start(f32[4,256,768]{2,1,0:T(8,128)} %get-tuple-element.184) | copy-start | bytes 9437188
  276.8 9.4 %collective-permute-start.25 = (bf16[256,768]{1,0:T(8,128)(2,1)}, bf16[256,768]{1,0:T(8,128)(2,1)S(1)}, u32[]{:S(2)}, u32[]{:S(2)}) collective-permute-start(bf16[256,768]{1,0:T(8,128)(2,1)} %get-tuple-element.213), channel_id=1, source_target_pairs={{0,8},{4,12},{8,0},{12,4},{16,24},{20,28},{24,16},{28,20},{1,9},{5... | collective-permute-start | bytes 1179656 | tf_op jit(solution)/shard_map/ppermute | solution.py:438
  277.6 9.4 %collective-permute-start.23 = (bf16[256,768]{1,0:T(8,128)(2,1)}, bf16[256,768]{1,0:T(8,128)(2,1)}, u32[]{:S(2)}, u32[]{:S(2)}) collective-permute-start(bf16[256,768]{1,0:T(8,128)(2,1)} %get-tuple-element.214), channel_id=1, source_target_pairs={{0,16},{4,20},{8,24},{12,28},{16,0},{20,4},{24,8},{28,12},{1,17},{... | collective-permute-start | bytes 1179656 | tf_op jit(solution)/shard_map/ppermute | solution.py:438
  279.2 7.8 %copy-start.13 = (bf16[2,256,768]{2,1,0:T(8,128)(2,1)S(1)}, bf16[2,256,768]{2,1,0:T(8,128)(2,1)}, u32[]{:S(2)}) copy-start(bf16[2,256,768]{2,1,0:T(8,128)(2,1)} %copy-done.12) | copy-start | bytes 2359300
  279.2 7.8 %copy-start.15 = (bf16[2,256,768]{2,1,0:T(8,128)(2,1)S(1)}, bf16[2,256,768]{2,1,0:T(8,128)(2,1)}, u32[]{:S(2)}) copy-start(bf16[2,256,768]{2,1,0:T(8,128)(2,1)} %copy-done.14) | copy-start | bytes 2359300
  289.3 8.8 %collective-permute-start.26 = (bf16[256,768]{1,0:T(8,128)(2,1)S(1)}, bf16[256,768]{1,0:T(8,128)(2,1)S(1)}, u32[]{:S(2)}, u32[]{:S(2)}) collective-permute-start(bf16[256,768]{1,0:T(8,128)(2,1)S(1)} %get-tuple-element.211), channel_id=1, source_target_pairs={{0,4},{4,0},{8,12},{12,8},{16,20},{20,16},{24,28},{28,24},{1,5},{5... | collective-permute-start | bytes 1179656 | tf_op jit(solution)/shard_map/ppermute | solution.py:438
  289.3 18.3 %all-to-all-start.3 = ((bf16[8,48,640]{2,1,0:T(8,128)(2,1)}), bf16[8,48,640]{2,1,0:T(8,128)(2,1)S(1)}, u32[]{:S(2)}, u32[]{:S(2)}) async-start(bf16[8,48,640]{2,1,0:T(8,128)(2,1)} %pad_maximum_fusion.1), calls=%async_computation.4 | async-start | bytes 983040 | tf_op jit(solution)/shard_map/all_to_all | solution.py:1319
  294.6 12.5 %collective-permute-start.29 = (bf16[96,768]{1,0:T(8,128)(2,1)S(1)}, bf16[96,768]{1,0:T(8,128)(2,1)S(1)}, u32[]{:S(2)}, u32[]{:S(2)}) collective-permute-start(bf16[96,768]{1,0:T(8,128)(2,1)S(1)} %get-tuple-element.220), channel_id=1, source_target_pairs={{0,24},{4,28},{8,16},{12,20},{16,8},{20,12},{24,0},{28,4},{1,25},{... | collective-permute-start | bytes 442376 | tf_op jit(solution)/shard_map/ppermute | solution.py:438
  297.4 10.1 %collective-permute-start.28 = (bf16[96,768]{1,0:T(8,128)(2,1)S(1)}, bf16[96,768]{1,0:T(8,128)(2,1)S(1)}, u32[]{:S(2)}, u32[]{:S(2)}) collective-permute-start(bf16[96,768]{1,0:T(8,128)(2,1)S(1)} %get-tuple-element.221), channel_id=1, source_target_pairs={{0,16},{4,20},{8,24},{12,28},{16,0},{20,4},{24,8},{28,12},{1,17},{... | collective-permute-start | bytes 442376 | tf_op jit(solution)/shard_map/ppermute | solution.py:438
  298.0 9.6 %collective-permute-start.27 = (bf16[96,768]{1,0:T(8,128)(2,1)S(1)}, bf16[96,768]{1,0:T(8,128)(2,1)S(1)}, u32[]{:S(2)}, u32[]{:S(2)}) collective-permute-start(bf16[96,768]{1,0:T(8,128)(2,1)S(1)} %get-tuple-element.222), channel_id=1, source_target_pairs={{0,8},{4,12},{8,0},{12,4},{16,24},{20,28},{24,16},{28,20},{1,9},{5... | collective-permute-start | bytes 442376 | tf_op jit(solution)/shard_map/ppermute | solution.py:438
  305.8 1.8 collective-permute-start.30
  (20 other events, 19.4 us)
Sparse Core Ops, SparseCore 0:
  11.0 50.4 all-gather.2
  166.3 45.2 reduce-scatter.5
  253.5 25.6 reduce-scatter.9
  281.3 23.5 reduce-scatter.7

commit v6 on v5

--- a/solution.py
+++ b/solution.py
@@ -1157,7 +1157,7 @@
 
     @pl.when(i >= 4)
     def _():
-        stay[0] = ng
+        stay[0] = low
 
     gs_ref[0:1] += jnp.sum(ng * n.astype(F32), axis=0, keepdims=True)
     gs_ref[1:2] += jnp.sum(ng * mk[:, :1].astype(F32), axis=0, keepdims=True)
@@ -1205,7 +1205,7 @@
         out_shape=(
             jax.ShapeDtypeStruct((2, CHUNK, dim), BF),
             jax.ShapeDtypeStruct((2, CHUNK, dim), BF),
-            jax.ShapeDtypeStruct((4, CHUNK, dim), F32),
+            jax.ShapeDtypeStruct((4, CHUNK, dim), BF),
             jax.ShapeDtypeStruct((4, dim // 4 + 24, wide), BF),
         ),
         in_specs=[

time: 322 us -> 322 us (level)
    optimization_barrier x1, waiting for transfers between devices: 0.37 us -> 3.77 us  [after(): return lax.optimization_barrier((value, *needed))[0]]
    ppermute x27, waiting for transfers between devices: 51.4 us -> 48.2 us  [swap(): return lax.ppermute(v, 'ctx', [(i, i ^ bit) for i in range(8)])]
    unnamed x92 -> x84, local copies, waits for them, and re-layouts: 11.4 us -> 9.7 us
where the time goes in v6:
time: 322 us; the launch traced here: 320 us
  Pallas kernels  135 us (42%)
  waiting for transfers between devices  90.2 us (28%)
  starting transfers between devices  43.8 us (14%)
  local copies, waits for them, and re-layouts  25.7 us (8%)
  between operations  14.5 us (5%)
  other arithmetic  10.6 us (3%)
    pallas_call x11, Pallas kernels, call(): pl.pallas_call(run, out_shape=tuple((jax.ShapeDtypeStruct(s, d) for s, d...  122 us
    ppermute x27, waiting for transfers between devices, swap(): return lax.ppermute(v, 'ctx', [(i, i ^ bit) for i in range(8)])  48.2 us
    ppermute x27, starting transfers between devices, swap(): return lax.ppermute(v, 'ctx', [(i, i ^ bit) for i in range(8)])  22.7 us
    all_to_all x1, waiting for transfers between devices, exchange_z(): return lax.all_to_all(v, 'fsdp', 0, 0, tiled=True)  19.1 us
    pallas_call x1, Pallas kernels, project_back(): pl.pallas_call(project_back_body, grid=(8,), out_shape=(jax.ShapeDtypeStr...  13.6 us
    all_to_all x3, starting transfers between devices, exchange(): return lax.all_to_all(v, 'ctx', 0, 0, tiled=True)  10.6 us
    unnamed x84, local copies, waits for them, and re-layouts  9.7 us
    all_to_all x3, waiting for transfers between devices, exchange(): return lax.all_to_all(v, 'ctx', 0, 0, tiled=True)  8.95 us
  transfers between devices with their start and end apart: 39, of which 21 were waited for; matrix products, arithmetic and copies ran while one was open for 8% of the time, Pallas kernels for 28%

profile of v6, /device:TPU:0, one launch (start us, length us, event | category | flops | bytes accessed | tf_op | source)
XLA Modules:
  0.0 320.2 jit_solution(5552782834604448515)
XLA Ops:
  7.8 3.0 shard_map.212
  11.1 3.0 collective-permute-start.1
  14.1 1.5 collective-permute-start
  16.3 1.1 collective-permute-done.2.refs_6_
  17.9 0.9 broadcast_in_dim.92
  18.8 4.9 %all-to-all-start = ((bf16[4,112,576]{2,1,0:T(8,128)(2,1)}), bf16[4,112,576]{2,1,0:T(8,128)(2,1)}, u32[]{:S(2)}, u32[]{:S(2)}) async-start(bf16[4,112,576]{2,1,0:T(8,128)(2,1)} %broadcast_in_dim.92), calls=%async_computation | async-start | bytes 1146880 | tf_op jit(solution)/shard_map/all_to_all | solution.py:1328
  26.1 1.8 multiply_sine_fusion
  27.9 6.8 %collective-permute-done.4.refs_10_ = bf16[256,768]{1,0:T(8,128)(2,1)S(1)} collective-permute-done((bf16[256,768]{1,0:T(8,128)(2,1)}, bf16[256,768]{1,0:T(8,128)(2,1)S(1)}, u32[]{:S(2)}, u32[]{:S(2)}) %collective-permute-start.4) | collective-permute-done | bytes 393248 | tf_op jit(solution)/shard_map/ppermute | solution.py:438
  35.0 1.5 collective-permute-start.5
  37.0 19.1 %all-to-all-done.refs_13_ = bf16[4,112,576]{2,1,0:T(8,128)(2,1)} async-done(((bf16[4,112,576]{2,1,0:T(8,128)(2,1)}), bf16[4,112,576]{2,1,0:T(8,128)(2,1)}, u32[]{:S(2)}, u32[]{:S(2)}) %all-to-all-start) | async-done | bytes 516128 | tf_op jit(solution)/shard_map/all_to_all | solution.py:1328
  56.2 1.0 slice.108
  57.4 4.1 %all-gather.3.cloned.1.call-done = bf16[960,768]{1,0:T(8,128)(2,1)} async-done(((bf16[240,768]{1,0:T(8,128)(2,1)}), bf16[960,768]{1,0:T(8,128)(2,1)}) %all-gather.3.cloned.1.call-update) | async-done | bytes 1474576 | tf_op jit(solution)/shard_map/all_gather | solution.py:1356
  61.5 2.0 gather_fusion
  63.8 2.4 collective-permute-start.12
  68.7 13.2 %shard_map.213 = (bf16[8,192,256]{2,1,0:T(8,128)(2,1)}, bf16[4,384,256]{2,1,0:T(8,128)(2,1)}, bf16[4,384,256]{2,1,0:T(8,128)(2,1)}, bf16[8,256,768]{2,1,0:T(8,12...) custom-call(s32[20]{0:T(128)} %concatenate.25.refs_0_, f32[1,768]{1,0:T(1,128)} %reshape.347.refs_1_, ...), custom_call_target="tpu_custom_call" | custom-call | flops 2 | bytes 1 | tf_op jit(solution)/shard_map/pallas_call | solution.py:490
  82.0 1.3 collective-permute-start.9
  83.3 1.3 collective-permute-start.8
  85.4 1.3 collective-permute-done.8.refs_5_.refs_2_.refs_9_
  86.7 1.0 copy-done.2
  87.7 18.5 %shard_map.214 = (bf16[8,192,256]{2,1,0:T(8,128)(2,1)}, f32[8,192,256]{2,1,0:T(8,128)}, f32[8,8,768]{2,1,0:T(8,128)}) custom-call(s32[20]{0:T(128)} %concatenate.25.refs_0_, s32[8,8,256]{2,1,0:T(8,128)} %pad.8.refs_1_, bf16[8,192,256]{2,1,0:T(8,128)(2,1)} %get-tuple-element.123.refs_2_.refs_6_, ...), custom_call_target="tpu_custom_call" | custom-call | flops 5 | bytes 1 | tf_op jit(solution)/shard_map/pallas_call | solution.py:490
  106.2 8.5 %collective-permute-done.11.refs_8_.refs_10_ = bf16[3,240,768]{2,1,0:T(8,128)(2,1)} collective-permute-done((bf16[3,240,768]{2,1,0:T(8,128)(2,1)S(1)}, bf16[3,240,768]{2,1,0:T(8,128)(2,1)}, u32[]{:S(2)}, u32[]{:S(2)}) %collective-permute-start.11) | collective-permute-done | bytes 1105952 | tf_op jit(solution)/shard_map/ppermute | solution.py:438
  114.7 3.5 %all-to-all-start.1 = ((bf16[8,192,256]{2,1,0:T(8,128)(2,1)}), bf16[8,192,256]{2,1,0:T(8,128)(2,1)S(1)}, u32[]{:S(2)}, u32[]{:S(2)}) async-start(bf16[8,192,256]{2,1,0:T(8,128)(2,1)} %get-tuple-element.128), calls=%async_computation.1 | async-start | bytes 1572864 | tf_op jit(solution)/shard_map/all_to_all | solution.py:1319
  118.6 1.0 pad_maximum_fusion.refs_3_.refs_9_
  120.5 6.6 %shard_map.215 = (bf16[2,8,256,192]{3,2,1,0:T(8,128)(2,1)}, bf16[2,8,256,192]{3,2,1,0:T(8,128)(2,1)}) custom-call(bf16[4,384,256]{2,1,0:T(8,128)(2,1)} %get-tuple-element.129.refs_3_.refs_0_.refs_7_, bf16[4,384,256]{2,1,0:T(8,128)(2,1)} %get-tuple-element.130.refs_4_.refs_1_.refs_8_, bf16[4,384,256]{2,1,0:T(8,128)(2,1)} %copy-done.2, ...), custom_call_target="tpu_custom_call" | custom-call | flops 1 | bytes 1 | tf_op jit(solution)/shard_map/pallas_call | solution.py:490
  127.1 3.7 %all-to-all-done.1.refs_4_ = bf16[8,192,256]{2,1,0:T(8,128)(2,1)S(1)} async-done(((bf16[8,192,256]{2,1,0:T(8,128)(2,1)}), bf16[8,192,256]{2,1,0:T(8,128)(2,1)S(1)}, u32[]{:S(2)}, u32[]{:S(2)}) %all-to-all-start.1) | async-done | bytes 786464 | tf_op jit(solution)/shard_map/all_to_all | solution.py:1319
  130.8 0.9 copy-done.5
  131.7 6.3 %shard_map.216 = (f32[2,256,768]{2,1,0:T(8,128)}, bf16[512,768]{1,0:T(8,128)(2,1)}, bf16[2,768,256]{2,1,0:T(8,128)(2,1)}, bf16[768,768]{1,0:T(8,128)(2,1)}) custom-call(s32[20]{0:T(128)} %concatenate.25.refs_0_, f32[1,768]{1,0:T(1,128)} %reshape.344.refs_1_, f32[1,768]{1,0:T(1,128)} %reshape.346.refs_2_, ...), custom_call_target="tpu_custom_call" | custom-call | flops 1 | bytes 1 | tf_op jit(solution)/shard_map/pallas_call | solution.py:490
  138.7 1.8 collective-permute-done.13.refs_3_
  140.6 0.9 copy-done.17
  141.4 24.8 %shard_map.217 = (bf16[512,768]{1,0:T(8,128)(2,1)}, bf16[512,768]{1,0:T(8,128)(2,1)}, bf16[512,768]{1,0:T(8,128)(2,1)}, bf16[512,768]{1,0:T(8,128)(2,1)}, f32[1,...) custom-call(s32[20]{0:T(128)} %concatenate.25.refs_0_, f32[1,1536]{1,0:T(1,128)} %bitcast.90, ...), custom_call_target="tpu_custom_call" | custom-call | flops 15 | bytes 1 | tf_op jit(solution)/shard_map/pallas_call | solution.py:490
  166.2 1.1 copy-done.38
  168.5 1.1 collective-permute-done.15.refs_6_
  169.6 1.1 collective-permute-done.16.refs_7_
  170.7 0.9 copy-done.15
  171.6 8.1 %shard_map.218 = (bf16[2,256,768]{2,1,0:T(8,128)(2,1)}, bf16[2,256,768]{2,1,0:T(8,128)(2,1)}, f32[8,768]{1,0:T(8,128)}, bf16[8,192,256]{2,1,0:T(8,128)(2,1)}) custom-call(s32[20]{0:T(128)} %concatenate.25.refs_0_, f32[1,768]{1,0:T(1,128)} %reshape.344.refs_1_, f32[1,768]{1,0:T(1,128)} %reshape.345.refs_2_, f32[2,256,768]{2,1,0:T(8,128)} %get-tuple-element.140.refs_3_, ...), custom_call_target="tpu_custom_call" | custom-call | flops 1 | bytes 1 | tf_op jit(solution)/shard_map/pallas_call | solution.py:490
  179.8 3.6 %all-to-all-start.2 = ((bf16[8,192,256]{2,1,0:T(8,128)(2,1)}), bf16[8,192,256]{2,1,0:T(8,128)(2,1)S(1)}, u32[]{:S(2)}, u32[]{:S(2)}) async-start(bf16[8,192,256]{2,1,0:T(8,128)(2,1)} %get-tuple-element.154), calls=%async_computation.2 | async-start | bytes 1572864 | tf_op jit(solution)/shard_map/all_to_all | solution.py:1319
  183.5 6.4 %shard_map.219 = (bf16[4,144,768]{2,1,0:T(8,128)(2,1)}, bf16[4,144,768]{2,1,0:T(8,128)(2,1)}, bf16[4,144,768]{2,1,0:T(8,128)(2,1)}, bf16[4,144,768]{2,1,0:T(8,128)(2,1)}) custom-call(s32[20]{0:T(128)} %concatenate.25.refs_0_, bf16[2,768,256]{2,1,0:T(8,128)(2,1)} %get-tuple-element.157.refs_1_, bf16[2,256,768]{2,1,0:T(8,128)(2,1)} %get-tuple-element.149.refs_2_.refs_4_, ...), custom_call_target="tpu_custom_call" | custom-call | flops 1 | bytes 1 | tf_op jit(solution)/shard_map/pallas_call | solution.py:490
  190.6 5.2 %all-to-all-done.2.refs_13_ = bf16[8,192,256]{2,1,0:T(8,128)(2,1)S(1)} async-done(((bf16[8,192,256]{2,1,0:T(8,128)(2,1)}), bf16[8,192,256]{2,1,0:T(8,128)(2,1)S(1)}, u32[]{:S(2)}, u32[]{:S(2)}) %all-to-all-start.2) | async-done | bytes 786464 | tf_op jit(solution)/shard_map/all_to_all | solution.py:1319
  197.0 2.4 collective-permute-start.21
  199.4 26.1 %shard_map.220 = (bf16[8,192,256]{2,1,0:T(8,128)(2,1)}, bf16[8,384,256]{2,1,0:T(8,128)(2,1)}, bf16[4,384,256]{2,1,0:T(8,128)(2,1)}, bf16[4,384,256]{2,1,0:T(8,128)(2,1)}) custom-call(s32[20]{0:T(128)} %concatenate.25.refs_0_, s32[8,8,256]{2,1,0:T(8,128)} %pad.8.refs_1_, f32[8,32,256]{2,1,0:T(8,128)} %get-tuple-element.116.refs_3_.refs_2_.cos, ...), custom_call_target="tpu_custom_call" | custom-call | flops 11 | bytes 1 | tf_op jit(solution)/shard_map/pallas_call | solution.py:490
  225.5 1.3 collective-permute-start.17
  226.8 1.3 collective-permute-start.18
  228.1 8.9 %collective-permute-done.20 = bf16[4,144,768]{2,1,0:T(8,128)(2,1)S(1)} collective-permute-done((bf16[4,144,768]{2,1,0:T(8,128)(2,1)}, bf16[4,144,768]{2,1,0:T(8,128)(2,1)S(1)}, u32[]{:S(2)}, u32[]{:S(2)}) %collective-permute-start.20) | collective-permute-done | bytes 884768 | tf_op jit(solution)/shard_map/ppermute | solution.py:438
  237.0 1.4 add_convert_fusion
  238.4 0.9 copy-done.12
  239.5 13.6 %shard_map.221 = (bf16[2,256,768]{2,1,0:T(8,128)(2,1)}, bf16[2,256,768]{2,1,0:T(8,128)(2,1)}, bf16[4,256,768]{2,1,0:T(8,128)(2,1)}, bf16[4,216,640]{2,1,0:T(8,128)(2,1)}) custom-call(bf16[8,384,256]{2,1,0:T(8,128)(2,1)} %get-tuple-element.164.own, bf16[4,384,256]{2,1,0:T(8,128)(2,1)} %copy-done.12, bf16[4,384,256]{2,1,0:T(8,128)(2,1)} %copy-done.13, ...), custom_call_target="tpu_custom_call" | custom-call | flops 4 | bytes 1 | tf_op jit(solution)/shard_map/pallas_call | solution.py:1202
  253.5 1.4 collective-permute-start.24
  255.0 16.9 %collective-permute-done.22 = bf16[2,256,768]{2,1,0:T(8,128)(2,1)S(1)} collective-permute-done((bf16[2,256,768]{2,1,0:T(8,128)(2,1)}, bf16[2,256,768]{2,1,0:T(8,128)(2,1)S(1)}, u32[]{:S(2)}, u32[]{:S(2)}) %collective-permute-start.22) | collective-permute-done | bytes 786464 | tf_op jit(solution)/shard_map/ppermute | solution.py:438
  272.0 1.1 fusion.2
  273.1 1.7 collective-permute-start.25
  275.1 3.8 %reduce-scatter.10.cloned.1.call-done = bf16[216,640]{1,0:T(8,128)(2,1)} async-done(((bf16[864,640]{1,0:T(8,128)(2,1)}), bf16[216,640]{1,0:T(8,128)(2,1)}) %reduce-scatter.10.cloned.1.call-update) | async-done | bytes 276496 | tf_op jit(solution)/shard_map/optimization_barrier | solution.py:1311
  278.9 0.8 slice.123
  279.7 1.0 slice.122
  280.7 0.8 pad_maximum_fusion.1
  281.5 0.9 collective-permute-done.25
  283.7 2.3 fusion
  286.0 3.5 %all-to-all-start.3 = ((bf16[8,48,640]{2,1,0:T(8,128)(2,1)}), bf16[8,48,640]{2,1,0:T(8,128)(2,1)S(1)}, u32[]{:S(2)}, u32[]{:S(2)}) async-start(bf16[8,48,640]{2,1,0:T(8,128)(2,1)} %pad_maximum_fusion.1), calls=%async_computation.4 | async-start | bytes 983040 | tf_op jit(solution)/shard_map/all_to_all | solution.py:1319
  289.5 1.8 slice_bitcast_fusion.1
  291.3 2.8 collective-permute-start.29
  295.6 5.1 %shard_map.222 = bf16[2,256,768]{2,1,0:T(8,128)(2,1)} custom-call(s32[20]{0:T(128)} %concatenate.25.refs_0_, f32[1,768]{1,0:T(1,128)} %reshape.347.refs_1_, f32[1,768]{1,0:T(1,128)} %reshape.346.refs_2_, bf16[2,256,768]{2,1,0:T(8,128)(2,1)} %pad_maximum_fusion.refs_3_.refs_9_, bf16[2,256,768]{2,1,0:T(8,128)(2,1)} %get-tuple-element.149.refs_2_.refs_4_, ...), custom_call_target="tpu_custom_call" | custom-call | flops 1 | bytes 1 | tf_op jit(solution)/shard_map/pallas_call | solution.py:490
  300.7 4.0 %reduce-scatter.8.cloned.1.call-done.refs_4_ = bf16[144,768]{1,0:T(8,128)(2,1)} async-done(((bf16[576,768]{1,0:T(8,128)(2,1)}), bf16[144,768]{1,0:T(8,128)(2,1)}) %reduce-scatter.8.cloned.1.call-update) | async-done | bytes 221200 | tf_op jit(solution)/shard_map/reduce_scatter | solution.py:1454
  304.6 0.9 dynamic-slice_bitcast_fusion
  308.5 3.9 %shard_map.223 = (f32[24,2304]{1,0:T(8,128)}, f32[24,768]{1,0:T(8,128)}, f32[24,3072]{1,0:T(8,128)}, f32[96,768]{1,0:T(8,128)}, f32[1,96]{1,0:T(1,128)}, /*index=5*/f32[4,24]{1,0:T(4,128)}) custom-call(s32[20]{0:T(128)} %concatenate.25.refs_0_, f32[2,384]{1,0:T(2,128)} %reshape_reshape.6.refs_1_, f32[2,384]{1,0:T(2,128)} %reshape_reshape.7.refs_2_, ...), custom_call_target="tpu_custom_call" | custom-call | flops 1 | bytes 1 | tf_op jit(solution)/shard_map/pallas_call | solution.py:490
  312.4 1.3 slice_bitcast_fusion.5
  (176 shorter events, 20.8 us)
Async XLA Ops:
  7.2 54.3 %all-gather.3.cloned.1.call-start = ((), (), s32[]{:S(2)}) async-start(), calls=%async_computation.9 | async-start | bytes 1843200 | tf_op jit(solution)/shard_map/all_gather | solution.py:1356
  7.8 3.1 copy-start.39
  7.8 3.1 copy-start.4
  10.8 4.8 %copy-start.40 = (s32[1,16]{1,0:T(1,128)S(1)}, s32[1,16]{1,0:T(1,128)}, u32[]{:S(2)}) copy-start(s32[1,16]{1,0:T(1,128)} %param.15) | copy-start | bytes 196
  10.8 5.3 %copy-start.32 = (bf16[768]{0:T(1024)(128)(2,1)S(1)}, bf16[768]{0:T(1024)(128)(2,1)}, u32[]{:S(2)}) copy-start(bf16[768]{0:T(1024)(128)(2,1)} %param.19) | copy-start | bytes 4612
  10.8 5.3 %copy-start.33 = (bf16[192]{0:T(256)(128)(2,1)S(1)}, bf16[192]{0:T(256)(128)(2,1)}, u32[]{:S(2)}) copy-start(bf16[192]{0:T(256)(128)(2,1)} %param.21) | copy-start | bytes 1156
  10.8 5.3 %copy-start.34 = (bf16[192]{0:T(256)(128)(2,1)S(1)}, bf16[192]{0:T(256)(128)(2,1)}, u32[]{:S(2)}) copy-start(bf16[192]{0:T(256)(128)(2,1)} %param.22) | copy-start | bytes 1156
  10.8 5.3 %copy-start.35 = (bf16[192]{0:T(256)(128)(2,1)S(1)}, bf16[192]{0:T(256)(128)(2,1)}, u32[]{:S(2)}) copy-start(bf16[192]{0:T(256)(128)(2,1)} %param.23) | copy-start | bytes 1156
  10.8 5.2 %copy-start.36 = (bf16[192]{0:T(256)(128)(2,1)S(1)}, bf16[192]{0:T(256)(128)(2,1)}, u32[]{:S(2)}) copy-start(bf16[192]{0:T(256)(128)(2,1)} %param.24) | copy-start | bytes 1156
  10.9 6.6 %copy-start.10 = (bf16[192,2304]{1,0:T(8,128)(2,1)S(1)}, bf16[192,2304]{1,0:T(8,128)(2,1)}, u32[]{:S(2)}) copy-start(bf16[192,2304]{1,0:T(8,128)(2,1)} %param.16) | copy-start | bytes 2654212
  11.1 6.8 %copy-start.9 = (bf16[256,768]{1,0:T(8,128)(2,1)}, bf16[256,768]{1,0:T(8,128)(2,1)S(1)}, u32[]{:S(2)}) copy-start(bf16[256,768]{1,0:T(8,128)(2,1)S(1)} %get-tuple-element.219.refs_5_) | copy-start | bytes 1179652
  11.1 16.8 %collective-permute-start.1 = (bf16[256,768]{1,0:T(8,128)(2,1)S(1)}, bf16[256,768]{1,0:T(8,128)(2,1)S(1)}, u32[]{:S(2)}, u32[]{:S(2)}) collective-permute-start(bf16[256,768]{1,0:T(8,128)(2,1)S(1)} %get-tuple-element.219.refs_5_), channel_id=1, source_target_pairs={{0,16},{4,20},{8,24},{12,28},{16,0},{20,4},{24,8},{28,12},{1,17},{... | collective-permute-start | bytes 1179656 | tf_op jit(solution)/shard_map/ppermute | solution.py:438
  14.1 13.8 %collective-permute-start = (bf16[256,768]{1,0:T(8,128)(2,1)S(1)}, bf16[256,768]{1,0:T(8,128)(2,1)S(1)}, u32[]{:S(2)}, u32[]{:S(2)}) collective-permute-start(bf16[256,768]{1,0:T(8,128)(2,1)S(1)} %get-tuple-element.219.refs_5_), channel_id=1, source_target_pairs={{0,8},{4,12},{8,0},{12,4},{16,24},{20,28},{24,16},{28,20},{1,9},{5... | collective-permute-start | bytes 1179656 | tf_op jit(solution)/shard_map/ppermute | solution.py:438
  15.6 1.9 collective-permute-start.2
  18.8 37.3 %all-to-all-start = ((bf16[4,112,576]{2,1,0:T(8,128)(2,1)}), bf16[4,112,576]{2,1,0:T(8,128)(2,1)}, u32[]{:S(2)}, u32[]{:S(2)}) async-start(bf16[4,112,576]{2,1,0:T(8,128)(2,1)} %broadcast_in_dim.92), calls=%async_computation | async-start | bytes 1146880 | tf_op jit(solution)/shard_map/all_to_all | solution.py:1328
  23.7 11.1 %collective-permute-start.4 = (bf16[256,768]{1,0:T(8,128)(2,1)}, bf16[256,768]{1,0:T(8,128)(2,1)S(1)}, u32[]{:S(2)}, u32[]{:S(2)}) collective-permute-start(bf16[256,768]{1,0:T(8,128)(2,1)} %collective-permute-done.2.refs_6_), channel_id=1, source_target_pairs={{0,16},{4,20},{8,24},{12,28},{16,0},{20,4},{24,8},{28,12},{1,17},{... | collective-permute-start | bytes 1179656 | tf_op jit(solution)/shard_map/ppermute | solution.py:438
  24.2 10.8 %collective-permute-start.3 = (bf16[256,768]{1,0:T(8,128)(2,1)}, bf16[256,768]{1,0:T(8,128)(2,1)S(1)}, u32[]{:S(2)}, u32[]{:S(2)}) collective-permute-start(bf16[256,768]{1,0:T(8,128)(2,1)} %collective-permute-done.2.refs_6_), channel_id=1, source_target_pairs={{0,8},{4,12},{8,0},{12,4},{16,24},{20,28},{24,16},{28,20},{1,9},{5... | collective-permute-start | bytes 1179656 | tf_op jit(solution)/shard_map/ppermute | solution.py:438
  27.9 35.8 %copy-start.20 = (bf16[256,768]{1,0:T(8,128)(2,1)}, bf16[256,768]{1,0:T(8,128)(2,1)S(1)}, u32[]{:S(2)}) copy-start(bf16[256,768]{1,0:T(8,128)(2,1)S(1)} %collective-permute-done.1.refs_9_) | copy-start | bytes 1179652
  27.9 33.6 %copy-start.21 = (bf16[256,768]{1,0:T(8,128)(2,1)}, bf16[256,768]{1,0:T(8,128)(2,1)S(1)}, u32[]{:S(2)}) copy-start(bf16[256,768]{1,0:T(8,128)(2,1)S(1)} %collective-permute-done.refs_7_) | copy-start | bytes 1179652
  34.7 26.8 %copy-start.22 = (bf16[256,768]{1,0:T(8,128)(2,1)}, bf16[256,768]{1,0:T(8,128)(2,1)S(1)}, u32[]{:S(2)}) copy-start(bf16[256,768]{1,0:T(8,128)(2,1)S(1)} %collective-permute-done.4.refs_10_) | copy-start | bytes 1179652
  35.0 26.6 %copy-start.23 = (bf16[256,768]{1,0:T(8,128)(2,1)}, bf16[256,768]{1,0:T(8,128)(2,1)S(1)}, u32[]{:S(2)}) copy-start(bf16[256,768]{1,0:T(8,128)(2,1)S(1)} %collective-permute-done.3.refs_8_) | copy-start | bytes 1179652
  35.0 21.1 %collective-permute-start.5 = (bf16[256,768]{1,0:T(8,128)(2,1)S(1)}, bf16[256,768]{1,0:T(8,128)(2,1)S(1)}, u32[]{:S(2)}, u32[]{:S(2)}) collective-permute-start(bf16[256,768]{1,0:T(8,128)(2,1)S(1)} %collective-permute-done.refs_7_), channel_id=1, source_target_pairs={{0,16},{4,20},{8,24},{12,28},{16,0},{20,4},{24,8},{28,12},{1,17},{... | collective-permute-start | bytes 1179656 | tf_op jit(solution)/shard_map/ppermute | solution.py:438
  36.5 19.6 %collective-permute-start.6 = (bf16[256,768]{1,0:T(8,128)(2,1)S(1)}, bf16[256,768]{1,0:T(8,128)(2,1)S(1)}, u32[]{:S(2)}, u32[]{:S(2)}) collective-permute-start(bf16[256,768]{1,0:T(8,128)(2,1)S(1)} %collective-permute-done.4.refs_10_), channel_id=1, source_target_pairs={{0,8},{4,12},{8,0},{12,4},{16,24},{20,28},{24,16},{28,20},{1,9},{5... | collective-permute-start | bytes 1179656 | tf_op jit(solution)/shard_map/ppermute | solution.py:438
  56.1 5.5 %copy-start.24 = (bf16[256,768]{1,0:T(8,128)(2,1)}, bf16[256,768]{1,0:T(8,128)(2,1)S(1)}, u32[]{:S(2)}) copy-start(bf16[256,768]{1,0:T(8,128)(2,1)S(1)} %collective-permute-done.5.refs_11_) | copy-start | bytes 1179652
  56.1 5.4 %copy-start.25 = (bf16[256,768]{1,0:T(8,128)(2,1)}, bf16[256,768]{1,0:T(8,128)(2,1)S(1)}, u32[]{:S(2)}) copy-start(bf16[256,768]{1,0:T(8,128)(2,1)S(1)} %collective-permute-done.6.refs_12_) | copy-start | bytes 1179652
  56.1 7.6 %collective-permute-start.7 = (bf16[4,112,576]{2,1,0:T(8,128)(2,1)}, bf16[4,112,576]{2,1,0:T(8,128)(2,1)}, u32[]{:S(2)}, u32[]{:S(2)}) collective-permute-start(bf16[4,112,576]{2,1,0:T(8,128)(2,1)} %all-to-all-done.refs_13_), channel_id=1, source_target_pairs={{0,4},{4,0},{8,12},{12,8},{16,20},{20,16},{24,28},{28,24},{1,5},{5... | collective-permute-start | bytes 1548296 | tf_op jit(solution)/shard_map/ppermute | solution.py:438
  63.7 18.2 %copy-start = (bf16[3,240,768]{2,1,0:T(8,128)(2,1)}, bf16[3,240,768]{2,1,0:T(8,128)(2,1)S(1)}, u32[]{:S(2)}) copy-start(bf16[3,240,768]{2,1,0:T(8,128)(2,1)S(1)} %broadcast_select_fusion.refs_6_.refs_8_) | copy-start | bytes 3317764
  63.8 42.4 %collective-permute-start.12 = (bf16[3,240,768]{2,1,0:T(8,128)(2,1)S(1)}, bf16[3,240,768]{2,1,0:T(8,128)(2,1)}, u32[]{:S(2)}, u32[]{:S(2)}) collective-permute-start(bf16[3,240,768]{2,1,0:T(8,128)(2,1)S(1)} %broadcast_select_fusion.refs_6_.refs_8_), channel_id=1, source_target_pairs={{0,24},{4,28},{8,16},{12,20},{16,8},{20,12},{24,0},{28,4},{1,25},{... | collective-permute-start | bytes 3317768 | tf_op jit(solution)/shard_map/ppermute | solution.py:438
  66.2 48.5 %collective-permute-start.11 = (bf16[3,240,768]{2,1,0:T(8,128)(2,1)S(1)}, bf16[3,240,768]{2,1,0:T(8,128)(2,1)}, u32[]{:S(2)}, u32[]{:S(2)}) collective-permute-start(bf16[3,240,768]{2,1,0:T(8,128)(2,1)S(1)} %broadcast_select_fusion.refs_6_.refs_8_), channel_id=1, source_target_pairs={{0,16},{4,20},{8,24},{12,28},{16,0},{20,4},{24,8},{28,12},{1,17},{... | collective-permute-start | bytes 3317768 | tf_op jit(solution)/shard_map/ppermute | solution.py:438
  66.7 48.0 %collective-permute-start.10 = (bf16[3,240,768]{2,1,0:T(8,128)(2,1)S(1)}, bf16[3,240,768]{2,1,0:T(8,128)(2,1)}, u32[]{:S(2)}, u32[]{:S(2)}) collective-permute-start(bf16[3,240,768]{2,1,0:T(8,128)(2,1)S(1)} %broadcast_select_fusion.refs_6_.refs_8_), channel_id=1, source_target_pairs={{0,8},{4,12},{8,0},{12,4},{16,24},{20,28},{24,16},{28,20},{1,9},{5... | collective-permute-start | bytes 3317768 | tf_op jit(solution)/shard_map/ppermute | solution.py:438
  82.0 3.4 %collective-permute-start.9 = (bf16[4,384,256]{2,1,0:T(8,128)(2,1)}, bf16[4,384,256]{2,1,0:T(8,128)(2,1)S(1)}, u32[]{:S(2)}, u32[]{:S(2)}) collective-permute-start(bf16[4,384,256]{2,1,0:T(8,128)(2,1)} %get-tuple-element.130.refs_4_.refs_1_.refs_8_), channel_id=1, source_target_pairs={{0,4},{8,12},{16,20},{24,28},{1,5},{9,13},{17,21},{25,29},{2,6},{1... | collective-permute-start | bytes 2359304 | tf_op jit(solution)/shard_map/ppermute | solution.py:1417
  83.3 3.4 %collective-permute-start.8 = (bf16[4,384,256]{2,1,0:T(8,128)(2,1)}, bf16[4,384,256]{2,1,0:T(8,128)(2,1)S(1)}, u32[]{:S(2)}, u32[]{:S(2)}) collective-permute-start(bf16[4,384,256]{2,1,0:T(8,128)(2,1)} %get-tuple-element.129.refs_3_.refs_0_.refs_7_), channel_id=1, source_target_pairs={{0,4},{8,12},{16,20},{24,28},{1,5},{9,13},{17,21},{25,29},{2,6},{1... | collective-permute-start | bytes 2359304 | tf_op jit(solution)/shard_map/ppermute | solution.py:1417
  114.7 16.1 %all-to-all-start.1 = ((bf16[8,192,256]{2,1,0:T(8,128)(2,1)}), bf16[8,192,256]{2,1,0:T(8,128)(2,1)S(1)}, u32[]{:S(2)}, u32[]{:S(2)}) async-start(bf16[8,192,256]{2,1,0:T(8,128)(2,1)} %get-tuple-element.128), calls=%async_computation.1 | async-start | bytes 1572864 | tf_op jit(solution)/shard_map/all_to_all | solution.py:1319
  118.3 2.0 copy-start.6
  118.3 120.1 %reduce-scatter.6.cloned.1.call-start = ((), (), s32[]{:S(2)}) async-start(), calls=%async_computation.7 | async-start | bytes 2949120 | tf_op jit(solution)/shard_map/reduce_scatter | solution.py:1429
  120.3 18.4 %collective-permute-start.14 = (bf16[512,768]{1,0:T(8,128)(2,1)S(1)}, bf16[512,768]{1,0:T(8,128)(2,1)S(1)}, u32[]{:S(2)}, u32[]{:S(2)}) collective-permute-start(bf16[512,768]{1,0:T(8,128)(2,1)S(1)} %bitcast.76), channel_id=1, source_target_pairs={{0,4},{4,0},{8,12},{12,8},{16,20},{20,16},{24,28},{28,24},{1,5},{5... | collective-permute-start | bytes 2359304 | tf_op jit(solution)/shard_map/ppermute | solution.py:438
  138.0 2.6 collective-permute-start.13
  138.7 1.9 copy-start.16
  166.2 1.4 copy-start.37
  167.3 2.3 collective-permute-start.15
  167.6 3.2 collective-permute-start.16
  179.8 3.7 %copy-start.30 = (f32[1,1536]{1,0:T(1,128)S(1)}, f32[1,1536]{1,0:T(1,128)}, u32[]{:S(2)}) copy-start(f32[1,1536]{1,0:T(1,128)} %get-tuple-element.155) | copy-start | bytes 18436
  179.8 16.1 %all-to-all-start.2 = ((bf16[8,192,256]{2,1,0:T(8,128)(2,1)}), bf16[8,192,256]{2,1,0:T(8,128)(2,1)S(1)}, u32[]{:S(2)}, u32[]{:S(2)}) async-start(bf16[8,192,256]{2,1,0:T(8,128)(2,1)} %get-tuple-element.154), calls=%async_computation.2 | async-start | bytes 1572864 | tf_op jit(solution)/shard_map/all_to_all | solution.py:1319
  183.3 95.6 %reduce-scatter.10.cloned.1.call-start = ((), (), s32[]{:S(2)}) async-start(), calls=%async_computation.10 | async-start | bytes 1382400
  183.5 6.4 %copy-start.31 = (f32[8,768]{1,0:T(8,128)S(1)}, f32[8,768]{1,0:T(8,128)}, u32[]{:S(2)}) copy-start(f32[8,768]{1,0:T(8,128)} %get-tuple-element.156) | copy-start | bytes 73732
  195.9 3.5 %copy-start.3 = (bf16[8,192,256]{2,1,0:T(8,128)(2,1)}, bf16[8,192,256]{2,1,0:T(8,128)(2,1)S(1)}, u32[]{:S(2)}) copy-start(bf16[8,192,256]{2,1,0:T(8,128)(2,1)S(1)} %all-to-all-done.2.refs_13_) | copy-start | bytes 2359300
  195.9 32.2 %collective-permute-start.19 = (bf16[4,144,768]{2,1,0:T(8,128)(2,1)}, bf16[4,144,768]{2,1,0:T(8,128)(2,1)S(1)}, u32[]{:S(2)}, u32[]{:S(2)}) collective-permute-start(bf16[4,144,768]{2,1,0:T(8,128)(2,1)} %get-tuple-element.168), channel_id=1, source_target_pairs={{0,8},{4,12},{8,0},{12,4},{16,24},{20,28},{24,16},{28,20},{1,9},{5... | collective-permute-start | bytes 2654216 | tf_op jit(solution)/shard_map/ppermute | solution.py:438
  196.4 40.6 %collective-permute-start.20 = (bf16[4,144,768]{2,1,0:T(8,128)(2,1)}, bf16[4,144,768]{2,1,0:T(8,128)(2,1)S(1)}, u32[]{:S(2)}, u32[]{:S(2)}) collective-permute-start(bf16[4,144,768]{2,1,0:T(8,128)(2,1)} %get-tuple-element.169), channel_id=1, source_target_pairs={{0,16},{4,20},{8,24},{12,28},{16,0},{20,4},{24,8},{28,12},{1,17},{... | collective-permute-start | bytes 2654216 | tf_op jit(solution)/shard_map/ppermute | solution.py:438
  197.0 40.0 %collective-permute-start.21 = (bf16[4,144,768]{2,1,0:T(8,128)(2,1)}, bf16[4,144,768]{2,1,0:T(8,128)(2,1)S(1)}, u32[]{:S(2)}, u32[]{:S(2)}) collective-permute-start(bf16[4,144,768]{2,1,0:T(8,128)(2,1)} %get-tuple-element.170), channel_id=1, source_target_pairs={{0,24},{4,28},{8,16},{12,20},{16,8},{20,12},{24,0},{28,4},{1,25},{... | collective-permute-start | bytes 2654216 | tf_op jit(solution)/shard_map/ppermute | solution.py:438
  199.4 37.6 %copy-start.11 = (bf16[4,144,768]{2,1,0:T(8,128)(2,1)S(1)}, bf16[4,144,768]{2,1,0:T(8,128)(2,1)}, u32[]{:S(2)}) copy-start(bf16[4,144,768]{2,1,0:T(8,128)(2,1)} %get-tuple-element.172) | copy-start | bytes 2654212
  225.5 12.8 %collective-permute-start.17 = (bf16[4,384,256]{2,1,0:T(8,128)(2,1)}, bf16[4,384,256]{2,1,0:T(8,128)(2,1)S(1)}, u32[]{:S(2)}, u32[]{:S(2)}) collective-permute-start(bf16[4,384,256]{2,1,0:T(8,128)(2,1)} %get-tuple-element.165), channel_id=1, source_target_pairs={{4,0},{12,8},{20,16},{28,24},{5,1},{13,9},{21,17},{29,25},{6,2},{1... | collective-permute-start | bytes 2359304 | tf_op jit(solution)/shard_map/ppermute | solution.py:1448
  226.8 11.5 %collective-permute-start.18 = (bf16[4,384,256]{2,1,0:T(8,128)(2,1)}, bf16[4,384,256]{2,1,0:T(8,128)(2,1)S(1)}, u32[]{:S(2)}, u32[]{:S(2)}) collective-permute-start(bf16[4,384,256]{2,1,0:T(8,128)(2,1)} %get-tuple-element.166), channel_id=1, source_target_pairs={{4,0},{12,8},{20,16},{28,24},{5,1},{13,9},{21,17},{29,25},{6,2},{1... | collective-permute-start | bytes 2359304 | tf_op jit(solution)/shard_map/ppermute | solution.py:1448
  253.1 18.9 %copy-start.8 = (bf16[4,256,768]{2,1,0:T(8,128)(2,1)S(1)}, bf16[4,256,768]{2,1,0:T(8,128)(2,1)}, u32[]{:S(2)}) copy-start(bf16[4,256,768]{2,1,0:T(8,128)(2,1)} %get-tuple-element.184) | copy-start | bytes 4718596
  253.1 51.5 %reduce-scatter.8.cloned.1.call-start = ((), (), s32[]{:S(2)}) async-start(), calls=%async_computation.8 | async-start | bytes 1105920 | tf_op jit(solution)/shard_map/reduce_scatter | solution.py:1454
  253.2 18.7 %collective-permute-start.22 = (bf16[2,256,768]{2,1,0:T(8,128)(2,1)}, bf16[2,256,768]{2,1,0:T(8,128)(2,1)S(1)}, u32[]{:S(2)}, u32[]{:S(2)}) collective-permute-start(bf16[2,256,768]{2,1,0:T(8,128)(2,1)} %get-tuple-element.185), channel_id=1, source_target_pairs={{0,8},{4,12},{8,0},{12,4},{16,24},{20,28},{24,16},{28,20},{1,9},{5... | collective-permute-start | bytes 2359304 | tf_op jit(solution)/shard_map/ppermute | solution.py:438
  253.5 18.5 %collective-permute-start.24 = (bf16[2,256,768]{2,1,0:T(8,128)(2,1)}, bf16[2,256,768]{2,1,0:T(8,128)(2,1)S(1)}, u32[]{:S(2)}, u32[]{:S(2)}) collective-permute-start(bf16[2,256,768]{2,1,0:T(8,128)(2,1)} %get-tuple-element.186), channel_id=1, source_target_pairs={{0,16},{4,20},{8,24},{12,28},{16,0},{20,4},{24,8},{28,12},{1,17},{... | collective-permute-start | bytes 2359304 | tf_op jit(solution)/shard_map/ppermute | solution.py:438
  273.1 9.4 %collective-permute-start.25 = (bf16[256,768]{1,0:T(8,128)(2,1)}, bf16[256,768]{1,0:T(8,128)(2,1)S(1)}, u32[]{:S(2)}, u32[]{:S(2)}) collective-permute-start(bf16[256,768]{1,0:T(8,128)(2,1)} %get-tuple-element.213), channel_id=1, source_target_pairs={{0,8},{4,12},{8,0},{12,4},{16,24},{20,28},{24,16},{28,20},{1,9},{5... | collective-permute-start | bytes 1179656 | tf_op jit(solution)/shard_map/ppermute | solution.py:438
  274.7 9.0 %collective-permute-start.23 = (bf16[256,768]{1,0:T(8,128)(2,1)}, bf16[256,768]{1,0:T(8,128)(2,1)}, u32[]{:S(2)}, u32[]{:S(2)}) collective-permute-start(bf16[256,768]{1,0:T(8,128)(2,1)} %get-tuple-element.214), channel_id=1, source_target_pairs={{0,16},{4,20},{8,24},{12,28},{16,0},{20,4},{24,8},{28,12},{1,17},{... | collective-permute-start | bytes 1179656 | tf_op jit(solution)/shard_map/ppermute | solution.py:438
  286.0 8.8 %collective-permute-start.26 = (bf16[256,768]{1,0:T(8,128)(2,1)S(1)}, bf16[256,768]{1,0:T(8,128)(2,1)S(1)}, u32[]{:S(2)}, u32[]{:S(2)}) collective-permute-start(bf16[256,768]{1,0:T(8,128)(2,1)S(1)} %get-tuple-element.211), channel_id=1, source_target_pairs={{0,4},{4,0},{8,12},{12,8},{16,20},{20,16},{24,28},{28,24},{1,5},{5... | collective-permute-start | bytes 1179656 | tf_op jit(solution)/shard_map/ppermute | solution.py:438
  286.0 20.9 %all-to-all-start.3 = ((bf16[8,48,640]{2,1,0:T(8,128)(2,1)}), bf16[8,48,640]{2,1,0:T(8,128)(2,1)S(1)}, u32[]{:S(2)}, u32[]{:S(2)}) async-start(bf16[8,48,640]{2,1,0:T(8,128)(2,1)} %pad_maximum_fusion.1), calls=%async_computation.4 | async-start | bytes 983040 | tf_op jit(solution)/shard_map/all_to_all | solution.py:1319
  291.3 15.6 %collective-permute-start.29 = (bf16[96,768]{1,0:T(8,128)(2,1)S(1)}, bf16[96,768]{1,0:T(8,128)(2,1)S(1)}, u32[]{:S(2)}, u32[]{:S(2)}) collective-permute-start(bf16[96,768]{1,0:T(8,128)(2,1)S(1)} %get-tuple-element.220), channel_id=1, source_target_pairs={{0,24},{4,28},{8,16},{12,20},{16,8},{20,12},{24,0},{28,4},{1,25},{... | collective-permute-start | bytes 442376 | tf_op jit(solution)/shard_map/ppermute | solution.py:438
  294.2 12.7 %collective-permute-start.28 = (bf16[96,768]{1,0:T(8,128)(2,1)S(1)}, bf16[96,768]{1,0:T(8,128)(2,1)S(1)}, u32[]{:S(2)}, u32[]{:S(2)}) collective-permute-start(bf16[96,768]{1,0:T(8,128)(2,1)S(1)} %get-tuple-element.221), channel_id=1, source_target_pairs={{0,16},{4,20},{8,24},{12,28},{16,0},{20,4},{24,8},{28,12},{1,17},{... | collective-permute-start | bytes 442376 | tf_op jit(solution)/shard_map/ppermute | solution.py:438
  294.7 12.2 %collective-permute-start.27 = (bf16[96,768]{1,0:T(8,128)(2,1)S(1)}, bf16[96,768]{1,0:T(8,128)(2,1)S(1)}, u32[]{:S(2)}, u32[]{:S(2)}) collective-permute-start(bf16[96,768]{1,0:T(8,128)(2,1)S(1)} %get-tuple-element.222), channel_id=1, source_target_pairs={{0,8},{4,12},{8,0},{12,4},{16,24},{20,28},{24,16},{28,20},{1,9},{5... | collective-permute-start | bytes 442376 | tf_op jit(solution)/shard_map/ppermute | solution.py:438
  305.5 1.4 collective-permute-start.30
  (16 other events, 14.4 us)
Sparse Core Ops, SparseCore 0:
  11.0 50.4 all-gather.2
  166.4 45.2 reduce-scatter.5
  253.2 25.6 reduce-scatter.9
  281.1 23.5 reduce-scatter.7
